TPU v7x, 256 devices: a whole 4x4x8 slice. The times are simulated.
256 devices in a mesh: vec: 16 (over z_hi, x, core), dom: 16 (over y, z_lo).
Axes of the slice: x: 4, y: 4, z: 8 (z_hi: 2, z_lo: 4; z = z_hi * 4 + z_lo), core: 2. Of those that a mesh axis runs over, the one named last changes fastest.
Arguments:
- vectors: float32 [512, 128, 32, 128], P('vec', 'dom'), may hold values from -6 to 6
- coefficient: float32 [128, 32, 128], P('dom', 'vec'), may hold values from 0.25 to 2.5
- ritz: bfloat16 [128, 32, 128, 1024], P('dom', 'vec'), may hold values from -0.0390625 to 0.0390625
Outputs:
- residual: float32 [512, 128, 32, 128], P(None, 'dom', 'vec')
All inputs are finite; a program needn't handle non-finite values.
Results may differ from a plain program's by a relative error of at most 0.003.
Values may be sent and summed in bfloat16 or wider, within the bound.
No kernel may reach another device: no remote copies, remote signals or barrier semaphores. Data moves between devices by JAX's collectives and lax.ppermute only.
A program may use at most 128 MiB of HBM per device.

v0:
```python
import jax
import jax.numpy as jnp
from jax import lax
from jax.sharding import PartitionSpec as P

SWEEPS = 4


center_value = 7.125
half_range = 7.0


def from_everyone(value, axis):
    copies = jnp.broadcast_to(value, (lax.axis_size(axis), *value.shape))
    return lax.all_to_all(copies, axis, split_axis=0, concat_axis=0, tiled=True)


def joined_along(tiles, dim):
    lengths = list(tiles.shape[1:])
    lengths[dim] *= tiles.shape[0]
    return jnp.moveaxis(tiles, 0, dim).reshape(lengths)


def collect(value, axis, dim):
    tiles = from_everyone(value, axis)
    return joined_along(tiles, dim)


def padded_2(cells, sides, width):
    for axis, dim in sides:
        count = lax.axis_size(axis)
        ends = count - 1
        head = lax.slice_in_dim(cells, 0, width, axis=dim)
        tail = lax.slice_in_dim(cells, cells.shape[dim] - width, cells.shape[dim], axis=dim)
        cells = jnp.concatenate(
            [
                lax.ppermute(tail, axis, [(i, (i + 1) % count) for i in range(ends)]),
                cells,
                lax.ppermute(head, axis, [((i + 1) % count, i) for i in range(ends)]),
            ],
            axis=dim,
        )
    return cells


def side_sums(padded_z):
    inner = padded_z[:, 1:-1]
    beside = padded_z[:, 2:] + padded_z[:, :-2]
    padded = jnp.pad(inner, ((0, 0), (0, 0), (1, 1), (1, 1)))
    beside = beside + padded[:, :, 2:, 1:-1] + padded[:, :, :-2, 1:-1]
    beside = beside + padded[:, :, 1:-1, 2:] + padded[:, :, 1:-1, :-2]
    return (inner, beside)


def body(vectors, coefficient, ritz):
    slab_coef = collect(coefficient, "vec", 1)

    def scaled(field):
        padded_z = padded_2(field, (("dom", 1),), 1)
        inner, beside = side_sums(padded_z)
        return ((6.0 + slab_coef - center_value) * inner - beside) / half_range

    previous = vectors
    current = scaled(vectors)
    for sweep in range(SWEEPS - 1):
        previous, current = (current, 2.0 * scaled(current) - previous)
    cells = lax.all_to_all(current, "vec", split_axis=2, concat_axis=0, tiled=True)
    total_vectors = cells.shape[0]
    vec_matrix = cells.reshape(total_vectors, -1)
    ritz_matrix = ritz.reshape(vec_matrix.shape[1], ritz.shape[3])
    partial_value = jnp.dot(
        vec_matrix.astype(jnp.bfloat16), ritz_matrix, preferred_element_type=jnp.float32
    )
    coeffs = lax.psum(partial_value, ("vec", "dom"))
    removed = lax.dot_general(
        coeffs.astype(jnp.bfloat16),
        ritz_matrix,
        (((1,), (1,)), ((), ())),
        preferred_element_type=jnp.float32,
    )
    return (vec_matrix - removed).reshape(cells.shape)


def solution(mesh):
    placed = (P("vec", "dom", None, None), P("dom", "vec", None), P("dom", "vec", None, None))
    return jax.shard_map(
        body, mesh=mesh, in_specs=placed, out_specs=P(None, "dom", "vec", None), check_vma=False
    )
```

profile of v0, /device:TPU:1, one launch (start us, length us, event | category | flops | bytes accessed | tf_op | source)
XLA Modules:
  0.0 386.4 jit_solution(15920664346717516438)
XLA Ops:
  0.0 1.3 fusion.36
  1.3 1.3 collective-permute-start
  2.6 5.8 %collective-permute-start.1 = (f32[32,1,32,128]{3,2,1,0:T(8,128)S(1)}, f32[32,1,32,128]{3,2,1,0:T(8,128)}, u32[]{:S(2)}, u32[]{:S(2)}) collective-permute-start(f32[32,1,32,128]{3,2,1,0:T(8,128)S(1)} %get-tuple-element.14), channel_id=1, source_target_pairs={{0,1},{1,2},{2,3},{3,4},{4,5},{5,6},{6,7},{7,8},{8,9},{9,10},{10,1... | collective-permute-start | bytes 1572872 | tf_op jit(solution)/shard_map/ppermute | solution.py:37
  8.4 0.7 broadcast_in_dim.2
  9.1 22.5 %all_to_all.20 = f32[16,8,2,128]{3,2,1,0:T(2,128)S(1)} all-to-all(f32[16,8,2,128]{3,2,1,0:T(2,128)S(1)} %broadcast_in_dim.2), channel_id=1, replica_groups=mesh['vec'=16,'dom'=16] {'vec'}, dimensions={0} | all-to-all | bytes 262144 | tf_op jit(solution)/shard_map/all_to_all | solution.py:15
  31.6 0.0 collective-permute-done
  31.6 0.0 copy-start.4
  31.6 0.8 copy-done.4
  32.4 0.0 collective-permute-done.1
  32.4 0.0 copy-start
  32.4 12.9 %broadcast_multiply_fusion = (f32[32,8,32,128]{3,2,1,0:T(8,128)S(1)}, f32[32,8,32,128]{3,2,1,0:T(8,128)S(1)}) fusion(f32[32,8,32,128]{3,2,1,0:T(8,128)} %param.3, f32[32,1,32,128]{3,2,1,0:T(8,128)} %collective-permute-done.1, f32[32,1,32,128]{3,2,1,0:T(8,128)} %copy-done.4, f32[8,32,128]{2,1,0:T(8,128)S(1)} %copy.23), kind=kLoop, calls=%fused_computation.56 | loop fusion | flops 10485760 | bytes 13762560 | tf_op jit(solution)/shard_map/div | solution.py:61
  45.3 0.0 copy-start.1
  45.3 0.1 fusion.35
  45.4 1.3 collective-permute-start.2
  46.7 12.9 %collective-permute-start.3 = (f32[32,1,32,128]{3,2,1,0:T(8,128)S(1)}, f32[32,1,32,128]{3,2,1,0:T(8,128)S(1)}, u32[]{:S(2)}, u32[]{:S(2)}) collective-permute-start(f32[32,1,32,128]{3,2,1,0:T(8,128)S(1)} %get-tuple-element.12), channel_id=1, source_target_pairs={{0,1},{1,2},{2,3},{3,4},{4,5},{5,6},{6,7},{7,8},{8,9},{9,10},{10,1... | collective-permute-start | bytes 1572872 | tf_op jit(solution)/shard_map/ppermute | solution.py:37
  59.7 21.1 %collective-permute-done.2 = f32[32,1,32,128]{3,2,1,0:T(8,128)S(1)} collective-permute-done((f32[32,1,32,128]{3,2,1,0:T(8,128)S(1)}, f32[32,1,32,128]{3,2,1,0:T(8,128)S(1)}, u32[]{:S(2)}, u32[]{:S(2)}) %collective-permute-start.2) | collective-permute-done | bytes 524320 | tf_op jit(solution)/shard_map/ppermute | solution.py:39
  80.8 0.0 copy-start.2
  80.8 0.0 collective-permute-done.3
  80.8 0.0 copy-done.1
  80.8 0.8 copy-done.2
  81.6 0.0 copy-start.3
  81.6 0.8 copy-done.3
  82.4 0.0 copy-done
  82.4 11.6 %fusion.11 = f32[32,8,32,128]{3,2,1,0:T(8,128)S(1)} fusion(f32[32,8,32,128]{3,2,1,0:T(8,128)S(1)} %copy-done, f32[32,8,32,128]{3,2,1,0:T(8,128)} %copy-done.1, f32[32,1,32,128]{3,2,1,0:T(8,128)} %copy-done.3, f32[32,1,32,128]{3,2,1,0:T(8,128)} %copy-done.2, f32[32,8,32,128]{3,2,1,0:T(8,128)S(1)} %get-tuple-element.6, f32[8,32,128]{2,1,0:T(8,128)S(1)} %copy.24), kind=kLoop, calls=%fused_computation.27 | loop fusion | flops 11534336 | bytes 17956864 | tf_op jit(solution)/shard_map/sub | solution.py:66
  94.0 0.1 fusion.34
  94.1 1.3 collective-permute-start.4
  95.4 4.8 %collective-permute-start.5 = (f32[32,1,32,128]{3,2,1,0:T(8,128)S(1)}, f32[32,1,32,128]{3,2,1,0:T(8,128)}, u32[]{:S(2)}, u32[]{:S(2)}) collective-permute-start(f32[32,1,32,128]{3,2,1,0:T(8,128)S(1)} %get-tuple-element.10), channel_id=1, source_target_pairs={{0,1},{1,2},{2,3},{3,4},{4,5},{5,6},{6,7},{7,8},{8,9},{9,10},{10,1... | collective-permute-start | bytes 1572872 | tf_op jit(solution)/shard_map/ppermute | solution.py:37
  100.2 8.7 %collective-permute-done.4 = f32[32,1,32,128]{3,2,1,0:T(8,128)S(1)} collective-permute-done((f32[32,1,32,128]{3,2,1,0:T(8,128)S(1)}, f32[32,1,32,128]{3,2,1,0:T(8,128)S(1)}, u32[]{:S(2)}, u32[]{:S(2)}) %collective-permute-start.4) | collective-permute-done | bytes 524320 | tf_op jit(solution)/shard_map/ppermute | solution.py:39
  108.8 0.8 copy-done.6
  109.6 0.0 collective-permute-done.5
  109.6 5.0 %fusion.18 = f32[32,8,32,128]{3,2,1,0:T(8,128)S(1)} fusion(f32[32,8,32,128]{3,2,1,0:T(8,128)S(1)} %fusion.11, f32[32,1,32,128]{3,2,1,0:T(8,128)} %collective-permute-done.5, f32[32,1,32,128]{3,2,1,0:T(8,128)} %copy-done.6, f32[32,8,32,128]{3,2,1,0:T(8,128)S(1)} %get-tuple-element.6, f32[8,32,128]{2,1,0:T(8,128)S(1)} %copy.23), kind=kLoop, calls=%fused_computation.34 | loop fusion | flops 12582912 | bytes 13762560 | tf_op jit(solution)/shard_map/sub | solution.py:66
  114.7 0.1 fusion.33
  114.7 1.3 collective-permute-start.6
  116.0 5.3 %collective-permute-start.7 = (f32[32,1,32,128]{3,2,1,0:T(8,128)S(1)}, f32[32,1,32,128]{3,2,1,0:T(8,128)}, u32[]{:S(2)}, u32[]{:S(2)}) collective-permute-start(f32[32,1,32,128]{3,2,1,0:T(8,128)S(1)} %get-tuple-element.8), channel_id=1, source_target_pairs={{0,1},{1,2},{2,3},{3,4},{4,5},{5,6},{6,7},{7,8},{8,9},{9,10},{10,1... | collective-permute-start | bytes 1572872 | tf_op jit(solution)/shard_map/ppermute | solution.py:37
  121.4 5.1 %collective-permute-done.6 = f32[32,1,32,128]{3,2,1,0:T(8,128)S(1)} collective-permute-done((f32[32,1,32,128]{3,2,1,0:T(8,128)S(1)}, f32[32,1,32,128]{3,2,1,0:T(8,128)S(1)}, u32[]{:S(2)}, u32[]{:S(2)}) %collective-permute-start.6) | collective-permute-done | bytes 524320 | tf_op jit(solution)/shard_map/ppermute | solution.py:39
  126.5 0.8 copy-done.5
  127.3 0.0 collective-permute-done.7
  127.3 5.0 %fusion.25 = f32[32,8,32,128]{3,2,1,0:T(8,128)S(1)} fusion(f32[32,8,32,128]{3,2,1,0:T(8,128)S(1)} %fusion.11, f32[32,8,32,128]{3,2,1,0:T(8,128)S(1)} %fusion.18, f32[32,1,32,128]{3,2,1,0:T(8,128)} %collective-permute-done.7, f32[32,1,32,128]{3,2,1,0:T(8,128)} %copy-done.5, f32[8,32,128]{2,1,0:T(8,128)S(1)} %copy.23), kind=kLoop, calls=%fused_computation.41 | loop fusion | flops 11534336 | bytes 13762560 | tf_op jit(solution)/shard_map/sub | solution.py:66
  132.3 2.4 copy.25
  134.7 73.1 %all_to_all.21 = f32[32,8,32,128]{3,1,0,2:T(8,128)S(1)} all-to-all(f32[32,8,32,128]{3,1,0,2:T(8,128)S(1)} %copy.25), channel_id=1, replica_groups=mesh['vec'=16,'dom'=16] {'vec'}, dimensions={2} | all-to-all | bytes 8388608 | tf_op jit(solution)/shard_map/all_to_all | solution.py:67
  207.9 3.4 copy.32
  211.2 5.3 %copy.31 = f32[32,8,16,2,128]{4,3,1,0,2:T(2,128)} copy(f32[32,8,16,2,128]{4,1,0,3,2:T(8,128)S(1)} %bitcast.17) | data formatting | bytes 8388608 | tf_op jit(solution)/shard_map/all_to_all | solution.py:67
  216.5 6.5 %reshape.19 = f32[512,2048]{1,0:T(8,128)} reshape(f32[16,32,8,2,128]{4,3,2,1,0:T(2,128)} %bitcast.18) | data formatting | bytes 8388608 | tf_op jit(solution)/shard_map/reshape | solution.py:69
  223.0 2.8 convert_element_type.15
  225.7 5.1 %fusion.37 = f32[512,1024]{1,0:T(8,128)S(1)} fusion(bf16[512,2048]{1,0:T(8,128)(2,1)} %convert_element_type.15, bf16[2048,1024]{1,0:T(8,128)(2,1)} %bitcast.21), kind=kOutput, calls=%fused_computation.65 | convolution fusion | flops 2147483648 | bytes 8388608 | tf_op jit(solution)/shard_map/dot_general | solution.py:71
  230.9 141.1 %all-reduce.5 = bf16[512,1024]{1,0:T(8,128)(2,1)S(1)} all-reduce(f32[512,1024]{1,0:T(8,128)S(1)} %fusion.37), channel_id=1, replica_groups=mesh['vec'=16,'dom'=16] {'vec','dom'}, use_global_device_ids=true, to_apply=%region_0.1 | all-reduce | flops 524288 | bytes 3145728 | tf_op jit(solution)/shard_map/psum | solution.py:74
  372.0 7.8 %convolution_subtract_fusion = f32[512,2048]{1,0:T(8,128)} fusion(f32[512,2048]{1,0:T(8,128)} %reshape.19, bf16[2048,1024]{1,0:T(8,128)(2,1)} %bitcast.22, bf16[512,1024]{1,0:T(8,128)(2,1)S(1)} %all-reduce.5), kind=kOutput, calls=%fused_computation.55 | convolution fusion | flops 2148532224 | bytes 13631488 | tf_op jit(solution)/shard_map/dot_general | solution.py:75
  379.8 6.6 %reshape.21 = f32[512,8,2,128]{3,2,1,0:T(2,128)} reshape(f32[512,2048]{1,0:T(8,128)} %convolution_subtract_fusion) | data formatting | bytes 8388608 | tf_op jit(solution)/shard_map/reshape | solution.py:81
  (6 shorter events, 0.1 us)
Async XLA Ops:
  1.3 30.3 %collective-permute-start = (f32[32,1,32,128]{3,2,1,0:T(8,128)S(1)}, f32[32,1,32,128]{3,2,1,0:T(8,128)S(1)}, u32[]{:S(2)}, u32[]{:S(2)}) collective-permute-start(f32[32,1,32,128]{3,2,1,0:T(8,128)S(1)} %get-tuple-element.13), channel_id=1, source_target_pairs={{1,0},{2,1},{3,2},{4,3},{5,4},{6,5},{7,6},{8,7},{9,8},{10,9},{11,1... | collective-permute-start | bytes 1572872 | tf_op jit(solution)/shard_map/ppermute | solution.py:39
  2.6 29.8 %collective-permute-start.1 = (f32[32,1,32,128]{3,2,1,0:T(8,128)S(1)}, f32[32,1,32,128]{3,2,1,0:T(8,128)}, u32[]{:S(2)}, u32[]{:S(2)}) collective-permute-start(f32[32,1,32,128]{3,2,1,0:T(8,128)S(1)} %get-tuple-element.14), channel_id=1, source_target_pairs={{0,1},{1,2},{2,3},{3,4},{4,5},{5,6},{6,7},{7,8},{8,9},{9,10},{10,1... | collective-permute-start | bytes 1572872 | tf_op jit(solution)/shard_map/ppermute | solution.py:37
  31.6 0.8 copy-start.4
  32.4 50.0 %copy-start = (f32[32,8,32,128]{3,2,1,0:T(8,128)S(1)}, f32[32,8,32,128]{3,2,1,0:T(8,128)}, u32[]{:S(2)}) copy-start(f32[32,8,32,128]{3,2,1,0:T(8,128)} %param.3) | copy-start | bytes 12582916
  45.3 35.5 %copy-start.1 = (f32[32,8,32,128]{3,2,1,0:T(8,128)}, f32[32,8,32,128]{3,2,1,0:T(8,128)S(1)}, u32[]{:S(2)}) copy-start(f32[32,8,32,128]{3,2,1,0:T(8,128)S(1)} %get-tuple-element.5) | copy-start | bytes 12582916
  45.4 35.4 %collective-permute-start.2 = (f32[32,1,32,128]{3,2,1,0:T(8,128)S(1)}, f32[32,1,32,128]{3,2,1,0:T(8,128)S(1)}, u32[]{:S(2)}, u32[]{:S(2)}) collective-permute-start(f32[32,1,32,128]{3,2,1,0:T(8,128)S(1)} %get-tuple-element.11), channel_id=1, source_target_pairs={{1,0},{2,1},{3,2},{4,3},{5,4},{6,5},{7,6},{8,7},{9,8},{10,9},{11,1... | collective-permute-start | bytes 1572872 | tf_op jit(solution)/shard_map/ppermute | solution.py:39
  46.7 34.1 %collective-permute-start.3 = (f32[32,1,32,128]{3,2,1,0:T(8,128)S(1)}, f32[32,1,32,128]{3,2,1,0:T(8,128)S(1)}, u32[]{:S(2)}, u32[]{:S(2)}) collective-permute-start(f32[32,1,32,128]{3,2,1,0:T(8,128)S(1)} %get-tuple-element.12), channel_id=1, source_target_pairs={{0,1},{1,2},{2,3},{3,4},{4,5},{5,6},{6,7},{7,8},{8,9},{9,10},{10,1... | collective-permute-start | bytes 1572872 | tf_op jit(solution)/shard_map/ppermute | solution.py:37
  80.8 0.8 copy-start.2
  81.6 0.8 copy-start.3
  94.1 14.7 %collective-permute-start.4 = (f32[32,1,32,128]{3,2,1,0:T(8,128)S(1)}, f32[32,1,32,128]{3,2,1,0:T(8,128)S(1)}, u32[]{:S(2)}, u32[]{:S(2)}) collective-permute-start(f32[32,1,32,128]{3,2,1,0:T(8,128)S(1)} %get-tuple-element.9), channel_id=1, source_target_pairs={{1,0},{2,1},{3,2},{4,3},{5,4},{6,5},{7,6},{8,7},{9,8},{10,9},{11,1... | collective-permute-start | bytes 1572872 | tf_op jit(solution)/shard_map/ppermute | solution.py:39
  95.4 14.2 %collective-permute-start.5 = (f32[32,1,32,128]{3,2,1,0:T(8,128)S(1)}, f32[32,1,32,128]{3,2,1,0:T(8,128)}, u32[]{:S(2)}, u32[]{:S(2)}) collective-permute-start(f32[32,1,32,128]{3,2,1,0:T(8,128)S(1)} %get-tuple-element.10), channel_id=1, source_target_pairs={{0,1},{1,2},{2,3},{3,4},{4,5},{5,6},{6,7},{7,8},{8,9},{9,10},{10,1... | collective-permute-start | bytes 1572872 | tf_op jit(solution)/shard_map/ppermute | solution.py:37
  108.8 0.8 copy-start.6
  114.7 11.7 %collective-permute-start.6 = (f32[32,1,32,128]{3,2,1,0:T(8,128)S(1)}, f32[32,1,32,128]{3,2,1,0:T(8,128)S(1)}, u32[]{:S(2)}, u32[]{:S(2)}) collective-permute-start(f32[32,1,32,128]{3,2,1,0:T(8,128)S(1)} %get-tuple-element.7), channel_id=1, source_target_pairs={{1,0},{2,1},{3,2},{4,3},{5,4},{6,5},{7,6},{8,7},{9,8},{10,9},{11,1... | collective-permute-start | bytes 1572872 | tf_op jit(solution)/shard_map/ppermute | solution.py:39
  116.0 11.2 %collective-permute-start.7 = (f32[32,1,32,128]{3,2,1,0:T(8,128)S(1)}, f32[32,1,32,128]{3,2,1,0:T(8,128)}, u32[]{:S(2)}, u32[]{:S(2)}) collective-permute-start(f32[32,1,32,128]{3,2,1,0:T(8,128)S(1)} %get-tuple-element.8), channel_id=1, source_target_pairs={{0,1},{1,2},{2,3},{3,4},{4,5},{5,6},{6,7},{7,8},{8,9},{9,10},{10,1... | collective-permute-start | bytes 1572872 | tf_op jit(solution)/shard_map/ppermute | solution.py:37
  126.5 0.8 copy-start.5
where the time goes:
time: 387 us; the launch traced here: 386 us
  blocking collectives  237 us (61%)
  waiting for transfers between devices  34.8 us (9%)
  other arithmetic  34.6 us (9%)
  starting transfers between devices  34 us (9%)
  local copies, waits for them, and re-layouts  33.1 us (9%)
  matrix products  13 us (3%)
    psum x1, blocking collectives, body(): coeffs = lax.psum(partial_value, ('vec', 'dom'))  141 us
    all_to_all x1, blocking collectives, body(): lax.all_to_all(current, 'vec', split_axis=2, concat_axis=0, tiled=True)  73.1 us
    ppermute x4, waiting for transfers between devices, padded_2(): lax.ppermute(head, axis, [((i + 1) % count, i) for i in range(ends)])  34.8 us
    ppermute x4, starting transfers between devices, padded_2(): lax.ppermute(tail, axis, [(i, (i + 1) % count) for i in range(ends)])  28.9 us
    all_to_all x1, blocking collectives, from_everyone(): return lax.all_to_all(copies, axis, split_axis=0, concat_axis=0, tiled=True)  22.5 us
    sub x3, other arithmetic, body(): previous, current = (current, 2.0 * scaled(current) - previous)  21.6 us
    div x1, other arithmetic, scaled(): return ((6.0 + slab_coef - center_value) * inner - beside) / half_range  12.9 us
    all_to_all x2, local copies, waits for them, and re-layouts, body(): lax.all_to_all(current, 'vec', split_axis=2, concat_axis=0, tiled=True)  8.63 us
  transfers between devices with their start and end apart: 8, of which 3 were waited for; matrix products, arithmetic and copies ran while one was open for 0% of the time, Pallas kernels for 0%

commit v1 on v0

v1 whole, which is shorter than its diff:
```python
import functools

import jax
import jax.numpy as jnp
from jax import lax
from jax.experimental import pallas as pl
from jax.experimental.pallas import tpu as pltpu
from jax.sharding import Mesh, PartitionSpec as P

bf16 = jnp.bfloat16
f32 = jnp.float32

VEC = ("zh", "x", "c")
DOM = ("y", "zl")
NEAR = ("x", "c", "y")
LINE = ("zh", "zl")
HALO = 4
GROUP = 16


def filter_kernel(ends_ref, own_ref, low_ref, high_ref, diag_ref, out_ref, even, odd):
    planes, rows = own_ref.shape[0], own_ref.shape[1]
    total = planes + 2 * HALO
    lanes = own_ref.shape[3]
    lane = lax.broadcasted_iota(jnp.int32, (GROUP, lanes), 1)
    first, last = lane == 0, lane == lanes - 1

    def fill(p, carry):
        for y in range(rows):
            even[p, y] = low_ref[p, y].astype(f32)
            even[p + HALO + planes, y] = high_ref[p, y].astype(f32)
        return carry

    lax.fori_loop(0, HALO, fill, 0)

    def copy(p, carry):
        for y in range(rows):
            even[p + HALO, y] = own_ref[p, y]
        return carry

    lax.fori_loop(0, planes, copy, 0)

    def step(source, target, weight, reach, scale):
        def plane(p, carry):
            below = None
            here = source[p, 0]
            for y in range(rows):
                above = source[p, y + 1] if y + 1 < rows else None
                left = jnp.where(first, 0.0, pltpu.roll(here, 1, 1))
                right = jnp.where(last, 0.0, pltpu.roll(here, lanes - 1, 1))
                beside = (source[p - 1, y] + source[p + 1, y]) + (left + right)
                if below is not None:
                    beside = beside + below
                if above is not None:
                    beside = beside + above
                value = diag_ref[p, pl.ds(y, 1), :] * here - beside
                if weight:
                    value = value - weight * target[p, y]
                if scale:
                    out_ref[y // 2, 2 * (p - HALO) + y % 2] = (value * scale).astype(bf16)
                else:
                    target[p, y] = value
                below, here = here, above
            return carry

        lax.fori_loop(reach, total - reach, plane, 0)
        if reach < HALO:
            zero = jnp.zeros((GROUP, lanes), f32)

            def clear(at):
                def one(p, carry):
                    for y in range(rows):
                        target[at + p, y] = zero
                    return carry

                lax.fori_loop(0, HALO - reach, one, 0)

            @pl.when(ends_ref[0] == 1)
            def _():
                clear(reach)

            @pl.when(ends_ref[1] == 1)
            def _():
                clear(HALO + planes)

    step(even, odd, 0.0, 1, 0.0)
    step(odd, even, 24.5, 2, 0.0)
    step(even, odd, 12.25, 3, 0.0)
    step(odd, even, 12.25, 4, 8.0 / 2401.0)


def filtered(ends, own, low, high, diag):
    planes, rows, vectors, lanes = own.shape
    total = planes + 2 * HALO
    return pl.pallas_call(
        filter_kernel,
        out_shape=jax.ShapeDtypeStruct((rows // 2, 2 * planes, vectors, lanes), bf16),
        grid=(vectors // GROUP,),
        in_specs=[
            pl.BlockSpec(memory_space=pltpu.SMEM),
            pl.BlockSpec((planes, rows, GROUP, lanes), lambda g: (0, 0, g, 0)),
            pl.BlockSpec((HALO, rows, GROUP, lanes), lambda g: (0, 0, g, 0)),
            pl.BlockSpec((HALO, rows, GROUP, lanes), lambda g: (0, 0, g, 0)),
            pl.BlockSpec((total, rows, lanes), lambda g: (0, 0, 0)),
        ],
        out_specs=pl.BlockSpec((rows // 2, 2 * planes, GROUP, lanes), lambda g: (0, 0, g, 0)),
        scratch_shapes=[pltpu.VMEM((total, rows, GROUP, lanes), f32)] * 2,
        compiler_params=pltpu.CompilerParams(vmem_limit_bytes=48 << 20),
        cost_estimate=pl.CostEstimate(
            flops=12 * 44 * rows * vectors * lanes, bytes_accessed=10 << 20, transcendentals=0
        ),
    )(ends, own, low, high, diag)


def project_kernel(cells_ref, ritz_ref, out_ref, total):
    step = pl.program_id(0)
    blocks, _, vectors, lanes = cells_ref.shape

    @pl.when(step == 0)
    def _():
        total[...] = jnp.zeros_like(total)

    pair = jnp.concatenate(
        [cells_ref[:, 0].reshape(-1, lanes), cells_ref[:, 1].reshape(-1, lanes)], axis=1
    )
    total[...] += jnp.dot(
        pair, ritz_ref[...].reshape(2 * lanes, -1), preferred_element_type=f32
    )

    @pl.when(step == pl.num_programs(0) - 1)
    def _():
        out_ref[...] = total[...].astype(out_ref.dtype)


def projected(cells, ritz):
    blocks, rows, vectors, lanes = cells.shape
    kept = ritz.shape[2]
    count = blocks * vectors
    return pl.pallas_call(
        project_kernel,
        out_shape=jax.ShapeDtypeStruct((count, kept), bf16),
        grid=(rows // 2,),
        in_specs=[
            pl.BlockSpec((blocks, 2, vectors, lanes), lambda r: (0, r, 0, 0)),
            pl.BlockSpec((2, lanes, kept), lambda r: (r, 0, 0)),
        ],
        out_specs=pl.BlockSpec((count, kept), lambda r: (0, 0)),
        scratch_shapes=[pltpu.VMEM((count, kept), f32)],
        cost_estimate=pl.CostEstimate(
            flops=2 * count * rows * lanes * kept, bytes_accessed=7 << 20, transcendentals=0
        ),
    )(cells, ritz)


def remove_kernel(coeffs_ref, ritz_ref, cells_ref, out_ref):
    rows, lanes = cells_ref.shape[1], cells_ref.shape[3]
    count = coeffs_ref.shape[0]
    for r in range(0, rows, 2):
        removed = lax.dot_general(
            coeffs_ref[...],
            ritz_ref[r : r + 2].reshape(2 * lanes, -1),
            (((1,), (1,)), ((), ())),
            preferred_element_type=f32,
        )
        for k in range(2):
            held = cells_ref[:, r + k].reshape(count, lanes).astype(f32)
            out_ref[pl.ds(r + k, count, stride=rows), :] = (
                held - removed[:, k * lanes : (k + 1) * lanes]
            )


def residual(coeffs, ritz, cells, parts):
    blocks, rows, vectors, lanes = cells.shape
    kept = ritz.shape[2]
    count = blocks * vectors
    return pl.pallas_call(
        remove_kernel,
        out_shape=jax.ShapeDtypeStruct((count * rows, lanes), f32),
        grid=(parts,),
        in_specs=[
            pl.BlockSpec((count // parts, kept), lambda g: (g, 0)),
            pl.BlockSpec((rows, lanes, kept), lambda g: (0, 0, 0)),
            pl.BlockSpec((blocks // parts, rows, vectors, lanes), lambda g: (g, 0, 0, 0)),
        ],
        out_specs=pl.BlockSpec((count // parts * rows, lanes), lambda g: (g, 0)),
        cost_estimate=pl.CostEstimate(
            flops=2 * count * rows * lanes * kept, bytes_accessed=11 << 20, transcendentals=0
        ),
    )(coeffs, ritz, cells)


def summed(partial):
    near = lax.axis_size(NEAR)
    line = lax.axis_size(LINE)
    count, kept = partial.shape
    blocks = lax.all_to_all(
        partial.reshape(near, count // near, kept), NEAR, 0, 0, tiled=True
    )
    blocks = jnp.sum(blocks.astype(f32), axis=0).reshape(line, -1, kept)
    blocks = jnp.sum(lax.all_to_all(blocks, LINE, 0, 0, tiled=True), axis=0).astype(bf16)
    blocks = from_everyone(blocks, LINE).reshape(-1, kept)
    return from_everyone(blocks, NEAR).reshape(count, kept)


def from_everyone(value, axis):
    copies = jnp.broadcast_to(value, (lax.axis_size(axis), *value.shape))
    return lax.all_to_all(copies, axis, split_axis=0, concat_axis=0, tiled=True)


def swap_ends(low, high):
    count = lax.axis_size(DOM)
    from_below = lax.ppermute(high, DOM, [(i, i + 1) for i in range(count - 1)])
    from_above = lax.ppermute(low, DOM, [(i + 1, i) for i in range(count - 1)])
    return from_below, from_above


def body(vectors, coefficient, ritz):
    own = vectors.transpose(1, 2, 0, 3)
    low, high = swap_ends(own[:HALO].astype(bf16), own[-HALO:].astype(bf16))
    below, above = swap_ends(coefficient[:HALO], coefficient[-HALO:])
    diag = jnp.concatenate([below, coefficient, above], axis=0)
    diag = from_everyone(diag, VEC).transpose(1, 0, 2, 3)
    diag = diag.reshape(diag.shape[0], -1, diag.shape[3]) + (6.0 - 7.125)
    place = lax.axis_index(DOM)
    ends = jnp.stack([place == 0, place == lax.axis_size(DOM) - 1]).astype(jnp.int32)
    blocks = filtered(ends, own, low, high, diag)
    cells = lax.all_to_all(blocks, VEC, 0, 0, tiled=True)
    ritz_rows = ritz.reshape(-1, *ritz.shape[2:])
    coeffs = summed(projected(cells, ritz_rows))
    out = residual(coeffs, ritz_rows, cells, 2)
    return out.reshape(-1, *coefficient.shape)


def solution(mesh):
    fine = Mesh(mesh.devices.reshape(2, 4, 2, 4, 4), ("zh", "x", "c", "y", "zl"))
    placed = (P(VEC, DOM, None, None), P(DOM, VEC, None), P(DOM, VEC, None, None))
    return jax.shard_map(
        body, mesh=fine, in_specs=placed, out_specs=P(None, DOM, VEC, None), check_vma=False
    )
```

time: 387 us -> 243 us (0.63)
  blocking collectives: 237 us -> 147 us
  Pallas kernels: 0 us -> 37 us
  other arithmetic: 34.6 us -> 0.41 us
  local copies, waits for them, and re-layouts: 33.1 us -> 13.7 us
  waiting for transfers between devices: 34.8 us -> 19.7 us
  matrix products: 13 us -> 0 us
  starting transfers between devices: 34 us -> 25.2 us
    psum x1 -> x0, blocking collectives: 141 us -> none  [body(): coeffs = lax.psum(partial_value, ('vec', 'dom'))]
    all_to_all x1 -> x3, blocking collectives: 73.1 us -> 114 us  [the longest x1 66.2 us: summed(): lax.all_to_all(partial.reshape(near, count // near, kept), NEAR, 0, 0, ti...]
    pallas_call x0 -> x3, Pallas kernels: none -> 37 us  [the longest x1 21.3 us: filtered(): pl.pallas_call(filter_kernel, out_shape=jax.ShapeDtypeStruct((rows // 2,...]
    ppermute x8 -> x4, starting transfers between devices: 34 us -> 11.1 us  [the longest x2 8.53 us: swap_ends(): from_below = lax.ppermute(high, DOM, [(i, i + 1) for i in range(count - 1)])]
    sub x4 -> x0, other arithmetic: 21.7 us -> none  [the longest x3 21.6 us: body(): previous, current = (current, 2.0 * scaled(current) - previous)]
    ppermute x8 -> x4, waiting for transfers between devices: 34.8 us -> 15.2 us  [the longest x2 15.2 us: swap_ends(): from_below = lax.ppermute(high, DOM, [(i, i + 1) for i in range(count - 1)])]
    all_to_all x0 -> x1, starting transfers between devices: none -> 14.1 us  [from_everyone(): return lax.all_to_all(copies, axis, split_axis=0, concat_axis=0, tiled=True)]
    reshape x2, local copies, waits for them, and re-layouts: 13 us -> 0.06 us  [the longest x1 0.04 us: summed(): blocks = jnp.sum(blocks.astype(f32), axis=0).reshape(line, -1, kept)]
  transfers between devices with their start and end apart: 8 -> 5, of which waited for: 3 -> 2; matrix products, arithmetic and copies ran while one was open for 0% -> 3% of each run, Pallas kernels for 0% -> 0%
where the time goes in v1:
time: 243 us
  blocking collectives  147 us (60%)
  Pallas kernels  37 us (15%)
  starting transfers between devices  25.2 us (10%)
  waiting for transfers between devices  19.7 us (8%)
  local copies, waits for them, and re-layouts  13.7 us (6%)
    all_to_all x1, blocking collectives, summed(): lax.all_to_all(partial.reshape(near, count // near, kept), NEAR, 0, 0, ti...  66.2 us
    all_to_all x1, blocking collectives, body(): cells = lax.all_to_all(blocks, VEC, 0, 0, tiled=True)  35.6 us
    all_to_all x2, blocking collectives, from_everyone(): return lax.all_to_all(copies, axis, split_axis=0, concat_axis=0, tiled=True)  32.6 us
    pallas_call x1, Pallas kernels, filtered(): pl.pallas_call(filter_kernel, out_shape=jax.ShapeDtypeStruct((rows // 2,...  21.3 us
    ppermute x2, waiting for transfers between devices, swap_ends(): from_below = lax.ppermute(high, DOM, [(i, i + 1) for i in range(count - 1)])  15.2 us
    all_to_all x1, starting transfers between devices, from_everyone(): return lax.all_to_all(copies, axis, split_axis=0, concat_axis=0, tiled=True)  14.1 us
    all_to_all x1, blocking collectives, summed(): lax.all_to_all(blocks, LINE, 0, 0, tiled=True)  12.2 us
    unnamed x4, local copies, waits for them, and re-layouts  11.2 us
  transfers between devices with their start and end apart: 5, of which 2 were waited for; matrix products, arithmetic and copies ran while one was open for 3% of the time, Pallas kernels for 0%

profile of v1, /device:TPU:1, one launch (start us, length us, event | category | flops | bytes accessed | tf_op | source)
XLA Modules:
  0.0 242.6 jit_solution(4923751889528278445)
XLA Ops:
  0.0 4.6 %copy.17 = bf16[32,8,32,128]{3,0,2,1:T(8,128)(2,1)S(1)} copy(f32[32,8,32,128]{3,2,1,0:T(8,128)} %param.3) | data formatting | bytes 6291456 | tf_op args[0]
  4.6 0.0 copy-start
  4.6 1.3 fusion.1
  6.0 1.3 collective-permute-start.1
  7.3 5.1 %collective-permute-start = (bf16[4,32,32,128]{3,2,1,0:T(8,128)(2,1)S(1)}, bf16[4,32,32,128]{3,2,1,0:T(8,128)(2,1)S(1)}, u32[]{:S(2)}, u32[]{:S(2)}) collective-permute-start(bf16[4,32,32,128]{3,2,1,0:T(8,128)(2,1)S(1)} %get-tuple-element.6), channel_id=1, source_target_pairs={{0,1},{1,2},{2,3},{3,4},{4,5},{5,6},{6,7},{7,8},{8,9},{9,10},{10,1... | collective-permute-start | bytes 3145736 | tf_op jit(solution)/shard_map/ppermute | solution.py:212
  12.3 0.0 copy-done
  12.3 3.5 %collective-permute-start.2 = (f32[4,2,128]{2,1,0:T(2,128)S(1)}, f32[4,2,128]{2,1,0:T(2,128)S(1)}, u32[]{:S(2)}, u32[]{:S(2)}) collective-permute-start(f32[4,2,128]{2,1,0:T(2,128)S(1)} %get-tuple-element.7), channel_id=1, source_target_pairs={{0,1},{1,2},{2,3},{3,4},{4,5},{5,6},{6,7},{7,8},{8,9},{9,10},{10,1... | collective-permute-start | bytes 12296 | tf_op jit(solution)/shard_map/ppermute | solution.py:212
  15.8 1.3 collective-permute-start.3
  17.1 15.2 %collective-permute-done.2 = f32[4,2,128]{2,1,0:T(2,128)S(1)} collective-permute-done((f32[4,2,128]{2,1,0:T(2,128)S(1)}, f32[4,2,128]{2,1,0:T(2,128)S(1)}, u32[]{:S(2)}, u32[]{:S(2)}) %collective-permute-start.2) | collective-permute-done | bytes 4128 | tf_op jit(solution)/shard_map/ppermute | solution.py:212
  32.4 0.0 collective-permute-done.3
  32.4 0.8 broadcast_in_dim.9
  33.2 14.1 %all-to-all-start = ((f32[16,16,2,128]{3,2,1,0:T(2,128)}), f32[16,16,2,128]{3,2,1,0:T(2,128)S(1)}, u32[]{:S(2)}, u32[]{:S(2)}) async-start(f32[16,16,2,128]{3,2,1,0:T(2,128)} %broadcast_in_dim.9), calls=%async_computation | async-start | bytes 524288 | tf_op jit(solution)/shard_map/all_to_all | solution.py:207
  47.3 6.6 %copy.16 = f32[32,8,32,128]{3,0,2,1:T(8,128)} copy(f32[32,8,32,128]{3,2,1,0:T(8,128)} %param.3) | data formatting | bytes 8388608 | tf_op args[0]
  53.8 0.1 add_convert_fusion.ends_ref
  53.9 4.5 %all-to-all-done = f32[16,16,2,128]{3,2,1,0:T(2,128)S(1)} async-done(((f32[16,16,2,128]{3,2,1,0:T(2,128)}), f32[16,16,2,128]{3,2,1,0:T(2,128)S(1)}, u32[]{:S(2)}, u32[]{:S(2)}) %all-to-all-start) | async-done | bytes 262176 | tf_op jit(solution)/shard_map/all_to_all | solution.py:207
  58.4 0.1 add_bitcast_fusion
  58.5 0.1 copy.10
  58.6 0.0 collective-permute-done.1.high_ref
  58.7 0.0 collective-permute-done.low_ref
  58.7 21.3 %shard_map.37 = bf16[16,16,32,128]{3,2,1,0:T(8,128)(2,1)S(1)} custom-call(s32[2]{0:T(128)S(1)} %add_convert_fusion.ends_ref, f32[8,32,32,128]{3,2,1,0:T(8,128)} %bitcast.16, bf16[4,32,32,128]{3,2,1,0:T(8,128)(2,1)S(1)} %collective-permute-done.low_ref, bf16[4,32,32,128]{3,2,1,0:T(8,128)(2,1)S(1)} %collective-permute-done.1.high_ref, f32[16,32,128]{2,1,0:T(8,128)S(1)} %bitcast.15), custom_call_target="tpu_custom_call" | custom-call | flops 69206016 | bytes 10485760 | tf_op jit(solution)/shard_map/pallas_call | solution.py:95
  80.0 35.6 %all_to_all.30.cells_ref = bf16[16,16,32,128]{3,2,1,0:T(8,128)(2,1)} all-to-all(bf16[16,16,32,128]{3,2,1,0:T(8,128)(2,1)S(1)} %shard_map.37), channel_id=1, replica_groups=mesh['zh'=2,'x'=4,'c'=2,'y'=4,'zl'=4] {'zh','x','c'}, dimensions={0} | all-to-all | bytes 4194304 | tf_op jit(solution)/shard_map/all_to_all | solution.py:227
  115.6 8.1 %shard_map.38 = bf16[512,1024]{1,0:T(8,128)(2,1)} custom-call(bf16[16,16,32,128]{3,2,1,0:T(8,128)(2,1)} %all_to_all.30.cells_ref, bf16[16,128,1024]{2,1,0:T(8,128)(2,1)} %bitcast.18), custom_call_target="tpu_custom_call" | custom-call | flops 2147483648 | bytes 7340032 | tf_op jit(solution)/shard_map/pallas_call | solution.py:139
  123.7 66.2 %all_to_all.31 = bf16[32,16,1024]{2,1,0:T(8,128)(2,1)S(1)} all-to-all(bf16[32,16,1024]{2,1,0:T(8,128)(2,1)} %bitcast.21), channel_id=1, replica_groups=mesh['zh'=2,'x'=4,'c'=2,'y'=4,'zl'=4] {'x','c','y'}, dimensions={0} | all-to-all | bytes 2097152 | tf_op jit(solution)/shard_map/all_to_all | solution.py:196
  189.9 0.2 convert_reduce_fusion
  190.1 12.2 %all_to_all.32 = f32[8,2,1024]{2,1,0:T(2,128)S(1)} all-to-all(f32[8,2,1024]{2,1,0:T(2,128)S(1)} %reshape.23), channel_id=1, replica_groups=mesh['zh'=2,'x'=4,'c'=2,'y'=4,'zl'=4] {'zh','zl'}, dimensions={0} | all-to-all | bytes 131072 | tf_op jit(solution)/shard_map/all_to_all | solution.py:200
  202.4 9.3 %all_to_all.33 = bf16[8,2,1024]{2,1,0:T(2,128)(2,1)S(1)} all-to-all(bf16[8,2,1024]{2,1,0:T(2,128)(2,1)S(1)} %broadcast_in_dim.10), channel_id=1, replica_groups=mesh['zh'=2,'x'=4,'c'=2,'y'=4,'zl'=4] {'zh','zl'}, dimensions={0} | all-to-all | bytes 65536 | tf_op jit(solution)/shard_map/all_to_all | solution.py:207
  211.7 0.1 broadcast_in_dim.11
  211.8 23.3 %all_to_all.34 = bf16[32,16,1024]{2,1,0:T(8,128)(2,1)} all-to-all(bf16[32,16,1024]{2,1,0:T(8,128)(2,1)S(1)} %broadcast_in_dim.11), channel_id=1, replica_groups=mesh['zh'=2,'x'=4,'c'=2,'y'=4,'zl'=4] {'x','c','y'}, dimensions={0} | all-to-all | bytes 2097152 | tf_op jit(solution)/shard_map/all_to_all | solution.py:207
  235.1 7.5 %shard_map.39 = f32[8192,128]{1,0:T(8,128)} custom-call(bf16[512,1024]{1,0:T(8,128)(2,1)} %bitcast.20, bf16[16,128,1024]{2,1,0:T(8,128)(2,1)} %bitcast.19, bf16[16,16,32,128]{3,2,1,0:T(8,128)(2,1)} %all_to_all.30.cells_ref), custom_call_target="tpu_custom_call" | custom-call | flops 2147483648 | bytes 11534336 | tf_op jit(solution)/shard_map/pallas_call | solution.py:176
  (6 shorter events, 0.1 us)
Async XLA Ops:
  4.6 7.7 %copy-start = (f32[8,2,128]{2,1,0:T(2,128)S(1)}, f32[8,2,128]{2,1,0:T(2,128)}, u32[]{:S(2)}) copy-start(f32[8,2,128]{2,1,0:T(2,128)} %param.4) | copy-start | bytes 24580
  6.0 52.7 %collective-permute-start.1 = (bf16[4,32,32,128]{3,2,1,0:T(8,128)(2,1)}, bf16[4,32,32,128]{3,2,1,0:T(8,128)(2,1)S(1)}, u32[]{:S(2)}, u32[]{:S(2)}) collective-permute-start(bf16[4,32,32,128]{3,2,1,0:T(8,128)(2,1)} %get-tuple-element.5), channel_id=1, source_target_pairs={{1,0},{2,1},{3,2},{4,3},{5,4},{6,5},{7,6},{8,7},{9,8},{10,9},{11,1... | collective-permute-start | bytes 3145736 | tf_op jit(solution)/shard_map/ppermute | solution.py:213
  7.3 51.4 %collective-permute-start = (bf16[4,32,32,128]{3,2,1,0:T(8,128)(2,1)S(1)}, bf16[4,32,32,128]{3,2,1,0:T(8,128)(2,1)S(1)}, u32[]{:S(2)}, u32[]{:S(2)}) collective-permute-start(bf16[4,32,32,128]{3,2,1,0:T(8,128)(2,1)S(1)} %get-tuple-element.6), channel_id=1, source_target_pairs={{0,1},{1,2},{2,3},{3,4},{4,5},{5,6},{6,7},{7,8},{8,9},{9,10},{10,1... | collective-permute-start | bytes 3145736 | tf_op jit(solution)/shard_map/ppermute | solution.py:212
  12.3 20.0 %collective-permute-start.2 = (f32[4,2,128]{2,1,0:T(2,128)S(1)}, f32[4,2,128]{2,1,0:T(2,128)S(1)}, u32[]{:S(2)}, u32[]{:S(2)}) collective-permute-start(f32[4,2,128]{2,1,0:T(2,128)S(1)} %get-tuple-element.7), channel_id=1, source_target_pairs={{0,1},{1,2},{2,3},{3,4},{4,5},{5,6},{6,7},{7,8},{8,9},{9,10},{10,1... | collective-permute-start | bytes 12296 | tf_op jit(solution)/shard_map/ppermute | solution.py:212
  15.8 16.5 %collective-permute-start.3 = (f32[4,2,128]{2,1,0:T(2,128)S(1)}, f32[4,2,128]{2,1,0:T(2,128)S(1)}, u32[]{:S(2)}, u32[]{:S(2)}) collective-permute-start(f32[4,2,128]{2,1,0:T(2,128)S(1)} %get-tuple-element.8), channel_id=1, source_target_pairs={{1,0},{2,1},{3,2},{4,3},{5,4},{6,5},{7,6},{8,7},{9,8},{10,9},{11,1... | collective-permute-start | bytes 12296 | tf_op jit(solution)/shard_map/ppermute | solution.py:213
  33.2 25.2 %all-to-all-start = ((f32[16,16,2,128]{3,2,1,0:T(2,128)}), f32[16,16,2,128]{3,2,1,0:T(2,128)S(1)}, u32[]{:S(2)}, u32[]{:S(2)}) async-start(f32[16,16,2,128]{3,2,1,0:T(2,128)} %broadcast_in_dim.9), calls=%async_computation | async-start | bytes 524288 | tf_op jit(solution)/shard_map/all_to_all | solution.py:207

commit v2 on v1

v2 whole, which is shorter than its diff:
```python
import functools

import jax
import jax.numpy as jnp
from jax import lax
from jax.experimental import pallas as pl
from jax.experimental.pallas import tpu as pltpu
from jax.sharding import Mesh, PartitionSpec as P

bf16 = jnp.bfloat16
f32 = jnp.float32

VEC = ("zh", "x", "c")
DOM = ("y", "zl")
NEAR = ("x", "c", "y")
LINE = ("zh", "zl")
HALO = 4
GROUP = 16
CHUNKS = 2
PARTS = 2


def spread_kernel(first_ref, second_ref, *out_refs):
    for source, low, own in ((first_ref, *out_refs[:2]), (second_ref, *out_refs[2:])):
        vectors, rows, lanes = source.shape
        flat = source.reshape(vectors * rows, lanes)
        for y in range(rows):
            value = flat[pl.ds(y, vectors, stride=rows), :]
            low[0, y] = value.astype(bf16)
            own[0, y] = value


def spread(cells, rows, chunk, size):
    planes, lanes = cells.shape[1] // rows, cells.shape[2]
    half = planes // 2
    shape = (half, rows, size, lanes)
    out = pl.BlockSpec((1, rows, size, lanes), lambda p: (p, 0, 0, 0))
    return pl.pallas_call(
        spread_kernel,
        out_shape=[jax.ShapeDtypeStruct(shape, bf16), jax.ShapeDtypeStruct(shape, f32)] * 2,
        grid=(half,),
        in_specs=[
            pl.BlockSpec((size, rows, lanes), lambda p: (chunk, p, 0)),
            pl.BlockSpec((size, rows, lanes), lambda p: (chunk, p + half, 0)),
        ],
        out_specs=[out] * 4,
        cost_estimate=pl.CostEstimate(
            flops=size * planes * rows * lanes,
            bytes_accessed=10 * size * planes * rows * lanes,
            transcendentals=0,
        ),
    )(cells, cells)


def filter_kernel(ends_ref, near_ref, far_ref, low_ref, high_ref, diag_ref, out_ref, even, odd):
    half, rows, lanes = near_ref.shape[0], near_ref.shape[1], near_ref.shape[3]
    planes = 2 * half
    total = planes + 2 * HALO
    lane = lax.broadcasted_iota(jnp.int32, (GROUP, lanes), 1)
    first, last = lane == 0, lane == lanes - 1

    def fill(p, carry):
        for y in range(rows):
            even[p, y] = low_ref[p, y].astype(f32)
            even[p + HALO + planes, y] = high_ref[p, y].astype(f32)
        return carry

    lax.fori_loop(0, HALO, fill, 0)

    def copy(p, carry):
        for y in range(rows):
            even[p + HALO, y] = near_ref[p, y]
            even[p + HALO + half, y] = far_ref[p, y]
        return carry

    lax.fori_loop(0, half, copy, 0)

    def step(source, target, weight, reach, scale):
        def plane(p, carry):
            below = None
            here = source[p, 0]
            for y in range(rows):
                above = source[p, y + 1] if y + 1 < rows else None
                left = jnp.where(first, 0.0, pltpu.roll(here, 1, 1))
                right = jnp.where(last, 0.0, pltpu.roll(here, lanes - 1, 1))
                beside = (source[p - 1, y] + source[p + 1, y]) + (left + right)
                if below is not None:
                    beside = beside + below
                if above is not None:
                    beside = beside + above
                value = diag_ref[p, pl.ds(y, 1), :] * here - beside
                if weight:
                    value = value - weight * target[p, y]
                if scale:
                    out_ref[y // 2, 2 * (p - HALO) + y % 2] = (value * scale).astype(bf16)
                else:
                    target[p, y] = value
                below, here = here, above
            return carry

        lax.fori_loop(reach, total - reach, plane, 0)
        if reach < HALO:
            zero = jnp.zeros((GROUP, lanes), f32)

            def clear(at):
                def one(p, carry):
                    for y in range(rows):
                        target[at + p, y] = zero
                    return carry

                lax.fori_loop(0, HALO - reach, one, 0)

            @pl.when(ends_ref[0] == 1)
            def _():
                clear(reach)

            @pl.when(ends_ref[1] == 1)
            def _():
                clear(HALO + planes)

    step(even, odd, 0.0, 1, 0.0)
    step(odd, even, 24.5, 2, 0.0)
    step(even, odd, 12.25, 3, 0.0)
    step(odd, even, 12.25, 4, 8.0 / 2401.0)


def filtered(ends, near, far, low, high, diag):
    half, rows, vectors, lanes = near.shape
    planes = 2 * half
    total = planes + 2 * HALO
    return pl.pallas_call(
        filter_kernel,
        out_shape=jax.ShapeDtypeStruct((rows // 2, 2 * planes, vectors, lanes), bf16),
        grid=(vectors // GROUP,),
        in_specs=[
            pl.BlockSpec(memory_space=pltpu.SMEM),
            pl.BlockSpec((half, rows, GROUP, lanes), lambda g: (0, 0, g, 0)),
            pl.BlockSpec((half, rows, GROUP, lanes), lambda g: (0, 0, g, 0)),
            pl.BlockSpec((HALO, rows, GROUP, lanes), lambda g: (0, 0, g, 0)),
            pl.BlockSpec((HALO, rows, GROUP, lanes), lambda g: (0, 0, g, 0)),
            pl.BlockSpec((total, rows, lanes), lambda g: (0, 0, 0)),
        ],
        out_specs=pl.BlockSpec((rows // 2, 2 * planes, GROUP, lanes), lambda g: (0, 0, g, 0)),
        scratch_shapes=[pltpu.VMEM((total, rows, GROUP, lanes), f32)] * 2,
        compiler_params=pltpu.CompilerParams(vmem_limit_bytes=24 << 20),
        cost_estimate=pl.CostEstimate(
            flops=12 * 44 * rows * vectors * lanes, bytes_accessed=10 << 20, transcendentals=0
        ),
    )(ends, near, far, low, high, diag)


def project_kernel(cells_ref, ritz_ref, *refs):
    out_ref, total = refs[-2:]
    step = pl.program_id(0)
    lanes = cells_ref.shape[3]

    @pl.when(step == 0)
    def _():
        total[...] = jnp.zeros_like(total)

    pair = jnp.concatenate(
        [cells_ref[:, 0].reshape(-1, lanes), cells_ref[:, 1].reshape(-1, lanes)], axis=1
    )
    total[...] += jnp.dot(
        pair, ritz_ref[...].reshape(2 * lanes, -1), preferred_element_type=f32
    )

    @pl.when(step == pl.num_programs(0) - 1)
    def _():
        out_ref[...] = total[...].astype(bf16).reshape(out_ref.shape)


def projected(cells, ritz, held, chunk, near):
    blocks, rows, vectors, lanes = cells.shape
    kept = ritz.shape[2]
    count = blocks * vectors
    size = count // near
    specs = [
        pl.BlockSpec((blocks, 2, vectors, lanes), lambda r: (0, r, 0, 0)),
        pl.BlockSpec((2, lanes, kept), lambda r: (r, 0, 0)),
    ]
    operands = [cells, ritz]
    if held is not None:
        specs.append(pl.BlockSpec(memory_space=pl.ANY))
        operands.append(held)
    return pl.pallas_call(
        project_kernel,
        out_shape=jax.ShapeDtypeStruct((near, CHUNKS * size, kept), bf16),
        grid=(rows // 2,),
        in_specs=specs,
        out_specs=pl.BlockSpec((near, size, kept), lambda r: (0, chunk, 0)),
        scratch_shapes=[pltpu.VMEM((count, kept), f32)],
        input_output_aliases={} if held is None else {2: 0},
        compiler_params=pltpu.CompilerParams(vmem_limit_bytes=24 << 20),
        cost_estimate=pl.CostEstimate(
            flops=2 * count * rows * lanes * kept, bytes_accessed=7 << 20, transcendentals=0
        ),
    )(*operands)


def remove_kernel(coeffs_ref, ritz_ref, *refs):
    out_ref = refs[-1]
    blocks, rows, vectors, lanes = refs[0].shape

    def remove(cells_ref):
        coeffs = coeffs_ref[...].reshape(blocks * vectors, -1)
        for r in range(0, rows, 2):
            removed = lax.dot_general(
                coeffs,
                ritz_ref[r : r + 2].reshape(2 * lanes, -1),
                (((1,), (1,)), ((), ())),
                preferred_element_type=f32,
            )
            for k in range(2):
                for i in range(blocks):
                    held = cells_ref[i, r + k].astype(f32)
                    part = removed[i * vectors : (i + 1) * vectors, k * lanes : (k + 1) * lanes]
                    out_ref[i, pl.ds(r + k, vectors, stride=rows), :] = held - part

    for k, cells_ref in enumerate(refs[:-1]):
        pl.when(pl.program_id(0) == k)(functools.partial(remove, cells_ref))


def residual(coeffs, ritz, held):
    blocks, rows, vectors, lanes = held[0].shape
    near, _, kept = coeffs.shape
    count = blocks * vectors
    chunks = len(held)
    return pl.pallas_call(
        remove_kernel,
        out_shape=jax.ShapeDtypeStruct((blocks, chunks * vectors * rows, lanes), f32),
        grid=(chunks, PARTS),
        in_specs=[
            pl.BlockSpec((near // PARTS, count // near, kept), lambda k, g: (g, k, 0)),
            pl.BlockSpec((rows, lanes, kept), lambda k, g: (0, 0, 0)),
            *(
                pl.BlockSpec(
                    (blocks // PARTS, rows, vectors, lanes),
                    functools.partial(held_block, own),
                )
                for own in range(chunks)
            ),
        ],
        out_specs=pl.BlockSpec(
            (blocks // PARTS, vectors * rows, lanes), lambda k, g: (g, k, 0)
        ),
        compiler_params=pltpu.CompilerParams(vmem_limit_bytes=32 << 20),
        cost_estimate=pl.CostEstimate(
            flops=2 * chunks * count * rows * lanes * kept,
            bytes_accessed=11 << 20,
            transcendentals=0,
        ),
    )(coeffs, ritz, *held)


def held_block(own, k, g):
    return jnp.where(k == own, g, jnp.where(k < own, 0, PARTS - 1)), 0, 0, 0


def summed(partial):
    blocks = lax.all_to_all(partial, NEAR, 0, 0, tiled=True)
    blocks = jnp.sum(blocks.astype(f32), axis=0)
    blocks = jnp.sum(from_everyone(blocks, LINE), axis=0).astype(bf16)
    return from_everyone(blocks, NEAR)


def from_everyone(value, axis):
    copies = jnp.broadcast_to(value, (lax.axis_size(axis), *value.shape))
    return lax.all_to_all(copies, axis, split_axis=0, concat_axis=0, tiled=True)


def swap_ends(low, high):
    count = lax.axis_size(DOM)
    from_below = lax.ppermute(high, DOM, [(i, i + 1) for i in range(count - 1)])
    from_above = lax.ppermute(low, DOM, [(i + 1, i) for i in range(count - 1)])
    return from_below, from_above


def pipeline(vectors, coefficient, ritz):
    count, planes, rows, lanes = vectors.shape
    size = count // CHUNKS
    below, above = swap_ends(coefficient[:HALO], coefficient[-HALO:])
    diag = jnp.concatenate([below, coefficient, above], axis=0) + (6.0 - 7.125)
    diag = from_everyone(diag, VEC)
    diag = diag.transpose(1, 0, 2, 3).reshape(-1, rows, lanes)
    place = lax.axis_index(DOM)
    ends = jnp.stack([place == 0, place == lax.axis_size(DOM) - 1]).astype(jnp.int32)
    cells = vectors.reshape(count, planes * rows, lanes)
    ritz_rows = pltpu.with_memory_space_constraint(
        ritz.reshape(-1, *ritz.shape[2:]), pltpu.MemorySpace.HBM
    )
    held, total = [], None
    for k in range(CHUNKS):
        low, near, high, far = spread(cells, rows, k, size)
        low, high = swap_ends(low, high)
        blocks = filtered(ends, near, far, low, high, diag)
        held.append(lax.all_to_all(blocks, VEC, 0, 0, tiled=True))
    for k in range(CHUNKS):
        total = projected(held[k], ritz_rows, total, k, lax.axis_size(NEAR))
    coeffs = summed(total)
    out = residual(coeffs, ritz_rows, held)
    return out.reshape(-1, *coefficient.shape)


def solution(mesh):
    fine = Mesh(mesh.devices.reshape(2, 4, 2, 4, 4), ("zh", "x", "c", "y", "zl"))
    placed = (P(VEC, DOM, None, None), P(DOM, VEC, None), P(DOM, VEC, None, None))
    return jax.shard_map(
        pipeline, mesh=fine, in_specs=placed, out_specs=P(None, DOM, VEC, None), check_vma=False
    )
```

time: 243 us -> 254 us (1.045)
  blocking collectives: 147 us -> 69.4 us
  waiting for transfers between devices: 19.7 us -> 70.6 us
  starting transfers between devices: 25.2 us -> 52.6 us
  Pallas kernels: 37 us -> 53.2 us
  local copies, waits for them, and re-layouts: 13.7 us -> 6.7 us
    all_to_all x3 -> x1, blocking collectives: 114 us -> 26.3 us  [summed(): blocks = lax.all_to_all(partial, NEAR, 0, 0, tiled=True)]
    all_to_all x0 -> x2, starting transfers between devices: none -> 23 us  [pipeline(): held.append(lax.all_to_all(blocks, VEC, 0, 0, tiled=True))]
    all_to_all x0 -> x2, waiting for transfers between devices: none -> 20 us  [pipeline(): held.append(lax.all_to_all(blocks, VEC, 0, 0, tiled=True))]
    ppermute x2 -> x3, waiting for transfers between devices: 0.01 us -> 16.8 us  [swap_ends(): from_above = lax.ppermute(low, DOM, [(i + 1, i) for i in range(count - 1)])]
    pallas_call x2 -> x5, Pallas kernels: 15.7 us -> 31.1 us  [the longest x2 12.1 us: projected(): pl.pallas_call(project_kernel, out_shape=jax.ShapeDtypeStruct((near, CHUN...]
    all_to_all x2, blocking collectives: 32.6 us -> 43.1 us  [from_everyone(): return lax.all_to_all(copies, axis, split_axis=0, concat_axis=0, tiled=True)]
    ppermute x2 -> x3, waiting for transfers between devices: 15.2 us -> 22.7 us  [swap_ends(): from_below = lax.ppermute(high, DOM, [(i, i + 1) for i in range(count - 1)])]
    all_to_all x1, waiting for transfers between devices: 4.45 us -> 11.1 us  [from_everyone(): return lax.all_to_all(copies, axis, split_axis=0, concat_axis=0, tiled=True)]
  transfers between devices with their start and end apart: 5 -> 9, of which waited for: 2 -> 5; matrix products, arithmetic and copies ran while one was open for 3% -> 0% of each run, Pallas kernels for 0% -> 10%
where the time goes in v2:
time: 254 us; the launch traced here: 253 us
  waiting for transfers between devices  70.6 us (28%)
  blocking collectives  69.4 us (27%)
  Pallas kernels  53.2 us (21%)
  starting transfers between devices  52.6 us (21%)
  local copies, waits for them, and re-layouts  6.7 us (3%)
    all_to_all x2, blocking collectives, from_everyone(): return lax.all_to_all(copies, axis, split_axis=0, concat_axis=0, tiled=True)  43.1 us
    all_to_all x1, blocking collectives, summed(): blocks = lax.all_to_all(partial, NEAR, 0, 0, tiled=True)  26.3 us
    all_to_all x2, starting transfers between devices, pipeline(): held.append(lax.all_to_all(blocks, VEC, 0, 0, tiled=True))  23 us
    ppermute x3, waiting for transfers between devices, swap_ends(): from_below = lax.ppermute(high, DOM, [(i, i + 1) for i in range(count - 1)])  22.7 us
    pallas_call x2, Pallas kernels, filtered(): pl.pallas_call(filter_kernel, out_shape=jax.ShapeDtypeStruct((rows // 2,...  22.2 us
    all_to_all x2, waiting for transfers between devices, pipeline(): held.append(lax.all_to_all(blocks, VEC, 0, 0, tiled=True))  20 us
    ppermute x3, waiting for transfers between devices, swap_ends(): from_above = lax.ppermute(low, DOM, [(i + 1, i) for i in range(count - 1)])  16.8 us
    ppermute x3, starting transfers between devices, swap_ends(): from_below = lax.ppermute(high, DOM, [(i, i + 1) for i in range(count - 1)])  14.4 us
  transfers between devices with their start and end apart: 9, of which 5 were waited for; matrix products, arithmetic and copies ran while one was open for 0% of the time, Pallas kernels for 10%

profile of v2, /device:TPU:1, one launch (start us, length us, event | category | flops | bytes accessed | tf_op | source)
XLA Modules:
  0.0 253.0 jit_solution(9275358086659152810)
XLA Ops:
  0.0 0.7 fusion
  0.7 4.3 %collective-permute-start.2 = (f32[4,2,128]{2,1,0:T(2,128)S(1)}, f32[4,2,128]{2,1,0:T(2,128)S(1)}, u32[]{:S(2)}, u32[]{:S(2)}) collective-permute-start(f32[4,2,128]{2,1,0:T(2,128)S(1)} %get-tuple-element.21), channel_id=1, source_target_pairs={{0,1},{1,2},{2,3},{3,4},{4,5},{5,6},{6,7},{7,8},{8,9},{9,10},{10,1... | collective-permute-start | bytes 12296 | tf_op jit(solution)/shard_map/ppermute | solution.py:274
  5.1 1.3 collective-permute-start.3
  6.4 0.0 copy-start.4
  6.4 4.5 %shard_map.39 = (bf16[4,32,16,128]{3,2,1,0:T(8,128)(2,1)}, f32[4,32,16,128]{3,2,1,0:T(8,128)}, bf16[4,32,16,128]{3,2,1,0:T(8,128)(2,1)}, f32[4,32,16,128]{3,2,1,0:T(8,128)}) custom-call(f32[32,256,128]{2,1,0:T(8,128)} %bitcast.9, f32[32,256,128]{2,1,0:T(8,128)} %bitcast.10), custom_call_target="tpu_custom_call" | custom-call | flops 524288 | bytes 5242880 | tf_op jit(solution)/shard_map/pallas_call | solution.py:38
  10.8 4.2 %collective-permute-start.4 = (bf16[4,32,16,128]{3,2,1,0:T(8,128)(2,1)}, bf16[4,32,16,128]{3,2,1,0:T(8,128)(2,1)S(1)}, u32[]{:S(2)}, u32[]{:S(2)}) collective-permute-start(bf16[4,32,16,128]{3,2,1,0:T(8,128)(2,1)} %get-tuple-element.19), channel_id=1, source_target_pairs={{0,1},{1,2},{2,3},{3,4},{4,5},{5,6},{6,7},{7,8},{8,9},{9,10},{10,1... | collective-permute-start | bytes 1572872 | tf_op jit(solution)/shard_map/ppermute | solution.py:274
  15.1 1.3 collective-permute-start.5
  16.4 0.0 collective-permute-done.2
  16.4 0.0 collective-permute-done.3
  16.4 0.0 copy-done.4
  16.4 0.8 broadcast_in_dim.9
  17.2 11.4 %all-to-all-start = ((f32[16,16,2,128]{3,2,1,0:T(2,128)}), f32[16,16,2,128]{3,2,1,0:T(2,128)S(1)}, u32[]{:S(2)}, u32[]{:S(2)}) async-start(f32[16,16,2,128]{3,2,1,0:T(2,128)} %broadcast_in_dim.9), calls=%async_computation | async-start | bytes 524288 | tf_op jit(solution)/shard_map/all_to_all | solution.py:269
  28.6 0.1 add_convert_fusion.ends_ref
  28.7 11.1 %all-to-all-done = f32[16,16,2,128]{3,2,1,0:T(2,128)S(1)} async-done(((f32[16,16,2,128]{3,2,1,0:T(2,128)}), f32[16,16,2,128]{3,2,1,0:T(2,128)S(1)}, u32[]{:S(2)}, u32[]{:S(2)}) %all-to-all-start) | async-done | bytes 262176 | tf_op jit(solution)/shard_map/all_to_all | solution.py:269
  39.8 0.1 copy.6
  39.9 0.0 collective-permute-done.4.low_ref
  39.9 0.9 collective-permute-done.5.high_ref
  40.9 0.0 copy-start
  40.9 1.2 copy-done
  42.1 0.0 copy-start.1
  42.1 1.2 copy-done.1
  43.3 11.1 %shard_map.40 = bf16[16,16,16,128]{3,2,1,0:T(8,128)(2,1)} custom-call(s32[2]{0:T(128)S(1)} %add_convert_fusion.ends_ref, f32[4,32,16,128]{3,2,1,0:T(8,128)S(1)} %copy-done, f32[4,32,16,128]{3,2,1,0:T(8,128)S(1)} %copy-done.1, bf16[4,32,16,128]{3,2,1,0:T(8,128)(2,1)S(1)} %collective-permute-done.4.low_ref, ...), custom_call_target="tpu_custom_call" | custom-call | flops 34603008 | bytes 10485760 | tf_op jit(solution)/shard_map/pallas_call | solution.py:131
  54.4 13.1 %all-to-all-start.2 = ((bf16[16,16,16,128]{3,2,1,0:T(8,128)(2,1)}), bf16[16,16,16,128]{3,2,1,0:T(8,128)(2,1)S(1)}, u32[]{:S(2)}, u32[]{:S(2)}) async-start(bf16[16,16,16,128]{3,2,1,0:T(8,128)(2,1)} %shard_map.40), calls=%async_computation.2 | async-start | bytes 2097152 | tf_op jit(solution)/shard_map/all_to_all | solution.py:297
  67.5 4.5 %shard_map.37 = (bf16[4,32,16,128]{3,2,1,0:T(8,128)(2,1)}, f32[4,32,16,128]{3,2,1,0:T(8,128)}, bf16[4,32,16,128]{3,2,1,0:T(8,128)(2,1)}, f32[4,32,16,128]{3,2,1,0:T(8,128)}) custom-call(f32[32,256,128]{2,1,0:T(8,128)} %bitcast.11, f32[32,256,128]{2,1,0:T(8,128)} %bitcast.12), custom_call_target="tpu_custom_call" | custom-call | flops 524288 | bytes 5242880 | tf_op jit(solution)/shard_map/pallas_call | solution.py:38
  72.0 5.9 %collective-permute-start = (bf16[4,32,16,128]{3,2,1,0:T(8,128)(2,1)}, bf16[4,32,16,128]{3,2,1,0:T(8,128)(2,1)S(1)}, u32[]{:S(2)}, u32[]{:S(2)}) collective-permute-start(bf16[4,32,16,128]{3,2,1,0:T(8,128)(2,1)} %get-tuple-element.15), channel_id=1, source_target_pairs={{0,1},{1,2},{2,3},{3,4},{4,5},{5,6},{6,7},{7,8},{8,9},{9,10},{10,1... | collective-permute-start | bytes 1572872 | tf_op jit(solution)/shard_map/ppermute | solution.py:274
  77.9 1.3 collective-permute-start.1
  79.2 22.7 %collective-permute-done.low_ref = bf16[4,32,16,128]{3,2,1,0:T(8,128)(2,1)S(1)} collective-permute-done((bf16[4,32,16,128]{3,2,1,0:T(8,128)(2,1)}, bf16[4,32,16,128]{3,2,1,0:T(8,128)(2,1)S(1)}, u32[]{:S(2)}, u32[]{:S(2)}) %collective-permute-start) | collective-permute-done | bytes 524320 | tf_op jit(solution)/shard_map/ppermute | solution.py:274
  101.9 15.8 %collective-permute-done.1.high_ref = bf16[4,32,16,128]{3,2,1,0:T(8,128)(2,1)S(1)} collective-permute-done((bf16[4,32,16,128]{3,2,1,0:T(8,128)(2,1)}, bf16[4,32,16,128]{3,2,1,0:T(8,128)(2,1)S(1)}, u32[]{:S(2)}, u32[]{:S(2)}) %collective-permute-start.1) | collective-permute-done | bytes 524320 | tf_op jit(solution)/shard_map/ppermute | solution.py:275
  117.7 0.0 copy-start.2
  117.7 1.2 copy-done.2
  118.9 0.0 copy-start.3
  118.9 1.2 copy-done.3
  120.1 11.1 %shard_map.38 = bf16[16,16,16,128]{3,2,1,0:T(8,128)(2,1)} custom-call(s32[2]{0:T(128)S(1)} %add_convert_fusion.ends_ref, f32[4,32,16,128]{3,2,1,0:T(8,128)S(1)} %copy-done.2, f32[4,32,16,128]{3,2,1,0:T(8,128)S(1)} %copy-done.3, bf16[4,32,16,128]{3,2,1,0:T(8,128)(2,1)S(1)} %collective-permute-done.low_ref, ...), custom_call_target="tpu_custom_call" | custom-call | flops 34603008 | bytes 10485760 | tf_op jit(solution)/shard_map/pallas_call | solution.py:131
  131.2 0.0 all-to-all-done.2.cells_ref.refs_0_
  131.2 9.8 %all-to-all-start.1 = ((bf16[16,16,16,128]{3,2,1,0:T(8,128)(2,1)}), bf16[16,16,16,128]{3,2,1,0:T(8,128)(2,1)S(1)}, u32[]{:S(2)}, u32[]{:S(2)}) async-start(bf16[16,16,16,128]{3,2,1,0:T(8,128)(2,1)} %shard_map.38), calls=%async_computation.1 | async-start | bytes 2097152 | tf_op jit(solution)/shard_map/all_to_all | solution.py:297
  141.0 6.1 %shard_map.41.refs_0_ = bf16[32,16,1024]{2,1,0:T(8,128)(2,1)S(1)} custom-call(bf16[16,16,16,128]{3,2,1,0:T(8,128)(2,1)S(1)} %all-to-all-done.2.cells_ref.refs_0_, bf16[16,128,1024]{2,1,0:T(8,128)(2,1)} %bitcast.13), custom_call_target="tpu_custom_call" | custom-call | flops 1073741824 | bytes 7340032 | tf_op jit(solution)/shard_map/pallas_call | solution.py:186
  147.1 20.0 %all-to-all-done.1.cells_ref.refs_1_ = bf16[16,16,16,128]{3,2,1,0:T(8,128)(2,1)S(1)} async-done(((bf16[16,16,16,128]{3,2,1,0:T(8,128)(2,1)}), bf16[16,16,16,128]{3,2,1,0:T(8,128)(2,1)S(1)}, u32[]{:S(2)}, u32[]{:S(2)}) %all-to-all-start.1) | async-done | bytes 1048608 | tf_op jit(solution)/shard_map/all_to_all | solution.py:297
  167.2 6.1 %shard_map.42 = bf16[32,16,1024]{2,1,0:T(8,128)(2,1)S(1)} custom-call(bf16[16,16,16,128]{3,2,1,0:T(8,128)(2,1)S(1)} %all-to-all-done.1.cells_ref.refs_1_, bf16[16,128,1024]{2,1,0:T(8,128)(2,1)} %bitcast.14, bf16[32,16,1024]{2,1,0:T(8,128)(2,1)S(1)} %shard_map.41.refs_0_), custom_call_target="tpu_custom_call", output_to_operand_aliasing={{}: (2, {})} | custom-call | flops 1073741824 | bytes 7340032 | tf_op jit(solution)/shard_map/pallas_call | solution.py:186
  173.2 26.3 %all_to_all.30 = bf16[32,16,1024]{2,1,0:T(8,128)(2,1)S(1)} all-to-all(bf16[32,16,1024]{2,1,0:T(8,128)(2,1)S(1)} %shard_map.42), channel_id=1, replica_groups=mesh['zh'=2,'x'=4,'c'=2,'y'=4,'zl'=4] {'x','c','y'}, dimensions={0} | all-to-all | bytes 2097152 | tf_op jit(solution)/shard_map/all_to_all | solution.py:261
  199.5 0.2 convert_reduce_fusion
  199.7 20.4 %all_to_all.31 = f32[8,16,1024]{2,1,0:T(8,128)S(1)} all-to-all(f32[8,16,1024]{2,1,0:T(8,128)S(1)} %broadcast_in_dim.10), channel_id=1, replica_groups=mesh['zh'=2,'x'=4,'c'=2,'y'=4,'zl'=4] {'zh','zl'}, dimensions={0} | all-to-all | bytes 1048576 | tf_op jit(solution)/shard_map/all_to_all | solution.py:269
  220.2 0.1 broadcast_in_dim.11
  220.3 22.7 %all_to_all.32.coeffs_ref = bf16[32,16,1024]{2,1,0:T(8,128)(2,1)S(1)} all-to-all(bf16[32,16,1024]{2,1,0:T(8,128)(2,1)S(1)} %broadcast_in_dim.11), channel_id=1, replica_groups=mesh['zh'=2,'x'=4,'c'=2,'y'=4,'zl'=4] {'x','c','y'}, dimensions={0} | all-to-all | bytes 2097152 | tf_op jit(solution)/shard_map/all_to_all | solution.py:269
  243.0 10.0 %shard_map.43 = f32[16,512,128]{2,1,0:T(8,128)} custom-call(bf16[32,16,1024]{2,1,0:T(8,128)(2,1)S(1)} %all_to_all.32.coeffs_ref, bf16[16,128,1024]{2,1,0:T(8,128)(2,1)} %bitcast.15, bf16[16,16,16,128]{3,2,1,0:T(8,128)(2,1)S(1)} %all-to-all-done.2.cells_ref.refs_0_, bf16[16,16,16,128]{3,2,1,0:T(8,128)(2,1)S(1)} %all-to-all-done.1.cells_ref.refs_1_), custom_call_target="tpu_custom_call" | custom-call | flops 2147483648 | bytes 11534336 | tf_op jit(solution)/shard_map/pallas_call | solution.py:229
  (3 shorter events, 0.1 us)
Async XLA Ops:
  0.7 15.6 %collective-permute-start.2 = (f32[4,2,128]{2,1,0:T(2,128)S(1)}, f32[4,2,128]{2,1,0:T(2,128)S(1)}, u32[]{:S(2)}, u32[]{:S(2)}) collective-permute-start(f32[4,2,128]{2,1,0:T(2,128)S(1)} %get-tuple-element.21), channel_id=1, source_target_pairs={{0,1},{1,2},{2,3},{3,4},{4,5},{5,6},{6,7},{7,8},{8,9},{9,10},{10,1... | collective-permute-start | bytes 12296 | tf_op jit(solution)/shard_map/ppermute | solution.py:274
  5.1 11.3 %collective-permute-start.3 = (f32[4,2,128]{2,1,0:T(2,128)S(1)}, f32[4,2,128]{2,1,0:T(2,128)S(1)}, u32[]{:S(2)}, u32[]{:S(2)}) collective-permute-start(f32[4,2,128]{2,1,0:T(2,128)S(1)} %get-tuple-element.22), channel_id=1, source_target_pairs={{1,0},{2,1},{3,2},{4,3},{5,4},{6,5},{7,6},{8,7},{9,8},{10,9},{11,1... | collective-permute-start | bytes 12296 | tf_op jit(solution)/shard_map/ppermute | solution.py:275
  6.4 10.0 %copy-start.4 = (f32[8,2,128]{2,1,0:T(2,128)S(1)}, f32[8,2,128]{2,1,0:T(2,128)}, u32[]{:S(2)}) copy-start(f32[8,2,128]{2,1,0:T(2,128)} %param.4) | copy-start | bytes 24580
  10.8 29.1 %collective-permute-start.4 = (bf16[4,32,16,128]{3,2,1,0:T(8,128)(2,1)}, bf16[4,32,16,128]{3,2,1,0:T(8,128)(2,1)S(1)}, u32[]{:S(2)}, u32[]{:S(2)}) collective-permute-start(bf16[4,32,16,128]{3,2,1,0:T(8,128)(2,1)} %get-tuple-element.19), channel_id=1, source_target_pairs={{0,1},{1,2},{2,3},{3,4},{4,5},{5,6},{6,7},{7,8},{8,9},{9,10},{10,1... | collective-permute-start | bytes 1572872 | tf_op jit(solution)/shard_map/ppermute | solution.py:274
  15.1 25.8 %collective-permute-start.5 = (bf16[4,32,16,128]{3,2,1,0:T(8,128)(2,1)}, bf16[4,32,16,128]{3,2,1,0:T(8,128)(2,1)S(1)}, u32[]{:S(2)}, u32[]{:S(2)}) collective-permute-start(bf16[4,32,16,128]{3,2,1,0:T(8,128)(2,1)} %get-tuple-element.20), channel_id=1, source_target_pairs={{1,0},{2,1},{3,2},{4,3},{5,4},{6,5},{7,6},{8,7},{9,8},{10,9},{11,1... | collective-permute-start | bytes 1572872 | tf_op jit(solution)/shard_map/ppermute | solution.py:275
  17.2 22.6 %all-to-all-start = ((f32[16,16,2,128]{3,2,1,0:T(2,128)}), f32[16,16,2,128]{3,2,1,0:T(2,128)S(1)}, u32[]{:S(2)}, u32[]{:S(2)}) async-start(f32[16,16,2,128]{3,2,1,0:T(2,128)} %broadcast_in_dim.9), calls=%async_computation | async-start | bytes 524288 | tf_op jit(solution)/shard_map/all_to_all | solution.py:269
  40.9 1.2 copy-start
  42.1 1.2 copy-start.1
  54.4 76.8 %all-to-all-start.2 = ((bf16[16,16,16,128]{3,2,1,0:T(8,128)(2,1)}), bf16[16,16,16,128]{3,2,1,0:T(8,128)(2,1)S(1)}, u32[]{:S(2)}, u32[]{:S(2)}) async-start(bf16[16,16,16,128]{3,2,1,0:T(8,128)(2,1)} %shard_map.40), calls=%async_computation.2 | async-start | bytes 2097152 | tf_op jit(solution)/shard_map/all_to_all | solution.py:297
  72.0 29.9 %collective-permute-start = (bf16[4,32,16,128]{3,2,1,0:T(8,128)(2,1)}, bf16[4,32,16,128]{3,2,1,0:T(8,128)(2,1)S(1)}, u32[]{:S(2)}, u32[]{:S(2)}) collective-permute-start(bf16[4,32,16,128]{3,2,1,0:T(8,128)(2,1)} %get-tuple-element.15), channel_id=1, source_target_pairs={{0,1},{1,2},{2,3},{3,4},{4,5},{5,6},{6,7},{7,8},{8,9},{9,10},{10,1... | collective-permute-start | bytes 1572872 | tf_op jit(solution)/shard_map/ppermute | solution.py:274
  77.9 39.8 %collective-permute-start.1 = (bf16[4,32,16,128]{3,2,1,0:T(8,128)(2,1)}, bf16[4,32,16,128]{3,2,1,0:T(8,128)(2,1)S(1)}, u32[]{:S(2)}, u32[]{:S(2)}) collective-permute-start(bf16[4,32,16,128]{3,2,1,0:T(8,128)(2,1)} %get-tuple-element.16), channel_id=1, source_target_pairs={{1,0},{2,1},{3,2},{4,3},{5,4},{6,5},{7,6},{8,7},{9,8},{10,9},{11,1... | collective-permute-start | bytes 1572872 | tf_op jit(solution)/shard_map/ppermute | solution.py:275
  117.7 1.2 copy-start.2
  118.9 1.2 copy-start.3
  131.2 35.9 %all-to-all-start.1 = ((bf16[16,16,16,128]{3,2,1,0:T(8,128)(2,1)}), bf16[16,16,16,128]{3,2,1,0:T(8,128)(2,1)S(1)}, u32[]{:S(2)}, u32[]{:S(2)}) async-start(bf16[16,16,16,128]{3,2,1,0:T(8,128)(2,1)} %shard_map.38), calls=%async_computation.1 | async-start | bytes 2097152 | tf_op jit(solution)/shard_map/all_to_all | solution.py:297

commit v3 on v2

--- a/solution.py
+++ b/solution.py
@@ -12,50 +12,46 @@
 
 VEC = ("zh", "x", "c")
 DOM = ("y", "zl")
-NEAR = ("x", "c", "y")
-LINE = ("zh", "zl")
+SHARE = ("x", "y")
+NEAR = ("c", *SHARE)
 HALO = 4
 GROUP = 16
 CHUNKS = 2
-PARTS = 2
-
-
-def spread_kernel(first_ref, second_ref, *out_refs):
-    for source, low, own in ((first_ref, *out_refs[:2]), (second_ref, *out_refs[2:])):
+
+
+def spread_kernel(first_ref, second_ref, low_ref, high_ref):
+    for source, target in ((first_ref, low_ref), (second_ref, high_ref)):
         vectors, rows, lanes = source.shape
         flat = source.reshape(vectors * rows, lanes)
         for y in range(rows):
-            value = flat[pl.ds(y, vectors, stride=rows), :]
-            low[0, y] = value.astype(bf16)
-            own[0, y] = value
+            target[0, y] = flat[pl.ds(y, vectors, stride=rows), :].astype(bf16)
 
 
 def spread(cells, rows, chunk, size):
     planes, lanes = cells.shape[1] // rows, cells.shape[2]
     half = planes // 2
-    shape = (half, rows, size, lanes)
     out = pl.BlockSpec((1, rows, size, lanes), lambda p: (p, 0, 0, 0))
     return pl.pallas_call(
         spread_kernel,
-        out_shape=[jax.ShapeDtypeStruct(shape, bf16), jax.ShapeDtypeStruct(shape, f32)] * 2,
+        out_shape=[jax.ShapeDtypeStruct((half, rows, size, lanes), bf16)] * 2,
         grid=(half,),
         in_specs=[
             pl.BlockSpec((size, rows, lanes), lambda p: (chunk, p, 0)),
             pl.BlockSpec((size, rows, lanes), lambda p: (chunk, p + half, 0)),
         ],
-        out_specs=[out] * 4,
+        out_specs=[out] * 2,
         cost_estimate=pl.CostEstimate(
             flops=size * planes * rows * lanes,
-            bytes_accessed=10 * size * planes * rows * lanes,
+            bytes_accessed=6 * size * planes * rows * lanes,
             transcendentals=0,
         ),
     )(cells, cells)
 
 
-def filter_kernel(ends_ref, near_ref, far_ref, low_ref, high_ref, diag_ref, out_ref, even, odd):
-    half, rows, lanes = near_ref.shape[0], near_ref.shape[1], near_ref.shape[3]
-    planes = 2 * half
-    total = planes + 2 * HALO
+def filter_kernel(ends_ref, own_ref, low_ref, high_ref, diag_ref, out_ref, even, odd):
+    total, rows, lanes = diag_ref.shape
+    planes = total - 2 * HALO
+    flat = own_ref.reshape(GROUP * planes * rows, lanes)
     lane = lax.broadcasted_iota(jnp.int32, (GROUP, lanes), 1)
     first, last = lane == 0, lane == lanes - 1
 
@@ -69,11 +65,11 @@
 
     def copy(p, carry):
         for y in range(rows):
-            even[p + HALO, y] = near_ref[p, y]
-            even[p + HALO + half, y] = far_ref[p, y]
+            at = pl.ds(p * rows + y, GROUP, stride=planes * rows)
+            even[p + HALO, y] = flat[at, :]
         return carry
 
-    lax.fori_loop(0, half, copy, 0)
+    lax.fori_loop(0, planes, copy, 0)
 
     def step(source, target, weight, reach, scale):
         def plane(p, carry):
@@ -124,29 +120,29 @@
     step(odd, even, 12.25, 4, 8.0 / 2401.0)
 
 
-def filtered(ends, near, far, low, high, diag):
-    half, rows, vectors, lanes = near.shape
-    planes = 2 * half
-    total = planes + 2 * HALO
+def filtered(ends, cells, low, high, diag, chunk, size):
+    total, rows, lanes = diag.shape
+    planes = total - 2 * HALO
+    groups = size // GROUP
+    edge = pl.BlockSpec((HALO, rows, GROUP, lanes), lambda g: (0, 0, g, 0))
     return pl.pallas_call(
         filter_kernel,
-        out_shape=jax.ShapeDtypeStruct((rows // 2, 2 * planes, vectors, lanes), bf16),
-        grid=(vectors // GROUP,),
+        out_shape=jax.ShapeDtypeStruct((rows // 2, 2 * planes, size, lanes), bf16),
+        grid=(groups,),
         in_specs=[
             pl.BlockSpec(memory_space=pltpu.SMEM),
-            pl.BlockSpec((half, rows, GROUP, lanes), lambda g: (0, 0, g, 0)),
-            pl.BlockSpec((half, rows, GROUP, lanes), lambda g: (0, 0, g, 0)),
-            pl.BlockSpec((HALO, rows, GROUP, lanes), lambda g: (0, 0, g, 0)),
-            pl.BlockSpec((HALO, rows, GROUP, lanes), lambda g: (0, 0, g, 0)),
+            pl.BlockSpec((GROUP, planes * rows, lanes), lambda g: (chunk * groups + g, 0, 0)),
+            edge,
+            edge,
             pl.BlockSpec((total, rows, lanes), lambda g: (0, 0, 0)),
         ],
         out_specs=pl.BlockSpec((rows // 2, 2 * planes, GROUP, lanes), lambda g: (0, 0, g, 0)),
         scratch_shapes=[pltpu.VMEM((total, rows, GROUP, lanes), f32)] * 2,
         compiler_params=pltpu.CompilerParams(vmem_limit_bytes=24 << 20),
         cost_estimate=pl.CostEstimate(
-            flops=12 * 44 * rows * vectors * lanes, bytes_accessed=10 << 20, transcendentals=0
+            flops=12 * 44 * rows * size * lanes, bytes_accessed=5 << 20, transcendentals=0
         ),
-    )(ends, near, far, low, high, diag)
+    )(ends, cells, low, high, diag)
 
 
 def project_kernel(cells_ref, ritz_ref, *refs):
@@ -198,12 +194,17 @@
     )(*operands)
 
 
-def remove_kernel(coeffs_ref, ritz_ref, *refs):
+def remove_kernel(core_ref, mine_ref, other_ref, ritz_ref, *refs):
     out_ref = refs[-1]
     blocks, rows, vectors, lanes = refs[0].shape
+    mine = mine_ref[...].reshape(blocks * vectors // 2, -1)
+    other = other_ref[...].reshape(blocks * vectors // 2, -1)
+    first = core_ref[0] == 0
+    coeffs = jnp.concatenate(
+        [jnp.where(first, mine, other), jnp.where(first, other, mine)], axis=0
+    )
 
     def remove(cells_ref):
-        coeffs = coeffs_ref[...].reshape(blocks * vectors, -1)
         for r in range(0, rows, 2):
             removed = lax.dot_general(
                 coeffs,
@@ -221,47 +222,44 @@
         pl.when(pl.program_id(0) == k)(functools.partial(remove, cells_ref))
 
 
-def residual(coeffs, ritz, held):
+def residual(core, mine, other, ritz, held):
     blocks, rows, vectors, lanes = held[0].shape
-    near, _, kept = coeffs.shape
-    count = blocks * vectors
+    near, _, kept = mine.shape
     chunks = len(held)
+    size = mine.shape[1] // chunks
+    coeffs = pl.BlockSpec((near, size, kept), lambda k: (0, k, 0))
     return pl.pallas_call(
         remove_kernel,
         out_shape=jax.ShapeDtypeStruct((blocks, chunks * vectors * rows, lanes), f32),
-        grid=(chunks, PARTS),
+        grid=(chunks,),
         in_specs=[
-            pl.BlockSpec((near // PARTS, count // near, kept), lambda k, g: (g, k, 0)),
-            pl.BlockSpec((rows, lanes, kept), lambda k, g: (0, 0, 0)),
-            *(
-                pl.BlockSpec(
-                    (blocks // PARTS, rows, vectors, lanes),
-                    functools.partial(held_block, own),
-                )
-                for own in range(chunks)
-            ),
+            pl.BlockSpec(memory_space=pltpu.SMEM),
+            coeffs,
+            coeffs,
+            pl.BlockSpec((rows, lanes, kept), lambda k: (0, 0, 0)),
+            *([pl.BlockSpec((blocks, rows, vectors, lanes), lambda k: (0, 0, 0, 0))] * chunks),
         ],
-        out_specs=pl.BlockSpec(
-            (blocks // PARTS, vectors * rows, lanes), lambda k, g: (g, k, 0)
-        ),
+        out_specs=pl.BlockSpec((blocks, vectors * rows, lanes), lambda k: (0, k, 0)),
         compiler_params=pltpu.CompilerParams(vmem_limit_bytes=32 << 20),
         cost_estimate=pl.CostEstimate(
-            flops=2 * chunks * count * rows * lanes * kept,
+            flops=2 * chunks * blocks * vectors * rows * lanes * kept,
             bytes_accessed=11 << 20,
             transcendentals=0,
         ),
-    )(coeffs, ritz, *held)
-
-
-def held_block(own, k, g):
-    return jnp.where(k == own, g, jnp.where(k < own, 0, PARTS - 1)), 0, 0, 0
+    )(core, mine, other, ritz, *held)
 
 
 def summed(partial):
     blocks = lax.all_to_all(partial, NEAR, 0, 0, tiled=True)
     blocks = jnp.sum(blocks.astype(f32), axis=0)
-    blocks = jnp.sum(from_everyone(blocks, LINE), axis=0).astype(bf16)
-    return from_everyone(blocks, NEAR)
+    blocks = blocks + swapped(blocks, "zh")
+    blocks = jnp.sum(from_everyone(blocks, "zl"), axis=0).astype(bf16)
+    mine = from_everyone(blocks, SHARE)
+    return mine, swapped(mine, "c")
+
+
+def swapped(value, axis):
+    return lax.ppermute(value, axis, [(0, 1), (1, 0)])
 
 
 def from_everyone(value, axis):
@@ -279,26 +277,29 @@
 def pipeline(vectors, coefficient, ritz):
     count, planes, rows, lanes = vectors.shape
     size = count // CHUNKS
-    below, above = swap_ends(coefficient[:HALO], coefficient[-HALO:])
-    diag = jnp.concatenate([below, coefficient, above], axis=0) + (6.0 - 7.125)
-    diag = from_everyone(diag, VEC)
-    diag = diag.transpose(1, 0, 2, 3).reshape(-1, rows, lanes)
+    diag = from_everyone(coefficient, VEC)
+    diag = diag.transpose(1, 0, 2, 3).reshape(planes, rows, lanes)
+    below, above = swap_ends(diag[:HALO], diag[-HALO:])
+    diag = jnp.concatenate([below, diag, above], axis=0) + (6.0 - 7.125)
     place = lax.axis_index(DOM)
     ends = jnp.stack([place == 0, place == lax.axis_size(DOM) - 1]).astype(jnp.int32)
-    cells = vectors.reshape(count, planes * rows, lanes)
+    cells = pltpu.with_memory_space_constraint(
+        vectors.reshape(count, planes * rows, lanes), pltpu.MemorySpace.HBM
+    )
     ritz_rows = pltpu.with_memory_space_constraint(
         ritz.reshape(-1, *ritz.shape[2:]), pltpu.MemorySpace.HBM
     )
     held, total = [], None
     for k in range(CHUNKS):
-        low, near, high, far = spread(cells, rows, k, size)
+        low, high = spread(cells, rows, k, size)
         low, high = swap_ends(low, high)
-        blocks = filtered(ends, near, far, low, high, diag)
+        blocks = filtered(ends, cells, low, high, diag, k, size)
         held.append(lax.all_to_all(blocks, VEC, 0, 0, tiled=True))
     for k in range(CHUNKS):
         total = projected(held[k], ritz_rows, total, k, lax.axis_size(NEAR))
-    coeffs = summed(total)
-    out = residual(coeffs, ritz_rows, held)
+    mine, other = summed(total)
+    core = lax.axis_index("c").reshape(1).astype(jnp.int32)
+    out = residual(core, mine, other, ritz_rows, held)
     return out.reshape(-1, *coefficient.shape)
 
 

time: 254 us -> 245 us (0.965)
  blocking collectives: 69.4 us -> 48.9 us
  waiting for transfers between devices: 70.6 us -> 88.5 us
  local copies, waits for them, and re-layouts: 6.7 us -> 1.55 us
    all_to_all x2, blocking collectives: 43.1 us -> 26.8 us  [from_everyone(): return lax.all_to_all(copies, axis, split_axis=0, concat_axis=0, tiled=True)]
    ppermute x3, waiting for transfers between devices: 16.8 us -> 31.2 us  [swap_ends(): from_above = lax.ppermute(low, DOM, [(i + 1, i) for i in range(count - 1)])]
    all_to_all x1, waiting for transfers between devices: 11.1 us -> 2.08 us  [from_everyone(): return lax.all_to_all(copies, axis, split_axis=0, concat_axis=0, tiled=True)]
    ppermute x0 -> x2, waiting for transfers between devices: none -> 8.55 us  [swapped(): return lax.ppermute(value, axis, [(0, 1), (1, 0)])]
    ppermute x3, starting transfers between devices: 14.4 us -> 9.51 us  [swap_ends(): from_below = lax.ppermute(high, DOM, [(i, i + 1) for i in range(count - 1)])]
    unnamed x10 -> x0, local copies, waits for them, and re-layouts: 4.9 us -> none
    pallas_call x2, Pallas kernels: 22.2 us -> 26.5 us  [filtered(): pl.pallas_call(filter_kernel, out_shape=jax.ShapeDtypeStruct((rows // 2,...]
    ppermute x0 -> x2, starting transfers between devices: none -> 4.29 us  [swapped(): return lax.ppermute(value, axis, [(0, 1), (1, 0)])]
  transfers between devices with their start and end apart: 9 -> 11, of which waited for: 5 -> 7; matrix products, arithmetic and copies ran while one was open for 0% -> 0% of each run, Pallas kernels for 10% -> 11%
where the time goes in v3:
time: 245 us; the launch traced here: 244 us
  waiting for transfers between devices  88.5 us (36%)
  Pallas kernels  53.9 us (22%)
  starting transfers between devices  50.3 us (21%)
  blocking collectives  48.9 us (20%)
    ppermute x3, waiting for transfers between devices, swap_ends(): from_above = lax.ppermute(low, DOM, [(i + 1, i) for i in range(count - 1)])  31.2 us
    ppermute x3, waiting for transfers between devices, swap_ends(): from_below = lax.ppermute(high, DOM, [(i, i + 1) for i in range(count - 1)])  26.8 us
    all_to_all x2, blocking collectives, from_everyone(): return lax.all_to_all(copies, axis, split_axis=0, concat_axis=0, tiled=True)  26.8 us
    pallas_call x2, Pallas kernels, filtered(): pl.pallas_call(filter_kernel, out_shape=jax.ShapeDtypeStruct((rows // 2,...  26.5 us
    all_to_all x1, blocking collectives, summed(): blocks = lax.all_to_all(partial, NEAR, 0, 0, tiled=True)  22.2 us
    all_to_all x2, starting transfers between devices, pipeline(): held.append(lax.all_to_all(blocks, VEC, 0, 0, tiled=True))  20.2 us
    all_to_all x2, waiting for transfers between devices, pipeline(): held.append(lax.all_to_all(blocks, VEC, 0, 0, tiled=True))  19.9 us
    all_to_all x1, starting transfers between devices, from_everyone(): return lax.all_to_all(copies, axis, split_axis=0, concat_axis=0, tiled=True)  12.4 us
  transfers between devices with their start and end apart: 11, of which 7 were waited for; matrix products, arithmetic and copies ran while one was open for 0% of the time, Pallas kernels for 11%

profile of v3, /device:TPU:1, one launch (start us, length us, event | category | flops | bytes accessed | tf_op | source)
XLA Modules:
  0.0 243.7 jit_solution(10340644347082405869)
XLA Ops:
  0.0 1.4 broadcast_in_dim.9
  1.4 12.4 %all-to-all-start = ((f32[16,8,2,128]{3,2,1,0:T(2,128)}), f32[16,8,2,128]{3,2,1,0:T(2,128)S(1)}, u32[]{:S(2)}, u32[]{:S(2)}) async-start(f32[16,8,2,128]{3,2,1,0:T(2,128)} %broadcast_in_dim.9), calls=%async_computation | async-start | bytes 262144 | tf_op jit(solution)/shard_map/all_to_all | solution.py:267
  13.8 4.1 %shard_map.39 = (bf16[4,32,16,128]{3,2,1,0:T(8,128)(2,1)}, bf16[4,32,16,128]{3,2,1,0:T(8,128)(2,1)}) custom-call(f32[32,256,128]{2,1,0:T(8,128)} %bitcast.10, f32[32,256,128]{2,1,0:T(8,128)} %bitcast.11), custom_call_target="tpu_custom_call" | custom-call | flops 524288 | bytes 3145728 | tf_op jit(solution)/shard_map/pallas_call | solution.py:34
  17.9 2.7 %collective-permute-start.4 = (bf16[4,32,16,128]{3,2,1,0:T(8,128)(2,1)}, bf16[4,32,16,128]{3,2,1,0:T(8,128)(2,1)S(1)}, u32[]{:S(2)}, u32[]{:S(2)}) collective-permute-start(bf16[4,32,16,128]{3,2,1,0:T(8,128)(2,1)} %get-tuple-element.11), channel_id=1, source_target_pairs={{0,1},{1,2},{2,3},{3,4},{4,5},{5,6},{6,7},{7,8},{8,9},{9,10},{10,1... | collective-permute-start | bytes 1572872 | tf_op jit(solution)/shard_map/ppermute | solution.py:272
  20.5 1.3 collective-permute-start.5
  21.8 2.1 all-to-all-done
  24.0 1.3 collective-permute-start.3
  25.3 4.6 %collective-permute-start.2 = (f32[4,32,128]{2,1,0:T(8,128)S(1)}, f32[4,32,128]{2,1,0:T(8,128)S(1)}, u32[]{:S(2)}, u32[]{:S(2)}) collective-permute-start(f32[4,32,128]{2,1,0:T(8,128)S(1)} %bitcast.22), channel_id=1, source_target_pairs={{0,1},{1,2},{2,3},{3,4},{4,5},{5,6},{6,7},{7,8},{8,9},{9,10},{10,1... | collective-permute-start | bytes 196616 | tf_op jit(solution)/shard_map/ppermute | solution.py:272
  29.9 0.1 add_convert_fusion.ends_ref
  30.0 19.1 %collective-permute-done.3 = f32[4,32,128]{2,1,0:T(8,128)S(1)} collective-permute-done((f32[4,32,128]{2,1,0:T(8,128)S(1)}, f32[4,32,128]{2,1,0:T(8,128)S(1)}, u32[]{:S(2)}, u32[]{:S(2)}) %collective-permute-start.3) | collective-permute-done | bytes 65568 | tf_op jit(solution)/shard_map/ppermute | solution.py:273
  49.1 0.0 collective-permute-done.2
  49.2 0.0 collective-permute-done.4.low_ref
  49.2 0.0 collective-permute-done.5.high_ref
  49.2 13.2 %shard_map.40 = bf16[16,16,16,128]{3,2,1,0:T(8,128)(2,1)} custom-call(s32[2]{0:T(128)S(1)} %add_convert_fusion.ends_ref, f32[32,256,128]{2,1,0:T(8,128)} %bitcast.12, bf16[4,32,16,128]{3,2,1,0:T(8,128)(2,1)S(1)} %collective-permute-done.4.low_ref, bf16[4,32,16,128]{3,2,1,0:T(8,128)(2,1)S(1)} %collective-permute-done.5.high_ref, ...), custom_call_target="tpu_custom_call" | custom-call | flops 34603008 | bytes 5242880 | tf_op jit(solution)/shard_map/pallas_call | solution.py:128
  62.4 10.4 %all-to-all-start.2 = ((bf16[16,16,16,128]{3,2,1,0:T(8,128)(2,1)}), bf16[16,16,16,128]{3,2,1,0:T(8,128)(2,1)S(1)}, u32[]{:S(2)}, u32[]{:S(2)}) async-start(bf16[16,16,16,128]{3,2,1,0:T(8,128)(2,1)} %shard_map.40), calls=%async_computation.2 | async-start | bytes 2097152 | tf_op jit(solution)/shard_map/all_to_all | solution.py:297
  72.8 4.1 %shard_map.37 = (bf16[4,32,16,128]{3,2,1,0:T(8,128)(2,1)}, bf16[4,32,16,128]{3,2,1,0:T(8,128)(2,1)}) custom-call(f32[32,256,128]{2,1,0:T(8,128)} %bitcast.13, f32[32,256,128]{2,1,0:T(8,128)} %bitcast.14), custom_call_target="tpu_custom_call" | custom-call | flops 524288 | bytes 3145728 | tf_op jit(solution)/shard_map/pallas_call | solution.py:34
  76.9 2.3 collective-permute-start
  79.1 1.3 collective-permute-start.1
  80.4 26.8 %collective-permute-done.low_ref = bf16[4,32,16,128]{3,2,1,0:T(8,128)(2,1)S(1)} collective-permute-done((bf16[4,32,16,128]{3,2,1,0:T(8,128)(2,1)}, bf16[4,32,16,128]{3,2,1,0:T(8,128)(2,1)S(1)}, u32[]{:S(2)}, u32[]{:S(2)}) %collective-permute-start) | collective-permute-done | bytes 524320 | tf_op jit(solution)/shard_map/ppermute | solution.py:272
  107.3 12.1 %collective-permute-done.1.high_ref = bf16[4,32,16,128]{3,2,1,0:T(8,128)(2,1)S(1)} collective-permute-done((bf16[4,32,16,128]{3,2,1,0:T(8,128)(2,1)}, bf16[4,32,16,128]{3,2,1,0:T(8,128)(2,1)S(1)}, u32[]{:S(2)}, u32[]{:S(2)}) %collective-permute-start.1) | collective-permute-done | bytes 524320 | tf_op jit(solution)/shard_map/ppermute | solution.py:273
  119.4 13.3 %shard_map.38 = bf16[16,16,16,128]{3,2,1,0:T(8,128)(2,1)} custom-call(s32[2]{0:T(128)S(1)} %add_convert_fusion.ends_ref, f32[32,256,128]{2,1,0:T(8,128)} %bitcast.15, bf16[4,32,16,128]{3,2,1,0:T(8,128)(2,1)S(1)} %collective-permute-done.low_ref, bf16[4,32,16,128]{3,2,1,0:T(8,128)(2,1)S(1)} %collective-permute-done.1.high_ref, ...), custom_call_target="tpu_custom_call" | custom-call | flops 34603008 | bytes 5242880 | tf_op jit(solution)/shard_map/pallas_call | solution.py:128
  132.6 0.0 all-to-all-done.2.cells_ref.refs_0_
  132.6 9.8 %all-to-all-start.1 = ((bf16[16,16,16,128]{3,2,1,0:T(8,128)(2,1)}), bf16[16,16,16,128]{3,2,1,0:T(8,128)(2,1)S(1)}, u32[]{:S(2)}, u32[]{:S(2)}) async-start(bf16[16,16,16,128]{3,2,1,0:T(8,128)(2,1)} %shard_map.38), calls=%async_computation.1 | async-start | bytes 2097152 | tf_op jit(solution)/shard_map/all_to_all | solution.py:297
  142.4 6.1 %shard_map.41.refs_0_ = bf16[32,16,1024]{2,1,0:T(8,128)(2,1)S(1)} custom-call(bf16[16,16,16,128]{3,2,1,0:T(8,128)(2,1)S(1)} %all-to-all-done.2.cells_ref.refs_0_, bf16[16,128,1024]{2,1,0:T(8,128)(2,1)} %bitcast.16), custom_call_target="tpu_custom_call" | custom-call | flops 1073741824 | bytes 7340032 | tf_op jit(solution)/shard_map/pallas_call | solution.py:182
  148.5 19.9 %all-to-all-done.1.cells_ref.refs_1_ = bf16[16,16,16,128]{3,2,1,0:T(8,128)(2,1)S(1)} async-done(((bf16[16,16,16,128]{3,2,1,0:T(8,128)(2,1)}), bf16[16,16,16,128]{3,2,1,0:T(8,128)(2,1)S(1)}, u32[]{:S(2)}, u32[]{:S(2)}) %all-to-all-start.1) | async-done | bytes 1048608 | tf_op jit(solution)/shard_map/all_to_all | solution.py:297
  168.4 6.1 %shard_map.42 = bf16[32,16,1024]{2,1,0:T(8,128)(2,1)S(1)} custom-call(bf16[16,16,16,128]{3,2,1,0:T(8,128)(2,1)S(1)} %all-to-all-done.1.cells_ref.refs_1_, bf16[16,128,1024]{2,1,0:T(8,128)(2,1)} %bitcast.17, bf16[32,16,1024]{2,1,0:T(8,128)(2,1)S(1)} %shard_map.41.refs_0_), custom_call_target="tpu_custom_call", output_to_operand_aliasing={{}: (2, {})} | custom-call | flops 1073741824 | bytes 7340032 | tf_op jit(solution)/shard_map/pallas_call | solution.py:182
  174.5 22.2 %all_to_all.30 = bf16[32,16,1024]{2,1,0:T(8,128)(2,1)S(1)} all-to-all(bf16[32,16,1024]{2,1,0:T(8,128)(2,1)S(1)} %shard_map.42), channel_id=1, replica_groups=mesh['zh'=2,'x'=4,'c'=2,'y'=4,'zl'=4] {'c','x','y'}, dimensions={0} | all-to-all | bytes 2097152 | tf_op jit(solution)/shard_map/all_to_all | solution.py:253
  196.7 0.2 convert_reduce_fusion
  196.8 0.1 collective-permute-start.6
  196.9 7.0 %collective-permute-done.6 = f32[16,1024]{1,0:T(8,128)S(1)} collective-permute-done((f32[16,1024]{1,0:T(8,128)S(1)}, f32[16,1024]{1,0:T(8,128)S(1)}, u32[]{:S(2)}, u32[]{:S(2)}) %collective-permute-start.6) | collective-permute-done | bytes 65568 | tf_op jit(solution)/shard_map/ppermute | solution.py:262
  204.0 12.3 %all_to_all.31 = f32[4,16,1024]{2,1,0:T(8,128)S(1)} all-to-all(f32[4,16,1024]{2,1,0:T(8,128)S(1)} %broadcast_in_dim.10), channel_id=1, replica_groups=mesh['zh'=2,'x'=4,'c'=2,'y'=4,'zl'=4] {'zl'}, dimensions={0} | all-to-all | bytes 524288 | tf_op jit(solution)/shard_map/all_to_all | solution.py:267
  216.3 0.1 broadcast_in_dim.11
  216.3 14.5 %all_to_all.32.mine_ref = bf16[16,16,1024]{2,1,0:T(8,128)(2,1)S(1)} all-to-all(bf16[16,16,1024]{2,1,0:T(8,128)(2,1)S(1)} %broadcast_in_dim.11), channel_id=1, replica_groups=mesh['zh'=2,'x'=4,'c'=2,'y'=4,'zl'=4] {'x','y'}, dimensions={0} | all-to-all | bytes 1048576 | tf_op jit(solution)/shard_map/all_to_all | solution.py:267
  230.8 4.2 %collective-permute-start.7 = (bf16[16,16,1024]{2,1,0:T(8,128)(2,1)S(1)}, bf16[16,16,1024]{2,1,0:T(8,128)(2,1)S(1)}, u32[]{:S(2)}, u32[]{:S(2)}) collective-permute-start(bf16[16,16,1024]{2,1,0:T(8,128)(2,1)S(1)} %all_to_all.32.mine_ref), channel_id=1, source_target_pairs={{0,16},{16,0},{1,17},{17,1},{2,18},{18,2},{3,19},{19,3},{4,20},{20... | collective-permute-start | bytes 1572872 | tf_op jit(solution)/shard_map/ppermute | solution.py:262
  235.0 1.5 collective-permute-done.7.other_ref
  236.5 7.2 %shard_map.43 = f32[16,512,128]{2,1,0:T(8,128)} custom-call(s32[1]{0:T(128)} %bitcast.core_ref, bf16[16,16,1024]{2,1,0:T(8,128)(2,1)S(1)} %all_to_all.32.mine_ref, bf16[16,16,1024]{2,1,0:T(8,128)(2,1)S(1)} %collective-permute-done.7.other_ref, bf16[16,128,1024]{2,1,0:T(8,128)(2,1)} %bitcast.18, ...), custom_call_target="tpu_custom_call" | custom-call | flops 2147483648 | bytes 11534336 | tf_op jit(solution)/shard_map/pallas_call | solution.py:231
  (8 shorter events, 0.2 us)
Async XLA Ops:
  1.4 22.5 %all-to-all-start = ((f32[16,8,2,128]{3,2,1,0:T(2,128)}), f32[16,8,2,128]{3,2,1,0:T(2,128)S(1)}, u32[]{:S(2)}, u32[]{:S(2)}) async-start(f32[16,8,2,128]{3,2,1,0:T(2,128)} %broadcast_in_dim.9), calls=%async_computation | async-start | bytes 262144 | tf_op jit(solution)/shard_map/all_to_all | solution.py:267
  17.9 31.3 %collective-permute-start.4 = (bf16[4,32,16,128]{3,2,1,0:T(8,128)(2,1)}, bf16[4,32,16,128]{3,2,1,0:T(8,128)(2,1)S(1)}, u32[]{:S(2)}, u32[]{:S(2)}) collective-permute-start(bf16[4,32,16,128]{3,2,1,0:T(8,128)(2,1)} %get-tuple-element.11), channel_id=1, source_target_pairs={{0,1},{1,2},{2,3},{3,4},{4,5},{5,6},{6,7},{7,8},{8,9},{9,10},{10,1... | collective-permute-start | bytes 1572872 | tf_op jit(solution)/shard_map/ppermute | solution.py:272
  20.5 28.7 %collective-permute-start.5 = (bf16[4,32,16,128]{3,2,1,0:T(8,128)(2,1)}, bf16[4,32,16,128]{3,2,1,0:T(8,128)(2,1)S(1)}, u32[]{:S(2)}, u32[]{:S(2)}) collective-permute-start(bf16[4,32,16,128]{3,2,1,0:T(8,128)(2,1)} %get-tuple-element.12), channel_id=1, source_target_pairs={{1,0},{2,1},{3,2},{4,3},{5,4},{6,5},{7,6},{8,7},{9,8},{10,9},{11,1... | collective-permute-start | bytes 1572872 | tf_op jit(solution)/shard_map/ppermute | solution.py:273
  24.0 25.1 %collective-permute-start.3 = (f32[4,32,128]{2,1,0:T(8,128)S(1)}, f32[4,32,128]{2,1,0:T(8,128)S(1)}, u32[]{:S(2)}, u32[]{:S(2)}) collective-permute-start(f32[4,32,128]{2,1,0:T(8,128)S(1)} %bitcast.23), channel_id=1, source_target_pairs={{1,0},{2,1},{3,2},{4,3},{5,4},{6,5},{7,6},{8,7},{9,8},{10,9},{11,1... | collective-permute-start | bytes 196616 | tf_op jit(solution)/shard_map/ppermute | solution.py:273
  25.3 23.8 %collective-permute-start.2 = (f32[4,32,128]{2,1,0:T(8,128)S(1)}, f32[4,32,128]{2,1,0:T(8,128)S(1)}, u32[]{:S(2)}, u32[]{:S(2)}) collective-permute-start(f32[4,32,128]{2,1,0:T(8,128)S(1)} %bitcast.22), channel_id=1, source_target_pairs={{0,1},{1,2},{2,3},{3,4},{4,5},{5,6},{6,7},{7,8},{8,9},{9,10},{10,1... | collective-permute-start | bytes 196616 | tf_op jit(solution)/shard_map/ppermute | solution.py:272
  62.4 70.2 %all-to-all-start.2 = ((bf16[16,16,16,128]{3,2,1,0:T(8,128)(2,1)}), bf16[16,16,16,128]{3,2,1,0:T(8,128)(2,1)S(1)}, u32[]{:S(2)}, u32[]{:S(2)}) async-start(bf16[16,16,16,128]{3,2,1,0:T(8,128)(2,1)} %shard_map.40), calls=%async_computation.2 | async-start | bytes 2097152 | tf_op jit(solution)/shard_map/all_to_all | solution.py:297
  76.9 30.4 %collective-permute-start = (bf16[4,32,16,128]{3,2,1,0:T(8,128)(2,1)}, bf16[4,32,16,128]{3,2,1,0:T(8,128)(2,1)S(1)}, u32[]{:S(2)}, u32[]{:S(2)}) collective-permute-start(bf16[4,32,16,128]{3,2,1,0:T(8,128)(2,1)} %get-tuple-element.9), channel_id=1, source_target_pairs={{0,1},{1,2},{2,3},{3,4},{4,5},{5,6},{6,7},{7,8},{8,9},{9,10},{10,1... | collective-permute-start | bytes 1572872 | tf_op jit(solution)/shard_map/ppermute | solution.py:272
  79.1 40.2 %collective-permute-start.1 = (bf16[4,32,16,128]{3,2,1,0:T(8,128)(2,1)}, bf16[4,32,16,128]{3,2,1,0:T(8,128)(2,1)S(1)}, u32[]{:S(2)}, u32[]{:S(2)}) collective-permute-start(bf16[4,32,16,128]{3,2,1,0:T(8,128)(2,1)} %get-tuple-element.10), channel_id=1, source_target_pairs={{1,0},{2,1},{3,2},{4,3},{5,4},{6,5},{7,6},{8,7},{9,8},{10,9},{11,1... | collective-permute-start | bytes 1572872 | tf_op jit(solution)/shard_map/ppermute | solution.py:273
  132.6 35.8 %all-to-all-start.1 = ((bf16[16,16,16,128]{3,2,1,0:T(8,128)(2,1)}), bf16[16,16,16,128]{3,2,1,0:T(8,128)(2,1)S(1)}, u32[]{:S(2)}, u32[]{:S(2)}) async-start(bf16[16,16,16,128]{3,2,1,0:T(8,128)(2,1)} %shard_map.38), calls=%async_computation.1 | async-start | bytes 2097152 | tf_op jit(solution)/shard_map/all_to_all | solution.py:297
  196.8 7.1 %collective-permute-start.6 = (f32[16,1024]{1,0:T(8,128)S(1)}, f32[16,1024]{1,0:T(8,128)S(1)}, u32[]{:S(2)}, u32[]{:S(2)}) collective-permute-start(f32[16,1024]{1,0:T(8,128)S(1)} %convert_reduce_fusion), channel_id=1, source_target_pairs={{0,128},{128,0},{1,129},{129,1},{2,130},{130,2},{3,131},{131,3},{4... | collective-permute-start | bytes 196616 | tf_op jit(solution)/shard_map/ppermute | solution.py:262
  230.8 5.7 %collective-permute-start.7 = (bf16[16,16,1024]{2,1,0:T(8,128)(2,1)S(1)}, bf16[16,16,1024]{2,1,0:T(8,128)(2,1)S(1)}, u32[]{:S(2)}, u32[]{:S(2)}) collective-permute-start(bf16[16,16,1024]{2,1,0:T(8,128)(2,1)S(1)} %all_to_all.32.mine_ref), channel_id=1, source_target_pairs={{0,16},{16,0},{1,17},{17,1},{2,18},{18,2},{3,19},{19,3},{4,20},{20... | collective-permute-start | bytes 1572872 | tf_op jit(solution)/shard_map/ppermute | solution.py:262

commit v4 on v3

--- a/solution.py
+++ b/solution.py
@@ -253,7 +253,14 @@
     blocks = lax.all_to_all(partial, NEAR, 0, 0, tiled=True)
     blocks = jnp.sum(blocks.astype(f32), axis=0)
     blocks = blocks + swapped(blocks, "zh")
-    blocks = jnp.sum(from_everyone(blocks, "zl"), axis=0).astype(bf16)
+    count = lax.axis_size("zl")
+    terms = [blocks] + [
+        lax.ppermute(blocks, "zl", [(i, i ^ k) for i in range(count)])
+        for k in range(1, count)
+    ]
+    while len(terms) > 1:
+        terms = [a + b for a, b in zip(terms[::2], terms[1::2])]
+    blocks = terms[0].astype(bf16)
     mine = from_everyone(blocks, SHARE)
     return mine, swapped(mine, "c")
 
@@ -277,10 +284,13 @@
 def pipeline(vectors, coefficient, ritz):
     count, planes, rows, lanes = vectors.shape
     size = count // CHUNKS
-    diag = from_everyone(coefficient, VEC)
-    diag = diag.transpose(1, 0, 2, 3).reshape(planes, rows, lanes)
-    below, above = swap_ends(diag[:HALO], diag[-HALO:])
-    diag = jnp.concatenate([below, diag, above], axis=0) + (6.0 - 7.125)
+    below, above = swap_ends(coefficient[:HALO], coefficient[-HALO:])
+    diag = jnp.concatenate([below, coefficient, above], axis=0) + (6.0 - 7.125)
+    other = swapped(diag, "zh")
+    first = lax.axis_index("zh") == 0
+    diag = jnp.stack([jnp.where(first, diag, other), jnp.where(first, other, diag)])
+    diag = from_everyone(diag, ("x", "c"))
+    diag = diag.transpose(2, 1, 0, 3, 4).reshape(-1, rows, lanes)
     place = lax.axis_index(DOM)
     ends = jnp.stack([place == 0, place == lax.axis_size(DOM) - 1]).astype(jnp.int32)
     cells = pltpu.with_memory_space_constraint(

time: 245 us -> 240 us (0.980)
  blocking collectives: 48.9 us -> 41.8 us
    all_to_all x2 -> x1, blocking collectives: 26.8 us -> 16.7 us  [from_everyone(): return lax.all_to_all(copies, axis, split_axis=0, concat_axis=0, tiled=True)]
    all_to_all x1, starting transfers between devices: 12.4 us -> 6.96 us  [from_everyone(): return lax.all_to_all(copies, axis, split_axis=0, concat_axis=0, tiled=True)]
    ppermute x0 -> x3, starting transfers between devices: none -> 4.94 us  [summed(): lax.ppermute(blocks, 'zl', [(i, i ^ k) for i in range(count)])]
    ppermute x3, waiting for transfers between devices: 31.2 us -> 26.7 us  [swap_ends(): from_above = lax.ppermute(low, DOM, [(i + 1, i) for i in range(count - 1)])]
    all_to_all x1, waiting for transfers between devices: 2.08 us -> 6.4 us  [from_everyone(): return lax.all_to_all(copies, axis, split_axis=0, concat_axis=0, tiled=True)]
    all_to_all x2, starting transfers between devices: 20.2 us -> 16.2 us  [pipeline(): held.append(lax.all_to_all(blocks, VEC, 0, 0, tiled=True))]
    ppermute x2 -> x3, starting transfers between devices: 4.29 us -> 8.15 us  [swapped(): return lax.ppermute(value, axis, [(0, 1), (1, 0)])]
    ppermute x0 -> x3, waiting for transfers between devices: none -> 3.3 us  [summed(): lax.ppermute(blocks, 'zl', [(i, i ^ k) for i in range(count)])]
  transfers between devices with their start and end apart: 11 -> 15, of which waited for: 7 -> 11; matrix products, arithmetic and copies ran while one was open for 0% -> 0% of each run, Pallas kernels for 11% -> 12%
where the time goes in v4:
time: 240 us; the launch traced here: 239 us
  waiting for transfers between devices  89.3 us (37%)
  Pallas kernels  54 us (22%)
  starting transfers between devices  50.9 us (21%)
  blocking collectives  41.8 us (17%)
    ppermute x3, waiting for transfers between devices, swap_ends(): from_above = lax.ppermute(low, DOM, [(i + 1, i) for i in range(count - 1)])  26.7 us
    pallas_call x2, Pallas kernels, filtered(): pl.pallas_call(filter_kernel, out_shape=jax.ShapeDtypeStruct((rows // 2,...  26.5 us
    ppermute x3, waiting for transfers between devices, swap_ends(): from_below = lax.ppermute(high, DOM, [(i, i + 1) for i in range(count - 1)])  25.2 us
    all_to_all x1, blocking collectives, summed(): blocks = lax.all_to_all(partial, NEAR, 0, 0, tiled=True)  25.1 us
    all_to_all x2, waiting for transfers between devices, pipeline(): held.append(lax.all_to_all(blocks, VEC, 0, 0, tiled=True))  19.1 us
    all_to_all x1, blocking collectives, from_everyone(): return lax.all_to_all(copies, axis, split_axis=0, concat_axis=0, tiled=True)  16.7 us
    all_to_all x2, starting transfers between devices, pipeline(): held.append(lax.all_to_all(blocks, VEC, 0, 0, tiled=True))  16.2 us
    pallas_call x2, Pallas kernels, projected(): pl.pallas_call(project_kernel, out_shape=jax.ShapeDtypeStruct((near, CHUN...  12.1 us
  transfers between devices with their start and end apart: 15, of which 11 were waited for; matrix products, arithmetic and copies ran while one was open for 0% of the time, Pallas kernels for 12%

profile of v4, /device:TPU:1, one launch (start us, length us, event | category | flops | bytes accessed | tf_op | source)
XLA Modules:
  0.0 238.9 jit_solution(6361427476871015015)
XLA Ops:
  0.0 0.7 fusion
  0.7 4.3 %collective-permute-start.2 = (f32[4,2,128]{2,1,0:T(2,128)S(1)}, f32[4,2,128]{2,1,0:T(2,128)S(1)}, u32[]{:S(2)}, u32[]{:S(2)}) collective-permute-start(f32[4,2,128]{2,1,0:T(2,128)S(1)} %get-tuple-element.15), channel_id=1, source_target_pairs={{0,1},{1,2},{2,3},{3,4},{4,5},{5,6},{6,7},{7,8},{8,9},{9,10},{10,1... | collective-permute-start | bytes 12296 | tf_op jit(solution)/shard_map/ppermute | solution.py:279
  5.1 1.3 collective-permute-start.3
  6.4 0.0 collective-permute-done.2
  6.4 3.2 %collective-permute-done.3 = f32[4,2,128]{2,1,0:T(2,128)S(1)} collective-permute-done((f32[4,2,128]{2,1,0:T(2,128)S(1)}, f32[4,2,128]{2,1,0:T(2,128)S(1)}, u32[]{:S(2)}, u32[]{:S(2)}) %collective-permute-start.3) | collective-permute-done | bytes 4128 | tf_op jit(solution)/shard_map/ppermute | solution.py:280
  9.6 0.7 maximum_add_fusion
  10.3 5.9 %collective-permute-start.4 = (f32[16,2,128]{2,1,0:T(2,128)S(1)}, f32[16,2,128]{2,1,0:T(2,128)S(1)}, u32[]{:S(2)}, u32[]{:S(2)}) collective-permute-start(f32[16,2,128]{2,1,0:T(2,128)S(1)} %maximum_add_fusion), channel_id=1, source_target_pairs={{0,128},{128,0},{1,129},{129,1},{2,130},{130,2},{3,131},{131,3},{4... | collective-permute-start | bytes 49160 | tf_op jit(solution)/shard_map/ppermute | solution.py:269
  16.2 0.0 copy-start
  16.2 4.1 %shard_map.39 = (bf16[4,32,16,128]{3,2,1,0:T(8,128)(2,1)}, bf16[4,32,16,128]{3,2,1,0:T(8,128)(2,1)}) custom-call(f32[32,256,128]{2,1,0:T(8,128)} %bitcast.14, f32[32,256,128]{2,1,0:T(8,128)} %bitcast.15), custom_call_target="tpu_custom_call" | custom-call | flops 524288 | bytes 3145728 | tf_op jit(solution)/shard_map/pallas_call | solution.py:34
  20.3 2.7 %collective-permute-start.5 = (bf16[4,32,16,128]{3,2,1,0:T(8,128)(2,1)}, bf16[4,32,16,128]{3,2,1,0:T(8,128)(2,1)S(1)}, u32[]{:S(2)}, u32[]{:S(2)}) collective-permute-start(bf16[4,32,16,128]{3,2,1,0:T(8,128)(2,1)} %get-tuple-element.11), channel_id=1, source_target_pairs={{0,1},{1,2},{2,3},{3,4},{4,5},{5,6},{6,7},{7,8},{8,9},{9,10},{10,1... | collective-permute-start | bytes 1572872 | tf_op jit(solution)/shard_map/ppermute | solution.py:279
  23.0 1.3 collective-permute-start.6
  24.3 0.0 collective-permute-done.4
  24.3 0.0 copy-done
  24.4 0.8 broadcast_in_dim.6
  25.1 7.0 %all-to-all-start = ((f32[8,2,16,2,128]{4,3,1,2,0:T(2,128)}), f32[8,2,16,2,128]{4,3,1,2,0:T(2,128)S(1)}, u32[]{:S(2)}, u32[]{:S(2)}) async-start(f32[8,2,16,2,128]{4,3,1,2,0:T(2,128)} %broadcast_in_dim.6), calls=%async_computation | async-start | bytes 524288 | tf_op jit(solution)/shard_map/all_to_all | solution.py:274
  32.1 0.1 add_convert_fusion.1.ends_ref
  32.2 6.4 %all-to-all-done = f32[8,2,16,2,128]{4,3,1,2,0:T(2,128)S(1)} async-done(((f32[8,2,16,2,128]{4,3,1,2,0:T(2,128)}), f32[8,2,16,2,128]{4,3,1,2,0:T(2,128)S(1)}, u32[]{:S(2)}, u32[]{:S(2)}) %all-to-all-start) | async-done | bytes 262176 | tf_op jit(solution)/shard_map/all_to_all | solution.py:274
  38.6 0.1 copy.7
  38.7 0.0 collective-permute-done.5.low_ref
  38.7 10.2 %collective-permute-done.6.high_ref = bf16[4,32,16,128]{3,2,1,0:T(8,128)(2,1)S(1)} collective-permute-done((bf16[4,32,16,128]{3,2,1,0:T(8,128)(2,1)}, bf16[4,32,16,128]{3,2,1,0:T(8,128)(2,1)S(1)}, u32[]{:S(2)}, u32[]{:S(2)}) %collective-permute-start.6) | collective-permute-done | bytes 524320 | tf_op jit(solution)/shard_map/ppermute | solution.py:280
  48.9 13.3 %shard_map.40 = bf16[16,16,16,128]{3,2,1,0:T(8,128)(2,1)} custom-call(s32[2]{0:T(128)S(1)} %add_convert_fusion.1.ends_ref, f32[32,256,128]{2,1,0:T(8,128)} %bitcast.16, bf16[4,32,16,128]{3,2,1,0:T(8,128)(2,1)S(1)} %collective-permute-done.5.low_ref, bf16[4,32,16,128]{3,2,1,0:T(8,128)(2,1)S(1)} %collective-permute-done.6.high_ref, f32[16,32,128]{2,1,0:T(8,128)S(1)} %bitcast.12), custom_call_target="tpu_custom_call" | custom-call | flops 34603008 | bytes 5242880 | tf_op jit(solution)/shard_map/pallas_call | solution.py:128
  62.2 6.5 %all-to-all-start.2 = ((bf16[16,16,16,128]{3,2,1,0:T(8,128)(2,1)}), bf16[16,16,16,128]{3,2,1,0:T(8,128)(2,1)S(1)}, u32[]{:S(2)}, u32[]{:S(2)}) async-start(bf16[16,16,16,128]{3,2,1,0:T(8,128)(2,1)} %shard_map.40), calls=%async_computation.2 | async-start | bytes 2097152 | tf_op jit(solution)/shard_map/all_to_all | solution.py:307
  68.7 4.1 %shard_map.37 = (bf16[4,32,16,128]{3,2,1,0:T(8,128)(2,1)}, bf16[4,32,16,128]{3,2,1,0:T(8,128)(2,1)}) custom-call(f32[32,256,128]{2,1,0:T(8,128)} %bitcast.17, f32[32,256,128]{2,1,0:T(8,128)} %bitcast.18), custom_call_target="tpu_custom_call" | custom-call | flops 524288 | bytes 3145728 | tf_op jit(solution)/shard_map/pallas_call | solution.py:34
  72.7 3.8 %collective-permute-start = (bf16[4,32,16,128]{3,2,1,0:T(8,128)(2,1)}, bf16[4,32,16,128]{3,2,1,0:T(8,128)(2,1)S(1)}, u32[]{:S(2)}, u32[]{:S(2)}) collective-permute-start(bf16[4,32,16,128]{3,2,1,0:T(8,128)(2,1)} %get-tuple-element.9), channel_id=1, source_target_pairs={{0,1},{1,2},{2,3},{3,4},{4,5},{5,6},{6,7},{7,8},{8,9},{9,10},{10,1... | collective-permute-start | bytes 1572872 | tf_op jit(solution)/shard_map/ppermute | solution.py:279
  76.6 1.3 collective-permute-start.1
  77.9 25.2 %collective-permute-done.low_ref = bf16[4,32,16,128]{3,2,1,0:T(8,128)(2,1)S(1)} collective-permute-done((bf16[4,32,16,128]{3,2,1,0:T(8,128)(2,1)}, bf16[4,32,16,128]{3,2,1,0:T(8,128)(2,1)S(1)}, u32[]{:S(2)}, u32[]{:S(2)}) %collective-permute-start) | collective-permute-done | bytes 524320 | tf_op jit(solution)/shard_map/ppermute | solution.py:279
  103.1 13.3 %collective-permute-done.1.high_ref = bf16[4,32,16,128]{3,2,1,0:T(8,128)(2,1)S(1)} collective-permute-done((bf16[4,32,16,128]{3,2,1,0:T(8,128)(2,1)}, bf16[4,32,16,128]{3,2,1,0:T(8,128)(2,1)S(1)}, u32[]{:S(2)}, u32[]{:S(2)}) %collective-permute-start.1) | collective-permute-done | bytes 524320 | tf_op jit(solution)/shard_map/ppermute | solution.py:280
  116.4 13.3 %shard_map.38 = bf16[16,16,16,128]{3,2,1,0:T(8,128)(2,1)} custom-call(s32[2]{0:T(128)S(1)} %add_convert_fusion.1.ends_ref, f32[32,256,128]{2,1,0:T(8,128)} %bitcast.19, bf16[4,32,16,128]{3,2,1,0:T(8,128)(2,1)S(1)} %collective-permute-done.low_ref, bf16[4,32,16,128]{3,2,1,0:T(8,128)(2,1)S(1)} %collective-permute-done.1.high_ref, f32[16,32,128]{2,1,0:T(8,128)S(1)} %bitcast.13), custom_call_target="tpu_custom_call" | custom-call | flops 34603008 | bytes 5242880 | tf_op jit(solution)/shard_map/pallas_call | solution.py:128
  129.7 0.0 all-to-all-done.2.cells_ref.refs_0_
  129.7 9.7 %all-to-all-start.1 = ((bf16[16,16,16,128]{3,2,1,0:T(8,128)(2,1)}), bf16[16,16,16,128]{3,2,1,0:T(8,128)(2,1)S(1)}, u32[]{:S(2)}, u32[]{:S(2)}) async-start(bf16[16,16,16,128]{3,2,1,0:T(8,128)(2,1)} %shard_map.38), calls=%async_computation.1 | async-start | bytes 2097152 | tf_op jit(solution)/shard_map/all_to_all | solution.py:307
  139.4 6.1 %shard_map.41.refs_0_ = bf16[32,16,1024]{2,1,0:T(8,128)(2,1)S(1)} custom-call(bf16[16,16,16,128]{3,2,1,0:T(8,128)(2,1)S(1)} %all-to-all-done.2.cells_ref.refs_0_, bf16[16,128,1024]{2,1,0:T(8,128)(2,1)} %bitcast.20), custom_call_target="tpu_custom_call" | custom-call | flops 1073741824 | bytes 7340032 | tf_op jit(solution)/shard_map/pallas_call | solution.py:182
  145.5 19.1 %all-to-all-done.1.cells_ref.refs_1_ = bf16[16,16,16,128]{3,2,1,0:T(8,128)(2,1)S(1)} async-done(((bf16[16,16,16,128]{3,2,1,0:T(8,128)(2,1)}), bf16[16,16,16,128]{3,2,1,0:T(8,128)(2,1)S(1)}, u32[]{:S(2)}, u32[]{:S(2)}) %all-to-all-start.1) | async-done | bytes 1048608 | tf_op jit(solution)/shard_map/all_to_all | solution.py:307
  164.6 6.1 %shard_map.42 = bf16[32,16,1024]{2,1,0:T(8,128)(2,1)S(1)} custom-call(bf16[16,16,16,128]{3,2,1,0:T(8,128)(2,1)S(1)} %all-to-all-done.1.cells_ref.refs_1_, bf16[16,128,1024]{2,1,0:T(8,128)(2,1)} %bitcast.21, bf16[32,16,1024]{2,1,0:T(8,128)(2,1)S(1)} %shard_map.41.refs_0_), custom_call_target="tpu_custom_call", output_to_operand_aliasing={{}: (2, {})} | custom-call | flops 1073741824 | bytes 7340032 | tf_op jit(solution)/shard_map/pallas_call | solution.py:182
  170.7 25.1 %all_to_all.25 = bf16[32,16,1024]{2,1,0:T(8,128)(2,1)S(1)} all-to-all(bf16[32,16,1024]{2,1,0:T(8,128)(2,1)S(1)} %shard_map.42), channel_id=1, replica_groups=mesh['zh'=2,'x'=4,'c'=2,'y'=4,'zl'=4] {'c','x','y'}, dimensions={0} | all-to-all | bytes 2097152 | tf_op jit(solution)/shard_map/all_to_all | solution.py:253
  195.8 0.2 convert_reduce_fusion
  195.9 0.1 collective-permute-start.7
  196.0 7.0 %collective-permute-done.7 = f32[16,1024]{1,0:T(8,128)S(1)} collective-permute-done((f32[16,1024]{1,0:T(8,128)S(1)}, f32[16,1024]{1,0:T(8,128)S(1)}, u32[]{:S(2)}, u32[]{:S(2)}) %collective-permute-start.7) | collective-permute-done | bytes 65568 | tf_op jit(solution)/shard_map/ppermute | solution.py:269
  203.1 1.2 collective-permute-start.10
  204.3 3.7 %collective-permute-start.9 = (f32[16,1024]{1,0:T(8,128)S(1)}, f32[16,1024]{1,0:T(8,128)S(1)}, u32[]{:S(2)}, u32[]{:S(2)}) collective-permute-start(f32[16,1024]{1,0:T(8,128)S(1)} %add.24), channel_id=1, source_target_pairs={{0,2},{1,3},{2,0},{3,1},{4,6},{5,7},{6,4},{7,5},{8,10},{9,11},{10,... | collective-permute-start | bytes 196616 | tf_op jit(solution)/shard_map/ppermute | solution.py:258
  208.0 0.0 collective-permute-start.8
  208.0 0.4 collective-permute-done.10
  208.4 2.7 %collective-permute-done.9 = f32[16,1024]{1,0:T(8,128)S(1)} collective-permute-done((f32[16,1024]{1,0:T(8,128)S(1)}, f32[16,1024]{1,0:T(8,128)S(1)}, u32[]{:S(2)}, u32[]{:S(2)}) %collective-permute-start.9) | collective-permute-done | bytes 65568 | tf_op jit(solution)/shard_map/ppermute | solution.py:258
  211.1 0.2 collective-permute-done.8
  211.3 0.1 broadcast_in_dim.7
  211.4 16.7 %all_to_all.26.mine_ref = bf16[16,16,1024]{2,1,0:T(8,128)(2,1)S(1)} all-to-all(bf16[16,16,1024]{2,1,0:T(8,128)(2,1)S(1)} %broadcast_in_dim.7), channel_id=1, replica_groups=mesh['zh'=2,'x'=4,'c'=2,'y'=4,'zl'=4] {'x','y'}, dimensions={0} | all-to-all | bytes 1048576 | tf_op jit(solution)/shard_map/all_to_all | solution.py:274
  228.0 2.2 collective-permute-start.11
  230.2 1.5 collective-permute-done.11.other_ref
  231.7 7.2 %shard_map.43 = f32[16,512,128]{2,1,0:T(8,128)} custom-call(s32[1]{0:T(128)} %bitcast.core_ref, bf16[16,16,1024]{2,1,0:T(8,128)(2,1)S(1)} %all_to_all.26.mine_ref, bf16[16,16,1024]{2,1,0:T(8,128)(2,1)S(1)} %collective-permute-done.11.other_ref, bf16[16,128,1024]{2,1,0:T(8,128)(2,1)} %bitcast.22, ...), custom_call_target="tpu_custom_call" | custom-call | flops 2147483648 | bytes 11534336 | tf_op jit(solution)/shard_map/pallas_call | solution.py:231
  (5 shorter events, 0.1 us)
Async XLA Ops:
  0.7 5.7 %collective-permute-start.2 = (f32[4,2,128]{2,1,0:T(2,128)S(1)}, f32[4,2,128]{2,1,0:T(2,128)S(1)}, u32[]{:S(2)}, u32[]{:S(2)}) collective-permute-start(f32[4,2,128]{2,1,0:T(2,128)S(1)} %get-tuple-element.15), channel_id=1, source_target_pairs={{0,1},{1,2},{2,3},{3,4},{4,5},{5,6},{6,7},{7,8},{8,9},{9,10},{10,1... | collective-permute-start | bytes 12296 | tf_op jit(solution)/shard_map/ppermute | solution.py:279
  5.1 4.5 %collective-permute-start.3 = (f32[4,2,128]{2,1,0:T(2,128)S(1)}, f32[4,2,128]{2,1,0:T(2,128)S(1)}, u32[]{:S(2)}, u32[]{:S(2)}) collective-permute-start(f32[4,2,128]{2,1,0:T(2,128)S(1)} %get-tuple-element.16), channel_id=1, source_target_pairs={{1,0},{2,1},{3,2},{4,3},{5,4},{6,5},{7,6},{8,7},{9,8},{10,9},{11,1... | collective-permute-start | bytes 12296 | tf_op jit(solution)/shard_map/ppermute | solution.py:280
  10.3 14.0 %collective-permute-start.4 = (f32[16,2,128]{2,1,0:T(2,128)S(1)}, f32[16,2,128]{2,1,0:T(2,128)S(1)}, u32[]{:S(2)}, u32[]{:S(2)}) collective-permute-start(f32[16,2,128]{2,1,0:T(2,128)S(1)} %maximum_add_fusion), channel_id=1, source_target_pairs={{0,128},{128,0},{1,129},{129,1},{2,130},{130,2},{3,131},{131,3},{4... | collective-permute-start | bytes 49160 | tf_op jit(solution)/shard_map/ppermute | solution.py:269
  16.2 8.1 %copy-start = (f32[8,2,128]{2,1,0:T(2,128)S(1)}, f32[8,2,128]{2,1,0:T(2,128)}, u32[]{:S(2)}) copy-start(f32[8,2,128]{2,1,0:T(2,128)} %param.4) | copy-start | bytes 24580
  20.3 18.4 %collective-permute-start.5 = (bf16[4,32,16,128]{3,2,1,0:T(8,128)(2,1)}, bf16[4,32,16,128]{3,2,1,0:T(8,128)(2,1)S(1)}, u32[]{:S(2)}, u32[]{:S(2)}) collective-permute-start(bf16[4,32,16,128]{3,2,1,0:T(8,128)(2,1)} %get-tuple-element.11), channel_id=1, source_target_pairs={{0,1},{1,2},{2,3},{3,4},{4,5},{5,6},{6,7},{7,8},{8,9},{9,10},{10,1... | collective-permute-start | bytes 1572872 | tf_op jit(solution)/shard_map/ppermute | solution.py:279
  23.0 25.9 %collective-permute-start.6 = (bf16[4,32,16,128]{3,2,1,0:T(8,128)(2,1)}, bf16[4,32,16,128]{3,2,1,0:T(8,128)(2,1)S(1)}, u32[]{:S(2)}, u32[]{:S(2)}) collective-permute-start(bf16[4,32,16,128]{3,2,1,0:T(8,128)(2,1)} %get-tuple-element.12), channel_id=1, source_target_pairs={{1,0},{2,1},{3,2},{4,3},{5,4},{6,5},{7,6},{8,7},{9,8},{10,9},{11,1... | collective-permute-start | bytes 1572872 | tf_op jit(solution)/shard_map/ppermute | solution.py:280
  25.1 13.4 %all-to-all-start = ((f32[8,2,16,2,128]{4,3,1,2,0:T(2,128)}), f32[8,2,16,2,128]{4,3,1,2,0:T(2,128)S(1)}, u32[]{:S(2)}, u32[]{:S(2)}) async-start(f32[8,2,16,2,128]{4,3,1,2,0:T(2,128)} %broadcast_in_dim.6), calls=%async_computation | async-start | bytes 524288 | tf_op jit(solution)/shard_map/all_to_all | solution.py:274
  62.2 67.5 %all-to-all-start.2 = ((bf16[16,16,16,128]{3,2,1,0:T(8,128)(2,1)}), bf16[16,16,16,128]{3,2,1,0:T(8,128)(2,1)S(1)}, u32[]{:S(2)}, u32[]{:S(2)}) async-start(bf16[16,16,16,128]{3,2,1,0:T(8,128)(2,1)} %shard_map.40), calls=%async_computation.2 | async-start | bytes 2097152 | tf_op jit(solution)/shard_map/all_to_all | solution.py:307
  72.7 30.3 %collective-permute-start = (bf16[4,32,16,128]{3,2,1,0:T(8,128)(2,1)}, bf16[4,32,16,128]{3,2,1,0:T(8,128)(2,1)S(1)}, u32[]{:S(2)}, u32[]{:S(2)}) collective-permute-start(bf16[4,32,16,128]{3,2,1,0:T(8,128)(2,1)} %get-tuple-element.9), channel_id=1, source_target_pairs={{0,1},{1,2},{2,3},{3,4},{4,5},{5,6},{6,7},{7,8},{8,9},{9,10},{10,1... | collective-permute-start | bytes 1572872 | tf_op jit(solution)/shard_map/ppermute | solution.py:279
  76.6 39.8 %collective-permute-start.1 = (bf16[4,32,16,128]{3,2,1,0:T(8,128)(2,1)}, bf16[4,32,16,128]{3,2,1,0:T(8,128)(2,1)S(1)}, u32[]{:S(2)}, u32[]{:S(2)}) collective-permute-start(bf16[4,32,16,128]{3,2,1,0:T(8,128)(2,1)} %get-tuple-element.10), channel_id=1, source_target_pairs={{1,0},{2,1},{3,2},{4,3},{5,4},{6,5},{7,6},{8,7},{9,8},{10,9},{11,1... | collective-permute-start | bytes 1572872 | tf_op jit(solution)/shard_map/ppermute | solution.py:280
  129.7 34.9 %all-to-all-start.1 = ((bf16[16,16,16,128]{3,2,1,0:T(8,128)(2,1)}), bf16[16,16,16,128]{3,2,1,0:T(8,128)(2,1)S(1)}, u32[]{:S(2)}, u32[]{:S(2)}) async-start(bf16[16,16,16,128]{3,2,1,0:T(8,128)(2,1)} %shard_map.38), calls=%async_computation.1 | async-start | bytes 2097152 | tf_op jit(solution)/shard_map/all_to_all | solution.py:307
  195.9 7.1 %collective-permute-start.7 = (f32[16,1024]{1,0:T(8,128)S(1)}, f32[16,1024]{1,0:T(8,128)S(1)}, u32[]{:S(2)}, u32[]{:S(2)}) collective-permute-start(f32[16,1024]{1,0:T(8,128)S(1)} %convert_reduce_fusion), channel_id=1, source_target_pairs={{0,128},{128,0},{1,129},{129,1},{2,130},{130,2},{3,131},{131,3},{4... | collective-permute-start | bytes 196616 | tf_op jit(solution)/shard_map/ppermute | solution.py:269
  203.1 5.3 %collective-permute-start.10 = (f32[16,1024]{1,0:T(8,128)S(1)}, f32[16,1024]{1,0:T(8,128)S(1)}, u32[]{:S(2)}, u32[]{:S(2)}) collective-permute-start(f32[16,1024]{1,0:T(8,128)S(1)} %add.24), channel_id=1, source_target_pairs={{0,3},{1,2},{2,1},{3,0},{4,7},{5,6},{6,5},{7,4},{8,11},{9,10},{10,... | collective-permute-start | bytes 196616 | tf_op jit(solution)/shard_map/ppermute | solution.py:258
  204.3 6.9 %collective-permute-start.9 = (f32[16,1024]{1,0:T(8,128)S(1)}, f32[16,1024]{1,0:T(8,128)S(1)}, u32[]{:S(2)}, u32[]{:S(2)}) collective-permute-start(f32[16,1024]{1,0:T(8,128)S(1)} %add.24), channel_id=1, source_target_pairs={{0,2},{1,3},{2,0},{3,1},{4,6},{5,7},{6,4},{7,5},{8,10},{9,11},{10,... | collective-permute-start | bytes 196616 | tf_op jit(solution)/shard_map/ppermute | solution.py:258
  208.0 3.3 %collective-permute-start.8 = (f32[16,1024]{1,0:T(8,128)S(1)}, f32[16,1024]{1,0:T(8,128)S(1)}, u32[]{:S(2)}, u32[]{:S(2)}) collective-permute-start(f32[16,1024]{1,0:T(8,128)S(1)} %add.24), channel_id=1, source_target_pairs={{0,1},{1,0},{2,3},{3,2},{4,5},{5,4},{6,7},{7,6},{8,9},{9,8},{10,11... | collective-permute-start | bytes 196616 | tf_op jit(solution)/shard_map/ppermute | solution.py:258
  228.0 3.7 %collective-permute-start.11 = (bf16[16,16,1024]{2,1,0:T(8,128)(2,1)S(1)}, bf16[16,16,1024]{2,1,0:T(8,128)(2,1)S(1)}, u32[]{:S(2)}, u32[]{:S(2)}) collective-permute-start(bf16[16,16,1024]{2,1,0:T(8,128)(2,1)S(1)} %all_to_all.26.mine_ref), channel_id=1, source_target_pairs={{0,16},{16,0},{1,17},{17,1},{2,18},{18,2},{3,19},{19,3},{4,20},{20... | collective-permute-start | bytes 1572872 | tf_op jit(solution)/shard_map/ppermute | solution.py:269

commit v5 on v4

--- a/solution.py
+++ b/solution.py
@@ -120,14 +120,36 @@
     step(odd, even, 12.25, 4, 8.0 / 2401.0)
 
 
-def filtered(ends, cells, low, high, diag, chunk, size):
+def split_filter_kernel(ends_ref, own_ref, low_ref, high_ref, diag_ref, *refs):
+    *out_refs, even, odd, blocks, sems = refs
+    filter_kernel(ends_ref, own_ref, low_ref, high_ref, diag_ref, blocks, even, odd)
+    copies = [
+        pltpu.make_async_copy(blocks.at[ends_ref[2] ^ k], out_ref, sems.at[k])
+        for k, out_ref in enumerate(out_refs)
+    ]
+    for copy in copies:
+        copy.start()
+    for copy in copies:
+        copy.wait()
+
+
+def filtered(ends, cells, low, high, diag, chunk, size, split):
     total, rows, lanes = diag.shape
     planes = total - 2 * HALO
     groups = size // GROUP
     edge = pl.BlockSpec((HALO, rows, GROUP, lanes), lambda g: (0, 0, g, 0))
+    count, shape = rows // 2, (2 * planes, GROUP, lanes)
+    scratch = [pltpu.VMEM((total, rows, GROUP, lanes), f32)] * 2
+    if split:
+        out_shape = [jax.ShapeDtypeStruct(shape, bf16)] * count
+        out_specs = [pl.BlockSpec(memory_space=pl.ANY)] * count
+        scratch += [pltpu.VMEM((count, *shape), bf16), pltpu.SemaphoreType.DMA((count,))]
+    else:
+        out_shape = jax.ShapeDtypeStruct((count, 2 * planes, size, lanes), bf16)
+        out_specs = pl.BlockSpec((count, *shape), lambda g: (0, 0, g, 0))
     return pl.pallas_call(
-        filter_kernel,
-        out_shape=jax.ShapeDtypeStruct((rows // 2, 2 * planes, size, lanes), bf16),
+        split_filter_kernel if split else filter_kernel,
+        out_shape=out_shape,
         grid=(groups,),
         in_specs=[
             pl.BlockSpec(memory_space=pltpu.SMEM),
@@ -136,8 +158,8 @@
             edge,
             pl.BlockSpec((total, rows, lanes), lambda g: (0, 0, 0)),
         ],
-        out_specs=pl.BlockSpec((rows // 2, 2 * planes, GROUP, lanes), lambda g: (0, 0, g, 0)),
-        scratch_shapes=[pltpu.VMEM((total, rows, GROUP, lanes), f32)] * 2,
+        out_specs=out_specs,
+        scratch_shapes=scratch,
         compiler_params=pltpu.CompilerParams(vmem_limit_bytes=24 << 20),
         cost_estimate=pl.CostEstimate(
             flops=12 * 44 * rows * size * lanes, bytes_accessed=5 << 20, transcendentals=0
@@ -145,20 +167,23 @@
     )(ends, cells, low, high, diag)
 
 
-def project_kernel(cells_ref, ritz_ref, *refs):
-    out_ref, total = refs[-2:]
+def project_kernel(ritz_ref, cells_ref, out_ref, total):
+    lanes = cells_ref.shape[3]
+    pair = jnp.concatenate(
+        [cells_ref[:, 0].reshape(-1, lanes), cells_ref[:, 1].reshape(-1, lanes)], axis=1
+    )
+    accumulate(pair, ritz_ref, out_ref, total)
+
+
+def accumulate(pair, ritz_ref, out_ref, total):
     step = pl.program_id(0)
-    lanes = cells_ref.shape[3]
 
     @pl.when(step == 0)
     def _():
         total[...] = jnp.zeros_like(total)
 
-    pair = jnp.concatenate(
-        [cells_ref[:, 0].reshape(-1, lanes), cells_ref[:, 1].reshape(-1, lanes)], axis=1
-    )
     total[...] += jnp.dot(
-        pair, ritz_ref[...].reshape(2 * lanes, -1), preferred_element_type=f32
+        pair, ritz_ref[...].reshape(pair.shape[1], -1), preferred_element_type=f32
     )
 
     @pl.when(step == pl.num_programs(0) - 1)
@@ -166,32 +191,49 @@
         out_ref[...] = total[...].astype(bf16).reshape(out_ref.shape)
 
 
-def projected(cells, ritz, held, chunk, near):
-    blocks, rows, vectors, lanes = cells.shape
+def joined_project_kernel(place_ref, ritz_ref, *refs):
+    *block_refs, out_ref, held_ref, total, pairs = refs
+    for k, block_ref in enumerate(block_refs):
+        source = place_ref[0] ^ k
+        held_ref[source] = block_ref[...]
+        pairs[source] = jnp.concatenate([block_ref[0], block_ref[1]], axis=1)
+    accumulate(pairs[...].reshape(-1, pairs.shape[2]), ritz_ref, out_ref, total)
+
+
+def projected(cells, ritz, near, place):
+    joined = isinstance(cells, list)
+    blocks = len(cells)
+    rows, vectors, lanes = cells[0].shape
     kept = ritz.shape[2]
     count = blocks * vectors
-    size = count // near
-    specs = [
-        pl.BlockSpec((blocks, 2, vectors, lanes), lambda r: (0, r, 0, 0)),
-        pl.BlockSpec((2, lanes, kept), lambda r: (r, 0, 0)),
-    ]
-    operands = [cells, ritz]
-    if held is not None:
-        specs.append(pl.BlockSpec(memory_space=pl.ANY))
-        operands.append(held)
-    return pl.pallas_call(
-        project_kernel,
-        out_shape=jax.ShapeDtypeStruct((near, CHUNKS * size, kept), bf16),
+    out_shape = [jax.ShapeDtypeStruct((near, count // near, kept), bf16)]
+    out_specs = [pl.BlockSpec((near, count // near, kept), lambda r: (0, 0, 0))]
+    in_specs = [pl.BlockSpec((2, lanes, kept), lambda r: (r, 0, 0))]
+    scratch = [pltpu.VMEM((count, kept), f32)]
+    block = pl.BlockSpec((blocks, 2, vectors, lanes), lambda r: (0, r, 0, 0))
+    if joined:
+        in_specs.insert(0, pl.BlockSpec(memory_space=pltpu.SMEM))
+        in_specs += [pl.BlockSpec((2, vectors, lanes), lambda r: (r, 0, 0))] * blocks
+        out_shape.append(jax.ShapeDtypeStruct((blocks, rows, vectors, lanes), bf16))
+        out_specs.append(block)
+        scratch.append(pltpu.VMEM((blocks, vectors, 2 * lanes), bf16))
+        operands = [place, ritz, *cells]
+    else:
+        in_specs.append(block)
+        operands = [ritz, cells]
+    out = pl.pallas_call(
+        joined_project_kernel if joined else project_kernel,
+        out_shape=out_shape,
         grid=(rows // 2,),
-        in_specs=specs,
-        out_specs=pl.BlockSpec((near, size, kept), lambda r: (0, chunk, 0)),
-        scratch_shapes=[pltpu.VMEM((count, kept), f32)],
-        input_output_aliases={} if held is None else {2: 0},
+        in_specs=in_specs,
+        out_specs=out_specs,
+        scratch_shapes=scratch,
         compiler_params=pltpu.CompilerParams(vmem_limit_bytes=24 << 20),
         cost_estimate=pl.CostEstimate(
             flops=2 * count * rows * lanes * kept, bytes_accessed=7 << 20, transcendentals=0
         ),
     )(*operands)
+    return (out[0], out[1]) if joined else (out[0], cells)
 
 
 def remove_kernel(core_ref, mine_ref, other_ref, ritz_ref, *refs):
@@ -249,9 +291,22 @@
     )(core, mine, other, ritz, *held)
 
 
-def summed(partial):
+def exchanged(blocks, axis):
+    size = len(blocks)
+    half = size // 2
+    received = list(blocks)
+    for k in [*range(half, size), *range(1, half)]:
+        received[k] = lax.ppermute(blocks[k], axis, [(i, i ^ k) for i in range(size)])
+    return received
+
+
+def near_sum(partial):
     blocks = lax.all_to_all(partial, NEAR, 0, 0, tiled=True)
-    blocks = jnp.sum(blocks.astype(f32), axis=0)
+    return jnp.sum(blocks.astype(f32), axis=0)
+
+
+def summed(parts):
+    blocks = jnp.concatenate(parts, axis=0)
     blocks = blocks + swapped(blocks, "zh")
     count = lax.axis_size("zl")
     terms = [blocks] + [
@@ -292,22 +347,31 @@
     diag = from_everyone(diag, ("x", "c"))
     diag = diag.transpose(2, 1, 0, 3, 4).reshape(-1, rows, lanes)
     place = lax.axis_index(DOM)
+    column = lax.axis_index(VEC).astype(jnp.int32)
     ends = jnp.stack([place == 0, place == lax.axis_size(DOM) - 1]).astype(jnp.int32)
+    ends = jnp.concatenate([ends, column.reshape(1)])
     cells = pltpu.with_memory_space_constraint(
         vectors.reshape(count, planes * rows, lanes), pltpu.MemorySpace.HBM
     )
     ritz_rows = pltpu.with_memory_space_constraint(
         ritz.reshape(-1, *ritz.shape[2:]), pltpu.MemorySpace.HBM
     )
-    held, total = [], None
+    held, parts = [], []
     for k in range(CHUNKS):
+        last = k == CHUNKS - 1
         low, high = spread(cells, rows, k, size)
         low, high = swap_ends(low, high)
-        blocks = filtered(ends, cells, low, high, diag, k, size)
-        held.append(lax.all_to_all(blocks, VEC, 0, 0, tiled=True))
+        blocks = filtered(ends, cells, low, high, diag, k, size, last)
+        if last:
+            held.append(exchanged(list(blocks), VEC))
+        else:
+            held.append(lax.all_to_all(blocks, VEC, 0, 0, tiled=True))
     for k in range(CHUNKS):
-        total = projected(held[k], ritz_rows, total, k, lax.axis_size(NEAR))
-    mine, other = summed(total)
+        partial, held[k] = projected(
+            held[k], ritz_rows, lax.axis_size(NEAR), column.reshape(1)
+        )
+        parts.append(near_sum(partial))
+    mine, other = summed(parts)
     core = lax.axis_index("c").reshape(1).astype(jnp.int32)
     out = residual(core, mine, other, ritz_rows, held)
     return out.reshape(-1, *coefficient.shape)

time: 240 us -> 259 us (1.079)
  starting transfers between devices: 50.9 us -> 92.2 us
  blocking collectives: 41.8 us -> 14.1 us
    ppermute x0 -> x15, starting transfers between devices: none -> 36.9 us  [exchanged(): lax.ppermute(blocks[k], axis, [(i, i ^ k) for i in range(size)])]
    all_to_all x1 -> x0, blocking collectives: 25.1 us -> none  [summed(): blocks = lax.all_to_all(partial, NEAR, 0, 0, tiled=True)]
    all_to_all x2 -> x1, waiting for transfers between devices: 19.1 us -> 0.01 us  [pipeline(): held.append(lax.all_to_all(blocks, VEC, 0, 0, tiled=True))]
    all_to_all x0 -> x2, waiting for transfers between devices: none -> 15.2 us  [near_sum(): blocks = lax.all_to_all(partial, NEAR, 0, 0, tiled=True)]
    all_to_all x0 -> x2, starting transfers between devices: none -> 10.7 us  [near_sum(): blocks = lax.all_to_all(partial, NEAR, 0, 0, tiled=True)]
    all_to_all x2 -> x1, starting transfers between devices: 16.2 us -> 6.47 us  [pipeline(): held.append(lax.all_to_all(blocks, VEC, 0, 0, tiled=True))]
    ppermute x0 -> x15, waiting for transfers between devices: none -> 9.56 us  [exchanged(): lax.ppermute(blocks[k], axis, [(i, i ^ k) for i in range(size)])]
    ppermute x3, starting transfers between devices: 8.15 us -> 12.8 us  [swapped(): return lax.ppermute(value, axis, [(0, 1), (1, 0)])]
  transfers between devices with their start and end apart: 15 -> 31, of which waited for: 11 -> 14; matrix products, arithmetic and copies ran while one was open for 0% -> 0% of each run, Pallas kernels for 12% -> 14%
where the time goes in v5:
time: 259 us; the launch traced here: 257 us
  starting transfers between devices  92.2 us (36%)
  waiting for transfers between devices  91.8 us (35%)
  Pallas kernels  56.3 us (22%)
  blocking collectives  14.1 us (5%)
    ppermute x15, starting transfers between devices, exchanged(): lax.ppermute(blocks[k], axis, [(i, i ^ k) for i in range(size)])  36.9 us
    pallas_call x2, Pallas kernels, filtered(): pl.pallas_call(split_filter_kernel if split else filter_kernel, out_shape...  27.1 us
    ppermute x3, waiting for transfers between devices, swap_ends(): from_above = lax.ppermute(low, DOM, [(i + 1, i) for i in range(count - 1)])  26.7 us
    ppermute x3, waiting for transfers between devices, swap_ends(): from_below = lax.ppermute(high, DOM, [(i, i + 1) for i in range(count - 1)])  25.2 us
    all_to_all x2, waiting for transfers between devices, near_sum(): blocks = lax.all_to_all(partial, NEAR, 0, 0, tiled=True)  15.2 us
    all_to_all x1, blocking collectives, from_everyone(): return lax.all_to_all(copies, axis, split_axis=0, concat_axis=0, tiled=True)  14.1 us
    pallas_call x2, Pallas kernels, projected(): pl.pallas_call(joined_project_kernel if joined else project_kernel, out_s...  13.8 us
    ppermute x3, starting transfers between devices, swapped(): return lax.ppermute(value, axis, [(0, 1), (1, 0)])  12.8 us
  transfers between devices with their start and end apart: 31, of which 14 were waited for; matrix products, arithmetic and copies ran while one was open for 0% of the time, Pallas kernels for 14%

profile of v5, /device:TPU:1, one launch (start us, length us, event | category | flops | bytes accessed | tf_op | source)
XLA Modules:
  0.0 257.4 jit_solution(10519199056448614678)
XLA Ops:
  0.7 4.3 %collective-permute-start.2 = (f32[4,2,128]{2,1,0:T(2,128)S(1)}, f32[4,2,128]{2,1,0:T(2,128)S(1)}, u32[]{:S(2)}, u32[]{:S(2)}) collective-permute-start(f32[4,2,128]{2,1,0:T(2,128)S(1)} %get-tuple-element.51), channel_id=1, source_target_pairs={{0,1},{1,2},{2,3},{3,4},{4,5},{5,6},{6,7},{7,8},{8,9},{9,10},{10,1... | collective-permute-start | bytes 12296 | tf_op jit(solution)/shard_map/ppermute | solution.py:334
  5.1 1.3 collective-permute-start.3
  6.4 3.2 %collective-permute-done.3 = f32[4,2,128]{2,1,0:T(2,128)S(1)} collective-permute-done((f32[4,2,128]{2,1,0:T(2,128)S(1)}, f32[4,2,128]{2,1,0:T(2,128)S(1)}, u32[]{:S(2)}, u32[]{:S(2)}) %collective-permute-start.3) | collective-permute-done | bytes 4128 | tf_op jit(solution)/shard_map/ppermute | solution.py:335
  10.3 5.9 %collective-permute-start.4 = (f32[16,2,128]{2,1,0:T(2,128)S(1)}, f32[16,2,128]{2,1,0:T(2,128)S(1)}, u32[]{:S(2)}, u32[]{:S(2)}) collective-permute-start(f32[16,2,128]{2,1,0:T(2,128)S(1)} %maximum_add_fusion), channel_id=1, source_target_pairs={{0,128},{128,0},{1,129},{129,1},{2,130},{130,2},{3,131},{131,3},{4... | collective-permute-start | bytes 49160 | tf_op jit(solution)/shard_map/ppermute | solution.py:324
  16.2 4.1 %shard_map.37 = (bf16[4,32,16,128]{3,2,1,0:T(8,128)(2,1)}, bf16[4,32,16,128]{3,2,1,0:T(8,128)(2,1)}) custom-call(f32[32,256,128]{2,1,0:T(8,128)} %bitcast.15, f32[32,256,128]{2,1,0:T(8,128)} %bitcast.16), custom_call_target="tpu_custom_call" | custom-call | flops 524288 | bytes 3145728 | tf_op jit(solution)/shard_map/pallas_call | solution.py:34
  20.3 2.7 %collective-permute-start = (bf16[4,32,16,128]{3,2,1,0:T(8,128)(2,1)}, bf16[4,32,16,128]{3,2,1,0:T(8,128)(2,1)S(1)}, u32[]{:S(2)}, u32[]{:S(2)}) collective-permute-start(bf16[4,32,16,128]{3,2,1,0:T(8,128)(2,1)} %get-tuple-element.27), channel_id=1, source_target_pairs={{0,1},{1,2},{2,3},{3,4},{4,5},{5,6},{6,7},{7,8},{8,9},{9,10},{10,1... | collective-permute-start | bytes 1572872 | tf_op jit(solution)/shard_map/ppermute | solution.py:334
  23.0 1.3 collective-permute-start.1
  25.1 7.0 %all-to-all-start = ((f32[8,2,16,2,128]{4,3,1,2,0:T(2,128)}), f32[8,2,16,2,128]{4,3,1,2,0:T(2,128)S(1)}, u32[]{:S(2)}, u32[]{:S(2)}) async-start(f32[8,2,16,2,128]{4,3,1,2,0:T(2,128)} %broadcast_in_dim.6), calls=%async_computation | async-start | bytes 524288 | tf_op jit(solution)/shard_map/all_to_all | solution.py:329
  32.3 6.3 %all-to-all-done = f32[8,2,16,2,128]{4,3,1,2,0:T(2,128)S(1)} async-done(((f32[8,2,16,2,128]{4,3,1,2,0:T(2,128)}), f32[8,2,16,2,128]{4,3,1,2,0:T(2,128)S(1)}, u32[]{:S(2)}, u32[]{:S(2)}) %all-to-all-start) | async-done | bytes 262176 | tf_op jit(solution)/shard_map/all_to_all | solution.py:329
  38.7 10.2 %collective-permute-done.1.high_ref = bf16[4,32,16,128]{3,2,1,0:T(8,128)(2,1)S(1)} collective-permute-done((bf16[4,32,16,128]{3,2,1,0:T(8,128)(2,1)}, bf16[4,32,16,128]{3,2,1,0:T(8,128)(2,1)S(1)}, u32[]{:S(2)}, u32[]{:S(2)}) %collective-permute-start.1) | collective-permute-done | bytes 524320 | tf_op jit(solution)/shard_map/ppermute | solution.py:335
  48.9 13.2 %shard_map.38 = bf16[16,16,16,128]{3,2,1,0:T(8,128)(2,1)} custom-call(s32[3]{0:T(128)S(1)} %pad_add_fusion.ends_ref, f32[32,256,128]{2,1,0:T(8,128)} %bitcast.17, bf16[4,32,16,128]{3,2,1,0:T(8,128)(2,1)S(1)} %collective-permute-done.low_ref, bf16[4,32,16,128]{3,2,1,0:T(8,128)(2,1)S(1)} %collective-permute-done.1.high_ref, f32[16,32,128]{2,1,0:T(8,128)S(1)} %bitcast.13), custom_call_target="tpu_custom_call" | custom-call | flops 34603008 | bytes 5242880 | tf_op jit(solution)/shard_map/pallas_call | solution.py:150
  62.2 6.5 %all-to-all-start.1 = ((bf16[16,16,16,128]{3,2,1,0:T(8,128)(2,1)}), bf16[16,16,16,128]{3,2,1,0:T(8,128)(2,1)S(1)}, u32[]{:S(2)}, u32[]{:S(2)}) async-start(bf16[16,16,16,128]{3,2,1,0:T(8,128)(2,1)} %shard_map.38), calls=%async_computation.1 | async-start | bytes 2097152 | tf_op jit(solution)/shard_map/all_to_all | solution.py:368
  68.6 4.1 %shard_map.40 = (bf16[4,32,16,128]{3,2,1,0:T(8,128)(2,1)}, bf16[4,32,16,128]{3,2,1,0:T(8,128)(2,1)}) custom-call(f32[32,256,128]{2,1,0:T(8,128)} %bitcast.18, f32[32,256,128]{2,1,0:T(8,128)} %bitcast.19), custom_call_target="tpu_custom_call" | custom-call | flops 524288 | bytes 3145728 | tf_op jit(solution)/shard_map/pallas_call | solution.py:34
  72.7 3.8 %collective-permute-start.5 = (bf16[4,32,16,128]{3,2,1,0:T(8,128)(2,1)}, bf16[4,32,16,128]{3,2,1,0:T(8,128)(2,1)S(1)}, u32[]{:S(2)}, u32[]{:S(2)}) collective-permute-start(bf16[4,32,16,128]{3,2,1,0:T(8,128)(2,1)} %get-tuple-element.29), channel_id=1, source_target_pairs={{0,1},{1,2},{2,3},{3,4},{4,5},{5,6},{6,7},{7,8},{8,9},{9,10},{10,1... | collective-permute-start | bytes 1572872 | tf_op jit(solution)/shard_map/ppermute | solution.py:334
  76.6 1.3 collective-permute-start.6
  77.9 25.2 %collective-permute-done.5.low_ref = bf16[4,32,16,128]{3,2,1,0:T(8,128)(2,1)S(1)} collective-permute-done((bf16[4,32,16,128]{3,2,1,0:T(8,128)(2,1)}, bf16[4,32,16,128]{3,2,1,0:T(8,128)(2,1)S(1)}, u32[]{:S(2)}, u32[]{:S(2)}) %collective-permute-start.5) | collective-permute-done | bytes 524320 | tf_op jit(solution)/shard_map/ppermute | solution.py:334
  103.1 13.3 %collective-permute-done.6.high_ref = bf16[4,32,16,128]{3,2,1,0:T(8,128)(2,1)S(1)} collective-permute-done((bf16[4,32,16,128]{3,2,1,0:T(8,128)(2,1)}, bf16[4,32,16,128]{3,2,1,0:T(8,128)(2,1)S(1)}, u32[]{:S(2)}, u32[]{:S(2)}) %collective-permute-start.6) | collective-permute-done | bytes 524320 | tf_op jit(solution)/shard_map/ppermute | solution.py:335
  116.4 13.9 %shard_map.41 = (bf16[16,16,128]{2,1,0:T(8,128)(2,1)S(1)}, bf16[16,16,128]{2,1,0:T(8,128)(2,1)S(1)}, bf16[16,16,128]{2,1,0:T(8,128)(2,1)S(1)}, bf16[16,16,128]{2...) custom-call(s32[3]{0:T(128)S(1)} %pad_add_fusion.ends_ref, ...), custom_call_target="tpu_custom_call" | custom-call | flops 34603008 | bytes 5242880 | tf_op jit(solution)/shard_map/pallas_call | solution.py:150
  130.8 1.6 collective-permute-start.8
  132.5 2.9 %collective-permute-start.10 = (bf16[16,16,128]{2,1,0:T(8,128)(2,1)S(1)}, bf16[16,16,128]{2,1,0:T(8,128)(2,1)S(1)}, u32[]{:S(2)}, u32[]{:S(2)}) collective-permute-start(bf16[16,16,128]{2,1,0:T(8,128)(2,1)S(1)} %get-tuple-element.35), channel_id=1, source_target_pairs={{0,64},{16,80},{32,96},{48,112},{64,0},{80,16},{96,32},{112,48},{1... | collective-permute-start | bytes 196616 | tf_op jit(solution)/shard_map/ppermute | solution.py:299
  135.9 2.4 collective-permute-start.12
  138.7 5.2 %collective-permute-start.14 = (bf16[16,16,128]{2,1,0:T(8,128)(2,1)S(1)}, bf16[16,16,128]{2,1,0:T(8,128)(2,1)S(1)}, u32[]{:S(2)}, u32[]{:S(2)}) collective-permute-start(bf16[16,16,128]{2,1,0:T(8,128)(2,1)S(1)} %get-tuple-element.39), channel_id=1, source_target_pairs={{0,128},{16,144},{32,160},{48,176},{64,192},{80,208},{96,224},{112... | collective-permute-start | bytes 196616 | tf_op jit(solution)/shard_map/ppermute | solution.py:299
  144.0 1.4 collective-permute-start.15
  145.3 4.2 %collective-permute-start.16 = (bf16[16,16,128]{2,1,0:T(8,128)(2,1)S(1)}, bf16[16,16,128]{2,1,0:T(8,128)(2,1)S(1)}, u32[]{:S(2)}, u32[]{:S(2)}) collective-permute-start(bf16[16,16,128]{2,1,0:T(8,128)(2,1)S(1)} %get-tuple-element.41), channel_id=1, source_target_pairs={{0,160},{16,176},{32,128},{48,144},{64,224},{80,240},{96,192},{112... | collective-permute-start | bytes 196616 | tf_op jit(solution)/shard_map/ppermute | solution.py:299
  149.5 1.9 collective-permute-start.17
  151.4 6.1 %collective-permute-start.18 = (bf16[16,16,128]{2,1,0:T(8,128)(2,1)S(1)}, bf16[16,16,128]{2,1,0:T(8,128)(2,1)S(1)}, u32[]{:S(2)}, u32[]{:S(2)}) collective-permute-start(bf16[16,16,128]{2,1,0:T(8,128)(2,1)S(1)} %get-tuple-element.43), channel_id=1, source_target_pairs={{0,192},{16,208},{32,224},{48,240},{64,128},{80,144},{96,160},{112... | collective-permute-start | bytes 196616 | tf_op jit(solution)/shard_map/ppermute | solution.py:299
  157.4 2.5 collective-permute-start.19
  160.0 6.4 %collective-permute-start.20 = (bf16[16,16,128]{2,1,0:T(8,128)(2,1)S(1)}, bf16[16,16,128]{2,1,0:T(8,128)(2,1)S(1)}, u32[]{:S(2)}, u32[]{:S(2)}) collective-permute-start(bf16[16,16,128]{2,1,0:T(8,128)(2,1)S(1)} %get-tuple-element.45), channel_id=1, source_target_pairs={{0,224},{16,240},{32,192},{48,208},{64,160},{80,176},{96,128},{112... | collective-permute-start | bytes 196616 | tf_op jit(solution)/shard_map/ppermute | solution.py:299
  166.4 0.9 collective-permute-start.21
  167.2 1.9 collective-permute-done.19.refs_13_
  169.1 1.1 collective-permute-done.20.refs_14_
  170.2 6.5 %collective-permute-done.21.refs_15_ = bf16[16,16,128]{2,1,0:T(8,128)(2,1)S(1)} collective-permute-done((bf16[16,16,128]{2,1,0:T(8,128)(2,1)S(1)}, bf16[16,16,128]{2,1,0:T(8,128)(2,1)S(1)}, u32[]{:S(2)}, u32[]{:S(2)}) %collective-permute-start.21) | collective-permute-done | bytes 65568 | tf_op jit(solution)/shard_map/ppermute | solution.py:299
  176.8 7.0 %shard_map.42 = (bf16[32,8,1024]{2,1,0:T(8,128)(2,1)}, bf16[16,16,16,128]{3,2,1,0:T(8,128)(2,1)S(1)}) custom-call(s32[1]{0:T(128)} %bitcast.4.place_ref, bf16[16,128,1024]{2,1,0:T(8,128)(2,1)} %bitcast.21, bf16[16,16,128]{2,1,0:T(8,128)(2,1)S(1)} %get-tuple-element.31.refs_0_, bf16[16,16,128]{2,1,0:T(8,128)(2,1)S(1)} %collective-permute-done.7.refs_1_, ...), custom_call_target="tpu_custom_call" | custom-call | flops 1073741824 | bytes 7340032 | tf_op jit(solution)/shard_map/pallas_call | solution.py:224
  183.8 5.8 %all-to-all-start.3 = ((bf16[32,8,1024]{2,1,0:T(8,128)(2,1)}), bf16[32,8,1024]{2,1,0:T(8,128)(2,1)S(1)}, u32[]{:S(2)}, u32[]{:S(2)}) async-start(bf16[32,8,1024]{2,1,0:T(8,128)(2,1)} %get-tuple-element.47), calls=%async_computation.3 | async-start | bytes 1048576 | tf_op jit(solution)/shard_map/all_to_all | solution.py:304
  189.6 6.8 %shard_map.39 = bf16[32,8,1024]{2,1,0:T(8,128)(2,1)} custom-call(bf16[16,128,1024]{2,1,0:T(8,128)(2,1)} %bitcast.22, bf16[16,16,16,128]{3,2,1,0:T(8,128)(2,1)S(1)} %all-to-all-done.1.cells_ref.refs_0_), custom_call_target="tpu_custom_call" | custom-call | flops 1073741824 | bytes 7340032 | tf_op jit(solution)/shard_map/pallas_call | solution.py:224
  196.4 4.1 %all-to-all-done.3 = bf16[32,8,1024]{2,1,0:T(8,128)(2,1)S(1)} async-done(((bf16[32,8,1024]{2,1,0:T(8,128)(2,1)}), bf16[32,8,1024]{2,1,0:T(8,128)(2,1)S(1)}, u32[]{:S(2)}, u32[]{:S(2)}) %all-to-all-start.3) | async-done | bytes 524320 | tf_op jit(solution)/shard_map/all_to_all | solution.py:304
  200.4 5.0 %all-to-all-start.2 = ((bf16[32,8,1024]{2,1,0:T(8,128)(2,1)}), bf16[32,8,1024]{2,1,0:T(8,128)(2,1)S(1)}, u32[]{:S(2)}, u32[]{:S(2)}) async-start(bf16[32,8,1024]{2,1,0:T(8,128)(2,1)} %shard_map.39), calls=%async_computation.2 | async-start | bytes 1048576 | tf_op jit(solution)/shard_map/all_to_all | solution.py:304
  205.5 11.1 %all-to-all-done.2 = bf16[32,8,1024]{2,1,0:T(8,128)(2,1)S(1)} async-done(((bf16[32,8,1024]{2,1,0:T(8,128)(2,1)}), bf16[32,8,1024]{2,1,0:T(8,128)(2,1)S(1)}, u32[]{:S(2)}, u32[]{:S(2)}) %all-to-all-start.2) | async-done | bytes 524320 | tf_op jit(solution)/shard_map/all_to_all | solution.py:304
  216.7 2.9 %collective-permute-start.22 = (f32[16,1024]{1,0:T(8,128)S(1)}, f32[16,1024]{1,0:T(8,128)S(1)}, u32[]{:S(2)}, u32[]{:S(2)}) collective-permute-start(f32[16,1024]{1,0:T(8,128)S(1)} %pad_maximum_fusion), channel_id=1, source_target_pairs={{0,128},{128,0},{1,129},{129,1},{2,130},{130,2},{3,131},{131,3},{4... | collective-permute-start | bytes 196616 | tf_op jit(solution)/shard_map/ppermute | solution.py:324
  219.6 5.0 %collective-permute-done.22 = f32[16,1024]{1,0:T(8,128)S(1)} collective-permute-done((f32[16,1024]{1,0:T(8,128)S(1)}, f32[16,1024]{1,0:T(8,128)S(1)}, u32[]{:S(2)}, u32[]{:S(2)}) %collective-permute-start.22) | collective-permute-done | bytes 65568 | tf_op jit(solution)/shard_map/ppermute | solution.py:324
  225.0 1.2 collective-permute-start.24
  226.2 1.9 collective-permute-start.23
  228.2 1.5 collective-permute-done.25
  229.7 0.8 collective-permute-done.24
  230.6 14.1 %all_to_all.25.mine_ref = bf16[16,16,1024]{2,1,0:T(8,128)(2,1)S(1)} all-to-all(bf16[16,16,1024]{2,1,0:T(8,128)(2,1)S(1)} %broadcast_in_dim.7), channel_id=1, replica_groups=mesh['zh'=2,'x'=4,'c'=2,'y'=4,'zl'=4] {'x','y'}, dimensions={0} | all-to-all | bytes 1048576 | tf_op jit(solution)/shard_map/all_to_all | solution.py:329
  244.6 4.0 %collective-permute-start.26 = (bf16[16,16,1024]{2,1,0:T(8,128)(2,1)S(1)}, bf16[16,16,1024]{2,1,0:T(8,128)(2,1)S(1)}, u32[]{:S(2)}, u32[]{:S(2)}) collective-permute-start(bf16[16,16,1024]{2,1,0:T(8,128)(2,1)S(1)} %all_to_all.25.mine_ref), channel_id=1, source_target_pairs={{0,16},{16,0},{1,17},{17,1},{2,18},{18,2},{3,19},{19,3},{4,20},{20... | collective-permute-start | bytes 1572872 | tf_op jit(solution)/shard_map/ppermute | solution.py:324
  248.6 1.5 collective-permute-done.26.other_ref
  250.2 7.2 %shard_map.43 = f32[16,512,128]{2,1,0:T(8,128)} custom-call(s32[1]{0:T(128)} %bitcast.core_ref, bf16[16,16,1024]{2,1,0:T(8,128)(2,1)S(1)} %all_to_all.25.mine_ref, bf16[16,16,1024]{2,1,0:T(8,128)(2,1)S(1)} %collective-permute-done.26.other_ref, bf16[16,128,1024]{2,1,0:T(8,128)(2,1)} %bitcast.23, ...), custom_call_target="tpu_custom_call" | custom-call | flops 2147483648 | bytes 11534336 | tf_op jit(solution)/shard_map/pallas_call | solution.py:273
  (39 shorter events, 4.8 us)
Async XLA Ops:
  0.7 5.7 %collective-permute-start.2 = (f32[4,2,128]{2,1,0:T(2,128)S(1)}, f32[4,2,128]{2,1,0:T(2,128)S(1)}, u32[]{:S(2)}, u32[]{:S(2)}) collective-permute-start(f32[4,2,128]{2,1,0:T(2,128)S(1)} %get-tuple-element.51), channel_id=1, source_target_pairs={{0,1},{1,2},{2,3},{3,4},{4,5},{5,6},{6,7},{7,8},{8,9},{9,10},{10,1... | collective-permute-start | bytes 12296 | tf_op jit(solution)/shard_map/ppermute | solution.py:334
  5.1 4.5 %collective-permute-start.3 = (f32[4,2,128]{2,1,0:T(2,128)S(1)}, f32[4,2,128]{2,1,0:T(2,128)S(1)}, u32[]{:S(2)}, u32[]{:S(2)}) collective-permute-start(f32[4,2,128]{2,1,0:T(2,128)S(1)} %get-tuple-element.52), channel_id=1, source_target_pairs={{1,0},{2,1},{3,2},{4,3},{5,4},{6,5},{7,6},{8,7},{9,8},{10,9},{11,1... | collective-permute-start | bytes 12296 | tf_op jit(solution)/shard_map/ppermute | solution.py:335
  10.3 14.0 %collective-permute-start.4 = (f32[16,2,128]{2,1,0:T(2,128)S(1)}, f32[16,2,128]{2,1,0:T(2,128)S(1)}, u32[]{:S(2)}, u32[]{:S(2)}) collective-permute-start(f32[16,2,128]{2,1,0:T(2,128)S(1)} %maximum_add_fusion), channel_id=1, source_target_pairs={{0,128},{128,0},{1,129},{129,1},{2,130},{130,2},{3,131},{131,3},{4... | collective-permute-start | bytes 49160 | tf_op jit(solution)/shard_map/ppermute | solution.py:324
  16.2 8.1 %copy-start = (f32[8,2,128]{2,1,0:T(2,128)S(1)}, f32[8,2,128]{2,1,0:T(2,128)}, u32[]{:S(2)}) copy-start(f32[8,2,128]{2,1,0:T(2,128)} %param.4) | copy-start | bytes 24580
  20.3 18.4 %collective-permute-start = (bf16[4,32,16,128]{3,2,1,0:T(8,128)(2,1)}, bf16[4,32,16,128]{3,2,1,0:T(8,128)(2,1)S(1)}, u32[]{:S(2)}, u32[]{:S(2)}) collective-permute-start(bf16[4,32,16,128]{3,2,1,0:T(8,128)(2,1)} %get-tuple-element.27), channel_id=1, source_target_pairs={{0,1},{1,2},{2,3},{3,4},{4,5},{5,6},{6,7},{7,8},{8,9},{9,10},{10,1... | collective-permute-start | bytes 1572872 | tf_op jit(solution)/shard_map/ppermute | solution.py:334
  23.0 25.9 %collective-permute-start.1 = (bf16[4,32,16,128]{3,2,1,0:T(8,128)(2,1)}, bf16[4,32,16,128]{3,2,1,0:T(8,128)(2,1)S(1)}, u32[]{:S(2)}, u32[]{:S(2)}) collective-permute-start(bf16[4,32,16,128]{3,2,1,0:T(8,128)(2,1)} %get-tuple-element.28), channel_id=1, source_target_pairs={{1,0},{2,1},{3,2},{4,3},{5,4},{6,5},{7,6},{8,7},{9,8},{10,9},{11,1... | collective-permute-start | bytes 1572872 | tf_op jit(solution)/shard_map/ppermute | solution.py:335
  25.1 13.4 %all-to-all-start = ((f32[8,2,16,2,128]{4,3,1,2,0:T(2,128)}), f32[8,2,16,2,128]{4,3,1,2,0:T(2,128)S(1)}, u32[]{:S(2)}, u32[]{:S(2)}) async-start(f32[8,2,16,2,128]{4,3,1,2,0:T(2,128)} %broadcast_in_dim.6), calls=%async_computation | async-start | bytes 524288 | tf_op jit(solution)/shard_map/all_to_all | solution.py:329
  62.2 121.6 %all-to-all-start.1 = ((bf16[16,16,16,128]{3,2,1,0:T(8,128)(2,1)}), bf16[16,16,16,128]{3,2,1,0:T(8,128)(2,1)S(1)}, u32[]{:S(2)}, u32[]{:S(2)}) async-start(bf16[16,16,16,128]{3,2,1,0:T(8,128)(2,1)} %shard_map.38), calls=%async_computation.1 | async-start | bytes 2097152 | tf_op jit(solution)/shard_map/all_to_all | solution.py:368
  72.7 30.3 %collective-permute-start.5 = (bf16[4,32,16,128]{3,2,1,0:T(8,128)(2,1)}, bf16[4,32,16,128]{3,2,1,0:T(8,128)(2,1)S(1)}, u32[]{:S(2)}, u32[]{:S(2)}) collective-permute-start(bf16[4,32,16,128]{3,2,1,0:T(8,128)(2,1)} %get-tuple-element.29), channel_id=1, source_target_pairs={{0,1},{1,2},{2,3},{3,4},{4,5},{5,6},{6,7},{7,8},{8,9},{9,10},{10,1... | collective-permute-start | bytes 1572872 | tf_op jit(solution)/shard_map/ppermute | solution.py:334
  76.6 39.8 %collective-permute-start.6 = (bf16[4,32,16,128]{3,2,1,0:T(8,128)(2,1)}, bf16[4,32,16,128]{3,2,1,0:T(8,128)(2,1)S(1)}, u32[]{:S(2)}, u32[]{:S(2)}) collective-permute-start(bf16[4,32,16,128]{3,2,1,0:T(8,128)(2,1)} %get-tuple-element.30), channel_id=1, source_target_pairs={{1,0},{2,1},{3,2},{4,3},{5,4},{6,5},{7,6},{8,7},{9,8},{10,9},{11,1... | collective-permute-start | bytes 1572872 | tf_op jit(solution)/shard_map/ppermute | solution.py:335
  130.3 5.6 %collective-permute-start.7 = (bf16[16,16,128]{2,1,0:T(8,128)(2,1)S(1)}, bf16[16,16,128]{2,1,0:T(8,128)(2,1)S(1)}, u32[]{:S(2)}, u32[]{:S(2)}) collective-permute-start(bf16[16,16,128]{2,1,0:T(8,128)(2,1)S(1)} %get-tuple-element.32), channel_id=1, source_target_pairs={{0,16},{16,0},{32,48},{48,32},{64,80},{80,64},{96,112},{112,96},{1... | collective-permute-start | bytes 196616 | tf_op jit(solution)/shard_map/ppermute | solution.py:299
  130.8 7.5 %collective-permute-start.8 = (bf16[16,16,128]{2,1,0:T(8,128)(2,1)S(1)}, bf16[16,16,128]{2,1,0:T(8,128)(2,1)S(1)}, u32[]{:S(2)}, u32[]{:S(2)}) collective-permute-start(bf16[16,16,128]{2,1,0:T(8,128)(2,1)S(1)} %get-tuple-element.33), channel_id=1, source_target_pairs={{0,32},{16,48},{32,0},{48,16},{64,96},{80,112},{96,64},{112,80},{1... | collective-permute-start | bytes 196616 | tf_op jit(solution)/shard_map/ppermute | solution.py:299
  132.4 6.3 %collective-permute-start.9 = (bf16[16,16,128]{2,1,0:T(8,128)(2,1)S(1)}, bf16[16,16,128]{2,1,0:T(8,128)(2,1)S(1)}, u32[]{:S(2)}, u32[]{:S(2)}) collective-permute-start(bf16[16,16,128]{2,1,0:T(8,128)(2,1)S(1)} %get-tuple-element.34), channel_id=1, source_target_pairs={{0,48},{16,32},{32,16},{48,0},{64,112},{80,96},{96,80},{112,64},{1... | collective-permute-start | bytes 196616 | tf_op jit(solution)/shard_map/ppermute | solution.py:299
  132.5 11.5 %collective-permute-start.10 = (bf16[16,16,128]{2,1,0:T(8,128)(2,1)S(1)}, bf16[16,16,128]{2,1,0:T(8,128)(2,1)S(1)}, u32[]{:S(2)}, u32[]{:S(2)}) collective-permute-start(bf16[16,16,128]{2,1,0:T(8,128)(2,1)S(1)} %get-tuple-element.35), channel_id=1, source_target_pairs={{0,64},{16,80},{32,96},{48,112},{64,0},{80,16},{96,32},{112,48},{1... | collective-permute-start | bytes 196616 | tf_op jit(solution)/shard_map/ppermute | solution.py:299
  135.3 10.0 %collective-permute-start.11 = (bf16[16,16,128]{2,1,0:T(8,128)(2,1)S(1)}, bf16[16,16,128]{2,1,0:T(8,128)(2,1)S(1)}, u32[]{:S(2)}, u32[]{:S(2)}) collective-permute-start(bf16[16,16,128]{2,1,0:T(8,128)(2,1)S(1)} %get-tuple-element.36), channel_id=1, source_target_pairs={{0,80},{16,64},{32,112},{48,96},{64,16},{80,0},{96,48},{112,32},{1... | collective-permute-start | bytes 196616 | tf_op jit(solution)/shard_map/ppermute | solution.py:299
  135.9 13.6 %collective-permute-start.12 = (bf16[16,16,128]{2,1,0:T(8,128)(2,1)S(1)}, bf16[16,16,128]{2,1,0:T(8,128)(2,1)S(1)}, u32[]{:S(2)}, u32[]{:S(2)}) collective-permute-start(bf16[16,16,128]{2,1,0:T(8,128)(2,1)S(1)} %get-tuple-element.37), channel_id=1, source_target_pairs={{0,96},{16,112},{32,64},{48,80},{64,32},{80,48},{96,0},{112,16},{1... | collective-permute-start | bytes 196616 | tf_op jit(solution)/shard_map/ppermute | solution.py:299
  138.3 13.1 %collective-permute-start.13 = (bf16[16,16,128]{2,1,0:T(8,128)(2,1)S(1)}, bf16[16,16,128]{2,1,0:T(8,128)(2,1)S(1)}, u32[]{:S(2)}, u32[]{:S(2)}) collective-permute-start(bf16[16,16,128]{2,1,0:T(8,128)(2,1)S(1)} %get-tuple-element.38), channel_id=1, source_target_pairs={{0,112},{16,96},{32,80},{48,64},{64,48},{80,32},{96,16},{112,0},{1... | collective-permute-start | bytes 196616 | tf_op jit(solution)/shard_map/ppermute | solution.py:299
  138.7 18.7 %collective-permute-start.14 = (bf16[16,16,128]{2,1,0:T(8,128)(2,1)S(1)}, bf16[16,16,128]{2,1,0:T(8,128)(2,1)S(1)}, u32[]{:S(2)}, u32[]{:S(2)}) collective-permute-start(bf16[16,16,128]{2,1,0:T(8,128)(2,1)S(1)} %get-tuple-element.39), channel_id=1, source_target_pairs={{0,128},{16,144},{32,160},{48,176},{64,192},{80,208},{96,224},{112... | collective-permute-start | bytes 196616 | tf_op jit(solution)/shard_map/ppermute | solution.py:299
  144.0 16.0 %collective-permute-start.15 = (bf16[16,16,128]{2,1,0:T(8,128)(2,1)S(1)}, bf16[16,16,128]{2,1,0:T(8,128)(2,1)S(1)}, u32[]{:S(2)}, u32[]{:S(2)}) collective-permute-start(bf16[16,16,128]{2,1,0:T(8,128)(2,1)S(1)} %get-tuple-element.40), channel_id=1, source_target_pairs={{0,144},{16,128},{32,176},{48,160},{64,208},{80,192},{96,240},{112... | collective-permute-start | bytes 196616 | tf_op jit(solution)/shard_map/ppermute | solution.py:299
  145.3 21.0 %collective-permute-start.16 = (bf16[16,16,128]{2,1,0:T(8,128)(2,1)S(1)}, bf16[16,16,128]{2,1,0:T(8,128)(2,1)S(1)}, u32[]{:S(2)}, u32[]{:S(2)}) collective-permute-start(bf16[16,16,128]{2,1,0:T(8,128)(2,1)S(1)} %get-tuple-element.41), channel_id=1, source_target_pairs={{0,160},{16,176},{32,128},{48,144},{64,224},{80,240},{96,192},{112... | collective-permute-start | bytes 196616 | tf_op jit(solution)/shard_map/ppermute | solution.py:299
  149.5 17.7 %collective-permute-start.17 = (bf16[16,16,128]{2,1,0:T(8,128)(2,1)S(1)}, bf16[16,16,128]{2,1,0:T(8,128)(2,1)S(1)}, u32[]{:S(2)}, u32[]{:S(2)}) collective-permute-start(bf16[16,16,128]{2,1,0:T(8,128)(2,1)S(1)} %get-tuple-element.42), channel_id=1, source_target_pairs={{0,176},{16,160},{32,144},{48,128},{64,240},{80,224},{96,208},{112... | collective-permute-start | bytes 196616 | tf_op jit(solution)/shard_map/ppermute | solution.py:299
  151.4 15.8 %collective-permute-start.18 = (bf16[16,16,128]{2,1,0:T(8,128)(2,1)S(1)}, bf16[16,16,128]{2,1,0:T(8,128)(2,1)S(1)}, u32[]{:S(2)}, u32[]{:S(2)}) collective-permute-start(bf16[16,16,128]{2,1,0:T(8,128)(2,1)S(1)} %get-tuple-element.43), channel_id=1, source_target_pairs={{0,192},{16,208},{32,224},{48,240},{64,128},{80,144},{96,160},{112... | collective-permute-start | bytes 196616 | tf_op jit(solution)/shard_map/ppermute | solution.py:299
  157.4 11.6 %collective-permute-start.19 = (bf16[16,16,128]{2,1,0:T(8,128)(2,1)S(1)}, bf16[16,16,128]{2,1,0:T(8,128)(2,1)S(1)}, u32[]{:S(2)}, u32[]{:S(2)}) collective-permute-start(bf16[16,16,128]{2,1,0:T(8,128)(2,1)S(1)} %get-tuple-element.44), channel_id=1, source_target_pairs={{0,208},{16,192},{32,240},{48,224},{64,144},{80,128},{96,176},{112... | collective-permute-start | bytes 196616 | tf_op jit(solution)/shard_map/ppermute | solution.py:299
  160.0 10.3 %collective-permute-start.20 = (bf16[16,16,128]{2,1,0:T(8,128)(2,1)S(1)}, bf16[16,16,128]{2,1,0:T(8,128)(2,1)S(1)}, u32[]{:S(2)}, u32[]{:S(2)}) collective-permute-start(bf16[16,16,128]{2,1,0:T(8,128)(2,1)S(1)} %get-tuple-element.45), channel_id=1, source_target_pairs={{0,224},{16,240},{32,192},{48,208},{64,160},{80,176},{96,128},{112... | collective-permute-start | bytes 196616 | tf_op jit(solution)/shard_map/ppermute | solution.py:299
  166.4 10.4 %collective-permute-start.21 = (bf16[16,16,128]{2,1,0:T(8,128)(2,1)S(1)}, bf16[16,16,128]{2,1,0:T(8,128)(2,1)S(1)}, u32[]{:S(2)}, u32[]{:S(2)}) collective-permute-start(bf16[16,16,128]{2,1,0:T(8,128)(2,1)S(1)} %get-tuple-element.46), channel_id=1, source_target_pairs={{0,240},{16,224},{32,208},{48,192},{64,176},{80,160},{96,144},{112... | collective-permute-start | bytes 196616 | tf_op jit(solution)/shard_map/ppermute | solution.py:299
  183.8 16.7 %all-to-all-start.3 = ((bf16[32,8,1024]{2,1,0:T(8,128)(2,1)}), bf16[32,8,1024]{2,1,0:T(8,128)(2,1)S(1)}, u32[]{:S(2)}, u32[]{:S(2)}) async-start(bf16[32,8,1024]{2,1,0:T(8,128)(2,1)} %get-tuple-element.47), calls=%async_computation.3 | async-start | bytes 1048576 | tf_op jit(solution)/shard_map/all_to_all | solution.py:304
  200.4 16.1 %all-to-all-start.2 = ((bf16[32,8,1024]{2,1,0:T(8,128)(2,1)}), bf16[32,8,1024]{2,1,0:T(8,128)(2,1)S(1)}, u32[]{:S(2)}, u32[]{:S(2)}) async-start(bf16[32,8,1024]{2,1,0:T(8,128)(2,1)} %shard_map.39), calls=%async_computation.2 | async-start | bytes 1048576 | tf_op jit(solution)/shard_map/all_to_all | solution.py:304
  216.7 7.8 %collective-permute-start.22 = (f32[16,1024]{1,0:T(8,128)S(1)}, f32[16,1024]{1,0:T(8,128)S(1)}, u32[]{:S(2)}, u32[]{:S(2)}) collective-permute-start(f32[16,1024]{1,0:T(8,128)S(1)} %pad_maximum_fusion), channel_id=1, source_target_pairs={{0,128},{128,0},{1,129},{129,1},{2,130},{130,2},{3,131},{131,3},{4... | collective-permute-start | bytes 196616 | tf_op jit(solution)/shard_map/ppermute | solution.py:324
  224.5 5.2 %collective-permute-start.25 = (f32[16,1024]{1,0:T(8,128)S(1)}, f32[16,1024]{1,0:T(8,128)S(1)}, u32[]{:S(2)}, u32[]{:S(2)}) collective-permute-start(f32[16,1024]{1,0:T(8,128)S(1)} %fusion), channel_id=1, source_target_pairs={{0,3},{1,2},{2,1},{3,0},{4,7},{5,6},{6,5},{7,4},{8,11},{9,10},{10,... | collective-permute-start | bytes 196616 | tf_op jit(solution)/shard_map/ppermute | solution.py:313
  225.0 5.5 %collective-permute-start.24 = (f32[16,1024]{1,0:T(8,128)S(1)}, f32[16,1024]{1,0:T(8,128)S(1)}, u32[]{:S(2)}, u32[]{:S(2)}) collective-permute-start(f32[16,1024]{1,0:T(8,128)S(1)} %fusion), channel_id=1, source_target_pairs={{0,2},{1,3},{2,0},{3,1},{4,6},{5,7},{6,4},{7,5},{8,10},{9,11},{10,... | collective-permute-start | bytes 196616 | tf_op jit(solution)/shard_map/ppermute | solution.py:313
  226.2 4.3 %collective-permute-start.23 = (f32[16,1024]{1,0:T(8,128)S(1)}, f32[16,1024]{1,0:T(8,128)S(1)}, u32[]{:S(2)}, u32[]{:S(2)}) collective-permute-start(f32[16,1024]{1,0:T(8,128)S(1)} %fusion), channel_id=1, source_target_pairs={{0,1},{1,0},{2,3},{3,2},{4,5},{5,4},{6,7},{7,6},{8,9},{9,8},{10,11... | collective-permute-start | bytes 196616 | tf_op jit(solution)/shard_map/ppermute | solution.py:313
  244.6 5.5 %collective-permute-start.26 = (bf16[16,16,1024]{2,1,0:T(8,128)(2,1)S(1)}, bf16[16,16,1024]{2,1,0:T(8,128)(2,1)S(1)}, u32[]{:S(2)}, u32[]{:S(2)}) collective-permute-start(bf16[16,16,1024]{2,1,0:T(8,128)(2,1)S(1)} %all_to_all.25.mine_ref), channel_id=1, source_target_pairs={{0,16},{16,0},{1,17},{17,1},{2,18},{18,2},{3,19},{19,3},{4,20},{20... | collective-permute-start | bytes 1572872 | tf_op jit(solution)/shard_map/ppermute | solution.py:324

commit v6 on v3

--- a/solution.py
+++ b/solution.py
@@ -12,7 +12,7 @@
 
 VEC = ("zh", "x", "c")
 DOM = ("y", "zl")
-SHARE = ("x", "y")
+SHARE = ("y", "x")
 NEAR = ("c", *SHARE)
 HALO = 4
 GROUP = 16
@@ -145,8 +145,7 @@
     )(ends, cells, low, high, diag)
 
 
-def project_kernel(cells_ref, ritz_ref, *refs):
-    out_ref, total = refs[-2:]
+def project_kernel(place_ref, ritz_ref, cells_ref, out_ref, total):
     step = pl.program_id(0)
     lanes = cells_ref.shape[3]
 
@@ -163,35 +162,34 @@
 
     @pl.when(step == pl.num_programs(0) - 1)
     def _():
-        out_ref[...] = total[...].astype(bf16).reshape(out_ref.shape)
-
-
-def projected(cells, ritz, held, chunk, near):
+        near, size, _ = out_ref.shape
+        if out_ref.dtype == f32:
+            for q in range(near):
+                out_ref[place_ref[0] ^ q] = total[q * size : (q + 1) * size, :]
+        else:
+            out_ref[...] = total[...].astype(bf16).reshape(out_ref.shape)
+
+
+def projected(cells, ritz, near, place, kind):
     blocks, rows, vectors, lanes = cells.shape
     kept = ritz.shape[2]
     count = blocks * vectors
-    size = count // near
-    specs = [
-        pl.BlockSpec((blocks, 2, vectors, lanes), lambda r: (0, r, 0, 0)),
-        pl.BlockSpec((2, lanes, kept), lambda r: (r, 0, 0)),
-    ]
-    operands = [cells, ritz]
-    if held is not None:
-        specs.append(pl.BlockSpec(memory_space=pl.ANY))
-        operands.append(held)
     return pl.pallas_call(
         project_kernel,
-        out_shape=jax.ShapeDtypeStruct((near, CHUNKS * size, kept), bf16),
+        out_shape=jax.ShapeDtypeStruct((near, count // near, kept), kind),
         grid=(rows // 2,),
-        in_specs=specs,
-        out_specs=pl.BlockSpec((near, size, kept), lambda r: (0, chunk, 0)),
+        in_specs=[
+            pl.BlockSpec(memory_space=pltpu.SMEM),
+            pl.BlockSpec((2, lanes, kept), lambda r: (r, 0, 0)),
+            pl.BlockSpec((blocks, 2, vectors, lanes), lambda r: (0, r, 0, 0)),
+        ],
+        out_specs=pl.BlockSpec((near, count // near, kept), lambda r: (0, 0, 0)),
         scratch_shapes=[pltpu.VMEM((count, kept), f32)],
-        input_output_aliases={} if held is None else {2: 0},
         compiler_params=pltpu.CompilerParams(vmem_limit_bytes=24 << 20),
         cost_estimate=pl.CostEstimate(
             flops=2 * count * rows * lanes * kept, bytes_accessed=7 << 20, transcendentals=0
         ),
-    )(*operands)
+    )(place, ritz, cells)
 
 
 def remove_kernel(core_ref, mine_ref, other_ref, ritz_ref, *refs):
@@ -249,11 +247,37 @@
     )(core, mine, other, ritz, *held)
 
 
-def summed(partial):
-    blocks = lax.all_to_all(partial, NEAR, 0, 0, tiled=True)
-    blocks = jnp.sum(blocks.astype(f32), axis=0)
+def total_of(terms):
+    while len(terms) > 1:
+        terms = [a + b for a, b in zip(terms[::2], terms[1::2])]
+    return terms[0]
+
+
+def traded(blocks, axis):
+    count = lax.axis_size(axis)
+    return total_of(
+        [blocks[0]]
+        + [
+            lax.ppermute(blocks[k], axis, [(i, i ^ k) for i in range(count)])
+            for k in range(1, count)
+        ]
+    )
+
+
+def near_sum(partial):
+    if partial.dtype == bf16:
+        blocks = lax.all_to_all(partial, NEAR, 0, 0, tiled=True)
+        return jnp.sum(blocks.astype(f32), axis=0)
+    for axis in NEAR:
+        count = lax.axis_size(axis)
+        partial = traded(partial.reshape(count, -1, *partial.shape[-2:]), axis)
+    return partial[0]
+
+
+def summed(parts):
+    blocks = jnp.concatenate(parts, axis=0)
     blocks = blocks + swapped(blocks, "zh")
-    blocks = jnp.sum(from_everyone(blocks, "zl"), axis=0).astype(bf16)
+    blocks = traded([blocks] * lax.axis_size("zl"), "zl").astype(bf16)
     mine = from_everyone(blocks, SHARE)
     return mine, swapped(mine, "c")
 
@@ -277,10 +301,15 @@
 def pipeline(vectors, coefficient, ritz):
     count, planes, rows, lanes = vectors.shape
     size = count // CHUNKS
-    diag = from_everyone(coefficient, VEC)
-    diag = diag.transpose(1, 0, 2, 3).reshape(planes, rows, lanes)
+    other = swapped(coefficient, "zh")
+    first = lax.axis_index("zh") == 0
+    diag = jnp.stack(
+        [jnp.where(first, coefficient, other), jnp.where(first, other, coefficient)]
+    )
+    diag = from_everyone(diag, ("x", "c"))
+    diag = diag.transpose(2, 1, 0, 3, 4).reshape(planes, rows, lanes) + (6.0 - 7.125)
     below, above = swap_ends(diag[:HALO], diag[-HALO:])
-    diag = jnp.concatenate([below, diag, above], axis=0) + (6.0 - 7.125)
+    diag = jnp.concatenate([below, diag, above], axis=0)
     place = lax.axis_index(DOM)
     ends = jnp.stack([place == 0, place == lax.axis_size(DOM) - 1]).astype(jnp.int32)
     cells = pltpu.with_memory_space_constraint(
@@ -289,15 +318,18 @@
     ritz_rows = pltpu.with_memory_space_constraint(
         ritz.reshape(-1, *ritz.shape[2:]), pltpu.MemorySpace.HBM
     )
-    held, total = [], None
+    held, parts = [], []
     for k in range(CHUNKS):
         low, high = spread(cells, rows, k, size)
         low, high = swap_ends(low, high)
         blocks = filtered(ends, cells, low, high, diag, k, size)
         held.append(lax.all_to_all(blocks, VEC, 0, 0, tiled=True))
+    column = lax.axis_index(NEAR).reshape(1).astype(jnp.int32)
     for k in range(CHUNKS):
-        total = projected(held[k], ritz_rows, total, k, lax.axis_size(NEAR))
-    mine, other = summed(total)
+        kind = bf16 if k == CHUNKS - 1 else f32
+        partial = projected(held[k], ritz_rows, lax.axis_size(NEAR), column, kind)
+        parts.append(near_sum(partial))
+    mine, other = summed(parts)
     core = lax.axis_index("c").reshape(1).astype(jnp.int32)
     out = residual(core, mine, other, ritz_rows, held)
     return out.reshape(-1, *coefficient.shape)

time: 245 us -> 241 us (0.984)
  blocking collectives: 48.9 us -> 13.9 us
  starting transfers between devices: 50.3 us -> 71 us
  waiting for transfers between devices: 88.5 us -> 96.5 us
    all_to_all x1 -> x0, blocking collectives: 22.2 us -> none  [summed(): blocks = lax.all_to_all(partial, NEAR, 0, 0, tiled=True)]
    ppermute x0 -> x10, starting transfers between devices: none -> 13.8 us  [traded(): lax.ppermute(blocks[k], axis, [(i, i ^ k) for i in range(count)])]
    all_to_all x2 -> x1, blocking collectives: 26.8 us -> 13.9 us  [from_everyone(): return lax.all_to_all(copies, axis, split_axis=0, concat_axis=0, tiled=True)]
    all_to_all x0 -> x1, waiting for transfers between devices: none -> 7.11 us  [near_sum(): blocks = lax.all_to_all(partial, NEAR, 0, 0, tiled=True)]
    ppermute x2 -> x3, starting transfers between devices: 4.29 us -> 11 us  [swapped(): return lax.ppermute(value, axis, [(0, 1), (1, 0)])]
    all_to_all x1, starting transfers between devices: 12.4 us -> 5.84 us  [from_everyone(): return lax.all_to_all(copies, axis, split_axis=0, concat_axis=0, tiled=True)]
    all_to_all x0 -> x1, starting transfers between devices: none -> 6.09 us  [near_sum(): blocks = lax.all_to_all(partial, NEAR, 0, 0, tiled=True)]
    all_to_all x2, waiting for transfers between devices: 19.9 us -> 13.9 us  [pipeline(): held.append(lax.all_to_all(blocks, VEC, 0, 0, tiled=True))]
  transfers between devices with their start and end apart: 11 -> 23, of which waited for: 7 -> 11; matrix products, arithmetic and copies ran while one was open for 0% -> 1% of each run, Pallas kernels for 11% -> 14%
where the time goes in v6:
time: 241 us; the launch traced here: 240 us
  waiting for transfers between devices  96.5 us (40%)
  starting transfers between devices  71 us (29%)
  Pallas kernels  54.6 us (23%)
  blocking collectives  13.9 us (6%)
    ppermute x3, waiting for transfers between devices, swap_ends(): from_above = lax.ppermute(low, DOM, [(i + 1, i) for i in range(count - 1)])  33 us
    ppermute x3, waiting for transfers between devices, swap_ends(): from_below = lax.ppermute(high, DOM, [(i, i + 1) for i in range(count - 1)])  26.8 us
    pallas_call x2, Pallas kernels, filtered(): pl.pallas_call(filter_kernel, out_shape=jax.ShapeDtypeStruct((rows // 2,...  26.5 us
    all_to_all x2, starting transfers between devices, pipeline(): held.append(lax.all_to_all(blocks, VEC, 0, 0, tiled=True))  20.9 us
    all_to_all x1, blocking collectives, from_everyone(): return lax.all_to_all(copies, axis, split_axis=0, concat_axis=0, tiled=True)  13.9 us
    all_to_all x2, waiting for transfers between devices, pipeline(): held.append(lax.all_to_all(blocks, VEC, 0, 0, tiled=True))  13.9 us
    ppermute x10, starting transfers between devices, traded(): lax.ppermute(blocks[k], axis, [(i, i ^ k) for i in range(count)])  13.8 us
    pallas_call x2, Pallas kernels, projected(): pl.pallas_call(project_kernel, out_shape=jax.ShapeDtypeStruct((near, coun...  12.8 us
  transfers between devices with their start and end apart: 23, of which 11 were waited for; matrix products, arithmetic and copies ran while one was open for 1% of the time, Pallas kernels for 14%

profile of v6, /device:TPU:1, one launch (start us, length us, event | category | flops | bytes accessed | tf_op | source)
XLA Modules:
  0.0 239.9 jit_solution(4508671901301453723)
XLA Ops:
  0.0 7.7 %collective-permute-start.2 = (f32[8,2,128]{2,1,0:T(2,128)}, f32[8,2,128]{2,1,0:T(2,128)S(1)}, u32[]{:S(2)}, u32[]{:S(2)}) collective-permute-start(f32[8,2,128]{2,1,0:T(2,128)} %param.4), channel_id=1, source_target_pairs={{0,128},{128,0},{1,129},{129,1},{2,130},{130,2},{3,131},{131,3},{4... | collective-permute-start | bytes 24584 | tf_op jit(solution)/shard_map/ppermute | solution.py:286
  7.7 1.2 collective-permute-done.2
  9.0 0.7 select_bitcast_fusion.1
  9.7 0.7 broadcast_in_dim.6
  10.4 5.8 %all-to-all-start = ((f32[8,2,8,2,128]{4,3,1,2,0:T(2,128)}), f32[8,2,8,2,128]{4,3,1,2,0:T(2,128)S(1)}, u32[]{:S(2)}, u32[]{:S(2)}) async-start(f32[8,2,8,2,128]{4,3,1,2,0:T(2,128)} %broadcast_in_dim.6), calls=%async_computation | async-start | bytes 262144 | tf_op jit(solution)/shard_map/all_to_all | solution.py:291
  16.2 4.1 %shard_map.37 = (bf16[4,32,16,128]{3,2,1,0:T(8,128)(2,1)}, bf16[4,32,16,128]{3,2,1,0:T(8,128)(2,1)}) custom-call(f32[32,256,128]{2,1,0:T(8,128)} %bitcast.18, f32[32,256,128]{2,1,0:T(8,128)} %bitcast.19), custom_call_target="tpu_custom_call" | custom-call | flops 524288 | bytes 3145728 | tf_op jit(solution)/shard_map/pallas_call | solution.py:34
  20.3 2.7 %collective-permute-start = (bf16[4,32,16,128]{3,2,1,0:T(8,128)(2,1)}, bf16[4,32,16,128]{3,2,1,0:T(8,128)(2,1)S(1)}, u32[]{:S(2)}, u32[]{:S(2)}) collective-permute-start(bf16[4,32,16,128]{3,2,1,0:T(8,128)(2,1)} %get-tuple-element.9), channel_id=1, source_target_pairs={{0,1},{1,2},{2,3},{3,4},{4,5},{5,6},{6,7},{7,8},{8,9},{9,10},{10,1... | collective-permute-start | bytes 1572872 | tf_op jit(solution)/shard_map/ppermute | solution.py:296
  23.0 1.3 collective-permute-start.1
  24.3 0.1 add_bitcast_fusion
  24.5 1.3 collective-permute-start.4
  25.8 4.6 %collective-permute-start.3 = (f32[4,32,128]{2,1,0:T(8,128)S(1)}, f32[4,32,128]{2,1,0:T(8,128)S(1)}, u32[]{:S(2)}, u32[]{:S(2)}) collective-permute-start(f32[4,32,128]{2,1,0:T(8,128)S(1)} %bitcast.28), channel_id=1, source_target_pairs={{0,1},{1,2},{2,3},{3,4},{4,5},{5,6},{6,7},{7,8},{8,9},{9,10},{10,1... | collective-permute-start | bytes 196616 | tf_op jit(solution)/shard_map/ppermute | solution.py:296
  30.4 0.1 add_convert_fusion.1.ends_ref
  30.5 20.9 %collective-permute-done.4 = f32[4,32,128]{2,1,0:T(8,128)S(1)} collective-permute-done((f32[4,32,128]{2,1,0:T(8,128)S(1)}, f32[4,32,128]{2,1,0:T(8,128)S(1)}, u32[]{:S(2)}, u32[]{:S(2)}) %collective-permute-start.4) | collective-permute-done | bytes 65568 | tf_op jit(solution)/shard_map/ppermute | solution.py:297
  51.5 13.3 %shard_map.38 = bf16[16,16,16,128]{3,2,1,0:T(8,128)(2,1)} custom-call(s32[2]{0:T(128)S(1)} %add_convert_fusion.1.ends_ref, f32[32,256,128]{2,1,0:T(8,128)} %bitcast.20, bf16[4,32,16,128]{3,2,1,0:T(8,128)(2,1)S(1)} %collective-permute-done.low_ref, bf16[4,32,16,128]{3,2,1,0:T(8,128)(2,1)S(1)} %collective-permute-done.1.high_ref, ...), custom_call_target="tpu_custom_call" | custom-call | flops 34603008 | bytes 5242880 | tf_op jit(solution)/shard_map/pallas_call | solution.py:128
  64.8 11.1 %all-to-all-start.1 = ((bf16[16,16,16,128]{3,2,1,0:T(8,128)(2,1)}), bf16[16,16,16,128]{3,2,1,0:T(8,128)(2,1)S(1)}, u32[]{:S(2)}, u32[]{:S(2)}) async-start(bf16[16,16,16,128]{3,2,1,0:T(8,128)(2,1)} %shard_map.38), calls=%async_computation.1 | async-start | bytes 2097152 | tf_op jit(solution)/shard_map/all_to_all | solution.py:326
  75.8 4.1 %shard_map.40 = (bf16[4,32,16,128]{3,2,1,0:T(8,128)(2,1)}, bf16[4,32,16,128]{3,2,1,0:T(8,128)(2,1)}) custom-call(f32[32,256,128]{2,1,0:T(8,128)} %bitcast.21, f32[32,256,128]{2,1,0:T(8,128)} %bitcast.22), custom_call_target="tpu_custom_call" | custom-call | flops 524288 | bytes 3145728 | tf_op jit(solution)/shard_map/pallas_call | solution.py:34
  79.9 2.3 collective-permute-start.12
  82.2 1.3 collective-permute-start.13
  83.5 26.8 %collective-permute-done.12.low_ref = bf16[4,32,16,128]{3,2,1,0:T(8,128)(2,1)S(1)} collective-permute-done((bf16[4,32,16,128]{3,2,1,0:T(8,128)(2,1)}, bf16[4,32,16,128]{3,2,1,0:T(8,128)(2,1)S(1)}, u32[]{:S(2)}, u32[]{:S(2)}) %collective-permute-start.12) | collective-permute-done | bytes 524320 | tf_op jit(solution)/shard_map/ppermute | solution.py:296
  110.3 12.1 %collective-permute-done.13.high_ref = bf16[4,32,16,128]{3,2,1,0:T(8,128)(2,1)S(1)} collective-permute-done((bf16[4,32,16,128]{3,2,1,0:T(8,128)(2,1)}, bf16[4,32,16,128]{3,2,1,0:T(8,128)(2,1)S(1)}, u32[]{:S(2)}, u32[]{:S(2)}) %collective-permute-start.13) | collective-permute-done | bytes 524320 | tf_op jit(solution)/shard_map/ppermute | solution.py:297
  122.4 13.2 %shard_map.41 = bf16[16,16,16,128]{3,2,1,0:T(8,128)(2,1)} custom-call(s32[2]{0:T(128)S(1)} %add_convert_fusion.1.ends_ref, f32[32,256,128]{2,1,0:T(8,128)} %bitcast.23, bf16[4,32,16,128]{3,2,1,0:T(8,128)(2,1)S(1)} %collective-permute-done.12.low_ref, bf16[4,32,16,128]{3,2,1,0:T(8,128)(2,1)S(1)} %collective-permute-done.13.high_ref, ...), custom_call_target="tpu_custom_call" | custom-call | flops 34603008 | bytes 5242880 | tf_op jit(solution)/shard_map/pallas_call | solution.py:128
  135.6 9.8 %all-to-all-start.2 = ((bf16[16,16,16,128]{3,2,1,0:T(8,128)(2,1)}), bf16[16,16,16,128]{3,2,1,0:T(8,128)(2,1)S(1)}, u32[]{:S(2)}, u32[]{:S(2)}) async-start(bf16[16,16,16,128]{3,2,1,0:T(8,128)(2,1)} %shard_map.41), calls=%async_computation.2 | async-start | bytes 2097152 | tf_op jit(solution)/shard_map/all_to_all | solution.py:326
  145.4 6.0 %shard_map.39 = f32[32,8,1024]{2,1,0:T(8,128)S(1)} custom-call(s32[1]{0:T(128)} %bitcast.1.place_ref, bf16[16,128,1024]{2,1,0:T(8,128)(2,1)} %bitcast.24, bf16[16,16,16,128]{3,2,1,0:T(8,128)(2,1)S(1)} %all-to-all-done.1.cells_ref.refs_0_), custom_call_target="tpu_custom_call" | custom-call | flops 1073741824 | bytes 7340032 | tf_op jit(solution)/shard_map/pallas_call | solution.py:177
  151.5 0.2 collective-permute-start.5
  151.7 1.8 collective-permute-done.5
  153.5 0.1 slice_add_fusion
  153.5 0.7 fusion.4
  154.3 3.0 %collective-permute-start.7 = (f32[4,8,1024]{2,1,0:T(8,128)}, f32[4,8,1024]{2,1,0:T(8,128)S(1)}, u32[]{:S(2)}, u32[]{:S(2)}) collective-permute-start(f32[4,8,1024]{2,1,0:T(8,128)} %get-tuple-element.14), channel_id=1, source_target_pairs={{0,8},{4,12},{8,0},{12,4},{1,9},{5,13},{9,1},{13,5},{2,10},{6,14},... | collective-permute-start | bytes 393224 | tf_op jit(solution)/shard_map/ppermute | solution.py:261
  157.3 0.3 collective-permute-start.6
  157.5 13.8 %all-to-all-done.2.cells_ref.refs_1_ = bf16[16,16,16,128]{3,2,1,0:T(8,128)(2,1)S(1)} async-done(((bf16[16,16,16,128]{3,2,1,0:T(8,128)(2,1)}), bf16[16,16,16,128]{3,2,1,0:T(8,128)(2,1)S(1)}, u32[]{:S(2)}, u32[]{:S(2)}) %all-to-all-start.2) | async-done | bytes 1048608 | tf_op jit(solution)/shard_map/all_to_all | solution.py:326
  171.4 6.8 %shard_map.42 = bf16[32,8,1024]{2,1,0:T(8,128)(2,1)} custom-call(s32[1]{0:T(128)} %bitcast.1.place_ref, bf16[16,128,1024]{2,1,0:T(8,128)(2,1)} %bitcast.25, bf16[16,16,16,128]{3,2,1,0:T(8,128)(2,1)S(1)} %all-to-all-done.2.cells_ref.refs_1_), custom_call_target="tpu_custom_call" | custom-call | flops 1073741824 | bytes 7340032 | tf_op jit(solution)/shard_map/pallas_call | solution.py:177
  178.2 6.1 %all-to-all-start.3 = ((bf16[32,8,1024]{2,1,0:T(8,128)(2,1)}), bf16[32,8,1024]{2,1,0:T(8,128)(2,1)S(1)}, u32[]{:S(2)}, u32[]{:S(2)}) async-start(bf16[32,8,1024]{2,1,0:T(8,128)(2,1)} %shard_map.42), calls=%async_computation.3 | async-start | bytes 1048576 | tf_op jit(solution)/shard_map/all_to_all | solution.py:269
  184.3 0.9 fusion
  185.2 2.7 %collective-permute-start.11 = (f32[1,8,1024]{2,1,0:T(8,128)S(1)}, f32[1,8,1024]{2,1,0:T(8,128)S(1)}, u32[]{:S(2)}, u32[]{:S(2)}) collective-permute-start(f32[1,8,1024]{2,1,0:T(8,128)S(1)} %get-tuple-element.16), channel_id=1, source_target_pairs={{0,96},{32,64},{64,32},{96,0},{1,97},{33,65},{65,33},{97,1},{2,98}... | collective-permute-start | bytes 98312 | tf_op jit(solution)/shard_map/ppermute | solution.py:261
  187.9 0.6 collective-permute-start.10
  188.5 0.1 collective-permute-start.9
  188.6 7.1 %all-to-all-done.3 = bf16[32,8,1024]{2,1,0:T(8,128)(2,1)S(1)} async-done(((bf16[32,8,1024]{2,1,0:T(8,128)(2,1)}), bf16[32,8,1024]{2,1,0:T(8,128)(2,1)S(1)}, u32[]{:S(2)}, u32[]{:S(2)}) %all-to-all-start.3) | async-done | bytes 524320 | tf_op jit(solution)/shard_map/all_to_all | solution.py:269
  195.7 0.1 convert_reduce_fusion
  195.8 0.1 collective-permute-start.14
  195.9 7.0 %collective-permute-done.14 = f32[16,1024]{1,0:T(8,128)S(1)} collective-permute-done((f32[16,1024]{1,0:T(8,128)S(1)}, f32[16,1024]{1,0:T(8,128)S(1)}, u32[]{:S(2)}, u32[]{:S(2)}) %collective-permute-start.14) | collective-permute-done | bytes 65568 | tf_op jit(solution)/shard_map/ppermute | solution.py:286
  203.0 3.8 %collective-permute-start.17 = (f32[16,1024]{1,0:T(8,128)S(1)}, f32[16,1024]{1,0:T(8,128)S(1)}, u32[]{:S(2)}, u32[]{:S(2)}) collective-permute-start(f32[16,1024]{1,0:T(8,128)S(1)} %fusion.3), channel_id=1, source_target_pairs={{0,3},{1,2},{2,1},{3,0},{4,7},{5,6},{6,5},{7,4},{8,11},{9,10},{10,... | collective-permute-start | bytes 196616 | tf_op jit(solution)/shard_map/ppermute | solution.py:261
  206.7 3.2 %collective-permute-start.16 = (f32[16,1024]{1,0:T(8,128)S(1)}, f32[16,1024]{1,0:T(8,128)S(1)}, u32[]{:S(2)}, u32[]{:S(2)}) collective-permute-start(f32[16,1024]{1,0:T(8,128)S(1)} %fusion.3), channel_id=1, source_target_pairs={{0,2},{1,3},{2,0},{3,1},{4,6},{5,7},{6,4},{7,5},{8,10},{9,11},{10,... | collective-permute-start | bytes 196616 | tf_op jit(solution)/shard_map/ppermute | solution.py:261
  209.9 4.0 %collective-permute-done.16 = f32[16,1024]{1,0:T(8,128)S(1)} collective-permute-done((f32[16,1024]{1,0:T(8,128)S(1)}, f32[16,1024]{1,0:T(8,128)S(1)}, u32[]{:S(2)}, u32[]{:S(2)}) %collective-permute-start.16) | collective-permute-done | bytes 65568 | tf_op jit(solution)/shard_map/ppermute | solution.py:261
  213.9 0.1 collective-permute-done.15
  214.1 13.9 %all_to_all.25.mine_ref = bf16[16,16,1024]{2,1,0:T(8,128)(2,1)S(1)} all-to-all(bf16[16,16,1024]{2,1,0:T(8,128)(2,1)S(1)} %broadcast_in_dim.7), channel_id=1, replica_groups=mesh['zh'=2,'x'=4,'c'=2,'y'=4,'zl'=4] {'y','x'}, dimensions={0} | all-to-all | bytes 1048576 | tf_op jit(solution)/shard_map/all_to_all | solution.py:291
  228.0 3.2 %collective-permute-start.18 = (bf16[16,16,1024]{2,1,0:T(8,128)(2,1)S(1)}, bf16[16,16,1024]{2,1,0:T(8,128)(2,1)S(1)}, u32[]{:S(2)}, u32[]{:S(2)}) collective-permute-start(bf16[16,16,1024]{2,1,0:T(8,128)(2,1)S(1)} %all_to_all.25.mine_ref), channel_id=1, source_target_pairs={{0,16},{16,0},{1,17},{17,1},{2,18},{18,2},{3,19},{19,3},{4,20},{20... | collective-permute-start | bytes 1572872 | tf_op jit(solution)/shard_map/ppermute | solution.py:286
  231.1 1.5 collective-permute-done.18.other_ref
  232.7 7.2 %shard_map.43 = f32[16,512,128]{2,1,0:T(8,128)} custom-call(s32[1]{0:T(128)} %bitcast.core_ref, bf16[16,16,1024]{2,1,0:T(8,128)(2,1)S(1)} %all_to_all.25.mine_ref, bf16[16,16,1024]{2,1,0:T(8,128)(2,1)S(1)} %collective-permute-done.18.other_ref, bf16[16,128,1024]{2,1,0:T(8,128)(2,1)} %bitcast.26, ...), custom_call_target="tpu_custom_call" | custom-call | flops 2147483648 | bytes 11534336 | tf_op jit(solution)/shard_map/pallas_call | solution.py:229
  (28 shorter events, 0.3 us)
Async XLA Ops:
  0.0 9.0 %collective-permute-start.2 = (f32[8,2,128]{2,1,0:T(2,128)}, f32[8,2,128]{2,1,0:T(2,128)S(1)}, u32[]{:S(2)}, u32[]{:S(2)}) collective-permute-start(f32[8,2,128]{2,1,0:T(2,128)} %param.4), channel_id=1, source_target_pairs={{0,128},{128,0},{1,129},{129,1},{2,130},{130,2},{3,131},{131,3},{4... | collective-permute-start | bytes 24584 | tf_op jit(solution)/shard_map/ppermute | solution.py:286
  10.4 13.9 %all-to-all-start = ((f32[8,2,8,2,128]{4,3,1,2,0:T(2,128)}), f32[8,2,8,2,128]{4,3,1,2,0:T(2,128)S(1)}, u32[]{:S(2)}, u32[]{:S(2)}) async-start(f32[8,2,8,2,128]{4,3,1,2,0:T(2,128)} %broadcast_in_dim.6), calls=%async_computation | async-start | bytes 262144 | tf_op jit(solution)/shard_map/all_to_all | solution.py:291
  20.3 31.2 %collective-permute-start = (bf16[4,32,16,128]{3,2,1,0:T(8,128)(2,1)}, bf16[4,32,16,128]{3,2,1,0:T(8,128)(2,1)S(1)}, u32[]{:S(2)}, u32[]{:S(2)}) collective-permute-start(bf16[4,32,16,128]{3,2,1,0:T(8,128)(2,1)} %get-tuple-element.9), channel_id=1, source_target_pairs={{0,1},{1,2},{2,3},{3,4},{4,5},{5,6},{6,7},{7,8},{8,9},{9,10},{10,1... | collective-permute-start | bytes 1572872 | tf_op jit(solution)/shard_map/ppermute | solution.py:296
  23.0 28.5 %collective-permute-start.1 = (bf16[4,32,16,128]{3,2,1,0:T(8,128)(2,1)}, bf16[4,32,16,128]{3,2,1,0:T(8,128)(2,1)S(1)}, u32[]{:S(2)}, u32[]{:S(2)}) collective-permute-start(bf16[4,32,16,128]{3,2,1,0:T(8,128)(2,1)} %get-tuple-element.10), channel_id=1, source_target_pairs={{1,0},{2,1},{3,2},{4,3},{5,4},{6,5},{7,6},{8,7},{9,8},{10,9},{11,1... | collective-permute-start | bytes 1572872 | tf_op jit(solution)/shard_map/ppermute | solution.py:297
  24.5 27.0 %collective-permute-start.4 = (f32[4,32,128]{2,1,0:T(8,128)S(1)}, f32[4,32,128]{2,1,0:T(8,128)S(1)}, u32[]{:S(2)}, u32[]{:S(2)}) collective-permute-start(f32[4,32,128]{2,1,0:T(8,128)S(1)} %bitcast.29), channel_id=1, source_target_pairs={{1,0},{2,1},{3,2},{4,3},{5,4},{6,5},{7,6},{8,7},{9,8},{10,9},{11,1... | collective-permute-start | bytes 196616 | tf_op jit(solution)/shard_map/ppermute | solution.py:297
  25.8 25.7 %collective-permute-start.3 = (f32[4,32,128]{2,1,0:T(8,128)S(1)}, f32[4,32,128]{2,1,0:T(8,128)S(1)}, u32[]{:S(2)}, u32[]{:S(2)}) collective-permute-start(f32[4,32,128]{2,1,0:T(8,128)S(1)} %bitcast.28), channel_id=1, source_target_pairs={{0,1},{1,2},{2,3},{3,4},{4,5},{5,6},{6,7},{7,8},{8,9},{9,10},{10,1... | collective-permute-start | bytes 196616 | tf_op jit(solution)/shard_map/ppermute | solution.py:296
  64.8 70.8 %all-to-all-start.1 = ((bf16[16,16,16,128]{3,2,1,0:T(8,128)(2,1)}), bf16[16,16,16,128]{3,2,1,0:T(8,128)(2,1)S(1)}, u32[]{:S(2)}, u32[]{:S(2)}) async-start(bf16[16,16,16,128]{3,2,1,0:T(8,128)(2,1)} %shard_map.38), calls=%async_computation.1 | async-start | bytes 2097152 | tf_op jit(solution)/shard_map/all_to_all | solution.py:326
  79.9 30.4 %collective-permute-start.12 = (bf16[4,32,16,128]{3,2,1,0:T(8,128)(2,1)}, bf16[4,32,16,128]{3,2,1,0:T(8,128)(2,1)S(1)}, u32[]{:S(2)}, u32[]{:S(2)}) collective-permute-start(bf16[4,32,16,128]{3,2,1,0:T(8,128)(2,1)} %get-tuple-element.11), channel_id=1, source_target_pairs={{0,1},{1,2},{2,3},{3,4},{4,5},{5,6},{6,7},{7,8},{8,9},{9,10},{10,1... | collective-permute-start | bytes 1572872 | tf_op jit(solution)/shard_map/ppermute | solution.py:296
  82.2 40.2 %collective-permute-start.13 = (bf16[4,32,16,128]{3,2,1,0:T(8,128)(2,1)}, bf16[4,32,16,128]{3,2,1,0:T(8,128)(2,1)S(1)}, u32[]{:S(2)}, u32[]{:S(2)}) collective-permute-start(bf16[4,32,16,128]{3,2,1,0:T(8,128)(2,1)} %get-tuple-element.12), channel_id=1, source_target_pairs={{1,0},{2,1},{3,2},{4,3},{5,4},{6,5},{7,6},{8,7},{9,8},{10,9},{11,1... | collective-permute-start | bytes 1572872 | tf_op jit(solution)/shard_map/ppermute | solution.py:297
  135.6 35.8 %all-to-all-start.2 = ((bf16[16,16,16,128]{3,2,1,0:T(8,128)(2,1)}), bf16[16,16,16,128]{3,2,1,0:T(8,128)(2,1)S(1)}, u32[]{:S(2)}, u32[]{:S(2)}) async-start(bf16[16,16,16,128]{3,2,1,0:T(8,128)(2,1)} %shard_map.41), calls=%async_computation.2 | async-start | bytes 2097152 | tf_op jit(solution)/shard_map/all_to_all | solution.py:326
  151.5 2.0 collective-permute-start.5
  154.3 30.0 %collective-permute-start.8 = (f32[4,8,1024]{2,1,0:T(8,128)}, f32[4,8,1024]{2,1,0:T(8,128)S(1)}, u32[]{:S(2)}, u32[]{:S(2)}) collective-permute-start(f32[4,8,1024]{2,1,0:T(8,128)} %get-tuple-element.13), channel_id=1, source_target_pairs={{0,12},{4,8},{8,4},{12,0},{1,13},{5,9},{9,5},{13,1},{2,14},{6,10},... | collective-permute-start | bytes 393224 | tf_op jit(solution)/shard_map/ppermute | solution.py:261
  154.3 30.0 %collective-permute-start.7 = (f32[4,8,1024]{2,1,0:T(8,128)}, f32[4,8,1024]{2,1,0:T(8,128)S(1)}, u32[]{:S(2)}, u32[]{:S(2)}) collective-permute-start(f32[4,8,1024]{2,1,0:T(8,128)} %get-tuple-element.14), channel_id=1, source_target_pairs={{0,8},{4,12},{8,0},{12,4},{1,9},{5,13},{9,1},{13,5},{2,10},{6,14},... | collective-permute-start | bytes 393224 | tf_op jit(solution)/shard_map/ppermute | solution.py:261
  157.3 27.0 %collective-permute-start.6 = (f32[4,8,1024]{2,1,0:T(8,128)S(1)}, f32[4,8,1024]{2,1,0:T(8,128)}, u32[]{:S(2)}, u32[]{:S(2)}) collective-permute-start(f32[4,8,1024]{2,1,0:T(8,128)S(1)} %get-tuple-element.15), channel_id=1, source_target_pairs={{0,4},{4,0},{8,12},{12,8},{1,5},{5,1},{9,13},{13,9},{2,6},{6,2},{1... | collective-permute-start | bytes 393224 | tf_op jit(solution)/shard_map/ppermute | solution.py:261
  178.2 17.5 %all-to-all-start.3 = ((bf16[32,8,1024]{2,1,0:T(8,128)(2,1)}), bf16[32,8,1024]{2,1,0:T(8,128)(2,1)S(1)}, u32[]{:S(2)}, u32[]{:S(2)}) async-start(bf16[32,8,1024]{2,1,0:T(8,128)(2,1)} %shard_map.42), calls=%async_computation.3 | async-start | bytes 1048576 | tf_op jit(solution)/shard_map/all_to_all | solution.py:269
  185.2 10.5 %collective-permute-start.11 = (f32[1,8,1024]{2,1,0:T(8,128)S(1)}, f32[1,8,1024]{2,1,0:T(8,128)S(1)}, u32[]{:S(2)}, u32[]{:S(2)}) collective-permute-start(f32[1,8,1024]{2,1,0:T(8,128)S(1)} %get-tuple-element.16), channel_id=1, source_target_pairs={{0,96},{32,64},{64,32},{96,0},{1,97},{33,65},{65,33},{97,1},{2,98}... | collective-permute-start | bytes 98312 | tf_op jit(solution)/shard_map/ppermute | solution.py:261
  187.9 7.9 %collective-permute-start.10 = (f32[1,8,1024]{2,1,0:T(8,128)S(1)}, f32[1,8,1024]{2,1,0:T(8,128)S(1)}, u32[]{:S(2)}, u32[]{:S(2)}) collective-permute-start(f32[1,8,1024]{2,1,0:T(8,128)S(1)} %get-tuple-element.17), channel_id=1, source_target_pairs={{0,64},{32,96},{64,0},{96,32},{1,65},{33,97},{65,1},{97,33},{2,66}... | collective-permute-start | bytes 98312 | tf_op jit(solution)/shard_map/ppermute | solution.py:261
  188.5 7.3 %collective-permute-start.9 = (f32[1,8,1024]{2,1,0:T(8,128)S(1)}, f32[1,8,1024]{2,1,0:T(8,128)S(1)}, u32[]{:S(2)}, u32[]{:S(2)}) collective-permute-start(f32[1,8,1024]{2,1,0:T(8,128)S(1)} %get-tuple-element.18), channel_id=1, source_target_pairs={{0,32},{32,0},{64,96},{96,64},{1,33},{33,1},{65,97},{97,65},{2,34}... | collective-permute-start | bytes 98312 | tf_op jit(solution)/shard_map/ppermute | solution.py:261
  195.8 7.1 %collective-permute-start.14 = (f32[16,1024]{1,0:T(8,128)S(1)}, f32[16,1024]{1,0:T(8,128)S(1)}, u32[]{:S(2)}, u32[]{:S(2)}) collective-permute-start(f32[16,1024]{1,0:T(8,128)S(1)} %pad_maximum_fusion.1), channel_id=1, source_target_pairs={{0,128},{128,0},{1,129},{129,1},{2,130},{130,2},{3,131},{131,3},{4... | collective-permute-start | bytes 196616 | tf_op jit(solution)/shard_map/ppermute | solution.py:286
  203.0 7.0 %collective-permute-start.17 = (f32[16,1024]{1,0:T(8,128)S(1)}, f32[16,1024]{1,0:T(8,128)S(1)}, u32[]{:S(2)}, u32[]{:S(2)}) collective-permute-start(f32[16,1024]{1,0:T(8,128)S(1)} %fusion.3), channel_id=1, source_target_pairs={{0,3},{1,2},{2,1},{3,0},{4,7},{5,6},{6,5},{7,4},{8,11},{9,10},{10,... | collective-permute-start | bytes 196616 | tf_op jit(solution)/shard_map/ppermute | solution.py:261
  206.7 7.2 %collective-permute-start.16 = (f32[16,1024]{1,0:T(8,128)S(1)}, f32[16,1024]{1,0:T(8,128)S(1)}, u32[]{:S(2)}, u32[]{:S(2)}) collective-permute-start(f32[16,1024]{1,0:T(8,128)S(1)} %fusion.3), channel_id=1, source_target_pairs={{0,2},{1,3},{2,0},{3,1},{4,6},{5,7},{6,4},{7,5},{8,10},{9,11},{10,... | collective-permute-start | bytes 196616 | tf_op jit(solution)/shard_map/ppermute | solution.py:261
  209.9 4.1 %collective-permute-start.15 = (f32[16,1024]{1,0:T(8,128)S(1)}, f32[16,1024]{1,0:T(8,128)S(1)}, u32[]{:S(2)}, u32[]{:S(2)}) collective-permute-start(f32[16,1024]{1,0:T(8,128)S(1)} %fusion.3), channel_id=1, source_target_pairs={{0,1},{1,0},{2,3},{3,2},{4,5},{5,4},{6,7},{7,6},{8,9},{9,8},{10,11... | collective-permute-start | bytes 196616 | tf_op jit(solution)/shard_map/ppermute | solution.py:261
  228.0 4.7 %collective-permute-start.18 = (bf16[16,16,1024]{2,1,0:T(8,128)(2,1)S(1)}, bf16[16,16,1024]{2,1,0:T(8,128)(2,1)S(1)}, u32[]{:S(2)}, u32[]{:S(2)}) collective-permute-start(bf16[16,16,1024]{2,1,0:T(8,128)(2,1)S(1)} %all_to_all.25.mine_ref), channel_id=1, source_target_pairs={{0,16},{16,0},{1,17},{17,1},{2,18},{18,2},{3,19},{19,3},{4,20},{20... | collective-permute-start | bytes 1572872 | tf_op jit(solution)/shard_map/ppermute | solution.py:286

commit v7 on v6

--- a/solution.py
+++ b/solution.py
@@ -40,6 +40,7 @@
             pl.BlockSpec((size, rows, lanes), lambda p: (chunk, p + half, 0)),
         ],
         out_specs=[out] * 2,
+        compiler_params=pltpu.CompilerParams(vmem_limit_bytes=8 << 20),
         cost_estimate=pl.CostEstimate(
             flops=size * planes * rows * lanes,
             bytes_accessed=6 * size * planes * rows * lanes,
@@ -145,7 +146,8 @@
     )(ends, cells, low, high, diag)
 
 
-def project_kernel(place_ref, ritz_ref, cells_ref, out_ref, total):
+def project_kernel(place_ref, ritz_ref, cells_ref, out_ref, *refs):
+    *kept_refs, total = refs
     step = pl.program_id(0)
     lanes = cells_ref.shape[3]
 
@@ -159,6 +161,8 @@
     total[...] += jnp.dot(
         pair, ritz_ref[...].reshape(2 * lanes, -1), preferred_element_type=f32
     )
+    for kept_ref in kept_refs:
+        kept_ref[pl.ds(2 * step, 2)] = ritz_ref[...]
 
     @pl.when(step == pl.num_programs(0) - 1)
     def _():
@@ -174,16 +178,21 @@
     blocks, rows, vectors, lanes = cells.shape
     kept = ritz.shape[2]
     count = blocks * vectors
+    out_shape = [jax.ShapeDtypeStruct((near, count // near, kept), kind)]
+    out_specs = [pl.BlockSpec((near, count // near, kept), lambda r: (0, 0, 0))]
+    if kind == bf16:
+        out_shape.append(pltpu.VMEM(ritz.shape, ritz.dtype))
+        out_specs.append(pl.BlockSpec(memory_space=pltpu.VMEM))
     return pl.pallas_call(
         project_kernel,
-        out_shape=jax.ShapeDtypeStruct((near, count // near, kept), kind),
+        out_shape=out_shape,
         grid=(rows // 2,),
         in_specs=[
             pl.BlockSpec(memory_space=pltpu.SMEM),
             pl.BlockSpec((2, lanes, kept), lambda r: (r, 0, 0)),
             pl.BlockSpec((blocks, 2, vectors, lanes), lambda r: (0, r, 0, 0)),
         ],
-        out_specs=pl.BlockSpec((near, count // near, kept), lambda r: (0, 0, 0)),
+        out_specs=out_specs,
         scratch_shapes=[pltpu.VMEM((count, kept), f32)],
         compiler_params=pltpu.CompilerParams(vmem_limit_bytes=24 << 20),
         cost_estimate=pl.CostEstimate(
@@ -234,7 +243,7 @@
             pl.BlockSpec(memory_space=pltpu.SMEM),
             coeffs,
             coeffs,
-            pl.BlockSpec((rows, lanes, kept), lambda k: (0, 0, 0)),
+            pl.BlockSpec(memory_space=pltpu.VMEM),
             *([pl.BlockSpec((blocks, rows, vectors, lanes), lambda k: (0, 0, 0, 0))] * chunks),
         ],
         out_specs=pl.BlockSpec((blocks, vectors * rows, lanes), lambda k: (0, k, 0)),
@@ -327,11 +336,13 @@
     column = lax.axis_index(NEAR).reshape(1).astype(jnp.int32)
     for k in range(CHUNKS):
         kind = bf16 if k == CHUNKS - 1 else f32
-        partial = projected(held[k], ritz_rows, lax.axis_size(NEAR), column, kind)
+        partial, *kept = projected(held[k], ritz_rows, lax.axis_size(NEAR), column, kind)
+        if parts:
+            partial, parts[-1] = lax.optimization_barrier((partial, parts[-1]))
         parts.append(near_sum(partial))
     mine, other = summed(parts)
     core = lax.axis_index("c").reshape(1).astype(jnp.int32)
-    out = residual(core, mine, other, ritz_rows, held)
+    out = residual(core, mine, other, kept[0], held)
     return out.reshape(-1, *coefficient.shape)
 
 

time: 241 us -> 236 us (0.979)
  blocking collectives: 13.9 us -> 35.4 us
  waiting for transfers between devices: 96.5 us -> 85.1 us
  starting transfers between devices: 71 us -> 62.8 us
  Pallas kernels: 54.6 us -> 49.7 us
    all_to_all x0 -> x1, blocking collectives: none -> 18.9 us  [near_sum(): blocks = lax.all_to_all(partial, NEAR, 0, 0, tiled=True)]
    all_to_all x2, waiting for transfers between devices: 13.9 us -> 4.94 us  [pipeline(): held.append(lax.all_to_all(blocks, VEC, 0, 0, tiled=True))]
    all_to_all x1 -> x0, waiting for transfers between devices: 7.11 us -> none  [near_sum(): blocks = lax.all_to_all(partial, NEAR, 0, 0, tiled=True)]
    all_to_all x1 -> x0, starting transfers between devices: 6.09 us -> none  [near_sum(): blocks = lax.all_to_all(partial, NEAR, 0, 0, tiled=True)]
    ppermute x10, waiting for transfers between devices: 5.89 us -> 10.9 us  [traded(): lax.ppermute(blocks[k], axis, [(i, i ^ k) for i in range(count)])]
    all_to_all x1, blocking collectives: 13.9 us -> 16.5 us  [from_everyone(): return lax.all_to_all(copies, axis, split_axis=0, concat_axis=0, tiled=True)]
  transfers between devices with their start and end apart: 23 -> 22, of which waited for: 11 -> 13; matrix products, arithmetic and copies ran while one was open for 1% -> 0% of each run, Pallas kernels for 14% -> 13%
where the time goes in v7:
time: 236 us; the launch traced here: 235 us
  waiting for transfers between devices  85.1 us (36%)
  starting transfers between devices  62.8 us (27%)
  Pallas kernels  49.7 us (21%)
  blocking collectives  35.4 us (15%)
    ppermute x3, waiting for transfers between devices, swap_ends(): from_above = lax.ppermute(low, DOM, [(i + 1, i) for i in range(count - 1)])  32.9 us
    ppermute x3, waiting for transfers between devices, swap_ends(): from_below = lax.ppermute(high, DOM, [(i, i + 1) for i in range(count - 1)])  27.8 us
    pallas_call x2, Pallas kernels, filtered(): pl.pallas_call(filter_kernel, out_shape=jax.ShapeDtypeStruct((rows // 2,...  26.5 us
    all_to_all x2, starting transfers between devices, pipeline(): held.append(lax.all_to_all(blocks, VEC, 0, 0, tiled=True))  20.9 us
    all_to_all x1, blocking collectives, near_sum(): blocks = lax.all_to_all(partial, NEAR, 0, 0, tiled=True)  18.9 us
    all_to_all x1, blocking collectives, from_everyone(): return lax.all_to_all(copies, axis, split_axis=0, concat_axis=0, tiled=True)  16.5 us
    pallas_call x2, Pallas kernels, projected(): pl.pallas_call(project_kernel, out_shape=out_shape, grid=(rows // 2,), in...  12 us
    ppermute x10, starting transfers between devices, traded(): lax.ppermute(blocks[k], axis, [(i, i ^ k) for i in range(count)])  11.4 us
  transfers between devices with their start and end apart: 22, of which 13 were waited for; matrix products, arithmetic and copies ran while one was open for 0% of the time, Pallas kernels for 13%

profile of v7, /device:TPU:1, one launch (start us, length us, event | category | flops | bytes accessed | tf_op | source)
XLA Modules:
  0.0 235.2 jit_solution(16662788923892758426)
XLA Ops:
  0.0 7.7 %collective-permute-start.2 = (f32[8,2,128]{2,1,0:T(2,128)}, f32[8,2,128]{2,1,0:T(2,128)S(1)}, u32[]{:S(2)}, u32[]{:S(2)}) collective-permute-start(f32[8,2,128]{2,1,0:T(2,128)} %param.4), channel_id=1, source_target_pairs={{0,128},{128,0},{1,129},{129,1},{2,130},{130,2},{3,131},{131,3},{4... | collective-permute-start | bytes 24584 | tf_op jit(solution)/shard_map/ppermute | solution.py:295
  7.7 1.2 collective-permute-done.2
  9.0 0.7 select_bitcast_fusion.1
  9.7 0.7 broadcast_in_dim.6
  10.4 5.8 %all-to-all-start = ((f32[8,2,8,2,128]{4,3,1,2,0:T(2,128)}), f32[8,2,8,2,128]{4,3,1,2,0:T(2,128)S(1)}, u32[]{:S(2)}, u32[]{:S(2)}) async-start(f32[8,2,8,2,128]{4,3,1,2,0:T(2,128)} %broadcast_in_dim.6), calls=%async_computation | async-start | bytes 262144 | tf_op jit(solution)/shard_map/all_to_all | solution.py:300
  16.2 3.0 %shard_map.40 = (bf16[4,32,16,128]{3,2,1,0:T(8,128)(2,1)S(1)}, bf16[4,32,16,128]{3,2,1,0:T(8,128)(2,1)S(1)}) custom-call(f32[32,256,128]{2,1,0:T(8,128)} %bitcast.18, f32[32,256,128]{2,1,0:T(8,128)} %bitcast.19), custom_call_target="tpu_custom_call" | custom-call | flops 524288 | bytes 3145728 | tf_op jit(solution)/shard_map/pallas_call | solution.py:34
  19.3 2.7 %collective-permute-start.5 = (bf16[4,32,16,128]{3,2,1,0:T(8,128)(2,1)S(1)}, bf16[4,32,16,128]{3,2,1,0:T(8,128)(2,1)S(1)}, u32[]{:S(2)}, u32[]{:S(2)}) collective-permute-start(bf16[4,32,16,128]{3,2,1,0:T(8,128)(2,1)S(1)} %get-tuple-element.16), channel_id=1, source_target_pairs={{0,1},{1,2},{2,3},{3,4},{4,5},{5,6},{6,7},{7,8},{8,9},{9,10},{10,1... | collective-permute-start | bytes 1572872 | tf_op jit(solution)/shard_map/ppermute | solution.py:305
  22.0 1.3 collective-permute-start.6
  23.3 0.1 add_bitcast_fusion
  23.5 1.3 collective-permute-start.4
  24.8 4.6 %collective-permute-start.3 = (f32[4,32,128]{2,1,0:T(8,128)S(1)}, f32[4,32,128]{2,1,0:T(8,128)S(1)}, u32[]{:S(2)}, u32[]{:S(2)}) collective-permute-start(f32[4,32,128]{2,1,0:T(8,128)S(1)} %bitcast.27), channel_id=1, source_target_pairs={{0,1},{1,2},{2,3},{3,4},{4,5},{5,6},{6,7},{7,8},{8,9},{9,10},{10,1... | collective-permute-start | bytes 196616 | tf_op jit(solution)/shard_map/ppermute | solution.py:305
  29.4 0.1 add_convert_fusion.1.ends_ref
  29.5 20.7 %collective-permute-done.4 = f32[4,32,128]{2,1,0:T(8,128)S(1)} collective-permute-done((f32[4,32,128]{2,1,0:T(8,128)S(1)}, f32[4,32,128]{2,1,0:T(8,128)S(1)}, u32[]{:S(2)}, u32[]{:S(2)}) %collective-permute-start.4) | collective-permute-done | bytes 65568 | tf_op jit(solution)/shard_map/ppermute | solution.py:306
  50.3 13.3 %shard_map.41 = bf16[16,16,16,128]{3,2,1,0:T(8,128)(2,1)} custom-call(s32[2]{0:T(128)S(1)} %add_convert_fusion.1.ends_ref, f32[32,256,128]{2,1,0:T(8,128)} %bitcast.20, bf16[4,32,16,128]{3,2,1,0:T(8,128)(2,1)S(1)} %collective-permute-done.5.low_ref, bf16[4,32,16,128]{3,2,1,0:T(8,128)(2,1)S(1)} %collective-permute-done.6.high_ref, ...), custom_call_target="tpu_custom_call" | custom-call | flops 34603008 | bytes 5242880 | tf_op jit(solution)/shard_map/pallas_call | solution.py:129
  63.6 11.1 %all-to-all-start.2 = ((bf16[16,16,16,128]{3,2,1,0:T(8,128)(2,1)}), bf16[16,16,16,128]{3,2,1,0:T(8,128)(2,1)S(1)}, u32[]{:S(2)}, u32[]{:S(2)}) async-start(bf16[16,16,16,128]{3,2,1,0:T(8,128)(2,1)} %shard_map.41), calls=%async_computation.2 | async-start | bytes 2097152 | tf_op jit(solution)/shard_map/all_to_all | solution.py:335
  74.6 3.1 %shard_map.37 = (bf16[4,32,16,128]{3,2,1,0:T(8,128)(2,1)S(1)}, bf16[4,32,16,128]{3,2,1,0:T(8,128)(2,1)S(1)}) custom-call(f32[32,256,128]{2,1,0:T(8,128)} %bitcast.21, f32[32,256,128]{2,1,0:T(8,128)} %bitcast.22), custom_call_target="tpu_custom_call" | custom-call | flops 524288 | bytes 3145728 | tf_op jit(solution)/shard_map/pallas_call | solution.py:34
  77.7 2.3 collective-permute-start
  80.0 1.3 collective-permute-start.1
  81.3 27.7 %collective-permute-done.low_ref = bf16[4,32,16,128]{3,2,1,0:T(8,128)(2,1)S(1)} collective-permute-done((bf16[4,32,16,128]{3,2,1,0:T(8,128)(2,1)S(1)}, bf16[4,32,16,128]{3,2,1,0:T(8,128)(2,1)S(1)}, u32[]{:S(2)}, u32[]{:S(2)}) %collective-permute-start) | collective-permute-done | bytes 524320 | tf_op jit(solution)/shard_map/ppermute | solution.py:305
  109.0 12.1 %collective-permute-done.1.high_ref = bf16[4,32,16,128]{3,2,1,0:T(8,128)(2,1)S(1)} collective-permute-done((bf16[4,32,16,128]{3,2,1,0:T(8,128)(2,1)S(1)}, bf16[4,32,16,128]{3,2,1,0:T(8,128)(2,1)S(1)}, u32[]{:S(2)}, u32[]{:S(2)}) %collective-permute-start.1) | collective-permute-done | bytes 524320 | tf_op jit(solution)/shard_map/ppermute | solution.py:306
  121.2 13.2 %shard_map.38 = bf16[16,16,16,128]{3,2,1,0:T(8,128)(2,1)} custom-call(s32[2]{0:T(128)S(1)} %add_convert_fusion.1.ends_ref, f32[32,256,128]{2,1,0:T(8,128)} %bitcast.23, bf16[4,32,16,128]{3,2,1,0:T(8,128)(2,1)S(1)} %collective-permute-done.low_ref, bf16[4,32,16,128]{3,2,1,0:T(8,128)(2,1)S(1)} %collective-permute-done.1.high_ref, ...), custom_call_target="tpu_custom_call" | custom-call | flops 34603008 | bytes 5242880 | tf_op jit(solution)/shard_map/pallas_call | solution.py:129
  134.4 9.8 %all-to-all-start.1 = ((bf16[16,16,16,128]{3,2,1,0:T(8,128)(2,1)}), bf16[16,16,16,128]{3,2,1,0:T(8,128)(2,1)S(1)}, u32[]{:S(2)}, u32[]{:S(2)}) async-start(bf16[16,16,16,128]{3,2,1,0:T(8,128)(2,1)} %shard_map.38), calls=%async_computation.1 | async-start | bytes 2097152 | tf_op jit(solution)/shard_map/all_to_all | solution.py:335
  144.2 6.0 %shard_map.42 = f32[32,8,1024]{2,1,0:T(8,128)S(1)} custom-call(s32[1]{0:T(128)} %bitcast.1.place_ref, bf16[16,128,1024]{2,1,0:T(8,128)(2,1)} %bitcast.24, bf16[16,16,16,128]{3,2,1,0:T(8,128)(2,1)S(1)} %all-to-all-done.2.cells_ref.refs_0_), custom_call_target="tpu_custom_call" | custom-call | flops 1073741824 | bytes 7340032 | tf_op jit(solution)/shard_map/pallas_call | solution.py:186
  150.3 0.2 collective-permute-start.7
  150.5 1.8 collective-permute-done.7
  152.4 0.1 collective-permute-start.10
  152.5 3.0 %collective-permute-start.9 = (f32[4,8,1024]{2,1,0:T(8,128)S(1)}, f32[4,8,1024]{2,1,0:T(8,128)S(1)}, u32[]{:S(2)}, u32[]{:S(2)}) collective-permute-start(f32[4,8,1024]{2,1,0:T(8,128)S(1)} %get-tuple-element.22), channel_id=1, source_target_pairs={{0,8},{4,12},{8,0},{12,4},{1,9},{5,13},{9,1},{13,5},{2,10},{6,14},... | collective-permute-start | bytes 393224 | tf_op jit(solution)/shard_map/ppermute | solution.py:270
  155.5 0.3 collective-permute-start.8
  155.7 5.8 %collective-permute-done.10 = f32[4,8,1024]{2,1,0:T(8,128)S(1)} collective-permute-done((f32[4,8,1024]{2,1,0:T(8,128)S(1)}, f32[4,8,1024]{2,1,0:T(8,128)S(1)}, u32[]{:S(2)}, u32[]{:S(2)}) %collective-permute-start.10) | collective-permute-done | bytes 131104 | tf_op jit(solution)/shard_map/ppermute | solution.py:270
  161.5 0.2 collective-permute-done.8
  161.8 2.5 %collective-permute-start.13 = (f32[1,8,1024]{2,1,0:T(8,128)S(1)}, f32[1,8,1024]{2,1,0:T(8,128)S(1)}, u32[]{:S(2)}, u32[]{:S(2)}) collective-permute-start(f32[1,8,1024]{2,1,0:T(8,128)S(1)} %get-tuple-element.24), channel_id=1, source_target_pairs={{0,96},{32,64},{64,32},{96,0},{1,97},{33,65},{65,33},{97,1},{2,98}... | collective-permute-start | bytes 98312 | tf_op jit(solution)/shard_map/ppermute | solution.py:270
  164.2 0.6 collective-permute-start.12
  164.8 0.3 collective-permute-start.11
  165.1 4.9 %all-to-all-done.1.cells_ref.refs_1_ = bf16[16,16,16,128]{3,2,1,0:T(8,128)(2,1)S(1)} async-done(((bf16[16,16,16,128]{3,2,1,0:T(8,128)(2,1)}), bf16[16,16,16,128]{3,2,1,0:T(8,128)(2,1)S(1)}, u32[]{:S(2)}, u32[]{:S(2)}) %all-to-all-start.1) | async-done | bytes 1048608 | tf_op jit(solution)/shard_map/all_to_all | solution.py:335
  170.0 6.0 %shard_map.39 = (bf16[32,8,1024]{2,1,0:T(8,128)(2,1)S(1)}, bf16[16,128,1024]{2,1,0:T(8,128)(2,1)S(1)}) custom-call(s32[1]{0:T(128)} %bitcast.1.place_ref, bf16[16,128,1024]{2,1,0:T(8,128)(2,1)} %bitcast.25, bf16[16,16,16,128]{3,2,1,0:T(8,128)(2,1)S(1)} %all-to-all-done.1.cells_ref.refs_1_), custom_call_target="tpu_custom_call" | custom-call | flops 1073741824 | bytes 7340032 | tf_op jit(solution)/shard_map/pallas_call | solution.py:186
  176.1 18.9 %all_to_all.25 = bf16[32,8,1024]{2,1,0:T(8,128)(2,1)S(1)} all-to-all(bf16[32,8,1024]{2,1,0:T(8,128)(2,1)S(1)} %get-tuple-element.19), channel_id=1, replica_groups=mesh['zh'=2,'x'=4,'c'=2,'y'=4,'zl'=4] {'c','y','x'}, dimensions={0} | all-to-all | bytes 1048576 | tf_op jit(solution)/shard_map/all_to_all | solution.py:278
  195.0 0.1 convert_reduce_fusion
  195.1 1.3 collective-permute-start.14
  196.4 5.8 %collective-permute-done.14 = f32[16,1024]{1,0:T(8,128)S(1)} collective-permute-done((f32[16,1024]{1,0:T(8,128)S(1)}, f32[16,1024]{1,0:T(8,128)S(1)}, u32[]{:S(2)}, u32[]{:S(2)}) %collective-permute-start.14) | collective-permute-done | bytes 65568 | tf_op jit(solution)/shard_map/ppermute | solution.py:295
  202.2 0.8 collective-permute-start.17
  203.0 3.8 %collective-permute-start.16 = (f32[16,1024]{1,0:T(8,128)S(1)}, f32[16,1024]{1,0:T(8,128)S(1)}, u32[]{:S(2)}, u32[]{:S(2)}) collective-permute-start(f32[16,1024]{1,0:T(8,128)S(1)} %fusion.3), channel_id=1, source_target_pairs={{0,2},{1,3},{2,0},{3,1},{4,6},{5,7},{6,4},{7,5},{8,10},{9,11},{10,... | collective-permute-start | bytes 196616 | tf_op jit(solution)/shard_map/ppermute | solution.py:270
  206.7 0.6 collective-permute-done.17
  207.4 1.7 collective-permute-done.16
  209.1 0.8 collective-permute-done.15
  209.9 16.5 %all_to_all.26.mine_ref = bf16[16,16,1024]{2,1,0:T(8,128)(2,1)S(1)} all-to-all(bf16[16,16,1024]{2,1,0:T(8,128)(2,1)S(1)} %broadcast_in_dim.7), channel_id=1, replica_groups=mesh['zh'=2,'x'=4,'c'=2,'y'=4,'zl'=4] {'y','x'}, dimensions={0} | all-to-all | bytes 1048576 | tf_op jit(solution)/shard_map/all_to_all | solution.py:300
  226.4 2.2 collective-permute-start.18
  228.6 1.5 collective-permute-done.18.other_ref
  230.1 5.1 %shard_map.43 = f32[16,512,128]{2,1,0:T(8,128)} custom-call(s32[1]{0:T(128)} %bitcast.core_ref, bf16[16,16,1024]{2,1,0:T(8,128)(2,1)S(1)} %all_to_all.26.mine_ref, bf16[16,16,1024]{2,1,0:T(8,128)(2,1)S(1)} %collective-permute-done.18.other_ref, bf16[16,128,1024]{2,1,0:T(8,128)(2,1)S(1)} %get-tuple-element.20.ritz_ref, ...), custom_call_target="tpu_custom_call" | custom-call | flops 2147483648 | bytes 11534336 | tf_op jit(solution)/shard_map/pallas_call | solution.py:238
  (27 shorter events, 0.4 us)
Async XLA Ops:
  0.0 9.0 %collective-permute-start.2 = (f32[8,2,128]{2,1,0:T(2,128)}, f32[8,2,128]{2,1,0:T(2,128)S(1)}, u32[]{:S(2)}, u32[]{:S(2)}) collective-permute-start(f32[8,2,128]{2,1,0:T(2,128)} %param.4), channel_id=1, source_target_pairs={{0,128},{128,0},{1,129},{129,1},{2,130},{130,2},{3,131},{131,3},{4... | collective-permute-start | bytes 24584 | tf_op jit(solution)/shard_map/ppermute | solution.py:295
  10.4 12.9 %all-to-all-start = ((f32[8,2,8,2,128]{4,3,1,2,0:T(2,128)}), f32[8,2,8,2,128]{4,3,1,2,0:T(2,128)S(1)}, u32[]{:S(2)}, u32[]{:S(2)}) async-start(f32[8,2,8,2,128]{4,3,1,2,0:T(2,128)} %broadcast_in_dim.6), calls=%async_computation | async-start | bytes 262144 | tf_op jit(solution)/shard_map/all_to_all | solution.py:300
  19.3 31.0 %collective-permute-start.5 = (bf16[4,32,16,128]{3,2,1,0:T(8,128)(2,1)S(1)}, bf16[4,32,16,128]{3,2,1,0:T(8,128)(2,1)S(1)}, u32[]{:S(2)}, u32[]{:S(2)}) collective-permute-start(bf16[4,32,16,128]{3,2,1,0:T(8,128)(2,1)S(1)} %get-tuple-element.16), channel_id=1, source_target_pairs={{0,1},{1,2},{2,3},{3,4},{4,5},{5,6},{6,7},{7,8},{8,9},{9,10},{10,1... | collective-permute-start | bytes 1572872 | tf_op jit(solution)/shard_map/ppermute | solution.py:305
  22.0 28.3 %collective-permute-start.6 = (bf16[4,32,16,128]{3,2,1,0:T(8,128)(2,1)S(1)}, bf16[4,32,16,128]{3,2,1,0:T(8,128)(2,1)S(1)}, u32[]{:S(2)}, u32[]{:S(2)}) collective-permute-start(bf16[4,32,16,128]{3,2,1,0:T(8,128)(2,1)S(1)} %get-tuple-element.17), channel_id=1, source_target_pairs={{1,0},{2,1},{3,2},{4,3},{5,4},{6,5},{7,6},{8,7},{9,8},{10,9},{11,1... | collective-permute-start | bytes 1572872 | tf_op jit(solution)/shard_map/ppermute | solution.py:306
  23.5 26.8 %collective-permute-start.4 = (f32[4,32,128]{2,1,0:T(8,128)S(1)}, f32[4,32,128]{2,1,0:T(8,128)S(1)}, u32[]{:S(2)}, u32[]{:S(2)}) collective-permute-start(f32[4,32,128]{2,1,0:T(8,128)S(1)} %bitcast.28), channel_id=1, source_target_pairs={{1,0},{2,1},{3,2},{4,3},{5,4},{6,5},{7,6},{8,7},{9,8},{10,9},{11,1... | collective-permute-start | bytes 196616 | tf_op jit(solution)/shard_map/ppermute | solution.py:306
  24.8 25.5 %collective-permute-start.3 = (f32[4,32,128]{2,1,0:T(8,128)S(1)}, f32[4,32,128]{2,1,0:T(8,128)S(1)}, u32[]{:S(2)}, u32[]{:S(2)}) collective-permute-start(f32[4,32,128]{2,1,0:T(8,128)S(1)} %bitcast.27), channel_id=1, source_target_pairs={{0,1},{1,2},{2,3},{3,4},{4,5},{5,6},{6,7},{7,8},{8,9},{9,10},{10,1... | collective-permute-start | bytes 196616 | tf_op jit(solution)/shard_map/ppermute | solution.py:305
  63.6 70.8 %all-to-all-start.2 = ((bf16[16,16,16,128]{3,2,1,0:T(8,128)(2,1)}), bf16[16,16,16,128]{3,2,1,0:T(8,128)(2,1)S(1)}, u32[]{:S(2)}, u32[]{:S(2)}) async-start(bf16[16,16,16,128]{3,2,1,0:T(8,128)(2,1)} %shard_map.41), calls=%async_computation.2 | async-start | bytes 2097152 | tf_op jit(solution)/shard_map/all_to_all | solution.py:335
  77.7 31.3 %collective-permute-start = (bf16[4,32,16,128]{3,2,1,0:T(8,128)(2,1)S(1)}, bf16[4,32,16,128]{3,2,1,0:T(8,128)(2,1)S(1)}, u32[]{:S(2)}, u32[]{:S(2)}) collective-permute-start(bf16[4,32,16,128]{3,2,1,0:T(8,128)(2,1)S(1)} %get-tuple-element.13), channel_id=1, source_target_pairs={{0,1},{1,2},{2,3},{3,4},{4,5},{5,6},{6,7},{7,8},{8,9},{9,10},{10,1... | collective-permute-start | bytes 1572872 | tf_op jit(solution)/shard_map/ppermute | solution.py:305
  80.0 41.2 %collective-permute-start.1 = (bf16[4,32,16,128]{3,2,1,0:T(8,128)(2,1)S(1)}, bf16[4,32,16,128]{3,2,1,0:T(8,128)(2,1)S(1)}, u32[]{:S(2)}, u32[]{:S(2)}) collective-permute-start(bf16[4,32,16,128]{3,2,1,0:T(8,128)(2,1)S(1)} %get-tuple-element.14), channel_id=1, source_target_pairs={{1,0},{2,1},{3,2},{4,3},{5,4},{6,5},{7,6},{8,7},{9,8},{10,9},{11,1... | collective-permute-start | bytes 1572872 | tf_op jit(solution)/shard_map/ppermute | solution.py:306
  134.4 35.6 %all-to-all-start.1 = ((bf16[16,16,16,128]{3,2,1,0:T(8,128)(2,1)}), bf16[16,16,16,128]{3,2,1,0:T(8,128)(2,1)S(1)}, u32[]{:S(2)}, u32[]{:S(2)}) async-start(bf16[16,16,16,128]{3,2,1,0:T(8,128)(2,1)} %shard_map.38), calls=%async_computation.1 | async-start | bytes 2097152 | tf_op jit(solution)/shard_map/all_to_all | solution.py:335
  150.3 2.0 collective-permute-start.7
  152.4 9.1 %collective-permute-start.10 = (f32[4,8,1024]{2,1,0:T(8,128)S(1)}, f32[4,8,1024]{2,1,0:T(8,128)S(1)}, u32[]{:S(2)}, u32[]{:S(2)}) collective-permute-start(f32[4,8,1024]{2,1,0:T(8,128)S(1)} %get-tuple-element.21), channel_id=1, source_target_pairs={{0,12},{4,8},{8,4},{12,0},{1,13},{5,9},{9,5},{13,1},{2,14},{6,10},... | collective-permute-start | bytes 393224 | tf_op jit(solution)/shard_map/ppermute | solution.py:270
  152.5 9.0 %collective-permute-start.9 = (f32[4,8,1024]{2,1,0:T(8,128)S(1)}, f32[4,8,1024]{2,1,0:T(8,128)S(1)}, u32[]{:S(2)}, u32[]{:S(2)}) collective-permute-start(f32[4,8,1024]{2,1,0:T(8,128)S(1)} %get-tuple-element.22), channel_id=1, source_target_pairs={{0,8},{4,12},{8,0},{12,4},{1,9},{5,13},{9,1},{13,5},{2,10},{6,14},... | collective-permute-start | bytes 393224 | tf_op jit(solution)/shard_map/ppermute | solution.py:270
  155.5 6.3 %collective-permute-start.8 = (f32[4,8,1024]{2,1,0:T(8,128)S(1)}, f32[4,8,1024]{2,1,0:T(8,128)S(1)}, u32[]{:S(2)}, u32[]{:S(2)}) collective-permute-start(f32[4,8,1024]{2,1,0:T(8,128)S(1)} %get-tuple-element.23), channel_id=1, source_target_pairs={{0,4},{4,0},{8,12},{12,8},{1,5},{5,1},{9,13},{13,9},{2,6},{6,2},{1... | collective-permute-start | bytes 393224 | tf_op jit(solution)/shard_map/ppermute | solution.py:270
  161.8 14.3 %collective-permute-start.13 = (f32[1,8,1024]{2,1,0:T(8,128)S(1)}, f32[1,8,1024]{2,1,0:T(8,128)S(1)}, u32[]{:S(2)}, u32[]{:S(2)}) collective-permute-start(f32[1,8,1024]{2,1,0:T(8,128)S(1)} %get-tuple-element.24), channel_id=1, source_target_pairs={{0,96},{32,64},{64,32},{96,0},{1,97},{33,65},{65,33},{97,1},{2,98}... | collective-permute-start | bytes 98312 | tf_op jit(solution)/shard_map/ppermute | solution.py:270
  164.2 11.8 %collective-permute-start.12 = (f32[1,8,1024]{2,1,0:T(8,128)S(1)}, f32[1,8,1024]{2,1,0:T(8,128)S(1)}, u32[]{:S(2)}, u32[]{:S(2)}) collective-permute-start(f32[1,8,1024]{2,1,0:T(8,128)S(1)} %get-tuple-element.25), channel_id=1, source_target_pairs={{0,64},{32,96},{64,0},{96,32},{1,65},{33,97},{65,1},{97,33},{2,66}... | collective-permute-start | bytes 98312 | tf_op jit(solution)/shard_map/ppermute | solution.py:270
  164.8 11.2 %collective-permute-start.11 = (f32[1,8,1024]{2,1,0:T(8,128)S(1)}, f32[1,8,1024]{2,1,0:T(8,128)S(1)}, u32[]{:S(2)}, u32[]{:S(2)}) collective-permute-start(f32[1,8,1024]{2,1,0:T(8,128)S(1)} %get-tuple-element.26), channel_id=1, source_target_pairs={{0,32},{32,0},{64,96},{96,64},{1,33},{33,1},{65,97},{97,65},{2,34}... | collective-permute-start | bytes 98312 | tf_op jit(solution)/shard_map/ppermute | solution.py:270
  195.1 7.1 %collective-permute-start.14 = (f32[16,1024]{1,0:T(8,128)S(1)}, f32[16,1024]{1,0:T(8,128)S(1)}, u32[]{:S(2)}, u32[]{:S(2)}) collective-permute-start(f32[16,1024]{1,0:T(8,128)S(1)} %pad_maximum_fusion.1), channel_id=1, source_target_pairs={{0,128},{128,0},{1,129},{129,1},{2,130},{130,2},{3,131},{131,3},{4... | collective-permute-start | bytes 196616 | tf_op jit(solution)/shard_map/ppermute | solution.py:295
  202.2 5.2 %collective-permute-start.17 = (f32[16,1024]{1,0:T(8,128)S(1)}, f32[16,1024]{1,0:T(8,128)S(1)}, u32[]{:S(2)}, u32[]{:S(2)}) collective-permute-start(f32[16,1024]{1,0:T(8,128)S(1)} %fusion.3), channel_id=1, source_target_pairs={{0,3},{1,2},{2,1},{3,0},{4,7},{5,6},{6,5},{7,4},{8,11},{9,10},{10,... | collective-permute-start | bytes 196616 | tf_op jit(solution)/shard_map/ppermute | solution.py:270
  203.0 6.1 %collective-permute-start.16 = (f32[16,1024]{1,0:T(8,128)S(1)}, f32[16,1024]{1,0:T(8,128)S(1)}, u32[]{:S(2)}, u32[]{:S(2)}) collective-permute-start(f32[16,1024]{1,0:T(8,128)S(1)} %fusion.3), channel_id=1, source_target_pairs={{0,2},{1,3},{2,0},{3,1},{4,6},{5,7},{6,4},{7,5},{8,10},{9,11},{10,... | collective-permute-start | bytes 196616 | tf_op jit(solution)/shard_map/ppermute | solution.py:270
  206.7 3.1 %collective-permute-start.15 = (f32[16,1024]{1,0:T(8,128)S(1)}, f32[16,1024]{1,0:T(8,128)S(1)}, u32[]{:S(2)}, u32[]{:S(2)}) collective-permute-start(f32[16,1024]{1,0:T(8,128)S(1)} %fusion.3), channel_id=1, source_target_pairs={{0,1},{1,0},{2,3},{3,2},{4,5},{5,4},{6,7},{7,6},{8,9},{9,8},{10,11... | collective-permute-start | bytes 196616 | tf_op jit(solution)/shard_map/ppermute | solution.py:270
  226.4 3.7 %collective-permute-start.18 = (bf16[16,16,1024]{2,1,0:T(8,128)(2,1)S(1)}, bf16[16,16,1024]{2,1,0:T(8,128)(2,1)S(1)}, u32[]{:S(2)}, u32[]{:S(2)}) collective-permute-start(bf16[16,16,1024]{2,1,0:T(8,128)(2,1)S(1)} %all_to_all.26.mine_ref), channel_id=1, source_target_pairs={{0,16},{16,0},{1,17},{17,1},{2,18},{18,2},{3,19},{19,3},{4,20},{20... | collective-permute-start | bytes 1572872 | tf_op jit(solution)/shard_map/ppermute | solution.py:295

commit v8 on v6

--- a/solution.py
+++ b/solution.py
@@ -40,6 +40,7 @@
             pl.BlockSpec((size, rows, lanes), lambda p: (chunk, p + half, 0)),
         ],
         out_specs=[out] * 2,
+        compiler_params=pltpu.CompilerParams(vmem_limit_bytes=8 << 20),
         cost_estimate=pl.CostEstimate(
             flops=size * planes * rows * lanes,
             bytes_accessed=6 * size * planes * rows * lanes,
@@ -120,14 +121,43 @@
     step(odd, even, 12.25, 4, 8.0 / 2401.0)
 
 
-def filtered(ends, cells, low, high, diag, chunk, size):
+def split_filter_kernel(ends_ref, own_ref, low_ref, high_ref, diag_ref, *refs):
+    *out_refs, packed_ref, even, odd, blocks, sems = refs
+    filter_kernel(ends_ref, own_ref, low_ref, high_ref, diag_ref, blocks, even, odd)
+    half = len(out_refs)
+    copies = []
+    for k, out_ref in enumerate(out_refs):
+        copies.append(pltpu.make_async_copy(blocks.at[ends_ref[2] ^ k], out_ref, sems.at[k]))
+        copies.append(
+            pltpu.make_async_copy(
+                blocks.at[ends_ref[2] ^ (half + k)], packed_ref.at[k], sems.at[half + k]
+            )
+        )
+    for copy in copies:
+        copy.start()
+    for copy in copies:
+        copy.wait()
+
+
+def filtered(ends, cells, low, high, diag, chunk, size, split):
     total, rows, lanes = diag.shape
     planes = total - 2 * HALO
     groups = size // GROUP
     edge = pl.BlockSpec((HALO, rows, GROUP, lanes), lambda g: (0, 0, g, 0))
+    count, shape = rows // 2, (2 * planes, GROUP, lanes)
+    scratch = [pltpu.VMEM((total, rows, GROUP, lanes), f32)] * 2
+    if split:
+        half = count // 2
+        out_shape = [jax.ShapeDtypeStruct(shape, bf16)] * half
+        out_shape.append(jax.ShapeDtypeStruct((half, *shape), bf16))
+        out_specs = [pl.BlockSpec(memory_space=pl.ANY)] * (half + 1)
+        scratch += [pltpu.VMEM((count, *shape), bf16), pltpu.SemaphoreType.DMA((count,))]
+    else:
+        out_shape = jax.ShapeDtypeStruct((count, 2 * planes, size, lanes), bf16)
+        out_specs = pl.BlockSpec((count, *shape), lambda g: (0, 0, g, 0))
     return pl.pallas_call(
-        filter_kernel,
-        out_shape=jax.ShapeDtypeStruct((rows // 2, 2 * planes, size, lanes), bf16),
+        split_filter_kernel if split else filter_kernel,
+        out_shape=out_shape,
         grid=(groups,),
         in_specs=[
             pl.BlockSpec(memory_space=pltpu.SMEM),
@@ -136,8 +166,8 @@
             edge,
             pl.BlockSpec((total, rows, lanes), lambda g: (0, 0, 0)),
         ],
-        out_specs=pl.BlockSpec((rows // 2, 2 * planes, GROUP, lanes), lambda g: (0, 0, g, 0)),
-        scratch_shapes=[pltpu.VMEM((total, rows, GROUP, lanes), f32)] * 2,
+        out_specs=out_specs,
+        scratch_shapes=scratch,
         compiler_params=pltpu.CompilerParams(vmem_limit_bytes=24 << 20),
         cost_estimate=pl.CostEstimate(
             flops=12 * 44 * rows * size * lanes, bytes_accessed=5 << 20, transcendentals=0
@@ -145,51 +175,81 @@
     )(ends, cells, low, high, diag)
 
 
-def project_kernel(place_ref, ritz_ref, cells_ref, out_ref, total):
+def project_kernel(ritz_ref, cells_ref, out_ref, kept_ref, total):
     step = pl.program_id(0)
     lanes = cells_ref.shape[3]
-
-    @pl.when(step == 0)
+    pair = jnp.concatenate(
+        [cells_ref[:, 0].reshape(-1, lanes), cells_ref[:, 1].reshape(-1, lanes)], axis=1
+    )
+    accumulate(pair, ritz_ref, total)
+    kept_ref[pl.ds(2 * step, 2)] = ritz_ref[...]
+
+    @pl.when(step == pl.num_programs(0) - 1)
+    def _():
+        out_ref[...] = total[...].astype(bf16).reshape(out_ref.shape)
+
+
+def accumulate(pair, ritz_ref, total):
+    @pl.when(pl.program_id(0) == 0)
     def _():
         total[...] = jnp.zeros_like(total)
 
-    pair = jnp.concatenate(
-        [cells_ref[:, 0].reshape(-1, lanes), cells_ref[:, 1].reshape(-1, lanes)], axis=1
-    )
     total[...] += jnp.dot(
-        pair, ritz_ref[...].reshape(2 * lanes, -1), preferred_element_type=f32
-    )
-
-    @pl.when(step == pl.num_programs(0) - 1)
+        pair, ritz_ref[...].reshape(pair.shape[1], -1), preferred_element_type=f32
+    )
+
+
+def joined_project_kernel(place_ref, ritz_ref, *refs):
+    *block_refs, out_ref, held_ref, total, pairs = refs
+    for k, block_ref in enumerate(block_refs):
+        source = place_ref[1] ^ k
+        held_ref[source] = block_ref[...]
+        pairs[source] = jnp.concatenate([block_ref[0], block_ref[1]], axis=1)
+    accumulate(pairs[...].reshape(-1, pairs.shape[2]), ritz_ref, total)
+
+    @pl.when(pl.program_id(0) == pl.num_programs(0) - 1)
     def _():
         near, size, _ = out_ref.shape
-        if out_ref.dtype == f32:
-            for q in range(near):
-                out_ref[place_ref[0] ^ q] = total[q * size : (q + 1) * size, :]
-        else:
-            out_ref[...] = total[...].astype(bf16).reshape(out_ref.shape)
-
-
-def projected(cells, ritz, near, place, kind):
-    blocks, rows, vectors, lanes = cells.shape
+        for q in range(near):
+            out_ref[place_ref[0] ^ q] = total[q * size : (q + 1) * size, :]
+
+
+def projected(cells, ritz, near, place):
+    joined = isinstance(cells, list)
+    blocks = len(cells)
+    rows, vectors, lanes = cells[0].shape
     kept = ritz.shape[2]
     count = blocks * vectors
+    block = pl.BlockSpec((blocks, 2, vectors, lanes), lambda r: (0, r, 0, 0))
+    rhs = pl.BlockSpec((2, lanes, kept), lambda r: (r, 0, 0))
+    scratch = [pltpu.VMEM((count, kept), f32)]
+    if joined:
+        operands = [place, ritz, *cells]
+        in_specs = [pl.BlockSpec(memory_space=pltpu.SMEM), rhs]
+        in_specs += [pl.BlockSpec((2, vectors, lanes), lambda r: (r, 0, 0))] * blocks
+        second = jax.ShapeDtypeStruct((blocks, rows, vectors, lanes), bf16)
+        second_spec = block
+        scratch.append(pltpu.VMEM((blocks, vectors, 2 * lanes), bf16))
+    else:
+        operands = [ritz, cells]
+        in_specs = [rhs, block]
+        second = pltpu.VMEM(ritz.shape, ritz.dtype)
+        second_spec = pl.BlockSpec(memory_space=pltpu.VMEM)
     return pl.pallas_call(
-        project_kernel,
-        out_shape=jax.ShapeDtypeStruct((near, count // near, kept), kind),
+        joined_project_kernel if joined else project_kernel,
+        out_shape=[
+            jax.ShapeDtypeStruct((near, count // near, kept), f32 if joined else bf16),
+            second,
+        ],
         grid=(rows // 2,),
-        in_specs=[
-            pl.BlockSpec(memory_space=pltpu.SMEM),
-            pl.BlockSpec((2, lanes, kept), lambda r: (r, 0, 0)),
-            pl.BlockSpec((blocks, 2, vectors, lanes), lambda r: (0, r, 0, 0)),
-        ],
-        out_specs=pl.BlockSpec((near, count // near, kept), lambda r: (0, 0, 0)),
-        scratch_shapes=[pltpu.VMEM((count, kept), f32)],
+        in_specs=in_specs,
+        out_specs=[pl.BlockSpec((near, count // near, kept), lambda r: (0, 0, 0)), second_spec],
+        scratch_shapes=scratch,
         compiler_params=pltpu.CompilerParams(vmem_limit_bytes=24 << 20),
         cost_estimate=pl.CostEstimate(
             flops=2 * count * rows * lanes * kept, bytes_accessed=7 << 20, transcendentals=0
         ),
-    )(place, ritz, cells)
+    )(*operands)
 
 
 def remove_kernel(core_ref, mine_ref, other_ref, ritz_ref, *refs):
@@ -234,7 +294,7 @@
             pl.BlockSpec(memory_space=pltpu.SMEM),
             coeffs,
             coeffs,
-            pl.BlockSpec((rows, lanes, kept), lambda k: (0, 0, 0)),
+            pl.BlockSpec(memory_space=pltpu.VMEM),
             *([pl.BlockSpec((blocks, rows, vectors, lanes), lambda k: (0, 0, 0, 0))] * chunks),
         ],
         out_specs=pl.BlockSpec((blocks, vectors * rows, lanes), lambda k: (0, k, 0)),
@@ -264,6 +324,23 @@
     )
 
 
+def exchanged(blocks):
+    *own, packed = blocks
+    local = ("x", "c")
+    size = lax.axis_size(local)
+
+    def passed_on(pieces):
+        return [pieces[0]] + [
+            lax.ppermute(pieces[d], local, [(i, i ^ d) for i in range(size)])
+            for d in range(1, size)
+        ]
+
+    packed = swapped(packed, "zh")
+    own = passed_on(own)
+    rest = passed_on([packed[d] for d in range(size)])
+    return own + rest
+
+
 def near_sum(partial):
     if partial.dtype == bf16:
         blocks = lax.all_to_all(partial, NEAR, 0, 0, tiled=True)
@@ -312,6 +389,7 @@
     diag = jnp.concatenate([below, diag, above], axis=0)
     place = lax.axis_index(DOM)
     ends = jnp.stack([place == 0, place == lax.axis_size(DOM) - 1]).astype(jnp.int32)
+    ends = jnp.concatenate([ends, lax.axis_index(VEC).reshape(1).astype(jnp.int32)])
     cells = pltpu.with_memory_space_constraint(
         vectors.reshape(count, planes * rows, lanes), pltpu.MemorySpace.HBM
     )
@@ -320,18 +398,27 @@
     )
     held, parts = [], []
     for k in range(CHUNKS):
+        split = k < CHUNKS - 1
         low, high = spread(cells, rows, k, size)
         low, high = swap_ends(low, high)
-        blocks = filtered(ends, cells, low, high, diag, k, size)
-        held.append(lax.all_to_all(blocks, VEC, 0, 0, tiled=True))
-    column = lax.axis_index(NEAR).reshape(1).astype(jnp.int32)
+        blocks = filtered(ends, cells, low, high, diag, k, size, split)
+        if split:
+            held.append(exchanged(blocks))
+        else:
+            held.append(lax.all_to_all(blocks, VEC, 0, 0, tiled=True))
+    places = jnp.stack([lax.axis_index(NEAR), lax.axis_index(VEC)]).astype(jnp.int32)
     for k in range(CHUNKS):
-        kind = bf16 if k == CHUNKS - 1 else f32
-        partial = projected(held[k], ritz_rows, lax.axis_size(NEAR), column, kind)
+        partial, second = projected(held[k], ritz_rows, lax.axis_size(NEAR), places)
+        if isinstance(held[k], list):
+            held[k] = second
+        else:
+            kept = second
+        if parts:
+            partial, parts[-1] = lax.optimization_barrier((partial, parts[-1]))
         parts.append(near_sum(partial))
     mine, other = summed(parts)
     core = lax.axis_index("c").reshape(1).astype(jnp.int32)
-    out = residual(core, mine, other, ritz_rows, held)
+    out = residual(core, mine, other, kept, held)
     return out.reshape(-1, *coefficient.shape)
 
 

time: 241 us -> 242 us (level)
  waiting for transfers between devices: 96.5 us -> 75.5 us
  blocking collectives: 13.9 us -> 33.5 us
  starting transfers between devices: 71 us -> 77.7 us
  Pallas kernels: 54.6 us -> 51.6 us
    ppermute x3, waiting for transfers between devices: 26.8 us -> 0.01 us  [swap_ends(): from_below = lax.ppermute(high, DOM, [(i, i + 1) for i in range(count - 1)])]
    ppermute x0 -> x14, starting transfers between devices: none -> 19.4 us  [passed_on(): lax.ppermute(pieces[d], local, [(i, i ^ d) for i in range(size)])]
    all_to_all x0 -> x1, blocking collectives: none -> 19.3 us  [near_sum(): blocks = lax.all_to_all(partial, NEAR, 0, 0, tiled=True)]
    all_to_all x2 -> x1, starting transfers between devices: 20.9 us -> 3.55 us  [pipeline(): held.append(lax.all_to_all(blocks, VEC, 0, 0, tiled=True))]
    all_to_all x2 -> x1, waiting for transfers between devices: 13.9 us -> 0.01 us  [pipeline(): held.append(lax.all_to_all(blocks, VEC, 0, 0, tiled=True))]
    ppermute x3, waiting for transfers between devices: 33 us -> 43.8 us  [swap_ends(): from_above = lax.ppermute(low, DOM, [(i + 1, i) for i in range(count - 1)])]
    ppermute x10, waiting for transfers between devices: 5.89 us -> 16.4 us  [traded(): lax.ppermute(blocks[k], axis, [(i, i ^ k) for i in range(count)])]
    ppermute x3 -> x4, starting transfers between devices: 11 us -> 21.3 us  [swapped(): return lax.ppermute(value, axis, [(0, 1), (1, 0)])]
  transfers between devices with their start and end apart: 23 -> 36, of which waited for: 11 -> 14; matrix products, arithmetic and copies ran while one was open for 1% -> 0% of each run, Pallas kernels for 14% -> 17%
where the time goes in v8:
time: 242 us; the launch traced here: 241 us
  starting transfers between devices  77.7 us (32%)
  waiting for transfers between devices  75.5 us (31%)
  Pallas kernels  51.6 us (21%)
  blocking collectives  33.5 us (14%)
    ppermute x3, waiting for transfers between devices, swap_ends(): from_above = lax.ppermute(low, DOM, [(i + 1, i) for i in range(count - 1)])  43.8 us
    pallas_call x2, Pallas kernels, filtered(): pl.pallas_call(split_filter_kernel if split else filter_kernel, out_shape...  27 us
    ppermute x4, starting transfers between devices, swapped(): return lax.ppermute(value, axis, [(0, 1), (1, 0)])  21.3 us
    ppermute x14, starting transfers between devices, passed_on(): lax.ppermute(pieces[d], local, [(i, i ^ d) for i in range(size)])  19.4 us
    all_to_all x1, blocking collectives, near_sum(): blocks = lax.all_to_all(partial, NEAR, 0, 0, tiled=True)  19.3 us
    ppermute x10, waiting for transfers between devices, traded(): lax.ppermute(blocks[k], axis, [(i, i ^ k) for i in range(count)])  16.4 us
    ppermute x4, waiting for transfers between devices, swapped(): return lax.ppermute(value, axis, [(0, 1), (1, 0)])  15.2 us
    all_to_all x1, blocking collectives, from_everyone(): return lax.all_to_all(copies, axis, split_axis=0, concat_axis=0, tiled=True)  14.2 us
  transfers between devices with their start and end apart: 36, of which 14 were waited for; matrix products, arithmetic and copies ran while one was open for 0% of the time, Pallas kernels for 17%

profile of v8, /device:TPU:1, one launch (start us, length us, event | category | flops | bytes accessed | tf_op | source)
XLA Modules:
  0.0 240.7 jit_solution(11017469653066124068)
XLA Ops:
  0.0 7.7 %collective-permute-start.2 = (f32[8,2,128]{2,1,0:T(2,128)}, f32[8,2,128]{2,1,0:T(2,128)S(1)}, u32[]{:S(2)}, u32[]{:S(2)}) collective-permute-start(f32[8,2,128]{2,1,0:T(2,128)} %param.4), channel_id=1, source_target_pairs={{0,128},{128,0},{1,129},{129,1},{2,130},{130,2},{3,131},{131,3},{4... | collective-permute-start | bytes 24584 | tf_op jit(solution)/shard_map/ppermute | solution.py:363
  7.7 1.2 collective-permute-done.2
  9.0 0.7 select_bitcast_fusion.1
  10.4 5.8 %all-to-all-start = ((f32[8,2,8,2,128]{4,3,1,2,0:T(2,128)}), f32[8,2,8,2,128]{4,3,1,2,0:T(2,128)S(1)}, u32[]{:S(2)}, u32[]{:S(2)}) async-start(f32[8,2,8,2,128]{4,3,1,2,0:T(2,128)} %broadcast_in_dim.6), calls=%async_computation | async-start | bytes 262144 | tf_op jit(solution)/shard_map/all_to_all | solution.py:368
  16.2 4.0 %shard_map.40 = (bf16[4,32,16,128]{3,2,1,0:T(8,128)(2,1)S(1)}, bf16[4,32,16,128]{3,2,1,0:T(8,128)(2,1)}) custom-call(f32[32,256,128]{2,1,0:T(8,128)} %bitcast.35, f32[32,256,128]{2,1,0:T(8,128)} %bitcast.36), custom_call_target="tpu_custom_call" | custom-call | flops 524288 | bytes 3145728 | tf_op jit(solution)/shard_map/pallas_call | solution.py:34
  20.2 2.7 %collective-permute-start.5 = (bf16[4,32,16,128]{3,2,1,0:T(8,128)(2,1)}, bf16[4,32,16,128]{3,2,1,0:T(8,128)(2,1)S(1)}, u32[]{:S(2)}, u32[]{:S(2)}) collective-permute-start(bf16[4,32,16,128]{3,2,1,0:T(8,128)(2,1)} %get-tuple-element.27), channel_id=1, source_target_pairs={{0,1},{1,2},{2,3},{3,4},{4,5},{5,6},{6,7},{7,8},{8,9},{9,10},{10,1... | collective-permute-start | bytes 1572872 | tf_op jit(solution)/shard_map/ppermute | solution.py:373
  22.9 1.3 collective-permute-start.6
  24.2 3.1 %shard_map.37 = (bf16[4,32,16,128]{3,2,1,0:T(8,128)(2,1)S(1)}, bf16[4,32,16,128]{3,2,1,0:T(8,128)(2,1)S(1)}) custom-call(f32[32,256,128]{2,1,0:T(8,128)} %bitcast.37, f32[32,256,128]{2,1,0:T(8,128)} %bitcast.38), custom_call_target="tpu_custom_call" | custom-call | flops 524288 | bytes 3145728 | tf_op jit(solution)/shard_map/pallas_call | solution.py:34
  27.3 4.0 %collective-permute-start = (bf16[4,32,16,128]{3,2,1,0:T(8,128)(2,1)S(1)}, bf16[4,32,16,128]{3,2,1,0:T(8,128)(2,1)S(1)}, u32[]{:S(2)}, u32[]{:S(2)}) collective-permute-start(bf16[4,32,16,128]{3,2,1,0:T(8,128)(2,1)S(1)} %get-tuple-element.24), channel_id=1, source_target_pairs={{0,1},{1,2},{2,3},{3,4},{4,5},{5,6},{6,7},{7,8},{8,9},{9,10},{10,1... | collective-permute-start | bytes 1572872 | tf_op jit(solution)/shard_map/ppermute | solution.py:373
  31.5 1.3 collective-permute-start.4
  32.8 4.0 %collective-permute-start.3 = (f32[4,32,128]{2,1,0:T(8,128)S(1)}, f32[4,32,128]{2,1,0:T(8,128)S(1)}, u32[]{:S(2)}, u32[]{:S(2)}) collective-permute-start(f32[4,32,128]{2,1,0:T(8,128)S(1)} %bitcast.44), channel_id=1, source_target_pairs={{0,1},{1,2},{2,3},{3,4},{4,5},{5,6},{6,7},{7,8},{8,9},{9,10},{10,1... | collective-permute-start | bytes 196616 | tf_op jit(solution)/shard_map/ppermute | solution.py:373
  37.0 25.2 %collective-permute-done.4 = f32[4,32,128]{2,1,0:T(8,128)S(1)} collective-permute-done((f32[4,32,128]{2,1,0:T(8,128)S(1)}, f32[4,32,128]{2,1,0:T(8,128)S(1)}, u32[]{:S(2)}, u32[]{:S(2)}) %collective-permute-start.4) | collective-permute-done | bytes 65568 | tf_op jit(solution)/shard_map/ppermute | solution.py:374
  62.2 13.8 %shard_map.41 = (bf16[16,16,128]{2,1,0:T(8,128)(2,1)S(1)}, bf16[16,16,128]{2,1,0:T(8,128)(2,1)S(1)}, bf16[16,16,128]{2,1,0:T(8,128)(2,1)S(1)}, bf16[16,16,128]{2...) custom-call(s32[3]{0:T(128)S(1)} %pad_add_fusion.ends_ref, ...), custom_call_target="tpu_custom_call" | custom-call | flops 34603008 | bytes 5242880 | tf_op jit(solution)/shard_map/pallas_call | solution.py:158
  76.0 5.7 %collective-permute-start.14 = (bf16[8,16,16,128]{3,2,1,0:T(8,128)(2,1)S(1)}, bf16[8,16,16,128]{3,2,1,0:T(8,128)(2,1)S(1)}, u32[]{:S(2)}, u32[]{:S(2)}) collective-permute-start(bf16[8,16,16,128]{3,2,1,0:T(8,128)(2,1)S(1)} %get-tuple-element.37), channel_id=1, source_target_pairs={{0,128},{128,0},{1,129},{129,1},{2,130},{130,2},{3,131},{131,3},{4... | collective-permute-start | bytes 1572872 | tf_op jit(solution)/shard_map/ppermute | solution.py:363
  81.7 1.3 collective-permute-start.1
  83.0 1.2 collective-permute-start.7
  84.3 1.7 collective-permute-start.8
  86.1 10.5 %collective-permute-done.14 = bf16[8,16,16,128]{3,2,1,0:T(8,128)(2,1)S(1)} collective-permute-done((bf16[8,16,16,128]{3,2,1,0:T(8,128)(2,1)S(1)}, bf16[8,16,16,128]{3,2,1,0:T(8,128)(2,1)S(1)}, u32[]{:S(2)}, u32[]{:S(2)}) %collective-permute-start.14) | collective-permute-done | bytes 524320 | tf_op jit(solution)/shard_map/ppermute | solution.py:363
  96.6 2.3 collective-permute-start.10
  98.9 18.7 %collective-permute-done.1.high_ref = bf16[4,32,16,128]{3,2,1,0:T(8,128)(2,1)S(1)} collective-permute-done((bf16[4,32,16,128]{3,2,1,0:T(8,128)(2,1)S(1)}, bf16[4,32,16,128]{3,2,1,0:T(8,128)(2,1)S(1)}, u32[]{:S(2)}, u32[]{:S(2)}) %collective-permute-start.1) | collective-permute-done | bytes 524320 | tf_op jit(solution)/shard_map/ppermute | solution.py:374
  117.6 2.8 %collective-permute-start.11 = (bf16[16,16,128]{2,1,0:T(8,128)(2,1)S(1)}, bf16[16,16,128]{2,1,0:T(8,128)(2,1)S(1)}, u32[]{:S(2)}, u32[]{:S(2)}) collective-permute-start(bf16[16,16,128]{2,1,0:T(8,128)(2,1)S(1)} %get-tuple-element.34), channel_id=1, source_target_pairs={{0,80},{16,64},{32,112},{48,96},{64,16},{80,0},{96,48},{112,32},{1... | collective-permute-start | bytes 196616 | tf_op jit(solution)/shard_map/ppermute | solution.py:334
  120.4 0.9 collective-permute-start.12
  121.3 2.0 collective-permute-start.13
  123.3 1.0 collective-permute-start.21
  124.3 1.8 collective-permute-start.20
  126.2 3.3 %collective-permute-start.18 = (bf16[16,16,128]{2,1,0:T(8,128)(2,1)S(1)}, bf16[16,16,128]{2,1,0:T(8,128)(2,1)S(1)}, u32[]{:S(2)}, u32[]{:S(2)}) collective-permute-start(bf16[16,16,128]{2,1,0:T(8,128)(2,1)S(1)} %get-tuple-element.49), channel_id=1, source_target_pairs={{0,64},{16,80},{32,96},{48,112},{64,0},{80,16},{96,32},{112,48},{1... | collective-permute-start | bytes 196616 | tf_op jit(solution)/shard_map/ppermute | solution.py:334
  129.5 1.6 collective-permute-start.16
  131.7 13.2 %shard_map.38 = bf16[16,16,16,128]{3,2,1,0:T(8,128)(2,1)} custom-call(s32[3]{0:T(128)S(1)} %pad_add_fusion.ends_ref, f32[32,256,128]{2,1,0:T(8,128)} %bitcast.40, bf16[4,32,16,128]{3,2,1,0:T(8,128)(2,1)S(1)} %collective-permute-done.low_ref, bf16[4,32,16,128]{3,2,1,0:T(8,128)(2,1)S(1)} %collective-permute-done.1.high_ref, ...), custom_call_target="tpu_custom_call" | custom-call | flops 34603008 | bytes 5242880 | tf_op jit(solution)/shard_map/pallas_call | solution.py:158
  145.0 3.6 %all-to-all-start.1 = ((bf16[16,16,16,128]{3,2,1,0:T(8,128)(2,1)}), bf16[16,16,16,128]{3,2,1,0:T(8,128)(2,1)S(1)}, u32[]{:S(2)}, u32[]{:S(2)}) async-start(bf16[16,16,16,128]{3,2,1,0:T(8,128)(2,1)} %shard_map.38), calls=%async_computation.1 | async-start | bytes 2097152 | tf_op jit(solution)/shard_map/all_to_all | solution.py:408
  148.6 6.4 %shard_map.42 = (f32[32,8,1024]{2,1,0:T(8,128)S(1)}, bf16[16,16,16,128]{3,2,1,0:T(8,128)(2,1)S(1)}) custom-call(s32[2]{0:T(128)S(1)} %pad_add_fusion.1.place_ref, bf16[16,128,1024]{2,1,0:T(8,128)(2,1)} %bitcast.41, bf16[16,16,128]{2,1,0:T(8,128)(2,1)S(1)} %get-tuple-element.29.refs_0_, bf16[16,16,128]{2,1,0:T(8,128)(2,1)S(1)} %collective-permute-done.7.refs_1_, ...), custom_call_target="tpu_custom_call" | custom-call | flops 1073741824 | bytes 7340032 | tf_op jit(solution)/shard_map/pallas_call | solution.py:238
  155.2 1.8 collective-permute-done.22
  157.1 2.6 %collective-permute-start.25 = (f32[4,8,1024]{2,1,0:T(8,128)S(1)}, f32[4,8,1024]{2,1,0:T(8,128)S(1)}, u32[]{:S(2)}, u32[]{:S(2)}) collective-permute-start(f32[4,8,1024]{2,1,0:T(8,128)S(1)} %get-tuple-element.43), channel_id=1, source_target_pairs={{0,12},{4,8},{8,4},{12,0},{1,13},{5,9},{9,5},{13,1},{2,14},{6,10},... | collective-permute-start | bytes 393224 | tf_op jit(solution)/shard_map/ppermute | solution.py:321
  160.5 4.7 %collective-permute-done.25 = f32[4,8,1024]{2,1,0:T(8,128)S(1)} collective-permute-done((f32[4,8,1024]{2,1,0:T(8,128)S(1)}, f32[4,8,1024]{2,1,0:T(8,128)S(1)}, u32[]{:S(2)}, u32[]{:S(2)}) %collective-permute-start.25) | collective-permute-done | bytes 131104 | tf_op jit(solution)/shard_map/ppermute | solution.py:321
  165.2 0.7 collective-permute-done.24
  166.5 2.4 %collective-permute-start.28 = (f32[1,8,1024]{2,1,0:T(8,128)S(1)}, f32[1,8,1024]{2,1,0:T(8,128)S(1)}, u32[]{:S(2)}, u32[]{:S(2)}) collective-permute-start(f32[1,8,1024]{2,1,0:T(8,128)S(1)} %get-tuple-element.54), channel_id=1, source_target_pairs={{0,96},{32,64},{64,32},{96,0},{1,97},{33,65},{65,33},{97,1},{2,98}... | collective-permute-start | bytes 98312 | tf_op jit(solution)/shard_map/ppermute | solution.py:321
  169.9 1.3 collective-permute-done.28
  171.2 2.3 collective-permute-done.27
  173.6 6.0 %shard_map.39 = (bf16[32,8,1024]{2,1,0:T(8,128)(2,1)S(1)}, bf16[16,128,1024]{2,1,0:T(8,128)(2,1)S(1)}) custom-call(bf16[16,128,1024]{2,1,0:T(8,128)(2,1)} %bitcast.42, bf16[16,16,16,128]{3,2,1,0:T(8,128)(2,1)S(1)} %all-to-all-done.1.cells_ref.refs_1_), custom_call_target="tpu_custom_call" | custom-call | flops 1073741824 | bytes 7340032 | tf_op jit(solution)/shard_map/pallas_call | solution.py:238
  179.6 19.3 %all_to_all.20 = bf16[32,8,1024]{2,1,0:T(8,128)(2,1)S(1)} all-to-all(bf16[32,8,1024]{2,1,0:T(8,128)(2,1)S(1)} %get-tuple-element.40), channel_id=1, replica_groups=mesh['zh'=2,'x'=4,'c'=2,'y'=4,'zl'=4] {'c','y','x'}, dimensions={0} | all-to-all | bytes 1048576 | tf_op jit(solution)/shard_map/all_to_all | solution.py:346
  199.0 5.2 %collective-permute-start.29 = (f32[16,1024]{1,0:T(8,128)S(1)}, f32[16,1024]{1,0:T(8,128)S(1)}, u32[]{:S(2)}, u32[]{:S(2)}) collective-permute-start(f32[16,1024]{1,0:T(8,128)S(1)} %pad_maximum_fusion.1), channel_id=1, source_target_pairs={{0,128},{128,0},{1,129},{129,1},{2,130},{130,2},{3,131},{131,3},{4... | collective-permute-start | bytes 196616 | tf_op jit(solution)/shard_map/ppermute | solution.py:363
  204.1 1.9 collective-permute-done.29
  206.1 5.7 %collective-permute-start.32 = (f32[16,1024]{1,0:T(8,128)S(1)}, f32[16,1024]{1,0:T(8,128)S(1)}, u32[]{:S(2)}, u32[]{:S(2)}) collective-permute-start(f32[16,1024]{1,0:T(8,128)S(1)} %fusion.3), channel_id=1, source_target_pairs={{0,3},{1,2},{2,1},{3,0},{4,7},{5,6},{6,5},{7,4},{8,11},{9,10},{10,... | collective-permute-start | bytes 196616 | tf_op jit(solution)/shard_map/ppermute | solution.py:321
  212.2 1.4 collective-permute-done.32
  213.6 3.5 %collective-permute-done.31 = f32[16,1024]{1,0:T(8,128)S(1)} collective-permute-done((f32[16,1024]{1,0:T(8,128)S(1)}, f32[16,1024]{1,0:T(8,128)S(1)}, u32[]{:S(2)}, u32[]{:S(2)}) %collective-permute-start.31) | collective-permute-done | bytes 65568 | tf_op jit(solution)/shard_map/ppermute | solution.py:321
  217.2 14.2 %all_to_all.21.mine_ref = bf16[16,16,1024]{2,1,0:T(8,128)(2,1)S(1)} all-to-all(bf16[16,16,1024]{2,1,0:T(8,128)(2,1)S(1)} %broadcast_in_dim.7), channel_id=1, replica_groups=mesh['zh'=2,'x'=4,'c'=2,'y'=4,'zl'=4] {'y','x'}, dimensions={0} | all-to-all | bytes 1048576 | tf_op jit(solution)/shard_map/all_to_all | solution.py:368
  231.4 2.7 %collective-permute-start.33 = (bf16[16,16,1024]{2,1,0:T(8,128)(2,1)S(1)}, bf16[16,16,1024]{2,1,0:T(8,128)(2,1)S(1)}, u32[]{:S(2)}, u32[]{:S(2)}) collective-permute-start(bf16[16,16,1024]{2,1,0:T(8,128)(2,1)S(1)} %all_to_all.21.mine_ref), channel_id=1, source_target_pairs={{0,16},{16,0},{1,17},{17,1},{2,18},{18,2},{3,19},{19,3},{4,20},{20... | collective-permute-start | bytes 1572872 | tf_op jit(solution)/shard_map/ppermute | solution.py:363
  234.1 1.5 collective-permute-done.33.other_ref
  235.6 5.1 %shard_map.43 = f32[16,512,128]{2,1,0:T(8,128)} custom-call(s32[1]{0:T(128)} %bitcast.core_ref, bf16[16,16,1024]{2,1,0:T(8,128)(2,1)S(1)} %all_to_all.21.mine_ref, bf16[16,16,1024]{2,1,0:T(8,128)(2,1)S(1)} %collective-permute-done.33.other_ref, bf16[16,128,1024]{2,1,0:T(8,128)(2,1)S(1)} %get-tuple-element.41.ritz_ref, ...), custom_call_target="tpu_custom_call" | custom-call | flops 2147483648 | bytes 11534336 | tf_op jit(solution)/shard_map/pallas_call | solution.py:289
  (58 shorter events, 5.2 us)
Async XLA Ops:
  0.0 9.0 %collective-permute-start.2 = (f32[8,2,128]{2,1,0:T(2,128)}, f32[8,2,128]{2,1,0:T(2,128)S(1)}, u32[]{:S(2)}, u32[]{:S(2)}) collective-permute-start(f32[8,2,128]{2,1,0:T(2,128)} %param.4), channel_id=1, source_target_pairs={{0,128},{128,0},{1,129},{129,1},{2,130},{130,2},{3,131},{131,3},{4... | collective-permute-start | bytes 24584 | tf_op jit(solution)/shard_map/ppermute | solution.py:363
  10.4 21.0 %all-to-all-start = ((f32[8,2,8,2,128]{4,3,1,2,0:T(2,128)}), f32[8,2,8,2,128]{4,3,1,2,0:T(2,128)S(1)}, u32[]{:S(2)}, u32[]{:S(2)}) async-start(f32[8,2,8,2,128]{4,3,1,2,0:T(2,128)} %broadcast_in_dim.6), calls=%async_computation | async-start | bytes 262144 | tf_op jit(solution)/shard_map/all_to_all | solution.py:368
  20.2 42.0 %collective-permute-start.5 = (bf16[4,32,16,128]{3,2,1,0:T(8,128)(2,1)}, bf16[4,32,16,128]{3,2,1,0:T(8,128)(2,1)S(1)}, u32[]{:S(2)}, u32[]{:S(2)}) collective-permute-start(bf16[4,32,16,128]{3,2,1,0:T(8,128)(2,1)} %get-tuple-element.27), channel_id=1, source_target_pairs={{0,1},{1,2},{2,3},{3,4},{4,5},{5,6},{6,7},{7,8},{8,9},{9,10},{10,1... | collective-permute-start | bytes 1572872 | tf_op jit(solution)/shard_map/ppermute | solution.py:373
  22.9 39.3 %collective-permute-start.6 = (bf16[4,32,16,128]{3,2,1,0:T(8,128)(2,1)S(1)}, bf16[4,32,16,128]{3,2,1,0:T(8,128)(2,1)S(1)}, u32[]{:S(2)}, u32[]{:S(2)}) collective-permute-start(bf16[4,32,16,128]{3,2,1,0:T(8,128)(2,1)S(1)} %get-tuple-element.28), channel_id=1, source_target_pairs={{1,0},{2,1},{3,2},{4,3},{5,4},{6,5},{7,6},{8,7},{9,8},{10,9},{11,1... | collective-permute-start | bytes 1572872 | tf_op jit(solution)/shard_map/ppermute | solution.py:374
  27.3 58.8 %collective-permute-start = (bf16[4,32,16,128]{3,2,1,0:T(8,128)(2,1)S(1)}, bf16[4,32,16,128]{3,2,1,0:T(8,128)(2,1)S(1)}, u32[]{:S(2)}, u32[]{:S(2)}) collective-permute-start(bf16[4,32,16,128]{3,2,1,0:T(8,128)(2,1)S(1)} %get-tuple-element.24), channel_id=1, source_target_pairs={{0,1},{1,2},{2,3},{3,4},{4,5},{5,6},{6,7},{7,8},{8,9},{9,10},{10,1... | collective-permute-start | bytes 1572872 | tf_op jit(solution)/shard_map/ppermute | solution.py:373
  31.5 30.6 %collective-permute-start.4 = (f32[4,32,128]{2,1,0:T(8,128)S(1)}, f32[4,32,128]{2,1,0:T(8,128)S(1)}, u32[]{:S(2)}, u32[]{:S(2)}) collective-permute-start(f32[4,32,128]{2,1,0:T(8,128)S(1)} %bitcast.45), channel_id=1, source_target_pairs={{1,0},{2,1},{3,2},{4,3},{5,4},{6,5},{7,6},{8,7},{9,8},{10,9},{11,1... | collective-permute-start | bytes 196616 | tf_op jit(solution)/shard_map/ppermute | solution.py:374
  32.8 29.3 %collective-permute-start.3 = (f32[4,32,128]{2,1,0:T(8,128)S(1)}, f32[4,32,128]{2,1,0:T(8,128)S(1)}, u32[]{:S(2)}, u32[]{:S(2)}) collective-permute-start(f32[4,32,128]{2,1,0:T(8,128)S(1)} %bitcast.44), channel_id=1, source_target_pairs={{0,1},{1,2},{2,3},{3,4},{4,5},{5,6},{6,7},{7,8},{8,9},{9,10},{10,1... | collective-permute-start | bytes 196616 | tf_op jit(solution)/shard_map/ppermute | solution.py:373
  76.0 20.6 %collective-permute-start.14 = (bf16[8,16,16,128]{3,2,1,0:T(8,128)(2,1)S(1)}, bf16[8,16,16,128]{3,2,1,0:T(8,128)(2,1)S(1)}, u32[]{:S(2)}, u32[]{:S(2)}) collective-permute-start(bf16[8,16,16,128]{3,2,1,0:T(8,128)(2,1)S(1)} %get-tuple-element.37), channel_id=1, source_target_pairs={{0,128},{128,0},{1,129},{129,1},{2,130},{130,2},{3,131},{131,3},{4... | collective-permute-start | bytes 1572872 | tf_op jit(solution)/shard_map/ppermute | solution.py:363
  81.7 35.8 %collective-permute-start.1 = (bf16[4,32,16,128]{3,2,1,0:T(8,128)(2,1)S(1)}, bf16[4,32,16,128]{3,2,1,0:T(8,128)(2,1)S(1)}, u32[]{:S(2)}, u32[]{:S(2)}) collective-permute-start(bf16[4,32,16,128]{3,2,1,0:T(8,128)(2,1)S(1)} %get-tuple-element.25), channel_id=1, source_target_pairs={{1,0},{2,1},{3,2},{4,3},{5,4},{6,5},{7,6},{8,7},{9,8},{10,9},{11,1... | collective-permute-start | bytes 1572872 | tf_op jit(solution)/shard_map/ppermute | solution.py:374
  83.0 37.4 %collective-permute-start.7 = (bf16[16,16,128]{2,1,0:T(8,128)(2,1)S(1)}, bf16[16,16,128]{2,1,0:T(8,128)(2,1)S(1)}, u32[]{:S(2)}, u32[]{:S(2)}) collective-permute-start(bf16[16,16,128]{2,1,0:T(8,128)(2,1)S(1)} %get-tuple-element.30), channel_id=1, source_target_pairs={{0,16},{16,0},{32,48},{48,32},{64,80},{80,64},{96,112},{112,96},{1... | collective-permute-start | bytes 196616 | tf_op jit(solution)/shard_map/ppermute | solution.py:334
  84.3 37.0 %collective-permute-start.8 = (bf16[16,16,128]{2,1,0:T(8,128)(2,1)S(1)}, bf16[16,16,128]{2,1,0:T(8,128)(2,1)S(1)}, u32[]{:S(2)}, u32[]{:S(2)}) collective-permute-start(bf16[16,16,128]{2,1,0:T(8,128)(2,1)S(1)} %get-tuple-element.31), channel_id=1, source_target_pairs={{0,32},{16,48},{32,0},{48,16},{64,96},{80,112},{96,64},{112,80},{1... | collective-permute-start | bytes 196616 | tf_op jit(solution)/shard_map/ppermute | solution.py:334
  86.0 37.3 %collective-permute-start.9 = (bf16[16,16,128]{2,1,0:T(8,128)(2,1)S(1)}, bf16[16,16,128]{2,1,0:T(8,128)(2,1)S(1)}, u32[]{:S(2)}, u32[]{:S(2)}) collective-permute-start(bf16[16,16,128]{2,1,0:T(8,128)(2,1)S(1)} %get-tuple-element.32), channel_id=1, source_target_pairs={{0,48},{16,32},{32,16},{48,0},{64,112},{80,96},{96,80},{112,64},{1... | collective-permute-start | bytes 196616 | tf_op jit(solution)/shard_map/ppermute | solution.py:334
  96.6 27.7 %collective-permute-start.10 = (bf16[16,16,128]{2,1,0:T(8,128)(2,1)S(1)}, bf16[16,16,128]{2,1,0:T(8,128)(2,1)S(1)}, u32[]{:S(2)}, u32[]{:S(2)}) collective-permute-start(bf16[16,16,128]{2,1,0:T(8,128)(2,1)S(1)} %get-tuple-element.33), channel_id=1, source_target_pairs={{0,64},{16,80},{32,96},{48,112},{64,0},{80,16},{96,32},{112,48},{1... | collective-permute-start | bytes 196616 | tf_op jit(solution)/shard_map/ppermute | solution.py:334
  117.6 8.5 %collective-permute-start.11 = (bf16[16,16,128]{2,1,0:T(8,128)(2,1)S(1)}, bf16[16,16,128]{2,1,0:T(8,128)(2,1)S(1)}, u32[]{:S(2)}, u32[]{:S(2)}) collective-permute-start(bf16[16,16,128]{2,1,0:T(8,128)(2,1)S(1)} %get-tuple-element.34), channel_id=1, source_target_pairs={{0,80},{16,64},{32,112},{48,96},{64,16},{80,0},{96,48},{112,32},{1... | collective-permute-start | bytes 196616 | tf_op jit(solution)/shard_map/ppermute | solution.py:334
  120.4 5.8 %collective-permute-start.12 = (bf16[16,16,128]{2,1,0:T(8,128)(2,1)S(1)}, bf16[16,16,128]{2,1,0:T(8,128)(2,1)S(1)}, u32[]{:S(2)}, u32[]{:S(2)}) collective-permute-start(bf16[16,16,128]{2,1,0:T(8,128)(2,1)S(1)} %get-tuple-element.35), channel_id=1, source_target_pairs={{0,96},{16,112},{32,64},{48,80},{64,32},{80,48},{96,0},{112,16},{1... | collective-permute-start | bytes 196616 | tf_op jit(solution)/shard_map/ppermute | solution.py:334
  121.3 8.2 %collective-permute-start.13 = (bf16[16,16,128]{2,1,0:T(8,128)(2,1)S(1)}, bf16[16,16,128]{2,1,0:T(8,128)(2,1)S(1)}, u32[]{:S(2)}, u32[]{:S(2)}) collective-permute-start(bf16[16,16,128]{2,1,0:T(8,128)(2,1)S(1)} %get-tuple-element.36), channel_id=1, source_target_pairs={{0,112},{16,96},{32,80},{48,64},{64,48},{80,32},{96,16},{112,0},{1... | collective-permute-start | bytes 196616 | tf_op jit(solution)/shard_map/ppermute | solution.py:334
  123.3 6.2 %collective-permute-start.21 = (bf16[16,16,128]{2,1,0:T(8,128)(2,1)S(1)}, bf16[16,16,128]{2,1,0:T(8,128)(2,1)S(1)}, u32[]{:S(2)}, u32[]{:S(2)}) collective-permute-start(bf16[16,16,128]{2,1,0:T(8,128)(2,1)S(1)} %get-tuple-element.46), channel_id=1, source_target_pairs={{0,112},{16,96},{32,80},{48,64},{64,48},{80,32},{96,16},{112,0},{1... | collective-permute-start | bytes 196616 | tf_op jit(solution)/shard_map/ppermute | solution.py:334
  124.3 6.8 %collective-permute-start.20 = (bf16[16,16,128]{2,1,0:T(8,128)(2,1)S(1)}, bf16[16,16,128]{2,1,0:T(8,128)(2,1)S(1)}, u32[]{:S(2)}, u32[]{:S(2)}) collective-permute-start(bf16[16,16,128]{2,1,0:T(8,128)(2,1)S(1)} %get-tuple-element.47), channel_id=1, source_target_pairs={{0,96},{16,112},{32,64},{48,80},{64,32},{80,48},{96,0},{112,16},{1... | collective-permute-start | bytes 196616 | tf_op jit(solution)/shard_map/ppermute | solution.py:334
  126.1 22.5 %collective-permute-start.19 = (bf16[16,16,128]{2,1,0:T(8,128)(2,1)S(1)}, bf16[16,16,128]{2,1,0:T(8,128)(2,1)S(1)}, u32[]{:S(2)}, u32[]{:S(2)}) collective-permute-start(bf16[16,16,128]{2,1,0:T(8,128)(2,1)S(1)} %get-tuple-element.48), channel_id=1, source_target_pairs={{0,80},{16,64},{32,112},{48,96},{64,16},{80,0},{96,48},{112,32},{1... | collective-permute-start | bytes 196616 | tf_op jit(solution)/shard_map/ppermute | solution.py:334
  126.2 22.3 %collective-permute-start.18 = (bf16[16,16,128]{2,1,0:T(8,128)(2,1)S(1)}, bf16[16,16,128]{2,1,0:T(8,128)(2,1)S(1)}, u32[]{:S(2)}, u32[]{:S(2)}) collective-permute-start(bf16[16,16,128]{2,1,0:T(8,128)(2,1)S(1)} %get-tuple-element.49), channel_id=1, source_target_pairs={{0,64},{16,80},{32,96},{48,112},{64,0},{80,16},{96,32},{112,48},{1... | collective-permute-start | bytes 196616 | tf_op jit(solution)/shard_map/ppermute | solution.py:334
  129.5 19.1 %collective-permute-start.17 = (bf16[16,16,128]{2,1,0:T(8,128)(2,1)S(1)}, bf16[16,16,128]{2,1,0:T(8,128)(2,1)S(1)}, u32[]{:S(2)}, u32[]{:S(2)}) collective-permute-start(bf16[16,16,128]{2,1,0:T(8,128)(2,1)S(1)} %get-tuple-element.50), channel_id=1, source_target_pairs={{0,48},{16,32},{32,16},{48,0},{64,112},{80,96},{96,80},{112,64},{1... | collective-permute-start | bytes 196616 | tf_op jit(solution)/shard_map/ppermute | solution.py:334
  129.5 19.1 %collective-permute-start.16 = (bf16[16,16,128]{2,1,0:T(8,128)(2,1)S(1)}, bf16[16,16,128]{2,1,0:T(8,128)(2,1)S(1)}, u32[]{:S(2)}, u32[]{:S(2)}) collective-permute-start(bf16[16,16,128]{2,1,0:T(8,128)(2,1)S(1)} %get-tuple-element.51), channel_id=1, source_target_pairs={{0,32},{16,48},{32,0},{48,16},{64,96},{80,112},{96,64},{112,80},{1... | collective-permute-start | bytes 196616 | tf_op jit(solution)/shard_map/ppermute | solution.py:334
  131.1 17.5 %collective-permute-start.15 = (bf16[16,16,128]{2,1,0:T(8,128)(2,1)S(1)}, bf16[16,16,128]{2,1,0:T(8,128)(2,1)S(1)}, u32[]{:S(2)}, u32[]{:S(2)}) collective-permute-start(bf16[16,16,128]{2,1,0:T(8,128)(2,1)S(1)} %get-tuple-element.52), channel_id=1, source_target_pairs={{0,16},{16,0},{32,48},{48,32},{64,80},{80,64},{96,112},{112,96},{1... | collective-permute-start | bytes 196616 | tf_op jit(solution)/shard_map/ppermute | solution.py:334
  145.0 28.6 %all-to-all-start.1 = ((bf16[16,16,16,128]{3,2,1,0:T(8,128)(2,1)}), bf16[16,16,16,128]{3,2,1,0:T(8,128)(2,1)S(1)}, u32[]{:S(2)}, u32[]{:S(2)}) async-start(bf16[16,16,16,128]{3,2,1,0:T(8,128)(2,1)} %shard_map.38), calls=%async_computation.1 | async-start | bytes 2097152 | tf_op jit(solution)/shard_map/all_to_all | solution.py:408
  155.0 2.0 collective-permute-start.22
  157.1 8.0 %collective-permute-start.25 = (f32[4,8,1024]{2,1,0:T(8,128)S(1)}, f32[4,8,1024]{2,1,0:T(8,128)S(1)}, u32[]{:S(2)}, u32[]{:S(2)}) collective-permute-start(f32[4,8,1024]{2,1,0:T(8,128)S(1)} %get-tuple-element.43), channel_id=1, source_target_pairs={{0,12},{4,8},{8,4},{12,0},{1,13},{5,9},{9,5},{13,1},{2,14},{6,10},... | collective-permute-start | bytes 393224 | tf_op jit(solution)/shard_map/ppermute | solution.py:321
  159.7 6.1 %collective-permute-start.24 = (f32[4,8,1024]{2,1,0:T(8,128)S(1)}, f32[4,8,1024]{2,1,0:T(8,128)S(1)}, u32[]{:S(2)}, u32[]{:S(2)}) collective-permute-start(f32[4,8,1024]{2,1,0:T(8,128)S(1)} %get-tuple-element.44), channel_id=1, source_target_pairs={{0,8},{4,12},{8,0},{12,4},{1,9},{5,13},{9,1},{13,5},{2,10},{6,14},... | collective-permute-start | bytes 393224 | tf_op jit(solution)/shard_map/ppermute | solution.py:321
  160.2 6.3 %collective-permute-start.23 = (f32[4,8,1024]{2,1,0:T(8,128)S(1)}, f32[4,8,1024]{2,1,0:T(8,128)S(1)}, u32[]{:S(2)}, u32[]{:S(2)}) collective-permute-start(f32[4,8,1024]{2,1,0:T(8,128)S(1)} %get-tuple-element.45), channel_id=1, source_target_pairs={{0,4},{4,0},{8,12},{12,8},{1,5},{5,1},{9,13},{13,9},{2,6},{6,2},{1... | collective-permute-start | bytes 393224 | tf_op jit(solution)/shard_map/ppermute | solution.py:321
  166.5 4.7 %collective-permute-start.28 = (f32[1,8,1024]{2,1,0:T(8,128)S(1)}, f32[1,8,1024]{2,1,0:T(8,128)S(1)}, u32[]{:S(2)}, u32[]{:S(2)}) collective-permute-start(f32[1,8,1024]{2,1,0:T(8,128)S(1)} %get-tuple-element.54), channel_id=1, source_target_pairs={{0,96},{32,64},{64,32},{96,0},{1,97},{33,65},{65,33},{97,1},{2,98}... | collective-permute-start | bytes 98312 | tf_op jit(solution)/shard_map/ppermute | solution.py:321
  169.0 4.6 %collective-permute-start.27 = (f32[1,8,1024]{2,1,0:T(8,128)S(1)}, f32[1,8,1024]{2,1,0:T(8,128)S(1)}, u32[]{:S(2)}, u32[]{:S(2)}) collective-permute-start(f32[1,8,1024]{2,1,0:T(8,128)S(1)} %get-tuple-element.55), channel_id=1, source_target_pairs={{0,64},{32,96},{64,0},{96,32},{1,65},{33,97},{65,1},{97,33},{2,66}... | collective-permute-start | bytes 98312 | tf_op jit(solution)/shard_map/ppermute | solution.py:321
  169.6 4.0 %collective-permute-start.26 = (f32[1,8,1024]{2,1,0:T(8,128)S(1)}, f32[1,8,1024]{2,1,0:T(8,128)S(1)}, u32[]{:S(2)}, u32[]{:S(2)}) collective-permute-start(f32[1,8,1024]{2,1,0:T(8,128)S(1)} %get-tuple-element.56), channel_id=1, source_target_pairs={{0,32},{32,0},{64,96},{96,64},{1,33},{33,1},{65,97},{97,65},{2,34}... | collective-permute-start | bytes 98312 | tf_op jit(solution)/shard_map/ppermute | solution.py:321
  199.0 7.1 %collective-permute-start.29 = (f32[16,1024]{1,0:T(8,128)S(1)}, f32[16,1024]{1,0:T(8,128)S(1)}, u32[]{:S(2)}, u32[]{:S(2)}) collective-permute-start(f32[16,1024]{1,0:T(8,128)S(1)} %pad_maximum_fusion.1), channel_id=1, source_target_pairs={{0,128},{128,0},{1,129},{129,1},{2,130},{130,2},{3,131},{131,3},{4... | collective-permute-start | bytes 196616 | tf_op jit(solution)/shard_map/ppermute | solution.py:363
  206.1 7.5 %collective-permute-start.32 = (f32[16,1024]{1,0:T(8,128)S(1)}, f32[16,1024]{1,0:T(8,128)S(1)}, u32[]{:S(2)}, u32[]{:S(2)}) collective-permute-start(f32[16,1024]{1,0:T(8,128)S(1)} %fusion.3), channel_id=1, source_target_pairs={{0,3},{1,2},{2,1},{3,0},{4,7},{5,6},{6,5},{7,4},{8,11},{9,10},{10,... | collective-permute-start | bytes 196616 | tf_op jit(solution)/shard_map/ppermute | solution.py:321
  211.8 5.3 %collective-permute-start.31 = (f32[16,1024]{1,0:T(8,128)S(1)}, f32[16,1024]{1,0:T(8,128)S(1)}, u32[]{:S(2)}, u32[]{:S(2)}) collective-permute-start(f32[16,1024]{1,0:T(8,128)S(1)} %fusion.3), channel_id=1, source_target_pairs={{0,2},{1,3},{2,0},{3,1},{4,6},{5,7},{6,4},{7,5},{8,10},{9,11},{10,... | collective-permute-start | bytes 196616 | tf_op jit(solution)/shard_map/ppermute | solution.py:321
  211.8 5.3 %collective-permute-start.30 = (f32[16,1024]{1,0:T(8,128)S(1)}, f32[16,1024]{1,0:T(8,128)S(1)}, u32[]{:S(2)}, u32[]{:S(2)}) collective-permute-start(f32[16,1024]{1,0:T(8,128)S(1)} %fusion.3), channel_id=1, source_target_pairs={{0,1},{1,0},{2,3},{3,2},{4,5},{5,4},{6,7},{7,6},{8,9},{9,8},{10,11... | collective-permute-start | bytes 196616 | tf_op jit(solution)/shard_map/ppermute | solution.py:321
  231.4 4.2 %collective-permute-start.33 = (bf16[16,16,1024]{2,1,0:T(8,128)(2,1)S(1)}, bf16[16,16,1024]{2,1,0:T(8,128)(2,1)S(1)}, u32[]{:S(2)}, u32[]{:S(2)}) collective-permute-start(bf16[16,16,1024]{2,1,0:T(8,128)(2,1)S(1)} %all_to_all.21.mine_ref), channel_id=1, source_target_pairs={{0,16},{16,0},{1,17},{17,1},{2,18},{18,2},{3,19},{19,3},{4,20},{20... | collective-permute-start | bytes 1572872 | tf_op jit(solution)/shard_map/ppermute | solution.py:363

commit v9 on v7

--- a/solution.py
+++ b/solution.py
@@ -17,6 +17,7 @@
 HALO = 4
 GROUP = 16
 CHUNKS = 2
+STEP = 4
 
 
 def spread_kernel(first_ref, second_ref, low_ref, high_ref):
@@ -155,14 +156,14 @@
     def _():
         total[...] = jnp.zeros_like(total)
 
-    pair = jnp.concatenate(
-        [cells_ref[:, 0].reshape(-1, lanes), cells_ref[:, 1].reshape(-1, lanes)], axis=1
+    part = jnp.concatenate(
+        [cells_ref[:, k].reshape(-1, lanes) for k in range(STEP)], axis=1
     )
     total[...] += jnp.dot(
-        pair, ritz_ref[...].reshape(2 * lanes, -1), preferred_element_type=f32
+        part, ritz_ref[...].reshape(STEP * lanes, -1), preferred_element_type=f32
     )
     for kept_ref in kept_refs:
-        kept_ref[pl.ds(2 * step, 2)] = ritz_ref[...]
+        kept_ref[pl.ds(STEP * step, STEP)] = ritz_ref[...]
 
     @pl.when(step == pl.num_programs(0) - 1)
     def _():
@@ -186,11 +187,11 @@
     return pl.pallas_call(
         project_kernel,
         out_shape=out_shape,
-        grid=(rows // 2,),
+        grid=(rows // STEP,),
         in_specs=[
             pl.BlockSpec(memory_space=pltpu.SMEM),
-            pl.BlockSpec((2, lanes, kept), lambda r: (r, 0, 0)),
-            pl.BlockSpec((blocks, 2, vectors, lanes), lambda r: (0, r, 0, 0)),
+            pl.BlockSpec((STEP, lanes, kept), lambda r: (r, 0, 0)),
+            pl.BlockSpec((blocks, STEP, vectors, lanes), lambda r: (0, r, 0, 0)),
         ],
         out_specs=out_specs,
         scratch_shapes=[pltpu.VMEM((count, kept), f32)],

time: 236 us -> 234 us (level)
  Pallas kernels: 49.7 us -> 45.8 us
  waiting for transfers between devices: 85.1 us -> 88.2 us
    pallas_call x2, Pallas kernels: 12 us -> 8.11 us  [projected(): pl.pallas_call(project_kernel, out_shape=out_shape, grid=(rows // STEP,),...]
  transfers between devices with their start and end apart: 22 -> 22, of which waited for: 13 -> 13; matrix products, arithmetic and copies ran while one was open for 0% -> 0% of each run, Pallas kernels for 13% -> 12%
where the time goes in v9:
time: 234 us; the launch traced here: 233 us
  waiting for transfers between devices  88.2 us (38%)
  starting transfers between devices  61.6 us (26%)
  Pallas kernels  45.8 us (20%)
  blocking collectives  35.3 us (15%)
    ppermute x3, waiting for transfers between devices, swap_ends(): from_above = lax.ppermute(low, DOM, [(i + 1, i) for i in range(count - 1)])  32.9 us
    ppermute x3, waiting for transfers between devices, swap_ends(): from_below = lax.ppermute(high, DOM, [(i, i + 1) for i in range(count - 1)])  27.8 us
    pallas_call x2, Pallas kernels, filtered(): pl.pallas_call(filter_kernel, out_shape=jax.ShapeDtypeStruct((rows // 2,...  26.5 us
    all_to_all x2, starting transfers between devices, pipeline(): held.append(lax.all_to_all(blocks, VEC, 0, 0, tiled=True))  20.9 us
    all_to_all x1, blocking collectives, near_sum(): blocks = lax.all_to_all(partial, NEAR, 0, 0, tiled=True)  18.9 us
    all_to_all x1, blocking collectives, from_everyone(): return lax.all_to_all(copies, axis, split_axis=0, concat_axis=0, tiled=True)  16.4 us
    ppermute x10, starting transfers between devices, traded(): lax.ppermute(blocks[k], axis, [(i, i ^ k) for i in range(count)])  11.4 us
    ppermute x10, waiting for transfers between devices, traded(): lax.ppermute(blocks[k], axis, [(i, i ^ k) for i in range(count)])  10.9 us
  transfers between devices with their start and end apart: 22, of which 13 were waited for; matrix products, arithmetic and copies ran while one was open for 0% of the time, Pallas kernels for 12%

profile of v9, /device:TPU:1, one launch (start us, length us, event | category | flops | bytes accessed | tf_op | source)
XLA Modules:
  0.0 233.2 jit_solution(16898372458374109985)
XLA Ops:
  0.0 7.7 %collective-permute-start.2 = (f32[8,2,128]{2,1,0:T(2,128)}, f32[8,2,128]{2,1,0:T(2,128)S(1)}, u32[]{:S(2)}, u32[]{:S(2)}) collective-permute-start(f32[8,2,128]{2,1,0:T(2,128)} %param.4), channel_id=1, source_target_pairs={{0,128},{128,0},{1,129},{129,1},{2,130},{130,2},{3,131},{131,3},{4... | collective-permute-start | bytes 24584 | tf_op jit(solution)/shard_map/ppermute | solution.py:296
  7.7 1.2 collective-permute-done.2
  9.0 0.7 select_bitcast_fusion.1
  9.7 0.7 broadcast_in_dim.6
  10.4 5.8 %all-to-all-start = ((f32[8,2,8,2,128]{4,3,1,2,0:T(2,128)}), f32[8,2,8,2,128]{4,3,1,2,0:T(2,128)S(1)}, u32[]{:S(2)}, u32[]{:S(2)}) async-start(f32[8,2,8,2,128]{4,3,1,2,0:T(2,128)} %broadcast_in_dim.6), calls=%async_computation | async-start | bytes 262144 | tf_op jit(solution)/shard_map/all_to_all | solution.py:301
  16.2 3.0 %shard_map.40 = (bf16[4,32,16,128]{3,2,1,0:T(8,128)(2,1)S(1)}, bf16[4,32,16,128]{3,2,1,0:T(8,128)(2,1)S(1)}) custom-call(f32[32,256,128]{2,1,0:T(8,128)} %bitcast.18, f32[32,256,128]{2,1,0:T(8,128)} %bitcast.19), custom_call_target="tpu_custom_call" | custom-call | flops 524288 | bytes 3145728 | tf_op jit(solution)/shard_map/pallas_call | solution.py:35
  19.3 2.7 %collective-permute-start.5 = (bf16[4,32,16,128]{3,2,1,0:T(8,128)(2,1)S(1)}, bf16[4,32,16,128]{3,2,1,0:T(8,128)(2,1)S(1)}, u32[]{:S(2)}, u32[]{:S(2)}) collective-permute-start(bf16[4,32,16,128]{3,2,1,0:T(8,128)(2,1)S(1)} %get-tuple-element.16), channel_id=1, source_target_pairs={{0,1},{1,2},{2,3},{3,4},{4,5},{5,6},{6,7},{7,8},{8,9},{9,10},{10,1... | collective-permute-start | bytes 1572872 | tf_op jit(solution)/shard_map/ppermute | solution.py:306
  22.0 1.3 collective-permute-start.6
  23.3 0.1 add_bitcast_fusion
  23.5 1.3 collective-permute-start.4
  24.8 4.6 %collective-permute-start.3 = (f32[4,32,128]{2,1,0:T(8,128)S(1)}, f32[4,32,128]{2,1,0:T(8,128)S(1)}, u32[]{:S(2)}, u32[]{:S(2)}) collective-permute-start(f32[4,32,128]{2,1,0:T(8,128)S(1)} %bitcast.27), channel_id=1, source_target_pairs={{0,1},{1,2},{2,3},{3,4},{4,5},{5,6},{6,7},{7,8},{8,9},{9,10},{10,1... | collective-permute-start | bytes 196616 | tf_op jit(solution)/shard_map/ppermute | solution.py:306
  29.4 0.1 add_convert_fusion.1.ends_ref
  29.5 20.7 %collective-permute-done.4 = f32[4,32,128]{2,1,0:T(8,128)S(1)} collective-permute-done((f32[4,32,128]{2,1,0:T(8,128)S(1)}, f32[4,32,128]{2,1,0:T(8,128)S(1)}, u32[]{:S(2)}, u32[]{:S(2)}) %collective-permute-start.4) | collective-permute-done | bytes 65568 | tf_op jit(solution)/shard_map/ppermute | solution.py:307
  50.3 13.3 %shard_map.41 = bf16[16,16,16,128]{3,2,1,0:T(8,128)(2,1)} custom-call(s32[2]{0:T(128)S(1)} %add_convert_fusion.1.ends_ref, f32[32,256,128]{2,1,0:T(8,128)} %bitcast.20, bf16[4,32,16,128]{3,2,1,0:T(8,128)(2,1)S(1)} %collective-permute-done.5.low_ref, bf16[4,32,16,128]{3,2,1,0:T(8,128)(2,1)S(1)} %collective-permute-done.6.high_ref, ...), custom_call_target="tpu_custom_call" | custom-call | flops 34603008 | bytes 5242880 | tf_op jit(solution)/shard_map/pallas_call | solution.py:130
  63.6 11.1 %all-to-all-start.2 = ((bf16[16,16,16,128]{3,2,1,0:T(8,128)(2,1)}), bf16[16,16,16,128]{3,2,1,0:T(8,128)(2,1)S(1)}, u32[]{:S(2)}, u32[]{:S(2)}) async-start(bf16[16,16,16,128]{3,2,1,0:T(8,128)(2,1)} %shard_map.41), calls=%async_computation.2 | async-start | bytes 2097152 | tf_op jit(solution)/shard_map/all_to_all | solution.py:336
  74.6 3.1 %shard_map.37 = (bf16[4,32,16,128]{3,2,1,0:T(8,128)(2,1)S(1)}, bf16[4,32,16,128]{3,2,1,0:T(8,128)(2,1)S(1)}) custom-call(f32[32,256,128]{2,1,0:T(8,128)} %bitcast.21, f32[32,256,128]{2,1,0:T(8,128)} %bitcast.22), custom_call_target="tpu_custom_call" | custom-call | flops 524288 | bytes 3145728 | tf_op jit(solution)/shard_map/pallas_call | solution.py:35
  77.7 2.3 collective-permute-start
  80.0 1.3 collective-permute-start.1
  81.3 27.7 %collective-permute-done.low_ref = bf16[4,32,16,128]{3,2,1,0:T(8,128)(2,1)S(1)} collective-permute-done((bf16[4,32,16,128]{3,2,1,0:T(8,128)(2,1)S(1)}, bf16[4,32,16,128]{3,2,1,0:T(8,128)(2,1)S(1)}, u32[]{:S(2)}, u32[]{:S(2)}) %collective-permute-start) | collective-permute-done | bytes 524320 | tf_op jit(solution)/shard_map/ppermute | solution.py:306
  109.0 12.1 %collective-permute-done.1.high_ref = bf16[4,32,16,128]{3,2,1,0:T(8,128)(2,1)S(1)} collective-permute-done((bf16[4,32,16,128]{3,2,1,0:T(8,128)(2,1)S(1)}, bf16[4,32,16,128]{3,2,1,0:T(8,128)(2,1)S(1)}, u32[]{:S(2)}, u32[]{:S(2)}) %collective-permute-start.1) | collective-permute-done | bytes 524320 | tf_op jit(solution)/shard_map/ppermute | solution.py:307
  121.2 13.2 %shard_map.38 = bf16[16,16,16,128]{3,2,1,0:T(8,128)(2,1)} custom-call(s32[2]{0:T(128)S(1)} %add_convert_fusion.1.ends_ref, f32[32,256,128]{2,1,0:T(8,128)} %bitcast.23, bf16[4,32,16,128]{3,2,1,0:T(8,128)(2,1)S(1)} %collective-permute-done.low_ref, bf16[4,32,16,128]{3,2,1,0:T(8,128)(2,1)S(1)} %collective-permute-done.1.high_ref, ...), custom_call_target="tpu_custom_call" | custom-call | flops 34603008 | bytes 5242880 | tf_op jit(solution)/shard_map/pallas_call | solution.py:130
  134.4 9.8 %all-to-all-start.1 = ((bf16[16,16,16,128]{3,2,1,0:T(8,128)(2,1)}), bf16[16,16,16,128]{3,2,1,0:T(8,128)(2,1)S(1)}, u32[]{:S(2)}, u32[]{:S(2)}) async-start(bf16[16,16,16,128]{3,2,1,0:T(8,128)(2,1)} %shard_map.38), calls=%async_computation.1 | async-start | bytes 2097152 | tf_op jit(solution)/shard_map/all_to_all | solution.py:336
  144.2 4.1 %shard_map.42 = f32[32,8,1024]{2,1,0:T(8,128)S(1)} custom-call(s32[1]{0:T(128)} %bitcast.1.place_ref, bf16[16,128,1024]{2,1,0:T(8,128)(2,1)} %bitcast.24, bf16[16,16,16,128]{3,2,1,0:T(8,128)(2,1)S(1)} %all-to-all-done.2.cells_ref.refs_0_), custom_call_target="tpu_custom_call" | custom-call | flops 1073741824 | bytes 7340032 | tf_op jit(solution)/shard_map/pallas_call | solution.py:187
  148.3 0.2 collective-permute-start.7
  148.5 1.8 collective-permute-done.7
  150.4 0.1 collective-permute-start.10
  150.5 3.0 %collective-permute-start.9 = (f32[4,8,1024]{2,1,0:T(8,128)S(1)}, f32[4,8,1024]{2,1,0:T(8,128)S(1)}, u32[]{:S(2)}, u32[]{:S(2)}) collective-permute-start(f32[4,8,1024]{2,1,0:T(8,128)S(1)} %get-tuple-element.22), channel_id=1, source_target_pairs={{0,8},{4,12},{8,0},{12,4},{1,9},{5,13},{9,1},{13,5},{2,10},{6,14},... | collective-permute-start | bytes 393224 | tf_op jit(solution)/shard_map/ppermute | solution.py:271
  153.5 0.3 collective-permute-start.8
  153.8 5.8 %collective-permute-done.10 = f32[4,8,1024]{2,1,0:T(8,128)S(1)} collective-permute-done((f32[4,8,1024]{2,1,0:T(8,128)S(1)}, f32[4,8,1024]{2,1,0:T(8,128)S(1)}, u32[]{:S(2)}, u32[]{:S(2)}) %collective-permute-start.10) | collective-permute-done | bytes 131104 | tf_op jit(solution)/shard_map/ppermute | solution.py:271
  159.6 0.2 collective-permute-done.8
  159.8 2.5 %collective-permute-start.13 = (f32[1,8,1024]{2,1,0:T(8,128)S(1)}, f32[1,8,1024]{2,1,0:T(8,128)S(1)}, u32[]{:S(2)}, u32[]{:S(2)}) collective-permute-start(f32[1,8,1024]{2,1,0:T(8,128)S(1)} %get-tuple-element.24), channel_id=1, source_target_pairs={{0,96},{32,64},{64,32},{96,0},{1,97},{33,65},{65,33},{97,1},{2,98}... | collective-permute-start | bytes 98312 | tf_op jit(solution)/shard_map/ppermute | solution.py:271
  162.3 0.6 collective-permute-start.12
  162.9 0.3 collective-permute-start.11
  163.2 6.9 %all-to-all-done.1.cells_ref.refs_1_ = bf16[16,16,16,128]{3,2,1,0:T(8,128)(2,1)S(1)} async-done(((bf16[16,16,16,128]{3,2,1,0:T(8,128)(2,1)}), bf16[16,16,16,128]{3,2,1,0:T(8,128)(2,1)S(1)}, u32[]{:S(2)}, u32[]{:S(2)}) %all-to-all-start.1) | async-done | bytes 1048608 | tf_op jit(solution)/shard_map/all_to_all | solution.py:336
  170.0 4.1 %shard_map.39 = (bf16[32,8,1024]{2,1,0:T(8,128)(2,1)S(1)}, bf16[16,128,1024]{2,1,0:T(8,128)(2,1)S(1)}) custom-call(s32[1]{0:T(128)} %bitcast.1.place_ref, bf16[16,128,1024]{2,1,0:T(8,128)(2,1)} %bitcast.25, bf16[16,16,16,128]{3,2,1,0:T(8,128)(2,1)S(1)} %all-to-all-done.1.cells_ref.refs_1_), custom_call_target="tpu_custom_call" | custom-call | flops 1073741824 | bytes 7340032 | tf_op jit(solution)/shard_map/pallas_call | solution.py:187
  174.2 18.9 %all_to_all.25 = bf16[32,8,1024]{2,1,0:T(8,128)(2,1)S(1)} all-to-all(bf16[32,8,1024]{2,1,0:T(8,128)(2,1)S(1)} %get-tuple-element.19), channel_id=1, replica_groups=mesh['zh'=2,'x'=4,'c'=2,'y'=4,'zl'=4] {'c','y','x'}, dimensions={0} | all-to-all | bytes 1048576 | tf_op jit(solution)/shard_map/all_to_all | solution.py:279
  193.1 0.1 convert_reduce_fusion
  193.2 0.1 collective-permute-start.14
  193.3 7.0 %collective-permute-done.14 = f32[16,1024]{1,0:T(8,128)S(1)} collective-permute-done((f32[16,1024]{1,0:T(8,128)S(1)}, f32[16,1024]{1,0:T(8,128)S(1)}, u32[]{:S(2)}, u32[]{:S(2)}) %collective-permute-start.14) | collective-permute-done | bytes 65568 | tf_op jit(solution)/shard_map/ppermute | solution.py:296
  200.3 0.8 collective-permute-start.17
  201.0 3.7 %collective-permute-start.16 = (f32[16,1024]{1,0:T(8,128)S(1)}, f32[16,1024]{1,0:T(8,128)S(1)}, u32[]{:S(2)}, u32[]{:S(2)}) collective-permute-start(f32[16,1024]{1,0:T(8,128)S(1)} %fusion.3), channel_id=1, source_target_pairs={{0,2},{1,3},{2,0},{3,1},{4,6},{5,7},{6,4},{7,5},{8,10},{9,11},{10,... | collective-permute-start | bytes 196616 | tf_op jit(solution)/shard_map/ppermute | solution.py:271
  204.8 0.7 collective-permute-done.17
  205.4 1.7 collective-permute-done.16
  207.1 0.8 collective-permute-done.15
  208.0 16.4 %all_to_all.26.mine_ref = bf16[16,16,1024]{2,1,0:T(8,128)(2,1)S(1)} all-to-all(bf16[16,16,1024]{2,1,0:T(8,128)(2,1)S(1)} %broadcast_in_dim.7), channel_id=1, replica_groups=mesh['zh'=2,'x'=4,'c'=2,'y'=4,'zl'=4] {'y','x'}, dimensions={0} | all-to-all | bytes 1048576 | tf_op jit(solution)/shard_map/all_to_all | solution.py:301
  224.3 2.3 collective-permute-start.18
  226.6 1.5 collective-permute-done.18.other_ref
  228.2 5.1 %shard_map.43 = f32[16,512,128]{2,1,0:T(8,128)} custom-call(s32[1]{0:T(128)} %bitcast.core_ref, bf16[16,16,1024]{2,1,0:T(8,128)(2,1)S(1)} %all_to_all.26.mine_ref, bf16[16,16,1024]{2,1,0:T(8,128)(2,1)S(1)} %collective-permute-done.18.other_ref, bf16[16,128,1024]{2,1,0:T(8,128)(2,1)S(1)} %get-tuple-element.20.ritz_ref, ...), custom_call_target="tpu_custom_call" | custom-call | flops 2147483648 | bytes 11534336 | tf_op jit(solution)/shard_map/pallas_call | solution.py:239
  (27 shorter events, 0.4 us)
Async XLA Ops:
  0.0 9.0 %collective-permute-start.2 = (f32[8,2,128]{2,1,0:T(2,128)}, f32[8,2,128]{2,1,0:T(2,128)S(1)}, u32[]{:S(2)}, u32[]{:S(2)}) collective-permute-start(f32[8,2,128]{2,1,0:T(2,128)} %param.4), channel_id=1, source_target_pairs={{0,128},{128,0},{1,129},{129,1},{2,130},{130,2},{3,131},{131,3},{4... | collective-permute-start | bytes 24584 | tf_op jit(solution)/shard_map/ppermute | solution.py:296
  10.4 12.9 %all-to-all-start = ((f32[8,2,8,2,128]{4,3,1,2,0:T(2,128)}), f32[8,2,8,2,128]{4,3,1,2,0:T(2,128)S(1)}, u32[]{:S(2)}, u32[]{:S(2)}) async-start(f32[8,2,8,2,128]{4,3,1,2,0:T(2,128)} %broadcast_in_dim.6), calls=%async_computation | async-start | bytes 262144 | tf_op jit(solution)/shard_map/all_to_all | solution.py:301
  19.3 31.0 %collective-permute-start.5 = (bf16[4,32,16,128]{3,2,1,0:T(8,128)(2,1)S(1)}, bf16[4,32,16,128]{3,2,1,0:T(8,128)(2,1)S(1)}, u32[]{:S(2)}, u32[]{:S(2)}) collective-permute-start(bf16[4,32,16,128]{3,2,1,0:T(8,128)(2,1)S(1)} %get-tuple-element.16), channel_id=1, source_target_pairs={{0,1},{1,2},{2,3},{3,4},{4,5},{5,6},{6,7},{7,8},{8,9},{9,10},{10,1... | collective-permute-start | bytes 1572872 | tf_op jit(solution)/shard_map/ppermute | solution.py:306
  22.0 28.3 %collective-permute-start.6 = (bf16[4,32,16,128]{3,2,1,0:T(8,128)(2,1)S(1)}, bf16[4,32,16,128]{3,2,1,0:T(8,128)(2,1)S(1)}, u32[]{:S(2)}, u32[]{:S(2)}) collective-permute-start(bf16[4,32,16,128]{3,2,1,0:T(8,128)(2,1)S(1)} %get-tuple-element.17), channel_id=1, source_target_pairs={{1,0},{2,1},{3,2},{4,3},{5,4},{6,5},{7,6},{8,7},{9,8},{10,9},{11,1... | collective-permute-start | bytes 1572872 | tf_op jit(solution)/shard_map/ppermute | solution.py:307
  23.5 26.8 %collective-permute-start.4 = (f32[4,32,128]{2,1,0:T(8,128)S(1)}, f32[4,32,128]{2,1,0:T(8,128)S(1)}, u32[]{:S(2)}, u32[]{:S(2)}) collective-permute-start(f32[4,32,128]{2,1,0:T(8,128)S(1)} %bitcast.28), channel_id=1, source_target_pairs={{1,0},{2,1},{3,2},{4,3},{5,4},{6,5},{7,6},{8,7},{9,8},{10,9},{11,1... | collective-permute-start | bytes 196616 | tf_op jit(solution)/shard_map/ppermute | solution.py:307
  24.8 25.5 %collective-permute-start.3 = (f32[4,32,128]{2,1,0:T(8,128)S(1)}, f32[4,32,128]{2,1,0:T(8,128)S(1)}, u32[]{:S(2)}, u32[]{:S(2)}) collective-permute-start(f32[4,32,128]{2,1,0:T(8,128)S(1)} %bitcast.27), channel_id=1, source_target_pairs={{0,1},{1,2},{2,3},{3,4},{4,5},{5,6},{6,7},{7,8},{8,9},{9,10},{10,1... | collective-permute-start | bytes 196616 | tf_op jit(solution)/shard_map/ppermute | solution.py:306
  63.6 70.8 %all-to-all-start.2 = ((bf16[16,16,16,128]{3,2,1,0:T(8,128)(2,1)}), bf16[16,16,16,128]{3,2,1,0:T(8,128)(2,1)S(1)}, u32[]{:S(2)}, u32[]{:S(2)}) async-start(bf16[16,16,16,128]{3,2,1,0:T(8,128)(2,1)} %shard_map.41), calls=%async_computation.2 | async-start | bytes 2097152 | tf_op jit(solution)/shard_map/all_to_all | solution.py:336
  77.7 31.3 %collective-permute-start = (bf16[4,32,16,128]{3,2,1,0:T(8,128)(2,1)S(1)}, bf16[4,32,16,128]{3,2,1,0:T(8,128)(2,1)S(1)}, u32[]{:S(2)}, u32[]{:S(2)}) collective-permute-start(bf16[4,32,16,128]{3,2,1,0:T(8,128)(2,1)S(1)} %get-tuple-element.13), channel_id=1, source_target_pairs={{0,1},{1,2},{2,3},{3,4},{4,5},{5,6},{6,7},{7,8},{8,9},{9,10},{10,1... | collective-permute-start | bytes 1572872 | tf_op jit(solution)/shard_map/ppermute | solution.py:306
  80.0 41.2 %collective-permute-start.1 = (bf16[4,32,16,128]{3,2,1,0:T(8,128)(2,1)S(1)}, bf16[4,32,16,128]{3,2,1,0:T(8,128)(2,1)S(1)}, u32[]{:S(2)}, u32[]{:S(2)}) collective-permute-start(bf16[4,32,16,128]{3,2,1,0:T(8,128)(2,1)S(1)} %get-tuple-element.14), channel_id=1, source_target_pairs={{1,0},{2,1},{3,2},{4,3},{5,4},{6,5},{7,6},{8,7},{9,8},{10,9},{11,1... | collective-permute-start | bytes 1572872 | tf_op jit(solution)/shard_map/ppermute | solution.py:307
  134.4 35.6 %all-to-all-start.1 = ((bf16[16,16,16,128]{3,2,1,0:T(8,128)(2,1)}), bf16[16,16,16,128]{3,2,1,0:T(8,128)(2,1)S(1)}, u32[]{:S(2)}, u32[]{:S(2)}) async-start(bf16[16,16,16,128]{3,2,1,0:T(8,128)(2,1)} %shard_map.38), calls=%async_computation.1 | async-start | bytes 2097152 | tf_op jit(solution)/shard_map/all_to_all | solution.py:336
  148.3 2.0 collective-permute-start.7
  150.4 9.1 %collective-permute-start.10 = (f32[4,8,1024]{2,1,0:T(8,128)S(1)}, f32[4,8,1024]{2,1,0:T(8,128)S(1)}, u32[]{:S(2)}, u32[]{:S(2)}) collective-permute-start(f32[4,8,1024]{2,1,0:T(8,128)S(1)} %get-tuple-element.21), channel_id=1, source_target_pairs={{0,12},{4,8},{8,4},{12,0},{1,13},{5,9},{9,5},{13,1},{2,14},{6,10},... | collective-permute-start | bytes 393224 | tf_op jit(solution)/shard_map/ppermute | solution.py:271
  150.5 9.0 %collective-permute-start.9 = (f32[4,8,1024]{2,1,0:T(8,128)S(1)}, f32[4,8,1024]{2,1,0:T(8,128)S(1)}, u32[]{:S(2)}, u32[]{:S(2)}) collective-permute-start(f32[4,8,1024]{2,1,0:T(8,128)S(1)} %get-tuple-element.22), channel_id=1, source_target_pairs={{0,8},{4,12},{8,0},{12,4},{1,9},{5,13},{9,1},{13,5},{2,10},{6,14},... | collective-permute-start | bytes 393224 | tf_op jit(solution)/shard_map/ppermute | solution.py:271
  153.5 6.3 %collective-permute-start.8 = (f32[4,8,1024]{2,1,0:T(8,128)S(1)}, f32[4,8,1024]{2,1,0:T(8,128)S(1)}, u32[]{:S(2)}, u32[]{:S(2)}) collective-permute-start(f32[4,8,1024]{2,1,0:T(8,128)S(1)} %get-tuple-element.23), channel_id=1, source_target_pairs={{0,4},{4,0},{8,12},{12,8},{1,5},{5,1},{9,13},{13,9},{2,6},{6,2},{1... | collective-permute-start | bytes 393224 | tf_op jit(solution)/shard_map/ppermute | solution.py:271
  159.8 14.3 %collective-permute-start.13 = (f32[1,8,1024]{2,1,0:T(8,128)S(1)}, f32[1,8,1024]{2,1,0:T(8,128)S(1)}, u32[]{:S(2)}, u32[]{:S(2)}) collective-permute-start(f32[1,8,1024]{2,1,0:T(8,128)S(1)} %get-tuple-element.24), channel_id=1, source_target_pairs={{0,96},{32,64},{64,32},{96,0},{1,97},{33,65},{65,33},{97,1},{2,98}... | collective-permute-start | bytes 98312 | tf_op jit(solution)/shard_map/ppermute | solution.py:271
  162.3 11.8 %collective-permute-start.12 = (f32[1,8,1024]{2,1,0:T(8,128)S(1)}, f32[1,8,1024]{2,1,0:T(8,128)S(1)}, u32[]{:S(2)}, u32[]{:S(2)}) collective-permute-start(f32[1,8,1024]{2,1,0:T(8,128)S(1)} %get-tuple-element.25), channel_id=1, source_target_pairs={{0,64},{32,96},{64,0},{96,32},{1,65},{33,97},{65,1},{97,33},{2,66}... | collective-permute-start | bytes 98312 | tf_op jit(solution)/shard_map/ppermute | solution.py:271
  162.9 11.3 %collective-permute-start.11 = (f32[1,8,1024]{2,1,0:T(8,128)S(1)}, f32[1,8,1024]{2,1,0:T(8,128)S(1)}, u32[]{:S(2)}, u32[]{:S(2)}) collective-permute-start(f32[1,8,1024]{2,1,0:T(8,128)S(1)} %get-tuple-element.26), channel_id=1, source_target_pairs={{0,32},{32,0},{64,96},{96,64},{1,33},{33,1},{65,97},{97,65},{2,34}... | collective-permute-start | bytes 98312 | tf_op jit(solution)/shard_map/ppermute | solution.py:271
  193.2 7.1 %collective-permute-start.14 = (f32[16,1024]{1,0:T(8,128)S(1)}, f32[16,1024]{1,0:T(8,128)S(1)}, u32[]{:S(2)}, u32[]{:S(2)}) collective-permute-start(f32[16,1024]{1,0:T(8,128)S(1)} %pad_maximum_fusion.1), channel_id=1, source_target_pairs={{0,128},{128,0},{1,129},{129,1},{2,130},{130,2},{3,131},{131,3},{4... | collective-permute-start | bytes 196616 | tf_op jit(solution)/shard_map/ppermute | solution.py:296
  200.3 5.1 %collective-permute-start.17 = (f32[16,1024]{1,0:T(8,128)S(1)}, f32[16,1024]{1,0:T(8,128)S(1)}, u32[]{:S(2)}, u32[]{:S(2)}) collective-permute-start(f32[16,1024]{1,0:T(8,128)S(1)} %fusion.3), channel_id=1, source_target_pairs={{0,3},{1,2},{2,1},{3,0},{4,7},{5,6},{6,5},{7,4},{8,11},{9,10},{10,... | collective-permute-start | bytes 196616 | tf_op jit(solution)/shard_map/ppermute | solution.py:271
  201.0 6.1 %collective-permute-start.16 = (f32[16,1024]{1,0:T(8,128)S(1)}, f32[16,1024]{1,0:T(8,128)S(1)}, u32[]{:S(2)}, u32[]{:S(2)}) collective-permute-start(f32[16,1024]{1,0:T(8,128)S(1)} %fusion.3), channel_id=1, source_target_pairs={{0,2},{1,3},{2,0},{3,1},{4,6},{5,7},{6,4},{7,5},{8,10},{9,11},{10,... | collective-permute-start | bytes 196616 | tf_op jit(solution)/shard_map/ppermute | solution.py:271
  204.8 3.1 %collective-permute-start.15 = (f32[16,1024]{1,0:T(8,128)S(1)}, f32[16,1024]{1,0:T(8,128)S(1)}, u32[]{:S(2)}, u32[]{:S(2)}) collective-permute-start(f32[16,1024]{1,0:T(8,128)S(1)} %fusion.3), channel_id=1, source_target_pairs={{0,1},{1,0},{2,3},{3,2},{4,5},{5,4},{6,7},{7,6},{8,9},{9,8},{10,11... | collective-permute-start | bytes 196616 | tf_op jit(solution)/shard_map/ppermute | solution.py:271
  224.3 3.8 %collective-permute-start.18 = (bf16[16,16,1024]{2,1,0:T(8,128)(2,1)S(1)}, bf16[16,16,1024]{2,1,0:T(8,128)(2,1)S(1)}, u32[]{:S(2)}, u32[]{:S(2)}) collective-permute-start(bf16[16,16,1024]{2,1,0:T(8,128)(2,1)S(1)} %all_to_all.26.mine_ref), channel_id=1, source_target_pairs={{0,16},{16,0},{1,17},{17,1},{2,18},{18,2},{3,19},{19,3},{4,20},{20... | collective-permute-start | bytes 1572872 | tf_op jit(solution)/shard_map/ppermute | solution.py:296

commit v10 on v9

--- a/solution.py
+++ b/solution.py
@@ -22,26 +22,30 @@
 
 def spread_kernel(first_ref, second_ref, low_ref, high_ref):
     for source, target in ((first_ref, low_ref), (second_ref, high_ref)):
-        vectors, rows, lanes = source.shape
-        flat = source.reshape(vectors * rows, lanes)
-        for y in range(rows):
-            target[0, y] = flat[pl.ds(y, vectors, stride=rows), :].astype(bf16)
+        planes, rows = target.shape[:2]
+        vectors, span, lanes = source.shape
+        flat = source.reshape(vectors * span, lanes)
+        for p in range(planes):
+            for y in range(rows):
+                at = pl.ds(p * rows + y, vectors, stride=span)
+                target[p, y] = flat[at, :].astype(bf16)
 
 
 def spread(cells, rows, chunk, size):
     planes, lanes = cells.shape[1] // rows, cells.shape[2]
     half = planes // 2
-    out = pl.BlockSpec((1, rows, size, lanes), lambda p: (p, 0, 0, 0))
+    steps = half // 2
+    out = pl.BlockSpec((2, rows, size, lanes), lambda p: (p, 0, 0, 0))
     return pl.pallas_call(
         spread_kernel,
         out_shape=[jax.ShapeDtypeStruct((half, rows, size, lanes), bf16)] * 2,
-        grid=(half,),
+        grid=(steps,),
         in_specs=[
-            pl.BlockSpec((size, rows, lanes), lambda p: (chunk, p, 0)),
-            pl.BlockSpec((size, rows, lanes), lambda p: (chunk, p + half, 0)),
+            pl.BlockSpec((size, 2 * rows, lanes), lambda p: (chunk, p, 0)),
+            pl.BlockSpec((size, 2 * rows, lanes), lambda p: (chunk, p + steps, 0)),
         ],
         out_specs=[out] * 2,
-        compiler_params=pltpu.CompilerParams(vmem_limit_bytes=8 << 20),
+        compiler_params=pltpu.CompilerParams(vmem_limit_bytes=10 << 20),
         cost_estimate=pl.CostEstimate(
             flops=size * planes * rows * lanes,
             bytes_accessed=6 * size * planes * rows * lanes,

time: 234 us -> 232 us (level)
  blocking collectives: 35.3 us -> 29.2 us
  starting transfers between devices: 61.6 us -> 66.5 us
    all_to_all x1, blocking collectives: 16.4 us -> 12.2 us  [from_everyone(): return lax.all_to_all(copies, axis, split_axis=0, concat_axis=0, tiled=True)]
    ppermute x3, starting transfers between devices: 10.1 us -> 13.2 us  [swapped(): return lax.ppermute(value, axis, [(0, 1), (1, 0)])]
  transfers between devices with their start and end apart: 22 -> 22, of which waited for: 13 -> 11; matrix products, arithmetic and copies ran while one was open for 0% -> 0% of each run, Pallas kernels for 12% -> 11%
where the time goes in v10:
time: 232 us; the launch traced here: 231 us
  waiting for transfers between devices  89 us (38%)
  starting transfers between devices  66.5 us (29%)
  Pallas kernels  44.5 us (19%)
  blocking collectives  29.2 us (13%)
    ppermute x3, waiting for transfers between devices, swap_ends(): from_above = lax.ppermute(low, DOM, [(i + 1, i) for i in range(count - 1)])  32.9 us
    ppermute x3, waiting for transfers between devices, swap_ends(): from_below = lax.ppermute(high, DOM, [(i, i + 1) for i in range(count - 1)])  28.4 us
    pallas_call x2, Pallas kernels, filtered(): pl.pallas_call(filter_kernel, out_shape=jax.ShapeDtypeStruct((rows // 2,...  26.5 us
    all_to_all x2, starting transfers between devices, pipeline(): held.append(lax.all_to_all(blocks, VEC, 0, 0, tiled=True))  20.9 us
    all_to_all x1, blocking collectives, near_sum(): blocks = lax.all_to_all(partial, NEAR, 0, 0, tiled=True)  17 us
    ppermute x3, starting transfers between devices, swapped(): return lax.ppermute(value, axis, [(0, 1), (1, 0)])  13.2 us
    ppermute x10, starting transfers between devices, traded(): lax.ppermute(blocks[k], axis, [(i, i ^ k) for i in range(count)])  13.1 us
    all_to_all x1, blocking collectives, from_everyone(): return lax.all_to_all(copies, axis, split_axis=0, concat_axis=0, tiled=True)  12.2 us
  transfers between devices with their start and end apart: 22, of which 11 were waited for; matrix products, arithmetic and copies ran while one was open for 0% of the time, Pallas kernels for 11%

profile of v10, /device:TPU:1, one launch (start us, length us, event | category | flops | bytes accessed | tf_op | source)
XLA Modules:
  0.0 231.5 jit_solution(13249415274937230343)
XLA Ops:
  0.0 7.7 %collective-permute-start.2 = (f32[8,2,128]{2,1,0:T(2,128)}, f32[8,2,128]{2,1,0:T(2,128)S(1)}, u32[]{:S(2)}, u32[]{:S(2)}) collective-permute-start(f32[8,2,128]{2,1,0:T(2,128)} %param.4), channel_id=1, source_target_pairs={{0,128},{128,0},{1,129},{129,1},{2,130},{130,2},{3,131},{131,3},{4... | collective-permute-start | bytes 24584 | tf_op jit(solution)/shard_map/ppermute | solution.py:300
  7.7 1.2 collective-permute-done.2
  9.0 0.7 select_bitcast_fusion.1
  9.7 0.7 broadcast_in_dim.6
  10.4 5.8 %all-to-all-start = ((f32[8,2,8,2,128]{4,3,1,2,0:T(2,128)}), f32[8,2,8,2,128]{4,3,1,2,0:T(2,128)S(1)}, u32[]{:S(2)}, u32[]{:S(2)}) async-start(f32[8,2,8,2,128]{4,3,1,2,0:T(2,128)} %broadcast_in_dim.6), calls=%async_computation | async-start | bytes 262144 | tf_op jit(solution)/shard_map/all_to_all | solution.py:305
  16.2 2.4 %shard_map.40 = (bf16[4,32,16,128]{3,2,1,0:T(8,128)(2,1)S(1)}, bf16[4,32,16,128]{3,2,1,0:T(8,128)(2,1)S(1)}) custom-call(f32[32,256,128]{2,1,0:T(8,128)} %bitcast.18, f32[32,256,128]{2,1,0:T(8,128)} %bitcast.19), custom_call_target="tpu_custom_call" | custom-call | flops 524288 | bytes 3145728 | tf_op jit(solution)/shard_map/pallas_call | solution.py:39
  18.7 2.7 %collective-permute-start.5 = (bf16[4,32,16,128]{3,2,1,0:T(8,128)(2,1)S(1)}, bf16[4,32,16,128]{3,2,1,0:T(8,128)(2,1)S(1)}, u32[]{:S(2)}, u32[]{:S(2)}) collective-permute-start(bf16[4,32,16,128]{3,2,1,0:T(8,128)(2,1)S(1)} %get-tuple-element.16), channel_id=1, source_target_pairs={{0,1},{1,2},{2,3},{3,4},{4,5},{5,6},{6,7},{7,8},{8,9},{9,10},{10,1... | collective-permute-start | bytes 1572872 | tf_op jit(solution)/shard_map/ppermute | solution.py:310
  21.3 1.3 collective-permute-start.6
  22.7 0.1 add_bitcast_fusion
  22.8 1.3 collective-permute-start.4
  24.1 4.6 %collective-permute-start.3 = (f32[4,32,128]{2,1,0:T(8,128)S(1)}, f32[4,32,128]{2,1,0:T(8,128)S(1)}, u32[]{:S(2)}, u32[]{:S(2)}) collective-permute-start(f32[4,32,128]{2,1,0:T(8,128)S(1)} %bitcast.27), channel_id=1, source_target_pairs={{0,1},{1,2},{2,3},{3,4},{4,5},{5,6},{6,7},{7,8},{8,9},{9,10},{10,1... | collective-permute-start | bytes 196616 | tf_op jit(solution)/shard_map/ppermute | solution.py:310
  28.7 0.1 add_convert_fusion.1.ends_ref
  28.9 20.7 %collective-permute-done.4 = f32[4,32,128]{2,1,0:T(8,128)S(1)} collective-permute-done((f32[4,32,128]{2,1,0:T(8,128)S(1)}, f32[4,32,128]{2,1,0:T(8,128)S(1)}, u32[]{:S(2)}, u32[]{:S(2)}) %collective-permute-start.4) | collective-permute-done | bytes 65568 | tf_op jit(solution)/shard_map/ppermute | solution.py:311
  49.7 13.3 %shard_map.41 = bf16[16,16,16,128]{3,2,1,0:T(8,128)(2,1)} custom-call(s32[2]{0:T(128)S(1)} %add_convert_fusion.1.ends_ref, f32[32,256,128]{2,1,0:T(8,128)} %bitcast.20, bf16[4,32,16,128]{3,2,1,0:T(8,128)(2,1)S(1)} %collective-permute-done.5.low_ref, bf16[4,32,16,128]{3,2,1,0:T(8,128)(2,1)S(1)} %collective-permute-done.6.high_ref, ...), custom_call_target="tpu_custom_call" | custom-call | flops 34603008 | bytes 5242880 | tf_op jit(solution)/shard_map/pallas_call | solution.py:134
  62.9 11.1 %all-to-all-start.2 = ((bf16[16,16,16,128]{3,2,1,0:T(8,128)(2,1)}), bf16[16,16,16,128]{3,2,1,0:T(8,128)(2,1)S(1)}, u32[]{:S(2)}, u32[]{:S(2)}) async-start(bf16[16,16,16,128]{3,2,1,0:T(8,128)(2,1)} %shard_map.41), calls=%async_computation.2 | async-start | bytes 2097152 | tf_op jit(solution)/shard_map/all_to_all | solution.py:340
  74.0 2.4 %shard_map.37 = (bf16[4,32,16,128]{3,2,1,0:T(8,128)(2,1)S(1)}, bf16[4,32,16,128]{3,2,1,0:T(8,128)(2,1)S(1)}) custom-call(f32[32,256,128]{2,1,0:T(8,128)} %bitcast.21, f32[32,256,128]{2,1,0:T(8,128)} %bitcast.22), custom_call_target="tpu_custom_call" | custom-call | flops 524288 | bytes 3145728 | tf_op jit(solution)/shard_map/pallas_call | solution.py:39
  76.4 2.3 collective-permute-start
  78.7 1.3 collective-permute-start.1
  80.0 28.4 %collective-permute-done.low_ref = bf16[4,32,16,128]{3,2,1,0:T(8,128)(2,1)S(1)} collective-permute-done((bf16[4,32,16,128]{3,2,1,0:T(8,128)(2,1)S(1)}, bf16[4,32,16,128]{3,2,1,0:T(8,128)(2,1)S(1)}, u32[]{:S(2)}, u32[]{:S(2)}) %collective-permute-start) | collective-permute-done | bytes 524320 | tf_op jit(solution)/shard_map/ppermute | solution.py:310
  108.4 12.1 %collective-permute-done.1.high_ref = bf16[4,32,16,128]{3,2,1,0:T(8,128)(2,1)S(1)} collective-permute-done((bf16[4,32,16,128]{3,2,1,0:T(8,128)(2,1)S(1)}, bf16[4,32,16,128]{3,2,1,0:T(8,128)(2,1)S(1)}, u32[]{:S(2)}, u32[]{:S(2)}) %collective-permute-start.1) | collective-permute-done | bytes 524320 | tf_op jit(solution)/shard_map/ppermute | solution.py:311
  120.5 13.2 %shard_map.38 = bf16[16,16,16,128]{3,2,1,0:T(8,128)(2,1)} custom-call(s32[2]{0:T(128)S(1)} %add_convert_fusion.1.ends_ref, f32[32,256,128]{2,1,0:T(8,128)} %bitcast.23, bf16[4,32,16,128]{3,2,1,0:T(8,128)(2,1)S(1)} %collective-permute-done.low_ref, bf16[4,32,16,128]{3,2,1,0:T(8,128)(2,1)S(1)} %collective-permute-done.1.high_ref, ...), custom_call_target="tpu_custom_call" | custom-call | flops 34603008 | bytes 5242880 | tf_op jit(solution)/shard_map/pallas_call | solution.py:134
  133.8 9.8 %all-to-all-start.1 = ((bf16[16,16,16,128]{3,2,1,0:T(8,128)(2,1)}), bf16[16,16,16,128]{3,2,1,0:T(8,128)(2,1)S(1)}, u32[]{:S(2)}, u32[]{:S(2)}) async-start(bf16[16,16,16,128]{3,2,1,0:T(8,128)(2,1)} %shard_map.38), calls=%async_computation.1 | async-start | bytes 2097152 | tf_op jit(solution)/shard_map/all_to_all | solution.py:340
  143.6 4.0 %shard_map.42 = f32[32,8,1024]{2,1,0:T(8,128)S(1)} custom-call(s32[1]{0:T(128)} %bitcast.1.place_ref, bf16[16,128,1024]{2,1,0:T(8,128)(2,1)} %bitcast.24, bf16[16,16,16,128]{3,2,1,0:T(8,128)(2,1)S(1)} %all-to-all-done.2.cells_ref.refs_0_), custom_call_target="tpu_custom_call" | custom-call | flops 1073741824 | bytes 7340032 | tf_op jit(solution)/shard_map/pallas_call | solution.py:191
  147.7 0.2 collective-permute-start.7
  147.9 1.8 collective-permute-done.7
  149.7 0.1 slice_add_fusion
  149.8 0.1 collective-permute-start.10
  149.9 3.0 %collective-permute-start.9 = (f32[4,8,1024]{2,1,0:T(8,128)S(1)}, f32[4,8,1024]{2,1,0:T(8,128)S(1)}, u32[]{:S(2)}, u32[]{:S(2)}) collective-permute-start(f32[4,8,1024]{2,1,0:T(8,128)S(1)} %get-tuple-element.22), channel_id=1, source_target_pairs={{0,8},{4,12},{8,0},{12,4},{1,9},{5,13},{9,1},{13,5},{2,10},{6,14},... | collective-permute-start | bytes 393224 | tf_op jit(solution)/shard_map/ppermute | solution.py:275
  152.9 0.3 collective-permute-start.8
  153.1 5.8 %collective-permute-done.10 = f32[4,8,1024]{2,1,0:T(8,128)S(1)} collective-permute-done((f32[4,8,1024]{2,1,0:T(8,128)S(1)}, f32[4,8,1024]{2,1,0:T(8,128)S(1)}, u32[]{:S(2)}, u32[]{:S(2)}) %collective-permute-start.10) | collective-permute-done | bytes 131104 | tf_op jit(solution)/shard_map/ppermute | solution.py:275
  158.9 0.2 collective-permute-done.8
  159.2 2.5 %collective-permute-start.13 = (f32[1,8,1024]{2,1,0:T(8,128)S(1)}, f32[1,8,1024]{2,1,0:T(8,128)S(1)}, u32[]{:S(2)}, u32[]{:S(2)}) collective-permute-start(f32[1,8,1024]{2,1,0:T(8,128)S(1)} %get-tuple-element.24), channel_id=1, source_target_pairs={{0,96},{32,64},{64,32},{96,0},{1,97},{33,65},{65,33},{97,1},{2,98}... | collective-permute-start | bytes 98312 | tf_op jit(solution)/shard_map/ppermute | solution.py:275
  161.7 0.6 collective-permute-start.12
  162.2 0.3 collective-permute-start.11
  162.5 7.2 %all-to-all-done.1.cells_ref.refs_1_ = bf16[16,16,16,128]{3,2,1,0:T(8,128)(2,1)S(1)} async-done(((bf16[16,16,16,128]{3,2,1,0:T(8,128)(2,1)}), bf16[16,16,16,128]{3,2,1,0:T(8,128)(2,1)S(1)}, u32[]{:S(2)}, u32[]{:S(2)}) %all-to-all-start.1) | async-done | bytes 1048608 | tf_op jit(solution)/shard_map/all_to_all | solution.py:340
  169.7 4.1 %shard_map.39 = (bf16[32,8,1024]{2,1,0:T(8,128)(2,1)S(1)}, bf16[16,128,1024]{2,1,0:T(8,128)(2,1)S(1)}) custom-call(s32[1]{0:T(128)} %bitcast.1.place_ref, bf16[16,128,1024]{2,1,0:T(8,128)(2,1)} %bitcast.25, bf16[16,16,16,128]{3,2,1,0:T(8,128)(2,1)S(1)} %all-to-all-done.1.cells_ref.refs_1_), custom_call_target="tpu_custom_call" | custom-call | flops 1073741824 | bytes 7340032 | tf_op jit(solution)/shard_map/pallas_call | solution.py:191
  173.8 17.0 %all_to_all.25 = bf16[32,8,1024]{2,1,0:T(8,128)(2,1)S(1)} all-to-all(bf16[32,8,1024]{2,1,0:T(8,128)(2,1)S(1)} %get-tuple-element.19), channel_id=1, replica_groups=mesh['zh'=2,'x'=4,'c'=2,'y'=4,'zl'=4] {'c','y','x'}, dimensions={0} | all-to-all | bytes 1048576 | tf_op jit(solution)/shard_map/all_to_all | solution.py:283
  190.8 0.1 convert_reduce_fusion
  190.9 0.9 collective-permute-start.14
  191.9 6.2 %collective-permute-done.14 = f32[16,1024]{1,0:T(8,128)S(1)} collective-permute-done((f32[16,1024]{1,0:T(8,128)S(1)}, f32[16,1024]{1,0:T(8,128)S(1)}, u32[]{:S(2)}, u32[]{:S(2)}) %collective-permute-start.14) | collective-permute-done | bytes 65568 | tf_op jit(solution)/shard_map/ppermute | solution.py:300
  198.0 2.6 %collective-permute-start.17 = (f32[16,1024]{1,0:T(8,128)S(1)}, f32[16,1024]{1,0:T(8,128)S(1)}, u32[]{:S(2)}, u32[]{:S(2)}) collective-permute-start(f32[16,1024]{1,0:T(8,128)S(1)} %fusion.3), channel_id=1, source_target_pairs={{0,3},{1,2},{2,1},{3,0},{4,7},{5,6},{6,5},{7,4},{8,11},{9,10},{10,... | collective-permute-start | bytes 196616 | tf_op jit(solution)/shard_map/ppermute | solution.py:275
  200.6 3.7 %collective-permute-start.16 = (f32[16,1024]{1,0:T(8,128)S(1)}, f32[16,1024]{1,0:T(8,128)S(1)}, u32[]{:S(2)}, u32[]{:S(2)}) collective-permute-start(f32[16,1024]{1,0:T(8,128)S(1)} %fusion.3), channel_id=1, source_target_pairs={{0,2},{1,3},{2,0},{3,1},{4,6},{5,7},{6,4},{7,5},{8,10},{9,11},{10,... | collective-permute-start | bytes 196616 | tf_op jit(solution)/shard_map/ppermute | solution.py:275
  204.3 3.8 %collective-permute-done.16 = f32[16,1024]{1,0:T(8,128)S(1)} collective-permute-done((f32[16,1024]{1,0:T(8,128)S(1)}, f32[16,1024]{1,0:T(8,128)S(1)}, u32[]{:S(2)}, u32[]{:S(2)}) %collective-permute-start.16) | collective-permute-done | bytes 65568 | tf_op jit(solution)/shard_map/ppermute | solution.py:275
  208.1 0.1 broadcast_in_dim.7
  208.2 12.2 %all_to_all.26.mine_ref = bf16[16,16,1024]{2,1,0:T(8,128)(2,1)S(1)} all-to-all(bf16[16,16,1024]{2,1,0:T(8,128)(2,1)S(1)} %broadcast_in_dim.7), channel_id=1, replica_groups=mesh['zh'=2,'x'=4,'c'=2,'y'=4,'zl'=4] {'y','x'}, dimensions={0} | all-to-all | bytes 1048576 | tf_op jit(solution)/shard_map/all_to_all | solution.py:305
  220.4 4.5 %collective-permute-start.18 = (bf16[16,16,1024]{2,1,0:T(8,128)(2,1)S(1)}, bf16[16,16,1024]{2,1,0:T(8,128)(2,1)S(1)}, u32[]{:S(2)}, u32[]{:S(2)}) collective-permute-start(bf16[16,16,1024]{2,1,0:T(8,128)(2,1)S(1)} %all_to_all.26.mine_ref), channel_id=1, source_target_pairs={{0,16},{16,0},{1,17},{17,1},{2,18},{18,2},{3,19},{19,3},{4,20},{20... | collective-permute-start | bytes 1572872 | tf_op jit(solution)/shard_map/ppermute | solution.py:300
  224.9 1.5 collective-permute-done.18.other_ref
  226.4 5.1 %shard_map.43 = f32[16,512,128]{2,1,0:T(8,128)} custom-call(s32[1]{0:T(128)} %bitcast.core_ref, bf16[16,16,1024]{2,1,0:T(8,128)(2,1)S(1)} %all_to_all.26.mine_ref, bf16[16,16,1024]{2,1,0:T(8,128)(2,1)S(1)} %collective-permute-done.18.other_ref, bf16[16,128,1024]{2,1,0:T(8,128)(2,1)S(1)} %get-tuple-element.20.ritz_ref, ...), custom_call_target="tpu_custom_call" | custom-call | flops 2147483648 | bytes 11534336 | tf_op jit(solution)/shard_map/pallas_call | solution.py:243
  (27 shorter events, 0.3 us)
Async XLA Ops:
  0.0 9.0 %collective-permute-start.2 = (f32[8,2,128]{2,1,0:T(2,128)}, f32[8,2,128]{2,1,0:T(2,128)S(1)}, u32[]{:S(2)}, u32[]{:S(2)}) collective-permute-start(f32[8,2,128]{2,1,0:T(2,128)} %param.4), channel_id=1, source_target_pairs={{0,128},{128,0},{1,129},{129,1},{2,130},{130,2},{3,131},{131,3},{4... | collective-permute-start | bytes 24584 | tf_op jit(solution)/shard_map/ppermute | solution.py:300
  10.4 12.3 %all-to-all-start = ((f32[8,2,8,2,128]{4,3,1,2,0:T(2,128)}), f32[8,2,8,2,128]{4,3,1,2,0:T(2,128)S(1)}, u32[]{:S(2)}, u32[]{:S(2)}) async-start(f32[8,2,8,2,128]{4,3,1,2,0:T(2,128)} %broadcast_in_dim.6), calls=%async_computation | async-start | bytes 262144 | tf_op jit(solution)/shard_map/all_to_all | solution.py:305
  18.7 31.0 %collective-permute-start.5 = (bf16[4,32,16,128]{3,2,1,0:T(8,128)(2,1)S(1)}, bf16[4,32,16,128]{3,2,1,0:T(8,128)(2,1)S(1)}, u32[]{:S(2)}, u32[]{:S(2)}) collective-permute-start(bf16[4,32,16,128]{3,2,1,0:T(8,128)(2,1)S(1)} %get-tuple-element.16), channel_id=1, source_target_pairs={{0,1},{1,2},{2,3},{3,4},{4,5},{5,6},{6,7},{7,8},{8,9},{9,10},{10,1... | collective-permute-start | bytes 1572872 | tf_op jit(solution)/shard_map/ppermute | solution.py:310
  21.3 28.3 %collective-permute-start.6 = (bf16[4,32,16,128]{3,2,1,0:T(8,128)(2,1)S(1)}, bf16[4,32,16,128]{3,2,1,0:T(8,128)(2,1)S(1)}, u32[]{:S(2)}, u32[]{:S(2)}) collective-permute-start(bf16[4,32,16,128]{3,2,1,0:T(8,128)(2,1)S(1)} %get-tuple-element.17), channel_id=1, source_target_pairs={{1,0},{2,1},{3,2},{4,3},{5,4},{6,5},{7,6},{8,7},{9,8},{10,9},{11,1... | collective-permute-start | bytes 1572872 | tf_op jit(solution)/shard_map/ppermute | solution.py:311
  22.8 26.8 %collective-permute-start.4 = (f32[4,32,128]{2,1,0:T(8,128)S(1)}, f32[4,32,128]{2,1,0:T(8,128)S(1)}, u32[]{:S(2)}, u32[]{:S(2)}) collective-permute-start(f32[4,32,128]{2,1,0:T(8,128)S(1)} %bitcast.28), channel_id=1, source_target_pairs={{1,0},{2,1},{3,2},{4,3},{5,4},{6,5},{7,6},{8,7},{9,8},{10,9},{11,1... | collective-permute-start | bytes 196616 | tf_op jit(solution)/shard_map/ppermute | solution.py:311
  24.1 25.5 %collective-permute-start.3 = (f32[4,32,128]{2,1,0:T(8,128)S(1)}, f32[4,32,128]{2,1,0:T(8,128)S(1)}, u32[]{:S(2)}, u32[]{:S(2)}) collective-permute-start(f32[4,32,128]{2,1,0:T(8,128)S(1)} %bitcast.27), channel_id=1, source_target_pairs={{0,1},{1,2},{2,3},{3,4},{4,5},{5,6},{6,7},{7,8},{8,9},{9,10},{10,1... | collective-permute-start | bytes 196616 | tf_op jit(solution)/shard_map/ppermute | solution.py:310
  62.9 70.8 %all-to-all-start.2 = ((bf16[16,16,16,128]{3,2,1,0:T(8,128)(2,1)}), bf16[16,16,16,128]{3,2,1,0:T(8,128)(2,1)S(1)}, u32[]{:S(2)}, u32[]{:S(2)}) async-start(bf16[16,16,16,128]{3,2,1,0:T(8,128)(2,1)} %shard_map.41), calls=%async_computation.2 | async-start | bytes 2097152 | tf_op jit(solution)/shard_map/all_to_all | solution.py:340
  76.4 32.0 %collective-permute-start = (bf16[4,32,16,128]{3,2,1,0:T(8,128)(2,1)S(1)}, bf16[4,32,16,128]{3,2,1,0:T(8,128)(2,1)S(1)}, u32[]{:S(2)}, u32[]{:S(2)}) collective-permute-start(bf16[4,32,16,128]{3,2,1,0:T(8,128)(2,1)S(1)} %get-tuple-element.13), channel_id=1, source_target_pairs={{0,1},{1,2},{2,3},{3,4},{4,5},{5,6},{6,7},{7,8},{8,9},{9,10},{10,1... | collective-permute-start | bytes 1572872 | tf_op jit(solution)/shard_map/ppermute | solution.py:310
  78.7 41.8 %collective-permute-start.1 = (bf16[4,32,16,128]{3,2,1,0:T(8,128)(2,1)S(1)}, bf16[4,32,16,128]{3,2,1,0:T(8,128)(2,1)S(1)}, u32[]{:S(2)}, u32[]{:S(2)}) collective-permute-start(bf16[4,32,16,128]{3,2,1,0:T(8,128)(2,1)S(1)} %get-tuple-element.14), channel_id=1, source_target_pairs={{1,0},{2,1},{3,2},{4,3},{5,4},{6,5},{7,6},{8,7},{9,8},{10,9},{11,1... | collective-permute-start | bytes 1572872 | tf_op jit(solution)/shard_map/ppermute | solution.py:311
  133.8 35.9 %all-to-all-start.1 = ((bf16[16,16,16,128]{3,2,1,0:T(8,128)(2,1)}), bf16[16,16,16,128]{3,2,1,0:T(8,128)(2,1)S(1)}, u32[]{:S(2)}, u32[]{:S(2)}) async-start(bf16[16,16,16,128]{3,2,1,0:T(8,128)(2,1)} %shard_map.38), calls=%async_computation.1 | async-start | bytes 2097152 | tf_op jit(solution)/shard_map/all_to_all | solution.py:340
  147.7 2.0 collective-permute-start.7
  149.8 9.1 %collective-permute-start.10 = (f32[4,8,1024]{2,1,0:T(8,128)S(1)}, f32[4,8,1024]{2,1,0:T(8,128)S(1)}, u32[]{:S(2)}, u32[]{:S(2)}) collective-permute-start(f32[4,8,1024]{2,1,0:T(8,128)S(1)} %get-tuple-element.21), channel_id=1, source_target_pairs={{0,12},{4,8},{8,4},{12,0},{1,13},{5,9},{9,5},{13,1},{2,14},{6,10},... | collective-permute-start | bytes 393224 | tf_op jit(solution)/shard_map/ppermute | solution.py:275
  149.9 9.0 %collective-permute-start.9 = (f32[4,8,1024]{2,1,0:T(8,128)S(1)}, f32[4,8,1024]{2,1,0:T(8,128)S(1)}, u32[]{:S(2)}, u32[]{:S(2)}) collective-permute-start(f32[4,8,1024]{2,1,0:T(8,128)S(1)} %get-tuple-element.22), channel_id=1, source_target_pairs={{0,8},{4,12},{8,0},{12,4},{1,9},{5,13},{9,1},{13,5},{2,10},{6,14},... | collective-permute-start | bytes 393224 | tf_op jit(solution)/shard_map/ppermute | solution.py:275
  152.9 6.3 %collective-permute-start.8 = (f32[4,8,1024]{2,1,0:T(8,128)S(1)}, f32[4,8,1024]{2,1,0:T(8,128)S(1)}, u32[]{:S(2)}, u32[]{:S(2)}) collective-permute-start(f32[4,8,1024]{2,1,0:T(8,128)S(1)} %get-tuple-element.23), channel_id=1, source_target_pairs={{0,4},{4,0},{8,12},{12,8},{1,5},{5,1},{9,13},{13,9},{2,6},{6,2},{1... | collective-permute-start | bytes 393224 | tf_op jit(solution)/shard_map/ppermute | solution.py:275
  159.2 14.6 %collective-permute-start.13 = (f32[1,8,1024]{2,1,0:T(8,128)S(1)}, f32[1,8,1024]{2,1,0:T(8,128)S(1)}, u32[]{:S(2)}, u32[]{:S(2)}) collective-permute-start(f32[1,8,1024]{2,1,0:T(8,128)S(1)} %get-tuple-element.24), channel_id=1, source_target_pairs={{0,96},{32,64},{64,32},{96,0},{1,97},{33,65},{65,33},{97,1},{2,98}... | collective-permute-start | bytes 98312 | tf_op jit(solution)/shard_map/ppermute | solution.py:275
  161.7 12.1 %collective-permute-start.12 = (f32[1,8,1024]{2,1,0:T(8,128)S(1)}, f32[1,8,1024]{2,1,0:T(8,128)S(1)}, u32[]{:S(2)}, u32[]{:S(2)}) collective-permute-start(f32[1,8,1024]{2,1,0:T(8,128)S(1)} %get-tuple-element.25), channel_id=1, source_target_pairs={{0,64},{32,96},{64,0},{96,32},{1,65},{33,97},{65,1},{97,33},{2,66}... | collective-permute-start | bytes 98312 | tf_op jit(solution)/shard_map/ppermute | solution.py:275
  162.2 11.6 %collective-permute-start.11 = (f32[1,8,1024]{2,1,0:T(8,128)S(1)}, f32[1,8,1024]{2,1,0:T(8,128)S(1)}, u32[]{:S(2)}, u32[]{:S(2)}) collective-permute-start(f32[1,8,1024]{2,1,0:T(8,128)S(1)} %get-tuple-element.26), channel_id=1, source_target_pairs={{0,32},{32,0},{64,96},{96,64},{1,33},{33,1},{65,97},{97,65},{2,34}... | collective-permute-start | bytes 98312 | tf_op jit(solution)/shard_map/ppermute | solution.py:275
  190.9 7.1 %collective-permute-start.14 = (f32[16,1024]{1,0:T(8,128)S(1)}, f32[16,1024]{1,0:T(8,128)S(1)}, u32[]{:S(2)}, u32[]{:S(2)}) collective-permute-start(f32[16,1024]{1,0:T(8,128)S(1)} %pad_maximum_fusion.1), channel_id=1, source_target_pairs={{0,128},{128,0},{1,129},{129,1},{2,130},{130,2},{3,131},{131,3},{4... | collective-permute-start | bytes 196616 | tf_op jit(solution)/shard_map/ppermute | solution.py:300
  198.0 6.3 %collective-permute-start.17 = (f32[16,1024]{1,0:T(8,128)S(1)}, f32[16,1024]{1,0:T(8,128)S(1)}, u32[]{:S(2)}, u32[]{:S(2)}) collective-permute-start(f32[16,1024]{1,0:T(8,128)S(1)} %fusion.3), channel_id=1, source_target_pairs={{0,3},{1,2},{2,1},{3,0},{4,7},{5,6},{6,5},{7,4},{8,11},{9,10},{10,... | collective-permute-start | bytes 196616 | tf_op jit(solution)/shard_map/ppermute | solution.py:275
  200.6 7.5 %collective-permute-start.16 = (f32[16,1024]{1,0:T(8,128)S(1)}, f32[16,1024]{1,0:T(8,128)S(1)}, u32[]{:S(2)}, u32[]{:S(2)}) collective-permute-start(f32[16,1024]{1,0:T(8,128)S(1)} %fusion.3), channel_id=1, source_target_pairs={{0,2},{1,3},{2,0},{3,1},{4,6},{5,7},{6,4},{7,5},{8,10},{9,11},{10,... | collective-permute-start | bytes 196616 | tf_op jit(solution)/shard_map/ppermute | solution.py:275
  204.3 3.8 %collective-permute-start.15 = (f32[16,1024]{1,0:T(8,128)S(1)}, f32[16,1024]{1,0:T(8,128)S(1)}, u32[]{:S(2)}, u32[]{:S(2)}) collective-permute-start(f32[16,1024]{1,0:T(8,128)S(1)} %fusion.3), channel_id=1, source_target_pairs={{0,1},{1,0},{2,3},{3,2},{4,5},{5,4},{6,7},{7,6},{8,9},{9,8},{10,11... | collective-permute-start | bytes 196616 | tf_op jit(solution)/shard_map/ppermute | solution.py:275
  220.4 6.1 %collective-permute-start.18 = (bf16[16,16,1024]{2,1,0:T(8,128)(2,1)S(1)}, bf16[16,16,1024]{2,1,0:T(8,128)(2,1)S(1)}, u32[]{:S(2)}, u32[]{:S(2)}) collective-permute-start(bf16[16,16,1024]{2,1,0:T(8,128)(2,1)S(1)} %all_to_all.26.mine_ref), channel_id=1, source_target_pairs={{0,16},{16,0},{1,17},{17,1},{2,18},{18,2},{3,19},{19,3},{4,20},{20... | collective-permute-start | bytes 1572872 | tf_op jit(solution)/shard_map/ppermute | solution.py:300

commit v11 on v10

--- a/solution.py
+++ b/solution.py
@@ -217,18 +217,20 @@
     )
 
     def remove(cells_ref):
-        for r in range(0, rows, 2):
+        flat = out_ref.reshape(blocks * vectors * rows, lanes)
+        for r in range(0, rows, STEP):
             removed = lax.dot_general(
                 coeffs,
-                ritz_ref[r : r + 2].reshape(2 * lanes, -1),
+                ritz_ref[pl.ds(pl.program_id(1) * rows + r, STEP)].reshape(STEP * lanes, -1),
                 (((1,), (1,)), ((), ())),
                 preferred_element_type=f32,
             )
-            for k in range(2):
+            for k in range(STEP):
                 for i in range(blocks):
                     held = cells_ref[i, r + k].astype(f32)
                     part = removed[i * vectors : (i + 1) * vectors, k * lanes : (k + 1) * lanes]
-                    out_ref[i, pl.ds(r + k, vectors, stride=rows), :] = held - part
+                    at = pl.ds(i * vectors * rows + r + k, vectors, stride=rows)
+                    flat[at, :] = held - part
 
     for k, cells_ref in enumerate(refs[:-1]):
         pl.when(pl.program_id(0) == k)(functools.partial(remove, cells_ref))
@@ -239,20 +241,22 @@
     near, _, kept = mine.shape
     chunks = len(held)
     size = mine.shape[1] // chunks
-    coeffs = pl.BlockSpec((near, size, kept), lambda k: (0, k, 0))
+    coeffs = pl.BlockSpec((near, size, kept), lambda k, g: (0, k, 0))
+    part = rows // 2
+    cells = pl.BlockSpec((blocks, part, vectors, lanes), lambda k, g: (0, g, 0, 0))
     return pl.pallas_call(
         remove_kernel,
-        out_shape=jax.ShapeDtypeStruct((blocks, chunks * vectors * rows, lanes), f32),
-        grid=(chunks,),
+        out_shape=jax.ShapeDtypeStruct((blocks, chunks * vectors, rows, lanes), f32),
+        grid=(chunks, 2),
         in_specs=[
             pl.BlockSpec(memory_space=pltpu.SMEM),
             coeffs,
             coeffs,
             pl.BlockSpec(memory_space=pltpu.VMEM),
-            *([pl.BlockSpec((blocks, rows, vectors, lanes), lambda k: (0, 0, 0, 0))] * chunks),
+            *([cells] * chunks),
         ],
-        out_specs=pl.BlockSpec((blocks, vectors * rows, lanes), lambda k: (0, k, 0)),
-        compiler_params=pltpu.CompilerParams(vmem_limit_bytes=32 << 20),
+        out_specs=pl.BlockSpec((blocks, vectors, part, lanes), lambda k, g: (0, k, g, 0)),
+        compiler_params=pltpu.CompilerParams(vmem_limit_bytes=24 << 20),
         cost_estimate=pl.CostEstimate(
             flops=2 * chunks * blocks * vectors * rows * lanes * kept,
             bytes_accessed=11 << 20,

time: 232 us -> 232 us (level)
  no operation moved by 1% of the time
where the time goes in v11:
time: 232 us; the launch traced here: 231 us
  waiting for transfers between devices  89 us (38%)
  starting transfers between devices  66.5 us (29%)
  Pallas kernels  44.5 us (19%)
  blocking collectives  29.2 us (13%)
    ppermute x3, waiting for transfers between devices, swap_ends(): from_above = lax.ppermute(low, DOM, [(i + 1, i) for i in range(count - 1)])  32.9 us
    ppermute x3, waiting for transfers between devices, swap_ends(): from_below = lax.ppermute(high, DOM, [(i, i + 1) for i in range(count - 1)])  28.4 us
    pallas_call x2, Pallas kernels, filtered(): pl.pallas_call(filter_kernel, out_shape=jax.ShapeDtypeStruct((rows // 2,...  26.5 us
    all_to_all x2, starting transfers between devices, pipeline(): held.append(lax.all_to_all(blocks, VEC, 0, 0, tiled=True))  20.9 us
    all_to_all x1, blocking collectives, near_sum(): blocks = lax.all_to_all(partial, NEAR, 0, 0, tiled=True)  17 us
    ppermute x3, starting transfers between devices, swapped(): return lax.ppermute(value, axis, [(0, 1), (1, 0)])  13.2 us
    ppermute x10, starting transfers between devices, traded(): lax.ppermute(blocks[k], axis, [(i, i ^ k) for i in range(count)])  13.1 us
    all_to_all x1, blocking collectives, from_everyone(): return lax.all_to_all(copies, axis, split_axis=0, concat_axis=0, tiled=True)  12.2 us
  transfers between devices with their start and end apart: 22, of which 11 were waited for; matrix products, arithmetic and copies ran while one was open for 0% of the time, Pallas kernels for 11%

profile of v11, /device:TPU:1, one launch (start us, length us, event | category | flops | bytes accessed | tf_op | source)
XLA Modules:
  0.0 231.5 jit_solution(816682683203446812)
XLA Ops:
  0.0 7.7 %collective-permute-start.2 = (f32[8,2,128]{2,1,0:T(2,128)}, f32[8,2,128]{2,1,0:T(2,128)S(1)}, u32[]{:S(2)}, u32[]{:S(2)}) collective-permute-start(f32[8,2,128]{2,1,0:T(2,128)} %param.4), channel_id=1, source_target_pairs={{0,128},{128,0},{1,129},{129,1},{2,130},{130,2},{3,131},{131,3},{4... | collective-permute-start | bytes 24584 | tf_op jit(solution)/shard_map/ppermute | solution.py:304
  7.7 1.2 collective-permute-done.2
  9.0 0.7 select_bitcast_fusion.1
  9.7 0.7 broadcast_in_dim.6
  10.4 5.8 %all-to-all-start = ((f32[8,2,8,2,128]{4,3,1,2,0:T(2,128)}), f32[8,2,8,2,128]{4,3,1,2,0:T(2,128)S(1)}, u32[]{:S(2)}, u32[]{:S(2)}) async-start(f32[8,2,8,2,128]{4,3,1,2,0:T(2,128)} %broadcast_in_dim.6), calls=%async_computation | async-start | bytes 262144 | tf_op jit(solution)/shard_map/all_to_all | solution.py:309
  16.2 2.4 %shard_map.40 = (bf16[4,32,16,128]{3,2,1,0:T(8,128)(2,1)S(1)}, bf16[4,32,16,128]{3,2,1,0:T(8,128)(2,1)S(1)}) custom-call(f32[32,256,128]{2,1,0:T(8,128)} %bitcast.18, f32[32,256,128]{2,1,0:T(8,128)} %bitcast.19), custom_call_target="tpu_custom_call" | custom-call | flops 524288 | bytes 3145728 | tf_op jit(solution)/shard_map/pallas_call | solution.py:39
  18.7 2.7 %collective-permute-start.5 = (bf16[4,32,16,128]{3,2,1,0:T(8,128)(2,1)S(1)}, bf16[4,32,16,128]{3,2,1,0:T(8,128)(2,1)S(1)}, u32[]{:S(2)}, u32[]{:S(2)}) collective-permute-start(bf16[4,32,16,128]{3,2,1,0:T(8,128)(2,1)S(1)} %get-tuple-element.16), channel_id=1, source_target_pairs={{0,1},{1,2},{2,3},{3,4},{4,5},{5,6},{6,7},{7,8},{8,9},{9,10},{10,1... | collective-permute-start | bytes 1572872 | tf_op jit(solution)/shard_map/ppermute | solution.py:314
  21.3 1.3 collective-permute-start.6
  22.7 0.1 add_bitcast_fusion
  22.8 1.3 collective-permute-start.4
  24.1 4.6 %collective-permute-start.3 = (f32[4,32,128]{2,1,0:T(8,128)S(1)}, f32[4,32,128]{2,1,0:T(8,128)S(1)}, u32[]{:S(2)}, u32[]{:S(2)}) collective-permute-start(f32[4,32,128]{2,1,0:T(8,128)S(1)} %bitcast.27), channel_id=1, source_target_pairs={{0,1},{1,2},{2,3},{3,4},{4,5},{5,6},{6,7},{7,8},{8,9},{9,10},{10,1... | collective-permute-start | bytes 196616 | tf_op jit(solution)/shard_map/ppermute | solution.py:314
  28.7 0.1 add_convert_fusion.1.ends_ref
  28.9 20.7 %collective-permute-done.4 = f32[4,32,128]{2,1,0:T(8,128)S(1)} collective-permute-done((f32[4,32,128]{2,1,0:T(8,128)S(1)}, f32[4,32,128]{2,1,0:T(8,128)S(1)}, u32[]{:S(2)}, u32[]{:S(2)}) %collective-permute-start.4) | collective-permute-done | bytes 65568 | tf_op jit(solution)/shard_map/ppermute | solution.py:315
  49.7 13.3 %shard_map.41 = bf16[16,16,16,128]{3,2,1,0:T(8,128)(2,1)} custom-call(s32[2]{0:T(128)S(1)} %add_convert_fusion.1.ends_ref, f32[32,256,128]{2,1,0:T(8,128)} %bitcast.20, bf16[4,32,16,128]{3,2,1,0:T(8,128)(2,1)S(1)} %collective-permute-done.5.low_ref, bf16[4,32,16,128]{3,2,1,0:T(8,128)(2,1)S(1)} %collective-permute-done.6.high_ref, ...), custom_call_target="tpu_custom_call" | custom-call | flops 34603008 | bytes 5242880 | tf_op jit(solution)/shard_map/pallas_call | solution.py:134
  62.9 11.1 %all-to-all-start.2 = ((bf16[16,16,16,128]{3,2,1,0:T(8,128)(2,1)}), bf16[16,16,16,128]{3,2,1,0:T(8,128)(2,1)S(1)}, u32[]{:S(2)}, u32[]{:S(2)}) async-start(bf16[16,16,16,128]{3,2,1,0:T(8,128)(2,1)} %shard_map.41), calls=%async_computation.2 | async-start | bytes 2097152 | tf_op jit(solution)/shard_map/all_to_all | solution.py:344
  74.0 2.4 %shard_map.37 = (bf16[4,32,16,128]{3,2,1,0:T(8,128)(2,1)S(1)}, bf16[4,32,16,128]{3,2,1,0:T(8,128)(2,1)S(1)}) custom-call(f32[32,256,128]{2,1,0:T(8,128)} %bitcast.21, f32[32,256,128]{2,1,0:T(8,128)} %bitcast.22), custom_call_target="tpu_custom_call" | custom-call | flops 524288 | bytes 3145728 | tf_op jit(solution)/shard_map/pallas_call | solution.py:39
  76.4 2.3 collective-permute-start
  78.7 1.3 collective-permute-start.1
  80.0 28.4 %collective-permute-done.low_ref = bf16[4,32,16,128]{3,2,1,0:T(8,128)(2,1)S(1)} collective-permute-done((bf16[4,32,16,128]{3,2,1,0:T(8,128)(2,1)S(1)}, bf16[4,32,16,128]{3,2,1,0:T(8,128)(2,1)S(1)}, u32[]{:S(2)}, u32[]{:S(2)}) %collective-permute-start) | collective-permute-done | bytes 524320 | tf_op jit(solution)/shard_map/ppermute | solution.py:314
  108.4 12.1 %collective-permute-done.1.high_ref = bf16[4,32,16,128]{3,2,1,0:T(8,128)(2,1)S(1)} collective-permute-done((bf16[4,32,16,128]{3,2,1,0:T(8,128)(2,1)S(1)}, bf16[4,32,16,128]{3,2,1,0:T(8,128)(2,1)S(1)}, u32[]{:S(2)}, u32[]{:S(2)}) %collective-permute-start.1) | collective-permute-done | bytes 524320 | tf_op jit(solution)/shard_map/ppermute | solution.py:315
  120.5 13.2 %shard_map.38 = bf16[16,16,16,128]{3,2,1,0:T(8,128)(2,1)} custom-call(s32[2]{0:T(128)S(1)} %add_convert_fusion.1.ends_ref, f32[32,256,128]{2,1,0:T(8,128)} %bitcast.23, bf16[4,32,16,128]{3,2,1,0:T(8,128)(2,1)S(1)} %collective-permute-done.low_ref, bf16[4,32,16,128]{3,2,1,0:T(8,128)(2,1)S(1)} %collective-permute-done.1.high_ref, ...), custom_call_target="tpu_custom_call" | custom-call | flops 34603008 | bytes 5242880 | tf_op jit(solution)/shard_map/pallas_call | solution.py:134
  133.8 9.8 %all-to-all-start.1 = ((bf16[16,16,16,128]{3,2,1,0:T(8,128)(2,1)}), bf16[16,16,16,128]{3,2,1,0:T(8,128)(2,1)S(1)}, u32[]{:S(2)}, u32[]{:S(2)}) async-start(bf16[16,16,16,128]{3,2,1,0:T(8,128)(2,1)} %shard_map.38), calls=%async_computation.1 | async-start | bytes 2097152 | tf_op jit(solution)/shard_map/all_to_all | solution.py:344
  143.6 4.0 %shard_map.42 = f32[32,8,1024]{2,1,0:T(8,128)S(1)} custom-call(s32[1]{0:T(128)} %bitcast.1.place_ref, bf16[16,128,1024]{2,1,0:T(8,128)(2,1)} %bitcast.24, bf16[16,16,16,128]{3,2,1,0:T(8,128)(2,1)S(1)} %all-to-all-done.2.cells_ref.refs_0_), custom_call_target="tpu_custom_call" | custom-call | flops 1073741824 | bytes 7340032 | tf_op jit(solution)/shard_map/pallas_call | solution.py:191
  147.7 0.2 collective-permute-start.7
  147.9 1.8 collective-permute-done.7
  149.7 0.1 slice_add_fusion
  149.8 0.1 collective-permute-start.10
  149.9 3.0 %collective-permute-start.9 = (f32[4,8,1024]{2,1,0:T(8,128)S(1)}, f32[4,8,1024]{2,1,0:T(8,128)S(1)}, u32[]{:S(2)}, u32[]{:S(2)}) collective-permute-start(f32[4,8,1024]{2,1,0:T(8,128)S(1)} %get-tuple-element.22), channel_id=1, source_target_pairs={{0,8},{4,12},{8,0},{12,4},{1,9},{5,13},{9,1},{13,5},{2,10},{6,14},... | collective-permute-start | bytes 393224 | tf_op jit(solution)/shard_map/ppermute | solution.py:279
  152.9 0.3 collective-permute-start.8
  153.1 5.8 %collective-permute-done.10 = f32[4,8,1024]{2,1,0:T(8,128)S(1)} collective-permute-done((f32[4,8,1024]{2,1,0:T(8,128)S(1)}, f32[4,8,1024]{2,1,0:T(8,128)S(1)}, u32[]{:S(2)}, u32[]{:S(2)}) %collective-permute-start.10) | collective-permute-done | bytes 131104 | tf_op jit(solution)/shard_map/ppermute | solution.py:279
  158.9 0.2 collective-permute-done.8
  159.2 2.5 %collective-permute-start.13 = (f32[1,8,1024]{2,1,0:T(8,128)S(1)}, f32[1,8,1024]{2,1,0:T(8,128)S(1)}, u32[]{:S(2)}, u32[]{:S(2)}) collective-permute-start(f32[1,8,1024]{2,1,0:T(8,128)S(1)} %get-tuple-element.24), channel_id=1, source_target_pairs={{0,96},{32,64},{64,32},{96,0},{1,97},{33,65},{65,33},{97,1},{2,98}... | collective-permute-start | bytes 98312 | tf_op jit(solution)/shard_map/ppermute | solution.py:279
  161.7 0.6 collective-permute-start.12
  162.2 0.3 collective-permute-start.11
  162.5 7.2 %all-to-all-done.1.cells_ref.refs_1_ = bf16[16,16,16,128]{3,2,1,0:T(8,128)(2,1)S(1)} async-done(((bf16[16,16,16,128]{3,2,1,0:T(8,128)(2,1)}), bf16[16,16,16,128]{3,2,1,0:T(8,128)(2,1)S(1)}, u32[]{:S(2)}, u32[]{:S(2)}) %all-to-all-start.1) | async-done | bytes 1048608 | tf_op jit(solution)/shard_map/all_to_all | solution.py:344
  169.7 4.1 %shard_map.39 = (bf16[32,8,1024]{2,1,0:T(8,128)(2,1)S(1)}, bf16[16,128,1024]{2,1,0:T(8,128)(2,1)S(1)}) custom-call(s32[1]{0:T(128)} %bitcast.1.place_ref, bf16[16,128,1024]{2,1,0:T(8,128)(2,1)} %bitcast.25, bf16[16,16,16,128]{3,2,1,0:T(8,128)(2,1)S(1)} %all-to-all-done.1.cells_ref.refs_1_), custom_call_target="tpu_custom_call" | custom-call | flops 1073741824 | bytes 7340032 | tf_op jit(solution)/shard_map/pallas_call | solution.py:191
  173.8 17.0 %all_to_all.25 = bf16[32,8,1024]{2,1,0:T(8,128)(2,1)S(1)} all-to-all(bf16[32,8,1024]{2,1,0:T(8,128)(2,1)S(1)} %get-tuple-element.19), channel_id=1, replica_groups=mesh['zh'=2,'x'=4,'c'=2,'y'=4,'zl'=4] {'c','y','x'}, dimensions={0} | all-to-all | bytes 1048576 | tf_op jit(solution)/shard_map/all_to_all | solution.py:287
  190.8 0.1 convert_reduce_fusion
  190.9 0.9 collective-permute-start.14
  191.9 6.2 %collective-permute-done.14 = f32[16,1024]{1,0:T(8,128)S(1)} collective-permute-done((f32[16,1024]{1,0:T(8,128)S(1)}, f32[16,1024]{1,0:T(8,128)S(1)}, u32[]{:S(2)}, u32[]{:S(2)}) %collective-permute-start.14) | collective-permute-done | bytes 65568 | tf_op jit(solution)/shard_map/ppermute | solution.py:304
  198.0 2.6 %collective-permute-start.17 = (f32[16,1024]{1,0:T(8,128)S(1)}, f32[16,1024]{1,0:T(8,128)S(1)}, u32[]{:S(2)}, u32[]{:S(2)}) collective-permute-start(f32[16,1024]{1,0:T(8,128)S(1)} %fusion.3), channel_id=1, source_target_pairs={{0,3},{1,2},{2,1},{3,0},{4,7},{5,6},{6,5},{7,4},{8,11},{9,10},{10,... | collective-permute-start | bytes 196616 | tf_op jit(solution)/shard_map/ppermute | solution.py:279
  200.6 3.7 %collective-permute-start.16 = (f32[16,1024]{1,0:T(8,128)S(1)}, f32[16,1024]{1,0:T(8,128)S(1)}, u32[]{:S(2)}, u32[]{:S(2)}) collective-permute-start(f32[16,1024]{1,0:T(8,128)S(1)} %fusion.3), channel_id=1, source_target_pairs={{0,2},{1,3},{2,0},{3,1},{4,6},{5,7},{6,4},{7,5},{8,10},{9,11},{10,... | collective-permute-start | bytes 196616 | tf_op jit(solution)/shard_map/ppermute | solution.py:279
  204.3 3.8 %collective-permute-done.16 = f32[16,1024]{1,0:T(8,128)S(1)} collective-permute-done((f32[16,1024]{1,0:T(8,128)S(1)}, f32[16,1024]{1,0:T(8,128)S(1)}, u32[]{:S(2)}, u32[]{:S(2)}) %collective-permute-start.16) | collective-permute-done | bytes 65568 | tf_op jit(solution)/shard_map/ppermute | solution.py:279
  208.1 0.1 broadcast_in_dim.7
  208.2 12.2 %all_to_all.26.mine_ref = bf16[16,16,1024]{2,1,0:T(8,128)(2,1)S(1)} all-to-all(bf16[16,16,1024]{2,1,0:T(8,128)(2,1)S(1)} %broadcast_in_dim.7), channel_id=1, replica_groups=mesh['zh'=2,'x'=4,'c'=2,'y'=4,'zl'=4] {'y','x'}, dimensions={0} | all-to-all | bytes 1048576 | tf_op jit(solution)/shard_map/all_to_all | solution.py:309
  220.4 4.5 %collective-permute-start.18 = (bf16[16,16,1024]{2,1,0:T(8,128)(2,1)S(1)}, bf16[16,16,1024]{2,1,0:T(8,128)(2,1)S(1)}, u32[]{:S(2)}, u32[]{:S(2)}) collective-permute-start(bf16[16,16,1024]{2,1,0:T(8,128)(2,1)S(1)} %all_to_all.26.mine_ref), channel_id=1, source_target_pairs={{0,16},{16,0},{1,17},{17,1},{2,18},{18,2},{3,19},{19,3},{4,20},{20... | collective-permute-start | bytes 1572872 | tf_op jit(solution)/shard_map/ppermute | solution.py:304
  224.9 1.5 collective-permute-done.18.other_ref
  226.4 5.0 %shard_map.43 = f32[16,32,16,128]{3,2,1,0:T(8,128)} custom-call(s32[1]{0:T(128)} %bitcast.core_ref, bf16[16,16,1024]{2,1,0:T(8,128)(2,1)S(1)} %all_to_all.26.mine_ref, bf16[16,16,1024]{2,1,0:T(8,128)(2,1)S(1)} %collective-permute-done.18.other_ref, bf16[16,128,1024]{2,1,0:T(8,128)(2,1)S(1)} %get-tuple-element.20.ritz_ref, ...), custom_call_target="tpu_custom_call" | custom-call | flops 2147483648 | bytes 11534336 | tf_op jit(solution)/shard_map/pallas_call | solution.py:247
  (27 shorter events, 0.3 us)
Async XLA Ops:
  0.0 9.0 %collective-permute-start.2 = (f32[8,2,128]{2,1,0:T(2,128)}, f32[8,2,128]{2,1,0:T(2,128)S(1)}, u32[]{:S(2)}, u32[]{:S(2)}) collective-permute-start(f32[8,2,128]{2,1,0:T(2,128)} %param.4), channel_id=1, source_target_pairs={{0,128},{128,0},{1,129},{129,1},{2,130},{130,2},{3,131},{131,3},{4... | collective-permute-start | bytes 24584 | tf_op jit(solution)/shard_map/ppermute | solution.py:304
  10.4 12.3 %all-to-all-start = ((f32[8,2,8,2,128]{4,3,1,2,0:T(2,128)}), f32[8,2,8,2,128]{4,3,1,2,0:T(2,128)S(1)}, u32[]{:S(2)}, u32[]{:S(2)}) async-start(f32[8,2,8,2,128]{4,3,1,2,0:T(2,128)} %broadcast_in_dim.6), calls=%async_computation | async-start | bytes 262144 | tf_op jit(solution)/shard_map/all_to_all | solution.py:309
  18.7 31.0 %collective-permute-start.5 = (bf16[4,32,16,128]{3,2,1,0:T(8,128)(2,1)S(1)}, bf16[4,32,16,128]{3,2,1,0:T(8,128)(2,1)S(1)}, u32[]{:S(2)}, u32[]{:S(2)}) collective-permute-start(bf16[4,32,16,128]{3,2,1,0:T(8,128)(2,1)S(1)} %get-tuple-element.16), channel_id=1, source_target_pairs={{0,1},{1,2},{2,3},{3,4},{4,5},{5,6},{6,7},{7,8},{8,9},{9,10},{10,1... | collective-permute-start | bytes 1572872 | tf_op jit(solution)/shard_map/ppermute | solution.py:314
  21.3 28.3 %collective-permute-start.6 = (bf16[4,32,16,128]{3,2,1,0:T(8,128)(2,1)S(1)}, bf16[4,32,16,128]{3,2,1,0:T(8,128)(2,1)S(1)}, u32[]{:S(2)}, u32[]{:S(2)}) collective-permute-start(bf16[4,32,16,128]{3,2,1,0:T(8,128)(2,1)S(1)} %get-tuple-element.17), channel_id=1, source_target_pairs={{1,0},{2,1},{3,2},{4,3},{5,4},{6,5},{7,6},{8,7},{9,8},{10,9},{11,1... | collective-permute-start | bytes 1572872 | tf_op jit(solution)/shard_map/ppermute | solution.py:315
  22.8 26.8 %collective-permute-start.4 = (f32[4,32,128]{2,1,0:T(8,128)S(1)}, f32[4,32,128]{2,1,0:T(8,128)S(1)}, u32[]{:S(2)}, u32[]{:S(2)}) collective-permute-start(f32[4,32,128]{2,1,0:T(8,128)S(1)} %bitcast.28), channel_id=1, source_target_pairs={{1,0},{2,1},{3,2},{4,3},{5,4},{6,5},{7,6},{8,7},{9,8},{10,9},{11,1... | collective-permute-start | bytes 196616 | tf_op jit(solution)/shard_map/ppermute | solution.py:315
  24.1 25.5 %collective-permute-start.3 = (f32[4,32,128]{2,1,0:T(8,128)S(1)}, f32[4,32,128]{2,1,0:T(8,128)S(1)}, u32[]{:S(2)}, u32[]{:S(2)}) collective-permute-start(f32[4,32,128]{2,1,0:T(8,128)S(1)} %bitcast.27), channel_id=1, source_target_pairs={{0,1},{1,2},{2,3},{3,4},{4,5},{5,6},{6,7},{7,8},{8,9},{9,10},{10,1... | collective-permute-start | bytes 196616 | tf_op jit(solution)/shard_map/ppermute | solution.py:314
  62.9 70.8 %all-to-all-start.2 = ((bf16[16,16,16,128]{3,2,1,0:T(8,128)(2,1)}), bf16[16,16,16,128]{3,2,1,0:T(8,128)(2,1)S(1)}, u32[]{:S(2)}, u32[]{:S(2)}) async-start(bf16[16,16,16,128]{3,2,1,0:T(8,128)(2,1)} %shard_map.41), calls=%async_computation.2 | async-start | bytes 2097152 | tf_op jit(solution)/shard_map/all_to_all | solution.py:344
  76.4 32.0 %collective-permute-start = (bf16[4,32,16,128]{3,2,1,0:T(8,128)(2,1)S(1)}, bf16[4,32,16,128]{3,2,1,0:T(8,128)(2,1)S(1)}, u32[]{:S(2)}, u32[]{:S(2)}) collective-permute-start(bf16[4,32,16,128]{3,2,1,0:T(8,128)(2,1)S(1)} %get-tuple-element.13), channel_id=1, source_target_pairs={{0,1},{1,2},{2,3},{3,4},{4,5},{5,6},{6,7},{7,8},{8,9},{9,10},{10,1... | collective-permute-start | bytes 1572872 | tf_op jit(solution)/shard_map/ppermute | solution.py:314
  78.7 41.8 %collective-permute-start.1 = (bf16[4,32,16,128]{3,2,1,0:T(8,128)(2,1)S(1)}, bf16[4,32,16,128]{3,2,1,0:T(8,128)(2,1)S(1)}, u32[]{:S(2)}, u32[]{:S(2)}) collective-permute-start(bf16[4,32,16,128]{3,2,1,0:T(8,128)(2,1)S(1)} %get-tuple-element.14), channel_id=1, source_target_pairs={{1,0},{2,1},{3,2},{4,3},{5,4},{6,5},{7,6},{8,7},{9,8},{10,9},{11,1... | collective-permute-start | bytes 1572872 | tf_op jit(solution)/shard_map/ppermute | solution.py:315
  133.8 35.9 %all-to-all-start.1 = ((bf16[16,16,16,128]{3,2,1,0:T(8,128)(2,1)}), bf16[16,16,16,128]{3,2,1,0:T(8,128)(2,1)S(1)}, u32[]{:S(2)}, u32[]{:S(2)}) async-start(bf16[16,16,16,128]{3,2,1,0:T(8,128)(2,1)} %shard_map.38), calls=%async_computation.1 | async-start | bytes 2097152 | tf_op jit(solution)/shard_map/all_to_all | solution.py:344
  147.7 2.0 collective-permute-start.7
  149.8 9.1 %collective-permute-start.10 = (f32[4,8,1024]{2,1,0:T(8,128)S(1)}, f32[4,8,1024]{2,1,0:T(8,128)S(1)}, u32[]{:S(2)}, u32[]{:S(2)}) collective-permute-start(f32[4,8,1024]{2,1,0:T(8,128)S(1)} %get-tuple-element.21), channel_id=1, source_target_pairs={{0,12},{4,8},{8,4},{12,0},{1,13},{5,9},{9,5},{13,1},{2,14},{6,10},... | collective-permute-start | bytes 393224 | tf_op jit(solution)/shard_map/ppermute | solution.py:279
  149.9 9.0 %collective-permute-start.9 = (f32[4,8,1024]{2,1,0:T(8,128)S(1)}, f32[4,8,1024]{2,1,0:T(8,128)S(1)}, u32[]{:S(2)}, u32[]{:S(2)}) collective-permute-start(f32[4,8,1024]{2,1,0:T(8,128)S(1)} %get-tuple-element.22), channel_id=1, source_target_pairs={{0,8},{4,12},{8,0},{12,4},{1,9},{5,13},{9,1},{13,5},{2,10},{6,14},... | collective-permute-start | bytes 393224 | tf_op jit(solution)/shard_map/ppermute | solution.py:279
  152.9 6.3 %collective-permute-start.8 = (f32[4,8,1024]{2,1,0:T(8,128)S(1)}, f32[4,8,1024]{2,1,0:T(8,128)S(1)}, u32[]{:S(2)}, u32[]{:S(2)}) collective-permute-start(f32[4,8,1024]{2,1,0:T(8,128)S(1)} %get-tuple-element.23), channel_id=1, source_target_pairs={{0,4},{4,0},{8,12},{12,8},{1,5},{5,1},{9,13},{13,9},{2,6},{6,2},{1... | collective-permute-start | bytes 393224 | tf_op jit(solution)/shard_map/ppermute | solution.py:279
  159.2 14.6 %collective-permute-start.13 = (f32[1,8,1024]{2,1,0:T(8,128)S(1)}, f32[1,8,1024]{2,1,0:T(8,128)S(1)}, u32[]{:S(2)}, u32[]{:S(2)}) collective-permute-start(f32[1,8,1024]{2,1,0:T(8,128)S(1)} %get-tuple-element.24), channel_id=1, source_target_pairs={{0,96},{32,64},{64,32},{96,0},{1,97},{33,65},{65,33},{97,1},{2,98}... | collective-permute-start | bytes 98312 | tf_op jit(solution)/shard_map/ppermute | solution.py:279
  161.7 12.1 %collective-permute-start.12 = (f32[1,8,1024]{2,1,0:T(8,128)S(1)}, f32[1,8,1024]{2,1,0:T(8,128)S(1)}, u32[]{:S(2)}, u32[]{:S(2)}) collective-permute-start(f32[1,8,1024]{2,1,0:T(8,128)S(1)} %get-tuple-element.25), channel_id=1, source_target_pairs={{0,64},{32,96},{64,0},{96,32},{1,65},{33,97},{65,1},{97,33},{2,66}... | collective-permute-start | bytes 98312 | tf_op jit(solution)/shard_map/ppermute | solution.py:279
  162.2 11.6 %collective-permute-start.11 = (f32[1,8,1024]{2,1,0:T(8,128)S(1)}, f32[1,8,1024]{2,1,0:T(8,128)S(1)}, u32[]{:S(2)}, u32[]{:S(2)}) collective-permute-start(f32[1,8,1024]{2,1,0:T(8,128)S(1)} %get-tuple-element.26), channel_id=1, source_target_pairs={{0,32},{32,0},{64,96},{96,64},{1,33},{33,1},{65,97},{97,65},{2,34}... | collective-permute-start | bytes 98312 | tf_op jit(solution)/shard_map/ppermute | solution.py:279
  190.9 7.1 %collective-permute-start.14 = (f32[16,1024]{1,0:T(8,128)S(1)}, f32[16,1024]{1,0:T(8,128)S(1)}, u32[]{:S(2)}, u32[]{:S(2)}) collective-permute-start(f32[16,1024]{1,0:T(8,128)S(1)} %pad_maximum_fusion.1), channel_id=1, source_target_pairs={{0,128},{128,0},{1,129},{129,1},{2,130},{130,2},{3,131},{131,3},{4... | collective-permute-start | bytes 196616 | tf_op jit(solution)/shard_map/ppermute | solution.py:304
  198.0 6.3 %collective-permute-start.17 = (f32[16,1024]{1,0:T(8,128)S(1)}, f32[16,1024]{1,0:T(8,128)S(1)}, u32[]{:S(2)}, u32[]{:S(2)}) collective-permute-start(f32[16,1024]{1,0:T(8,128)S(1)} %fusion.3), channel_id=1, source_target_pairs={{0,3},{1,2},{2,1},{3,0},{4,7},{5,6},{6,5},{7,4},{8,11},{9,10},{10,... | collective-permute-start | bytes 196616 | tf_op jit(solution)/shard_map/ppermute | solution.py:279
  200.6 7.5 %collective-permute-start.16 = (f32[16,1024]{1,0:T(8,128)S(1)}, f32[16,1024]{1,0:T(8,128)S(1)}, u32[]{:S(2)}, u32[]{:S(2)}) collective-permute-start(f32[16,1024]{1,0:T(8,128)S(1)} %fusion.3), channel_id=1, source_target_pairs={{0,2},{1,3},{2,0},{3,1},{4,6},{5,7},{6,4},{7,5},{8,10},{9,11},{10,... | collective-permute-start | bytes 196616 | tf_op jit(solution)/shard_map/ppermute | solution.py:279
  204.3 3.8 %collective-permute-start.15 = (f32[16,1024]{1,0:T(8,128)S(1)}, f32[16,1024]{1,0:T(8,128)S(1)}, u32[]{:S(2)}, u32[]{:S(2)}) collective-permute-start(f32[16,1024]{1,0:T(8,128)S(1)} %fusion.3), channel_id=1, source_target_pairs={{0,1},{1,0},{2,3},{3,2},{4,5},{5,4},{6,7},{7,6},{8,9},{9,8},{10,11... | collective-permute-start | bytes 196616 | tf_op jit(solution)/shard_map/ppermute | solution.py:279
  220.4 6.1 %collective-permute-start.18 = (bf16[16,16,1024]{2,1,0:T(8,128)(2,1)S(1)}, bf16[16,16,1024]{2,1,0:T(8,128)(2,1)S(1)}, u32[]{:S(2)}, u32[]{:S(2)}) collective-permute-start(bf16[16,16,1024]{2,1,0:T(8,128)(2,1)S(1)} %all_to_all.26.mine_ref), channel_id=1, source_target_pairs={{0,16},{16,0},{1,17},{17,1},{2,18},{18,2},{3,19},{19,3},{4,20},{20... | collective-permute-start | bytes 1572872 | tf_op jit(solution)/shard_map/ppermute | solution.py:304

commit v12 on v11

--- a/solution.py
+++ b/solution.py
@@ -1,5 +1,3 @@
-import functools
-
 import jax
 import jax.numpy as jnp
 from jax import lax
@@ -206,63 +204,63 @@
     )(place, ritz, cells)
 
 
-def remove_kernel(core_ref, mine_ref, other_ref, ritz_ref, *refs):
-    out_ref = refs[-1]
-    blocks, rows, vectors, lanes = refs[0].shape
-    mine = mine_ref[...].reshape(blocks * vectors // 2, -1)
-    other = other_ref[...].reshape(blocks * vectors // 2, -1)
-    first = core_ref[0] == 0
-    coeffs = jnp.concatenate(
-        [jnp.where(first, mine, other), jnp.where(first, other, mine)], axis=0
-    )
-
-    def remove(cells_ref):
-        flat = out_ref.reshape(blocks * vectors * rows, lanes)
-        for r in range(0, rows, STEP):
-            removed = lax.dot_general(
-                coeffs,
-                ritz_ref[pl.ds(pl.program_id(1) * rows + r, STEP)].reshape(STEP * lanes, -1),
-                (((1,), (1,)), ((), ())),
-                preferred_element_type=f32,
-            )
+def remove_kernel(half_ref, coeffs_ref, ritz_ref, *refs):
+    out_ref, cells_refs = refs[-1], refs[:CHUNKS]
+    blocks, rows, vectors, lanes = cells_refs[0].shape
+    near, size, kept = coeffs_ref.shape
+    size = size // CHUNKS
+    coeffs = coeffs_ref[...].reshape(near * CHUNKS * size, kept)
+    flat = out_ref.reshape(blocks * CHUNKS * vectors * rows, lanes)
+    for r in range(0, rows, STEP):
+        removed = lax.dot_general(
+            coeffs,
+            ritz_ref[pl.ds(pl.program_id(0) * rows + r, STEP)].reshape(STEP * lanes, -1),
+            (((1,), (1,)), ((), ())),
+            preferred_element_type=f32,
+        )
+        for j in range(near * CHUNKS):
+            chunk, row = j % CHUNKS, j // CHUNKS * size
+            block, vector = row // vectors, row % vectors
             for k in range(STEP):
-                for i in range(blocks):
-                    held = cells_ref[i, r + k].astype(f32)
-                    part = removed[i * vectors : (i + 1) * vectors, k * lanes : (k + 1) * lanes]
-                    at = pl.ds(i * vectors * rows + r + k, vectors, stride=rows)
-                    flat[at, :] = held - part
-
-    for k, cells_ref in enumerate(refs[:-1]):
-        pl.when(pl.program_id(0) == k)(functools.partial(remove, cells_ref))
-
-
-def residual(core, mine, other, ritz, held):
+                held = cells_refs[chunk][block, r + k, vector : vector + size].astype(f32)
+                part = removed[j * size : (j + 1) * size, k * lanes : (k + 1) * lanes]
+                place = (block * CHUNKS + chunk) * vectors + vector
+                flat[pl.ds(place * rows + r + k, size, stride=rows), :] = held - part
+
+
+def residual(half, coeffs, ritz, held, out):
     blocks, rows, vectors, lanes = held[0].shape
-    near, _, kept = mine.shape
-    chunks = len(held)
-    size = mine.shape[1] // chunks
-    coeffs = pl.BlockSpec((near, size, kept), lambda k, g: (0, k, 0))
-    part = rows // 2
-    cells = pl.BlockSpec((blocks, part, vectors, lanes), lambda k, g: (0, g, 0, 0))
+    blocks, part = blocks // 2, rows // 2
+    cells = pl.BlockSpec((blocks, part, vectors, lanes), lambda g, half: (half[0], g, 0, 0))
+    specs = [
+        pl.BlockSpec(coeffs.shape, lambda g, half: (0, 0, 0)),
+        pl.BlockSpec(memory_space=pltpu.VMEM),
+        *([cells] * CHUNKS),
+    ]
+    operands = [half, coeffs, ritz, *held]
+    if out is not None:
+        specs.append(pl.BlockSpec(memory_space=pl.ANY))
+        operands.append(out)
+    count = CHUNKS * vectors
     return pl.pallas_call(
         remove_kernel,
-        out_shape=jax.ShapeDtypeStruct((blocks, chunks * vectors, rows, lanes), f32),
-        grid=(chunks, 2),
-        in_specs=[
-            pl.BlockSpec(memory_space=pltpu.SMEM),
-            coeffs,
-            coeffs,
-            pl.BlockSpec(memory_space=pltpu.VMEM),
-            *([cells] * chunks),
-        ],
-        out_specs=pl.BlockSpec((blocks, vectors, part, lanes), lambda k, g: (0, k, g, 0)),
+        out_shape=jax.ShapeDtypeStruct((2 * blocks, count, rows, lanes), f32),
+        grid_spec=pltpu.PrefetchScalarGridSpec(
+            num_scalar_prefetch=1,
+            grid=(2,),
+            in_specs=specs,
+            out_specs=pl.BlockSpec(
+                (blocks, count, part, lanes), lambda g, half: (half[0], 0, g, 0)
+            ),
+        ),
+        input_output_aliases={} if out is None else {len(operands) - 1: 0},
         compiler_params=pltpu.CompilerParams(vmem_limit_bytes=24 << 20),
         cost_estimate=pl.CostEstimate(
-            flops=2 * chunks * blocks * vectors * rows * lanes * kept,
-            bytes_accessed=11 << 20,
+            flops=2 * count * blocks * rows * lanes * ritz.shape[2],
+            bytes_accessed=4 << 20,
             transcendentals=0,
         ),
-    )(core, mine, other, ritz, *held)
+    )(*operands)
 
 
 def total_of(terms):
@@ -351,7 +349,8 @@
         parts.append(near_sum(partial))
     mine, other = summed(parts)
     core = lax.axis_index("c").reshape(1).astype(jnp.int32)
-    out = residual(core, mine, other, kept[0], held)
+    out = residual(core, mine, kept[0], held, None)
+    out = residual(1 - core, other, kept[0], held, out)
     return out.reshape(-1, *coefficient.shape)
 
 

time: 232 us -> 231 us (level)
    pallas_call x1 -> x2, Pallas kernels: 5.04 us -> 5.44 us  [residual(): pl.pallas_call(remove_kernel, out_shape=jax.ShapeDtypeStruct((2 * blocks,...]
  transfers between devices with their start and end apart: 22 -> 22, of which waited for: 11 -> 10; matrix products, arithmetic and copies ran while one was open for 0% -> 0% of each run, Pallas kernels for 11% -> 13%
where the time goes in v12:
time: 231 us; the launch traced here: 230 us
  waiting for transfers between devices  87.5 us (38%)
  starting transfers between devices  66.5 us (29%)
  Pallas kernels  44.9 us (19%)
  blocking collectives  29.2 us (13%)
    ppermute x3, waiting for transfers between devices, swap_ends(): from_above = lax.ppermute(low, DOM, [(i + 1, i) for i in range(count - 1)])  32.9 us
    ppermute x3, waiting for transfers between devices, swap_ends(): from_below = lax.ppermute(high, DOM, [(i, i + 1) for i in range(count - 1)])  28.4 us
    pallas_call x2, Pallas kernels, filtered(): pl.pallas_call(filter_kernel, out_shape=jax.ShapeDtypeStruct((rows // 2,...  26.5 us
    all_to_all x2, starting transfers between devices, pipeline(): held.append(lax.all_to_all(blocks, VEC, 0, 0, tiled=True))  20.9 us
    all_to_all x1, blocking collectives, near_sum(): blocks = lax.all_to_all(partial, NEAR, 0, 0, tiled=True)  17 us
    ppermute x3, starting transfers between devices, swapped(): return lax.ppermute(value, axis, [(0, 1), (1, 0)])  13.2 us
    ppermute x10, starting transfers between devices, traded(): lax.ppermute(blocks[k], axis, [(i, i ^ k) for i in range(count)])  13.1 us
    all_to_all x1, blocking collectives, from_everyone(): return lax.all_to_all(copies, axis, split_axis=0, concat_axis=0, tiled=True)  12.2 us
  transfers between devices with their start and end apart: 22, of which 10 were waited for; matrix products, arithmetic and copies ran while one was open for 0% of the time, Pallas kernels for 13%

profile of v12, /device:TPU:1, one launch (start us, length us, event | category | flops | bytes accessed | tf_op | source)
XLA Modules:
  0.0 230.3 jit_solution(631799375094215774)
XLA Ops:
  0.0 7.7 %collective-permute-start.2 = (f32[8,2,128]{2,1,0:T(2,128)}, f32[8,2,128]{2,1,0:T(2,128)S(1)}, u32[]{:S(2)}, u32[]{:S(2)}) collective-permute-start(f32[8,2,128]{2,1,0:T(2,128)} %param.4), channel_id=1, source_target_pairs={{0,128},{128,0},{1,129},{129,1},{2,130},{130,2},{3,131},{131,3},{4... | collective-permute-start | bytes 24584 | tf_op jit(solution)/shard_map/ppermute | solution.py:302
  7.7 1.2 collective-permute-done.2
  9.0 0.7 select_bitcast_fusion.1
  9.7 0.7 broadcast_in_dim.6
  10.4 5.8 %all-to-all-start = ((f32[8,2,8,2,128]{4,3,1,2,0:T(2,128)}), f32[8,2,8,2,128]{4,3,1,2,0:T(2,128)S(1)}, u32[]{:S(2)}, u32[]{:S(2)}) async-start(f32[8,2,8,2,128]{4,3,1,2,0:T(2,128)} %broadcast_in_dim.6), calls=%async_computation | async-start | bytes 262144 | tf_op jit(solution)/shard_map/all_to_all | solution.py:307
  16.2 2.4 %shard_map.40 = (bf16[4,32,16,128]{3,2,1,0:T(8,128)(2,1)S(1)}, bf16[4,32,16,128]{3,2,1,0:T(8,128)(2,1)S(1)}) custom-call(f32[32,256,128]{2,1,0:T(8,128)} %bitcast.18, f32[32,256,128]{2,1,0:T(8,128)} %bitcast.19), custom_call_target="tpu_custom_call" | custom-call | flops 524288 | bytes 3145728 | tf_op jit(solution)/shard_map/pallas_call | solution.py:37
  18.7 2.7 %collective-permute-start.5 = (bf16[4,32,16,128]{3,2,1,0:T(8,128)(2,1)S(1)}, bf16[4,32,16,128]{3,2,1,0:T(8,128)(2,1)S(1)}, u32[]{:S(2)}, u32[]{:S(2)}) collective-permute-start(bf16[4,32,16,128]{3,2,1,0:T(8,128)(2,1)S(1)} %get-tuple-element.16), channel_id=1, source_target_pairs={{0,1},{1,2},{2,3},{3,4},{4,5},{5,6},{6,7},{7,8},{8,9},{9,10},{10,1... | collective-permute-start | bytes 1572872 | tf_op jit(solution)/shard_map/ppermute | solution.py:312
  21.3 1.3 collective-permute-start.6
  22.7 0.1 add_bitcast_fusion
  22.8 1.3 collective-permute-start.4
  24.1 4.6 %collective-permute-start.3 = (f32[4,32,128]{2,1,0:T(8,128)S(1)}, f32[4,32,128]{2,1,0:T(8,128)S(1)}, u32[]{:S(2)}, u32[]{:S(2)}) collective-permute-start(f32[4,32,128]{2,1,0:T(8,128)S(1)} %bitcast.27), channel_id=1, source_target_pairs={{0,1},{1,2},{2,3},{3,4},{4,5},{5,6},{6,7},{7,8},{8,9},{9,10},{10,1... | collective-permute-start | bytes 196616 | tf_op jit(solution)/shard_map/ppermute | solution.py:312
  28.7 0.1 add_convert_fusion.1.ends_ref
  28.9 20.7 %collective-permute-done.4 = f32[4,32,128]{2,1,0:T(8,128)S(1)} collective-permute-done((f32[4,32,128]{2,1,0:T(8,128)S(1)}, f32[4,32,128]{2,1,0:T(8,128)S(1)}, u32[]{:S(2)}, u32[]{:S(2)}) %collective-permute-start.4) | collective-permute-done | bytes 65568 | tf_op jit(solution)/shard_map/ppermute | solution.py:313
  49.7 13.3 %shard_map.41 = bf16[16,16,16,128]{3,2,1,0:T(8,128)(2,1)} custom-call(s32[2]{0:T(128)S(1)} %add_convert_fusion.1.ends_ref, f32[32,256,128]{2,1,0:T(8,128)} %bitcast.20, bf16[4,32,16,128]{3,2,1,0:T(8,128)(2,1)S(1)} %collective-permute-done.5.low_ref, bf16[4,32,16,128]{3,2,1,0:T(8,128)(2,1)S(1)} %collective-permute-done.6.high_ref, ...), custom_call_target="tpu_custom_call" | custom-call | flops 34603008 | bytes 5242880 | tf_op jit(solution)/shard_map/pallas_call | solution.py:132
  62.9 11.1 %all-to-all-start.2 = ((bf16[16,16,16,128]{3,2,1,0:T(8,128)(2,1)}), bf16[16,16,16,128]{3,2,1,0:T(8,128)(2,1)S(1)}, u32[]{:S(2)}, u32[]{:S(2)}) async-start(bf16[16,16,16,128]{3,2,1,0:T(8,128)(2,1)} %shard_map.41), calls=%async_computation.2 | async-start | bytes 2097152 | tf_op jit(solution)/shard_map/all_to_all | solution.py:342
  74.0 2.4 %shard_map.37 = (bf16[4,32,16,128]{3,2,1,0:T(8,128)(2,1)S(1)}, bf16[4,32,16,128]{3,2,1,0:T(8,128)(2,1)S(1)}) custom-call(f32[32,256,128]{2,1,0:T(8,128)} %bitcast.21, f32[32,256,128]{2,1,0:T(8,128)} %bitcast.22), custom_call_target="tpu_custom_call" | custom-call | flops 524288 | bytes 3145728 | tf_op jit(solution)/shard_map/pallas_call | solution.py:37
  76.4 2.3 collective-permute-start
  78.7 1.3 collective-permute-start.1
  80.0 28.4 %collective-permute-done.low_ref = bf16[4,32,16,128]{3,2,1,0:T(8,128)(2,1)S(1)} collective-permute-done((bf16[4,32,16,128]{3,2,1,0:T(8,128)(2,1)S(1)}, bf16[4,32,16,128]{3,2,1,0:T(8,128)(2,1)S(1)}, u32[]{:S(2)}, u32[]{:S(2)}) %collective-permute-start) | collective-permute-done | bytes 524320 | tf_op jit(solution)/shard_map/ppermute | solution.py:312
  108.4 12.1 %collective-permute-done.1.high_ref = bf16[4,32,16,128]{3,2,1,0:T(8,128)(2,1)S(1)} collective-permute-done((bf16[4,32,16,128]{3,2,1,0:T(8,128)(2,1)S(1)}, bf16[4,32,16,128]{3,2,1,0:T(8,128)(2,1)S(1)}, u32[]{:S(2)}, u32[]{:S(2)}) %collective-permute-start.1) | collective-permute-done | bytes 524320 | tf_op jit(solution)/shard_map/ppermute | solution.py:313
  120.5 13.2 %shard_map.38 = bf16[16,16,16,128]{3,2,1,0:T(8,128)(2,1)} custom-call(s32[2]{0:T(128)S(1)} %add_convert_fusion.1.ends_ref, f32[32,256,128]{2,1,0:T(8,128)} %bitcast.23, bf16[4,32,16,128]{3,2,1,0:T(8,128)(2,1)S(1)} %collective-permute-done.low_ref, bf16[4,32,16,128]{3,2,1,0:T(8,128)(2,1)S(1)} %collective-permute-done.1.high_ref, ...), custom_call_target="tpu_custom_call" | custom-call | flops 34603008 | bytes 5242880 | tf_op jit(solution)/shard_map/pallas_call | solution.py:132
  133.8 9.8 %all-to-all-start.1 = ((bf16[16,16,16,128]{3,2,1,0:T(8,128)(2,1)}), bf16[16,16,16,128]{3,2,1,0:T(8,128)(2,1)S(1)}, u32[]{:S(2)}, u32[]{:S(2)}) async-start(bf16[16,16,16,128]{3,2,1,0:T(8,128)(2,1)} %shard_map.38), calls=%async_computation.1 | async-start | bytes 2097152 | tf_op jit(solution)/shard_map/all_to_all | solution.py:342
  143.6 4.0 %shard_map.42 = f32[32,8,1024]{2,1,0:T(8,128)S(1)} custom-call(s32[1]{0:T(128)} %bitcast.1.place_ref, bf16[16,128,1024]{2,1,0:T(8,128)(2,1)} %bitcast.24, bf16[16,16,16,128]{3,2,1,0:T(8,128)(2,1)S(1)} %all-to-all-done.2.cells_ref.refs_0_), custom_call_target="tpu_custom_call" | custom-call | flops 1073741824 | bytes 7340032 | tf_op jit(solution)/shard_map/pallas_call | solution.py:189
  147.7 0.2 collective-permute-start.7
  147.9 1.8 collective-permute-done.7
  149.7 0.1 slice_add_fusion
  149.8 0.1 collective-permute-start.10
  149.9 3.0 %collective-permute-start.9 = (f32[4,8,1024]{2,1,0:T(8,128)S(1)}, f32[4,8,1024]{2,1,0:T(8,128)S(1)}, u32[]{:S(2)}, u32[]{:S(2)}) collective-permute-start(f32[4,8,1024]{2,1,0:T(8,128)S(1)} %get-tuple-element.22), channel_id=1, source_target_pairs={{0,8},{4,12},{8,0},{12,4},{1,9},{5,13},{9,1},{13,5},{2,10},{6,14},... | collective-permute-start | bytes 393224 | tf_op jit(solution)/shard_map/ppermute | solution.py:277
  152.9 0.3 collective-permute-start.8
  153.1 5.8 %collective-permute-done.10 = f32[4,8,1024]{2,1,0:T(8,128)S(1)} collective-permute-done((f32[4,8,1024]{2,1,0:T(8,128)S(1)}, f32[4,8,1024]{2,1,0:T(8,128)S(1)}, u32[]{:S(2)}, u32[]{:S(2)}) %collective-permute-start.10) | collective-permute-done | bytes 131104 | tf_op jit(solution)/shard_map/ppermute | solution.py:277
  158.9 0.2 collective-permute-done.8
  159.2 2.5 %collective-permute-start.13 = (f32[1,8,1024]{2,1,0:T(8,128)S(1)}, f32[1,8,1024]{2,1,0:T(8,128)S(1)}, u32[]{:S(2)}, u32[]{:S(2)}) collective-permute-start(f32[1,8,1024]{2,1,0:T(8,128)S(1)} %get-tuple-element.24), channel_id=1, source_target_pairs={{0,96},{32,64},{64,32},{96,0},{1,97},{33,65},{65,33},{97,1},{2,98}... | collective-permute-start | bytes 98312 | tf_op jit(solution)/shard_map/ppermute | solution.py:277
  161.7 0.6 collective-permute-start.12
  162.2 0.3 collective-permute-start.11
  162.5 7.2 %all-to-all-done.1.cells_ref.refs_1_ = bf16[16,16,16,128]{3,2,1,0:T(8,128)(2,1)S(1)} async-done(((bf16[16,16,16,128]{3,2,1,0:T(8,128)(2,1)}), bf16[16,16,16,128]{3,2,1,0:T(8,128)(2,1)S(1)}, u32[]{:S(2)}, u32[]{:S(2)}) %all-to-all-start.1) | async-done | bytes 1048608 | tf_op jit(solution)/shard_map/all_to_all | solution.py:342
  169.7 4.1 %shard_map.39 = (bf16[32,8,1024]{2,1,0:T(8,128)(2,1)S(1)}, bf16[16,128,1024]{2,1,0:T(8,128)(2,1)S(1)}) custom-call(s32[1]{0:T(128)} %bitcast.1.place_ref, bf16[16,128,1024]{2,1,0:T(8,128)(2,1)} %bitcast.25, bf16[16,16,16,128]{3,2,1,0:T(8,128)(2,1)S(1)} %all-to-all-done.1.cells_ref.refs_1_), custom_call_target="tpu_custom_call" | custom-call | flops 1073741824 | bytes 7340032 | tf_op jit(solution)/shard_map/pallas_call | solution.py:189
  173.8 17.0 %all_to_all.25 = bf16[32,8,1024]{2,1,0:T(8,128)(2,1)S(1)} all-to-all(bf16[32,8,1024]{2,1,0:T(8,128)(2,1)S(1)} %get-tuple-element.19), channel_id=1, replica_groups=mesh['zh'=2,'x'=4,'c'=2,'y'=4,'zl'=4] {'c','y','x'}, dimensions={0} | all-to-all | bytes 1048576 | tf_op jit(solution)/shard_map/all_to_all | solution.py:285
  190.8 0.1 convert_reduce_fusion
  190.9 0.9 collective-permute-start.14
  191.9 6.2 %collective-permute-done.14 = f32[16,1024]{1,0:T(8,128)S(1)} collective-permute-done((f32[16,1024]{1,0:T(8,128)S(1)}, f32[16,1024]{1,0:T(8,128)S(1)}, u32[]{:S(2)}, u32[]{:S(2)}) %collective-permute-start.14) | collective-permute-done | bytes 65568 | tf_op jit(solution)/shard_map/ppermute | solution.py:302
  198.0 2.6 %collective-permute-start.17 = (f32[16,1024]{1,0:T(8,128)S(1)}, f32[16,1024]{1,0:T(8,128)S(1)}, u32[]{:S(2)}, u32[]{:S(2)}) collective-permute-start(f32[16,1024]{1,0:T(8,128)S(1)} %fusion.3), channel_id=1, source_target_pairs={{0,3},{1,2},{2,1},{3,0},{4,7},{5,6},{6,5},{7,4},{8,11},{9,10},{10,... | collective-permute-start | bytes 196616 | tf_op jit(solution)/shard_map/ppermute | solution.py:277
  200.6 3.7 %collective-permute-start.16 = (f32[16,1024]{1,0:T(8,128)S(1)}, f32[16,1024]{1,0:T(8,128)S(1)}, u32[]{:S(2)}, u32[]{:S(2)}) collective-permute-start(f32[16,1024]{1,0:T(8,128)S(1)} %fusion.3), channel_id=1, source_target_pairs={{0,2},{1,3},{2,0},{3,1},{4,6},{5,7},{6,4},{7,5},{8,10},{9,11},{10,... | collective-permute-start | bytes 196616 | tf_op jit(solution)/shard_map/ppermute | solution.py:277
  204.3 3.8 %collective-permute-done.16 = f32[16,1024]{1,0:T(8,128)S(1)} collective-permute-done((f32[16,1024]{1,0:T(8,128)S(1)}, f32[16,1024]{1,0:T(8,128)S(1)}, u32[]{:S(2)}, u32[]{:S(2)}) %collective-permute-start.16) | collective-permute-done | bytes 65568 | tf_op jit(solution)/shard_map/ppermute | solution.py:277
  208.1 0.1 broadcast_in_dim.7
  208.2 12.2 %all_to_all.26.coeffs_ref = bf16[16,16,1024]{2,1,0:T(8,128)(2,1)S(1)} all-to-all(bf16[16,16,1024]{2,1,0:T(8,128)(2,1)S(1)} %broadcast_in_dim.7), channel_id=1, replica_groups=mesh['zh'=2,'x'=4,'c'=2,'y'=4,'zl'=4] {'y','x'}, dimensions={0} | all-to-all | bytes 1048576 | tf_op jit(solution)/shard_map/all_to_all | solution.py:307
  220.4 4.5 %collective-permute-start.18 = (bf16[16,16,1024]{2,1,0:T(8,128)(2,1)S(1)}, bf16[16,16,1024]{2,1,0:T(8,128)(2,1)S(1)}, u32[]{:S(2)}, u32[]{:S(2)}) collective-permute-start(bf16[16,16,1024]{2,1,0:T(8,128)(2,1)S(1)} %all_to_all.26.coeffs_ref), channel_id=1, source_target_pairs={{0,16},{16,0},{1,17},{17,1},{2,18},{18,2},{3,19},{19,3},{4,20},{20... | collective-permute-start | bytes 1572872 | tf_op jit(solution)/shard_map/ppermute | solution.py:302
  224.9 2.7 %shard_map.43.refs_2_ = f32[16,32,16,128]{3,2,1,0:T(8,128)} custom-call(s32[1]{0:T(128)} %bitcast.half_ref, bf16[16,16,1024]{2,1,0:T(8,128)(2,1)S(1)} %all_to_all.26.coeffs_ref, bf16[16,128,1024]{2,1,0:T(8,128)(2,1)S(1)} %get-tuple-element.20.ritz_ref, bf16[16,16,16,128]{3,2,1,0:T(8,128)(2,1)S(1)} %all-to-all-done.2.cells_ref.refs_0_, ...), custom_call_target="tpu_custom_call" | custom-call | flops 1073741824 | bytes 4194304 | tf_op jit(solution)/shard_map/pallas_call | solution.py:245
  227.6 2.7 %shard_map.44 = f32[16,32,16,128]{3,2,1,0:T(8,128)} custom-call(s32[1]{0:T(128)S(6)} %sub.3.half_ref, bf16[16,16,1024]{2,1,0:T(8,128)(2,1)S(1)} %collective-permute-done.18.coeffs_ref, bf16[16,128,1024]{2,1,0:T(8,128)(2,1)S(1)} %get-tuple-element.20.ritz_ref, ...), custom_call_target="tpu_custom_call", output_to_operand_aliasing={{}: (5, {})} | custom-call | flops 1073741824 | bytes 4194304 | tf_op jit(solution)/shard_map/pallas_call | solution.py:245
  (28 shorter events, 0.3 us)
Async XLA Ops:
  0.0 9.0 %collective-permute-start.2 = (f32[8,2,128]{2,1,0:T(2,128)}, f32[8,2,128]{2,1,0:T(2,128)S(1)}, u32[]{:S(2)}, u32[]{:S(2)}) collective-permute-start(f32[8,2,128]{2,1,0:T(2,128)} %param.4), channel_id=1, source_target_pairs={{0,128},{128,0},{1,129},{129,1},{2,130},{130,2},{3,131},{131,3},{4... | collective-permute-start | bytes 24584 | tf_op jit(solution)/shard_map/ppermute | solution.py:302
  10.4 12.3 %all-to-all-start = ((f32[8,2,8,2,128]{4,3,1,2,0:T(2,128)}), f32[8,2,8,2,128]{4,3,1,2,0:T(2,128)S(1)}, u32[]{:S(2)}, u32[]{:S(2)}) async-start(f32[8,2,8,2,128]{4,3,1,2,0:T(2,128)} %broadcast_in_dim.6), calls=%async_computation | async-start | bytes 262144 | tf_op jit(solution)/shard_map/all_to_all | solution.py:307
  18.7 31.0 %collective-permute-start.5 = (bf16[4,32,16,128]{3,2,1,0:T(8,128)(2,1)S(1)}, bf16[4,32,16,128]{3,2,1,0:T(8,128)(2,1)S(1)}, u32[]{:S(2)}, u32[]{:S(2)}) collective-permute-start(bf16[4,32,16,128]{3,2,1,0:T(8,128)(2,1)S(1)} %get-tuple-element.16), channel_id=1, source_target_pairs={{0,1},{1,2},{2,3},{3,4},{4,5},{5,6},{6,7},{7,8},{8,9},{9,10},{10,1... | collective-permute-start | bytes 1572872 | tf_op jit(solution)/shard_map/ppermute | solution.py:312
  21.3 28.3 %collective-permute-start.6 = (bf16[4,32,16,128]{3,2,1,0:T(8,128)(2,1)S(1)}, bf16[4,32,16,128]{3,2,1,0:T(8,128)(2,1)S(1)}, u32[]{:S(2)}, u32[]{:S(2)}) collective-permute-start(bf16[4,32,16,128]{3,2,1,0:T(8,128)(2,1)S(1)} %get-tuple-element.17), channel_id=1, source_target_pairs={{1,0},{2,1},{3,2},{4,3},{5,4},{6,5},{7,6},{8,7},{9,8},{10,9},{11,1... | collective-permute-start | bytes 1572872 | tf_op jit(solution)/shard_map/ppermute | solution.py:313
  22.8 26.8 %collective-permute-start.4 = (f32[4,32,128]{2,1,0:T(8,128)S(1)}, f32[4,32,128]{2,1,0:T(8,128)S(1)}, u32[]{:S(2)}, u32[]{:S(2)}) collective-permute-start(f32[4,32,128]{2,1,0:T(8,128)S(1)} %bitcast.28), channel_id=1, source_target_pairs={{1,0},{2,1},{3,2},{4,3},{5,4},{6,5},{7,6},{8,7},{9,8},{10,9},{11,1... | collective-permute-start | bytes 196616 | tf_op jit(solution)/shard_map/ppermute | solution.py:313
  24.1 25.5 %collective-permute-start.3 = (f32[4,32,128]{2,1,0:T(8,128)S(1)}, f32[4,32,128]{2,1,0:T(8,128)S(1)}, u32[]{:S(2)}, u32[]{:S(2)}) collective-permute-start(f32[4,32,128]{2,1,0:T(8,128)S(1)} %bitcast.27), channel_id=1, source_target_pairs={{0,1},{1,2},{2,3},{3,4},{4,5},{5,6},{6,7},{7,8},{8,9},{9,10},{10,1... | collective-permute-start | bytes 196616 | tf_op jit(solution)/shard_map/ppermute | solution.py:312
  62.9 70.8 %all-to-all-start.2 = ((bf16[16,16,16,128]{3,2,1,0:T(8,128)(2,1)}), bf16[16,16,16,128]{3,2,1,0:T(8,128)(2,1)S(1)}, u32[]{:S(2)}, u32[]{:S(2)}) async-start(bf16[16,16,16,128]{3,2,1,0:T(8,128)(2,1)} %shard_map.41), calls=%async_computation.2 | async-start | bytes 2097152 | tf_op jit(solution)/shard_map/all_to_all | solution.py:342
  76.4 32.0 %collective-permute-start = (bf16[4,32,16,128]{3,2,1,0:T(8,128)(2,1)S(1)}, bf16[4,32,16,128]{3,2,1,0:T(8,128)(2,1)S(1)}, u32[]{:S(2)}, u32[]{:S(2)}) collective-permute-start(bf16[4,32,16,128]{3,2,1,0:T(8,128)(2,1)S(1)} %get-tuple-element.13), channel_id=1, source_target_pairs={{0,1},{1,2},{2,3},{3,4},{4,5},{5,6},{6,7},{7,8},{8,9},{9,10},{10,1... | collective-permute-start | bytes 1572872 | tf_op jit(solution)/shard_map/ppermute | solution.py:312
  78.7 41.8 %collective-permute-start.1 = (bf16[4,32,16,128]{3,2,1,0:T(8,128)(2,1)S(1)}, bf16[4,32,16,128]{3,2,1,0:T(8,128)(2,1)S(1)}, u32[]{:S(2)}, u32[]{:S(2)}) collective-permute-start(bf16[4,32,16,128]{3,2,1,0:T(8,128)(2,1)S(1)} %get-tuple-element.14), channel_id=1, source_target_pairs={{1,0},{2,1},{3,2},{4,3},{5,4},{6,5},{7,6},{8,7},{9,8},{10,9},{11,1... | collective-permute-start | bytes 1572872 | tf_op jit(solution)/shard_map/ppermute | solution.py:313
  133.8 35.9 %all-to-all-start.1 = ((bf16[16,16,16,128]{3,2,1,0:T(8,128)(2,1)}), bf16[16,16,16,128]{3,2,1,0:T(8,128)(2,1)S(1)}, u32[]{:S(2)}, u32[]{:S(2)}) async-start(bf16[16,16,16,128]{3,2,1,0:T(8,128)(2,1)} %shard_map.38), calls=%async_computation.1 | async-start | bytes 2097152 | tf_op jit(solution)/shard_map/all_to_all | solution.py:342
  147.7 2.0 collective-permute-start.7
  149.8 9.1 %collective-permute-start.10 = (f32[4,8,1024]{2,1,0:T(8,128)S(1)}, f32[4,8,1024]{2,1,0:T(8,128)S(1)}, u32[]{:S(2)}, u32[]{:S(2)}) collective-permute-start(f32[4,8,1024]{2,1,0:T(8,128)S(1)} %get-tuple-element.21), channel_id=1, source_target_pairs={{0,12},{4,8},{8,4},{12,0},{1,13},{5,9},{9,5},{13,1},{2,14},{6,10},... | collective-permute-start | bytes 393224 | tf_op jit(solution)/shard_map/ppermute | solution.py:277
  149.9 9.0 %collective-permute-start.9 = (f32[4,8,1024]{2,1,0:T(8,128)S(1)}, f32[4,8,1024]{2,1,0:T(8,128)S(1)}, u32[]{:S(2)}, u32[]{:S(2)}) collective-permute-start(f32[4,8,1024]{2,1,0:T(8,128)S(1)} %get-tuple-element.22), channel_id=1, source_target_pairs={{0,8},{4,12},{8,0},{12,4},{1,9},{5,13},{9,1},{13,5},{2,10},{6,14},... | collective-permute-start | bytes 393224 | tf_op jit(solution)/shard_map/ppermute | solution.py:277
  152.9 6.3 %collective-permute-start.8 = (f32[4,8,1024]{2,1,0:T(8,128)S(1)}, f32[4,8,1024]{2,1,0:T(8,128)S(1)}, u32[]{:S(2)}, u32[]{:S(2)}) collective-permute-start(f32[4,8,1024]{2,1,0:T(8,128)S(1)} %get-tuple-element.23), channel_id=1, source_target_pairs={{0,4},{4,0},{8,12},{12,8},{1,5},{5,1},{9,13},{13,9},{2,6},{6,2},{1... | collective-permute-start | bytes 393224 | tf_op jit(solution)/shard_map/ppermute | solution.py:277
  159.2 14.6 %collective-permute-start.13 = (f32[1,8,1024]{2,1,0:T(8,128)S(1)}, f32[1,8,1024]{2,1,0:T(8,128)S(1)}, u32[]{:S(2)}, u32[]{:S(2)}) collective-permute-start(f32[1,8,1024]{2,1,0:T(8,128)S(1)} %get-tuple-element.24), channel_id=1, source_target_pairs={{0,96},{32,64},{64,32},{96,0},{1,97},{33,65},{65,33},{97,1},{2,98}... | collective-permute-start | bytes 98312 | tf_op jit(solution)/shard_map/ppermute | solution.py:277
  161.7 12.1 %collective-permute-start.12 = (f32[1,8,1024]{2,1,0:T(8,128)S(1)}, f32[1,8,1024]{2,1,0:T(8,128)S(1)}, u32[]{:S(2)}, u32[]{:S(2)}) collective-permute-start(f32[1,8,1024]{2,1,0:T(8,128)S(1)} %get-tuple-element.25), channel_id=1, source_target_pairs={{0,64},{32,96},{64,0},{96,32},{1,65},{33,97},{65,1},{97,33},{2,66}... | collective-permute-start | bytes 98312 | tf_op jit(solution)/shard_map/ppermute | solution.py:277
  162.2 11.6 %collective-permute-start.11 = (f32[1,8,1024]{2,1,0:T(8,128)S(1)}, f32[1,8,1024]{2,1,0:T(8,128)S(1)}, u32[]{:S(2)}, u32[]{:S(2)}) collective-permute-start(f32[1,8,1024]{2,1,0:T(8,128)S(1)} %get-tuple-element.26), channel_id=1, source_target_pairs={{0,32},{32,0},{64,96},{96,64},{1,33},{33,1},{65,97},{97,65},{2,34}... | collective-permute-start | bytes 98312 | tf_op jit(solution)/shard_map/ppermute | solution.py:277
  190.9 7.1 %collective-permute-start.14 = (f32[16,1024]{1,0:T(8,128)S(1)}, f32[16,1024]{1,0:T(8,128)S(1)}, u32[]{:S(2)}, u32[]{:S(2)}) collective-permute-start(f32[16,1024]{1,0:T(8,128)S(1)} %pad_maximum_fusion.1), channel_id=1, source_target_pairs={{0,128},{128,0},{1,129},{129,1},{2,130},{130,2},{3,131},{131,3},{4... | collective-permute-start | bytes 196616 | tf_op jit(solution)/shard_map/ppermute | solution.py:302
  198.0 6.3 %collective-permute-start.17 = (f32[16,1024]{1,0:T(8,128)S(1)}, f32[16,1024]{1,0:T(8,128)S(1)}, u32[]{:S(2)}, u32[]{:S(2)}) collective-permute-start(f32[16,1024]{1,0:T(8,128)S(1)} %fusion.3), channel_id=1, source_target_pairs={{0,3},{1,2},{2,1},{3,0},{4,7},{5,6},{6,5},{7,4},{8,11},{9,10},{10,... | collective-permute-start | bytes 196616 | tf_op jit(solution)/shard_map/ppermute | solution.py:277
  200.6 7.5 %collective-permute-start.16 = (f32[16,1024]{1,0:T(8,128)S(1)}, f32[16,1024]{1,0:T(8,128)S(1)}, u32[]{:S(2)}, u32[]{:S(2)}) collective-permute-start(f32[16,1024]{1,0:T(8,128)S(1)} %fusion.3), channel_id=1, source_target_pairs={{0,2},{1,3},{2,0},{3,1},{4,6},{5,7},{6,4},{7,5},{8,10},{9,11},{10,... | collective-permute-start | bytes 196616 | tf_op jit(solution)/shard_map/ppermute | solution.py:277
  204.3 3.8 %collective-permute-start.15 = (f32[16,1024]{1,0:T(8,128)S(1)}, f32[16,1024]{1,0:T(8,128)S(1)}, u32[]{:S(2)}, u32[]{:S(2)}) collective-permute-start(f32[16,1024]{1,0:T(8,128)S(1)} %fusion.3), channel_id=1, source_target_pairs={{0,1},{1,0},{2,3},{3,2},{4,5},{5,4},{6,7},{7,6},{8,9},{9,8},{10,11... | collective-permute-start | bytes 196616 | tf_op jit(solution)/shard_map/ppermute | solution.py:277
  220.4 7.3 %collective-permute-start.18 = (bf16[16,16,1024]{2,1,0:T(8,128)(2,1)S(1)}, bf16[16,16,1024]{2,1,0:T(8,128)(2,1)S(1)}, u32[]{:S(2)}, u32[]{:S(2)}) collective-permute-start(bf16[16,16,1024]{2,1,0:T(8,128)(2,1)S(1)} %all_to_all.26.coeffs_ref), channel_id=1, source_target_pairs={{0,16},{16,0},{1,17},{17,1},{2,18},{18,2},{3,19},{19,3},{4,20},{20... | collective-permute-start | bytes 1572872 | tf_op jit(solution)/shard_map/ppermute | solution.py:302

commit v13 on v12

--- a/solution.py
+++ b/solution.py
@@ -16,6 +16,7 @@
 GROUP = 16
 CHUNKS = 2
 STEP = 4
+WIDE = 8
 
 
 def spread_kernel(first_ref, second_ref, low_ref, high_ref):
@@ -159,13 +160,13 @@
         total[...] = jnp.zeros_like(total)
 
     part = jnp.concatenate(
-        [cells_ref[:, k].reshape(-1, lanes) for k in range(STEP)], axis=1
+        [cells_ref[:, k].reshape(-1, lanes) for k in range(WIDE)], axis=1
     )
     total[...] += jnp.dot(
-        part, ritz_ref[...].reshape(STEP * lanes, -1), preferred_element_type=f32
+        part, ritz_ref[...].reshape(WIDE * lanes, -1), preferred_element_type=f32
     )
     for kept_ref in kept_refs:
-        kept_ref[pl.ds(STEP * step, STEP)] = ritz_ref[...]
+        kept_ref[pl.ds(WIDE * step, WIDE)] = ritz_ref[...]
 
     @pl.when(step == pl.num_programs(0) - 1)
     def _():
@@ -189,11 +190,11 @@
     return pl.pallas_call(
         project_kernel,
         out_shape=out_shape,
-        grid=(rows // STEP,),
+        grid=(rows // WIDE,),
         in_specs=[
             pl.BlockSpec(memory_space=pltpu.SMEM),
-            pl.BlockSpec((STEP, lanes, kept), lambda r: (r, 0, 0)),
-            pl.BlockSpec((blocks, STEP, vectors, lanes), lambda r: (0, r, 0, 0)),
+            pl.BlockSpec((WIDE, lanes, kept), lambda r: (r, 0, 0)),
+            pl.BlockSpec((blocks, WIDE, vectors, lanes), lambda r: (0, r, 0, 0)),
         ],
         out_specs=out_specs,
         scratch_shapes=[pltpu.VMEM((count, kept), f32)],

time: 231 us -> 231 us (level)
  transfers between devices with their start and end apart: 22 -> 22, of which waited for: 10 -> 11; matrix products, arithmetic and copies ran while one was open for 0% -> 0% of each run, Pallas kernels for 13% -> 12%
where the time goes in v13:
time: 231 us; the launch traced here: 230 us
  waiting for transfers between devices  89.2 us (39%)
  starting transfers between devices  65.9 us (29%)
  Pallas kernels  43.4 us (19%)
  blocking collectives  29.1 us (13%)
    ppermute x3, waiting for transfers between devices, swap_ends(): from_above = lax.ppermute(low, DOM, [(i + 1, i) for i in range(count - 1)])  32.9 us
    ppermute x3, waiting for transfers between devices, swap_ends(): from_below = lax.ppermute(high, DOM, [(i, i + 1) for i in range(count - 1)])  28.4 us
    pallas_call x2, Pallas kernels, filtered(): pl.pallas_call(filter_kernel, out_shape=jax.ShapeDtypeStruct((rows // 2,...  26.5 us
    all_to_all x2, starting transfers between devices, pipeline(): held.append(lax.all_to_all(blocks, VEC, 0, 0, tiled=True))  20.9 us
    all_to_all x1, blocking collectives, near_sum(): blocks = lax.all_to_all(partial, NEAR, 0, 0, tiled=True)  17 us
    ppermute x10, starting transfers between devices, traded(): lax.ppermute(blocks[k], axis, [(i, i ^ k) for i in range(count)])  13.1 us
    ppermute x3, starting transfers between devices, swapped(): return lax.ppermute(value, axis, [(0, 1), (1, 0)])  12.6 us
    all_to_all x1, blocking collectives, from_everyone(): return lax.all_to_all(copies, axis, split_axis=0, concat_axis=0, tiled=True)  12.1 us
  transfers between devices with their start and end apart: 22, of which 11 were waited for; matrix products, arithmetic and copies ran while one was open for 0% of the time, Pallas kernels for 12%

profile of v13, /device:TPU:1, one launch (start us, length us, event | category | flops | bytes accessed | tf_op | source)
XLA Modules:
  0.0 229.8 jit_solution(3079066619975460613)
XLA Ops:
  0.0 7.7 %collective-permute-start.2 = (f32[8,2,128]{2,1,0:T(2,128)}, f32[8,2,128]{2,1,0:T(2,128)S(1)}, u32[]{:S(2)}, u32[]{:S(2)}) collective-permute-start(f32[8,2,128]{2,1,0:T(2,128)} %param.4), channel_id=1, source_target_pairs={{0,128},{128,0},{1,129},{129,1},{2,130},{130,2},{3,131},{131,3},{4... | collective-permute-start | bytes 24584 | tf_op jit(solution)/shard_map/ppermute | solution.py:303
  7.7 1.2 collective-permute-done.2
  9.0 0.7 select_bitcast_fusion.1
  9.7 0.7 broadcast_in_dim.6
  10.4 5.8 %all-to-all-start = ((f32[8,2,8,2,128]{4,3,1,2,0:T(2,128)}), f32[8,2,8,2,128]{4,3,1,2,0:T(2,128)S(1)}, u32[]{:S(2)}, u32[]{:S(2)}) async-start(f32[8,2,8,2,128]{4,3,1,2,0:T(2,128)} %broadcast_in_dim.6), calls=%async_computation | async-start | bytes 262144 | tf_op jit(solution)/shard_map/all_to_all | solution.py:308
  16.2 2.4 %shard_map.40 = (bf16[4,32,16,128]{3,2,1,0:T(8,128)(2,1)S(1)}, bf16[4,32,16,128]{3,2,1,0:T(8,128)(2,1)S(1)}) custom-call(f32[32,256,128]{2,1,0:T(8,128)} %bitcast.18, f32[32,256,128]{2,1,0:T(8,128)} %bitcast.19), custom_call_target="tpu_custom_call" | custom-call | flops 524288 | bytes 3145728 | tf_op jit(solution)/shard_map/pallas_call | solution.py:38
  18.7 2.7 %collective-permute-start.5 = (bf16[4,32,16,128]{3,2,1,0:T(8,128)(2,1)S(1)}, bf16[4,32,16,128]{3,2,1,0:T(8,128)(2,1)S(1)}, u32[]{:S(2)}, u32[]{:S(2)}) collective-permute-start(bf16[4,32,16,128]{3,2,1,0:T(8,128)(2,1)S(1)} %get-tuple-element.16), channel_id=1, source_target_pairs={{0,1},{1,2},{2,3},{3,4},{4,5},{5,6},{6,7},{7,8},{8,9},{9,10},{10,1... | collective-permute-start | bytes 1572872 | tf_op jit(solution)/shard_map/ppermute | solution.py:313
  21.3 1.3 collective-permute-start.6
  22.7 0.1 add_bitcast_fusion
  22.8 1.3 collective-permute-start.4
  24.1 4.6 %collective-permute-start.3 = (f32[4,32,128]{2,1,0:T(8,128)S(1)}, f32[4,32,128]{2,1,0:T(8,128)S(1)}, u32[]{:S(2)}, u32[]{:S(2)}) collective-permute-start(f32[4,32,128]{2,1,0:T(8,128)S(1)} %bitcast.27), channel_id=1, source_target_pairs={{0,1},{1,2},{2,3},{3,4},{4,5},{5,6},{6,7},{7,8},{8,9},{9,10},{10,1... | collective-permute-start | bytes 196616 | tf_op jit(solution)/shard_map/ppermute | solution.py:313
  28.7 0.1 add_convert_fusion.1.ends_ref
  28.9 20.7 %collective-permute-done.4 = f32[4,32,128]{2,1,0:T(8,128)S(1)} collective-permute-done((f32[4,32,128]{2,1,0:T(8,128)S(1)}, f32[4,32,128]{2,1,0:T(8,128)S(1)}, u32[]{:S(2)}, u32[]{:S(2)}) %collective-permute-start.4) | collective-permute-done | bytes 65568 | tf_op jit(solution)/shard_map/ppermute | solution.py:314
  49.7 13.3 %shard_map.41 = bf16[16,16,16,128]{3,2,1,0:T(8,128)(2,1)} custom-call(s32[2]{0:T(128)S(1)} %add_convert_fusion.1.ends_ref, f32[32,256,128]{2,1,0:T(8,128)} %bitcast.20, bf16[4,32,16,128]{3,2,1,0:T(8,128)(2,1)S(1)} %collective-permute-done.5.low_ref, bf16[4,32,16,128]{3,2,1,0:T(8,128)(2,1)S(1)} %collective-permute-done.6.high_ref, ...), custom_call_target="tpu_custom_call" | custom-call | flops 34603008 | bytes 5242880 | tf_op jit(solution)/shard_map/pallas_call | solution.py:133
  62.9 11.1 %all-to-all-start.2 = ((bf16[16,16,16,128]{3,2,1,0:T(8,128)(2,1)}), bf16[16,16,16,128]{3,2,1,0:T(8,128)(2,1)S(1)}, u32[]{:S(2)}, u32[]{:S(2)}) async-start(bf16[16,16,16,128]{3,2,1,0:T(8,128)(2,1)} %shard_map.41), calls=%async_computation.2 | async-start | bytes 2097152 | tf_op jit(solution)/shard_map/all_to_all | solution.py:343
  74.0 2.4 %shard_map.37 = (bf16[4,32,16,128]{3,2,1,0:T(8,128)(2,1)S(1)}, bf16[4,32,16,128]{3,2,1,0:T(8,128)(2,1)S(1)}) custom-call(f32[32,256,128]{2,1,0:T(8,128)} %bitcast.21, f32[32,256,128]{2,1,0:T(8,128)} %bitcast.22), custom_call_target="tpu_custom_call" | custom-call | flops 524288 | bytes 3145728 | tf_op jit(solution)/shard_map/pallas_call | solution.py:38
  76.4 2.3 collective-permute-start
  78.7 1.3 collective-permute-start.1
  80.0 28.4 %collective-permute-done.low_ref = bf16[4,32,16,128]{3,2,1,0:T(8,128)(2,1)S(1)} collective-permute-done((bf16[4,32,16,128]{3,2,1,0:T(8,128)(2,1)S(1)}, bf16[4,32,16,128]{3,2,1,0:T(8,128)(2,1)S(1)}, u32[]{:S(2)}, u32[]{:S(2)}) %collective-permute-start) | collective-permute-done | bytes 524320 | tf_op jit(solution)/shard_map/ppermute | solution.py:313
  108.4 12.1 %collective-permute-done.1.high_ref = bf16[4,32,16,128]{3,2,1,0:T(8,128)(2,1)S(1)} collective-permute-done((bf16[4,32,16,128]{3,2,1,0:T(8,128)(2,1)S(1)}, bf16[4,32,16,128]{3,2,1,0:T(8,128)(2,1)S(1)}, u32[]{:S(2)}, u32[]{:S(2)}) %collective-permute-start.1) | collective-permute-done | bytes 524320 | tf_op jit(solution)/shard_map/ppermute | solution.py:314
  120.5 13.2 %shard_map.38 = bf16[16,16,16,128]{3,2,1,0:T(8,128)(2,1)} custom-call(s32[2]{0:T(128)S(1)} %add_convert_fusion.1.ends_ref, f32[32,256,128]{2,1,0:T(8,128)} %bitcast.23, bf16[4,32,16,128]{3,2,1,0:T(8,128)(2,1)S(1)} %collective-permute-done.low_ref, bf16[4,32,16,128]{3,2,1,0:T(8,128)(2,1)S(1)} %collective-permute-done.1.high_ref, ...), custom_call_target="tpu_custom_call" | custom-call | flops 34603008 | bytes 5242880 | tf_op jit(solution)/shard_map/pallas_call | solution.py:133
  133.8 9.8 %all-to-all-start.1 = ((bf16[16,16,16,128]{3,2,1,0:T(8,128)(2,1)}), bf16[16,16,16,128]{3,2,1,0:T(8,128)(2,1)S(1)}, u32[]{:S(2)}, u32[]{:S(2)}) async-start(bf16[16,16,16,128]{3,2,1,0:T(8,128)(2,1)} %shard_map.38), calls=%async_computation.1 | async-start | bytes 2097152 | tf_op jit(solution)/shard_map/all_to_all | solution.py:343
  143.6 3.2 %shard_map.42 = f32[32,8,1024]{2,1,0:T(8,128)S(1)} custom-call(s32[1]{0:T(128)} %bitcast.1.place_ref, bf16[16,128,1024]{2,1,0:T(8,128)(2,1)} %bitcast.24, bf16[16,16,16,128]{3,2,1,0:T(8,128)(2,1)S(1)} %all-to-all-done.2.cells_ref.refs_0_), custom_call_target="tpu_custom_call" | custom-call | flops 1073741824 | bytes 7340032 | tf_op jit(solution)/shard_map/pallas_call | solution.py:190
  146.8 0.2 collective-permute-start.7
  147.0 1.8 collective-permute-done.7
  148.8 0.1 slice_add_fusion
  148.9 0.1 collective-permute-start.10
  149.0 3.0 %collective-permute-start.9 = (f32[4,8,1024]{2,1,0:T(8,128)S(1)}, f32[4,8,1024]{2,1,0:T(8,128)S(1)}, u32[]{:S(2)}, u32[]{:S(2)}) collective-permute-start(f32[4,8,1024]{2,1,0:T(8,128)S(1)} %get-tuple-element.22), channel_id=1, source_target_pairs={{0,8},{4,12},{8,0},{12,4},{1,9},{5,13},{9,1},{13,5},{2,10},{6,14},... | collective-permute-start | bytes 393224 | tf_op jit(solution)/shard_map/ppermute | solution.py:278
  152.0 0.3 collective-permute-start.8
  152.3 5.8 %collective-permute-done.10 = f32[4,8,1024]{2,1,0:T(8,128)S(1)} collective-permute-done((f32[4,8,1024]{2,1,0:T(8,128)S(1)}, f32[4,8,1024]{2,1,0:T(8,128)S(1)}, u32[]{:S(2)}, u32[]{:S(2)}) %collective-permute-start.10) | collective-permute-done | bytes 131104 | tf_op jit(solution)/shard_map/ppermute | solution.py:278
  158.1 0.2 collective-permute-done.8
  158.3 2.5 %collective-permute-start.13 = (f32[1,8,1024]{2,1,0:T(8,128)S(1)}, f32[1,8,1024]{2,1,0:T(8,128)S(1)}, u32[]{:S(2)}, u32[]{:S(2)}) collective-permute-start(f32[1,8,1024]{2,1,0:T(8,128)S(1)} %get-tuple-element.24), channel_id=1, source_target_pairs={{0,96},{32,64},{64,32},{96,0},{1,97},{33,65},{65,33},{97,1},{2,98}... | collective-permute-start | bytes 98312 | tf_op jit(solution)/shard_map/ppermute | solution.py:278
  160.8 0.6 collective-permute-start.12
  161.4 0.3 collective-permute-start.11
  161.6 8.1 %all-to-all-done.1.cells_ref.refs_1_ = bf16[16,16,16,128]{3,2,1,0:T(8,128)(2,1)S(1)} async-done(((bf16[16,16,16,128]{3,2,1,0:T(8,128)(2,1)}), bf16[16,16,16,128]{3,2,1,0:T(8,128)(2,1)S(1)}, u32[]{:S(2)}, u32[]{:S(2)}) %all-to-all-start.1) | async-done | bytes 1048608 | tf_op jit(solution)/shard_map/all_to_all | solution.py:343
  169.7 3.4 %shard_map.39 = (bf16[32,8,1024]{2,1,0:T(8,128)(2,1)S(1)}, bf16[16,128,1024]{2,1,0:T(8,128)(2,1)S(1)}) custom-call(s32[1]{0:T(128)} %bitcast.1.place_ref, bf16[16,128,1024]{2,1,0:T(8,128)(2,1)} %bitcast.25, bf16[16,16,16,128]{3,2,1,0:T(8,128)(2,1)S(1)} %all-to-all-done.1.cells_ref.refs_1_), custom_call_target="tpu_custom_call" | custom-call | flops 1073741824 | bytes 7340032 | tf_op jit(solution)/shard_map/pallas_call | solution.py:190
  173.2 17.0 %all_to_all.25 = bf16[32,8,1024]{2,1,0:T(8,128)(2,1)S(1)} all-to-all(bf16[32,8,1024]{2,1,0:T(8,128)(2,1)S(1)} %get-tuple-element.19), channel_id=1, replica_groups=mesh['zh'=2,'x'=4,'c'=2,'y'=4,'zl'=4] {'c','y','x'}, dimensions={0} | all-to-all | bytes 1048576 | tf_op jit(solution)/shard_map/all_to_all | solution.py:286
  190.2 0.1 convert_reduce_fusion
  190.3 0.3 collective-permute-start.14
  190.6 7.0 %collective-permute-done.14 = f32[16,1024]{1,0:T(8,128)S(1)} collective-permute-done((f32[16,1024]{1,0:T(8,128)S(1)}, f32[16,1024]{1,0:T(8,128)S(1)}, u32[]{:S(2)}, u32[]{:S(2)}) %collective-permute-start.14) | collective-permute-done | bytes 65568 | tf_op jit(solution)/shard_map/ppermute | solution.py:303
  197.6 2.4 %collective-permute-start.17 = (f32[16,1024]{1,0:T(8,128)S(1)}, f32[16,1024]{1,0:T(8,128)S(1)}, u32[]{:S(2)}, u32[]{:S(2)}) collective-permute-start(f32[16,1024]{1,0:T(8,128)S(1)} %fusion.3), channel_id=1, source_target_pairs={{0,3},{1,2},{2,1},{3,0},{4,7},{5,6},{6,5},{7,4},{8,11},{9,10},{10,... | collective-permute-start | bytes 196616 | tf_op jit(solution)/shard_map/ppermute | solution.py:278
  199.9 3.8 %collective-permute-start.16 = (f32[16,1024]{1,0:T(8,128)S(1)}, f32[16,1024]{1,0:T(8,128)S(1)}, u32[]{:S(2)}, u32[]{:S(2)}) collective-permute-start(f32[16,1024]{1,0:T(8,128)S(1)} %fusion.3), channel_id=1, source_target_pairs={{0,2},{1,3},{2,0},{3,1},{4,6},{5,7},{6,4},{7,5},{8,10},{9,11},{10,... | collective-permute-start | bytes 196616 | tf_op jit(solution)/shard_map/ppermute | solution.py:278
  203.8 3.6 %collective-permute-done.16 = f32[16,1024]{1,0:T(8,128)S(1)} collective-permute-done((f32[16,1024]{1,0:T(8,128)S(1)}, f32[16,1024]{1,0:T(8,128)S(1)}, u32[]{:S(2)}, u32[]{:S(2)}) %collective-permute-start.16) | collective-permute-done | bytes 65568 | tf_op jit(solution)/shard_map/ppermute | solution.py:278
  207.4 0.2 collective-permute-done.15
  207.7 12.1 %all_to_all.26.coeffs_ref = bf16[16,16,1024]{2,1,0:T(8,128)(2,1)S(1)} all-to-all(bf16[16,16,1024]{2,1,0:T(8,128)(2,1)S(1)} %broadcast_in_dim.7), channel_id=1, replica_groups=mesh['zh'=2,'x'=4,'c'=2,'y'=4,'zl'=4] {'y','x'}, dimensions={0} | all-to-all | bytes 1048576 | tf_op jit(solution)/shard_map/all_to_all | solution.py:308
  219.8 4.6 %collective-permute-start.18 = (bf16[16,16,1024]{2,1,0:T(8,128)(2,1)S(1)}, bf16[16,16,1024]{2,1,0:T(8,128)(2,1)S(1)}, u32[]{:S(2)}, u32[]{:S(2)}) collective-permute-start(bf16[16,16,1024]{2,1,0:T(8,128)(2,1)S(1)} %all_to_all.26.coeffs_ref), channel_id=1, source_target_pairs={{0,16},{16,0},{1,17},{17,1},{2,18},{18,2},{3,19},{19,3},{4,20},{20... | collective-permute-start | bytes 1572872 | tf_op jit(solution)/shard_map/ppermute | solution.py:303
  224.4 2.7 %shard_map.43.refs_2_ = f32[16,32,16,128]{3,2,1,0:T(8,128)} custom-call(s32[1]{0:T(128)} %bitcast.half_ref, bf16[16,16,1024]{2,1,0:T(8,128)(2,1)S(1)} %all_to_all.26.coeffs_ref, bf16[16,128,1024]{2,1,0:T(8,128)(2,1)S(1)} %get-tuple-element.20.ritz_ref, bf16[16,16,16,128]{3,2,1,0:T(8,128)(2,1)S(1)} %all-to-all-done.2.cells_ref.refs_0_, ...), custom_call_target="tpu_custom_call" | custom-call | flops 1073741824 | bytes 4194304 | tf_op jit(solution)/shard_map/pallas_call | solution.py:246
  227.1 2.7 %shard_map.44 = f32[16,32,16,128]{3,2,1,0:T(8,128)} custom-call(s32[1]{0:T(128)S(6)} %sub.3.half_ref, bf16[16,16,1024]{2,1,0:T(8,128)(2,1)S(1)} %collective-permute-done.18.coeffs_ref, bf16[16,128,1024]{2,1,0:T(8,128)(2,1)S(1)} %get-tuple-element.20.ritz_ref, ...), custom_call_target="tpu_custom_call", output_to_operand_aliasing={{}: (5, {})} | custom-call | flops 1073741824 | bytes 4194304 | tf_op jit(solution)/shard_map/pallas_call | solution.py:246
  (28 shorter events, 0.4 us)
Async XLA Ops:
  0.0 9.0 %collective-permute-start.2 = (f32[8,2,128]{2,1,0:T(2,128)}, f32[8,2,128]{2,1,0:T(2,128)S(1)}, u32[]{:S(2)}, u32[]{:S(2)}) collective-permute-start(f32[8,2,128]{2,1,0:T(2,128)} %param.4), channel_id=1, source_target_pairs={{0,128},{128,0},{1,129},{129,1},{2,130},{130,2},{3,131},{131,3},{4... | collective-permute-start | bytes 24584 | tf_op jit(solution)/shard_map/ppermute | solution.py:303
  10.4 12.3 %all-to-all-start = ((f32[8,2,8,2,128]{4,3,1,2,0:T(2,128)}), f32[8,2,8,2,128]{4,3,1,2,0:T(2,128)S(1)}, u32[]{:S(2)}, u32[]{:S(2)}) async-start(f32[8,2,8,2,128]{4,3,1,2,0:T(2,128)} %broadcast_in_dim.6), calls=%async_computation | async-start | bytes 262144 | tf_op jit(solution)/shard_map/all_to_all | solution.py:308
  18.7 31.0 %collective-permute-start.5 = (bf16[4,32,16,128]{3,2,1,0:T(8,128)(2,1)S(1)}, bf16[4,32,16,128]{3,2,1,0:T(8,128)(2,1)S(1)}, u32[]{:S(2)}, u32[]{:S(2)}) collective-permute-start(bf16[4,32,16,128]{3,2,1,0:T(8,128)(2,1)S(1)} %get-tuple-element.16), channel_id=1, source_target_pairs={{0,1},{1,2},{2,3},{3,4},{4,5},{5,6},{6,7},{7,8},{8,9},{9,10},{10,1... | collective-permute-start | bytes 1572872 | tf_op jit(solution)/shard_map/ppermute | solution.py:313
  21.3 28.3 %collective-permute-start.6 = (bf16[4,32,16,128]{3,2,1,0:T(8,128)(2,1)S(1)}, bf16[4,32,16,128]{3,2,1,0:T(8,128)(2,1)S(1)}, u32[]{:S(2)}, u32[]{:S(2)}) collective-permute-start(bf16[4,32,16,128]{3,2,1,0:T(8,128)(2,1)S(1)} %get-tuple-element.17), channel_id=1, source_target_pairs={{1,0},{2,1},{3,2},{4,3},{5,4},{6,5},{7,6},{8,7},{9,8},{10,9},{11,1... | collective-permute-start | bytes 1572872 | tf_op jit(solution)/shard_map/ppermute | solution.py:314
  22.8 26.8 %collective-permute-start.4 = (f32[4,32,128]{2,1,0:T(8,128)S(1)}, f32[4,32,128]{2,1,0:T(8,128)S(1)}, u32[]{:S(2)}, u32[]{:S(2)}) collective-permute-start(f32[4,32,128]{2,1,0:T(8,128)S(1)} %bitcast.28), channel_id=1, source_target_pairs={{1,0},{2,1},{3,2},{4,3},{5,4},{6,5},{7,6},{8,7},{9,8},{10,9},{11,1... | collective-permute-start | bytes 196616 | tf_op jit(solution)/shard_map/ppermute | solution.py:314
  24.1 25.5 %collective-permute-start.3 = (f32[4,32,128]{2,1,0:T(8,128)S(1)}, f32[4,32,128]{2,1,0:T(8,128)S(1)}, u32[]{:S(2)}, u32[]{:S(2)}) collective-permute-start(f32[4,32,128]{2,1,0:T(8,128)S(1)} %bitcast.27), channel_id=1, source_target_pairs={{0,1},{1,2},{2,3},{3,4},{4,5},{5,6},{6,7},{7,8},{8,9},{9,10},{10,1... | collective-permute-start | bytes 196616 | tf_op jit(solution)/shard_map/ppermute | solution.py:313
  62.9 70.8 %all-to-all-start.2 = ((bf16[16,16,16,128]{3,2,1,0:T(8,128)(2,1)}), bf16[16,16,16,128]{3,2,1,0:T(8,128)(2,1)S(1)}, u32[]{:S(2)}, u32[]{:S(2)}) async-start(bf16[16,16,16,128]{3,2,1,0:T(8,128)(2,1)} %shard_map.41), calls=%async_computation.2 | async-start | bytes 2097152 | tf_op jit(solution)/shard_map/all_to_all | solution.py:343
  76.4 32.0 %collective-permute-start = (bf16[4,32,16,128]{3,2,1,0:T(8,128)(2,1)S(1)}, bf16[4,32,16,128]{3,2,1,0:T(8,128)(2,1)S(1)}, u32[]{:S(2)}, u32[]{:S(2)}) collective-permute-start(bf16[4,32,16,128]{3,2,1,0:T(8,128)(2,1)S(1)} %get-tuple-element.13), channel_id=1, source_target_pairs={{0,1},{1,2},{2,3},{3,4},{4,5},{5,6},{6,7},{7,8},{8,9},{9,10},{10,1... | collective-permute-start | bytes 1572872 | tf_op jit(solution)/shard_map/ppermute | solution.py:313
  78.7 41.8 %collective-permute-start.1 = (bf16[4,32,16,128]{3,2,1,0:T(8,128)(2,1)S(1)}, bf16[4,32,16,128]{3,2,1,0:T(8,128)(2,1)S(1)}, u32[]{:S(2)}, u32[]{:S(2)}) collective-permute-start(bf16[4,32,16,128]{3,2,1,0:T(8,128)(2,1)S(1)} %get-tuple-element.14), channel_id=1, source_target_pairs={{1,0},{2,1},{3,2},{4,3},{5,4},{6,5},{7,6},{8,7},{9,8},{10,9},{11,1... | collective-permute-start | bytes 1572872 | tf_op jit(solution)/shard_map/ppermute | solution.py:314
  133.8 35.9 %all-to-all-start.1 = ((bf16[16,16,16,128]{3,2,1,0:T(8,128)(2,1)}), bf16[16,16,16,128]{3,2,1,0:T(8,128)(2,1)S(1)}, u32[]{:S(2)}, u32[]{:S(2)}) async-start(bf16[16,16,16,128]{3,2,1,0:T(8,128)(2,1)} %shard_map.38), calls=%async_computation.1 | async-start | bytes 2097152 | tf_op jit(solution)/shard_map/all_to_all | solution.py:343
  146.8 2.0 collective-permute-start.7
  148.9 9.1 %collective-permute-start.10 = (f32[4,8,1024]{2,1,0:T(8,128)S(1)}, f32[4,8,1024]{2,1,0:T(8,128)S(1)}, u32[]{:S(2)}, u32[]{:S(2)}) collective-permute-start(f32[4,8,1024]{2,1,0:T(8,128)S(1)} %get-tuple-element.21), channel_id=1, source_target_pairs={{0,12},{4,8},{8,4},{12,0},{1,13},{5,9},{9,5},{13,1},{2,14},{6,10},... | collective-permute-start | bytes 393224 | tf_op jit(solution)/shard_map/ppermute | solution.py:278
  149.0 9.0 %collective-permute-start.9 = (f32[4,8,1024]{2,1,0:T(8,128)S(1)}, f32[4,8,1024]{2,1,0:T(8,128)S(1)}, u32[]{:S(2)}, u32[]{:S(2)}) collective-permute-start(f32[4,8,1024]{2,1,0:T(8,128)S(1)} %get-tuple-element.22), channel_id=1, source_target_pairs={{0,8},{4,12},{8,0},{12,4},{1,9},{5,13},{9,1},{13,5},{2,10},{6,14},... | collective-permute-start | bytes 393224 | tf_op jit(solution)/shard_map/ppermute | solution.py:278
  152.0 6.3 %collective-permute-start.8 = (f32[4,8,1024]{2,1,0:T(8,128)S(1)}, f32[4,8,1024]{2,1,0:T(8,128)S(1)}, u32[]{:S(2)}, u32[]{:S(2)}) collective-permute-start(f32[4,8,1024]{2,1,0:T(8,128)S(1)} %get-tuple-element.23), channel_id=1, source_target_pairs={{0,4},{4,0},{8,12},{12,8},{1,5},{5,1},{9,13},{13,9},{2,6},{6,2},{1... | collective-permute-start | bytes 393224 | tf_op jit(solution)/shard_map/ppermute | solution.py:278
  158.3 14.8 %collective-permute-start.13 = (f32[1,8,1024]{2,1,0:T(8,128)S(1)}, f32[1,8,1024]{2,1,0:T(8,128)S(1)}, u32[]{:S(2)}, u32[]{:S(2)}) collective-permute-start(f32[1,8,1024]{2,1,0:T(8,128)S(1)} %get-tuple-element.24), channel_id=1, source_target_pairs={{0,96},{32,64},{64,32},{96,0},{1,97},{33,65},{65,33},{97,1},{2,98}... | collective-permute-start | bytes 98312 | tf_op jit(solution)/shard_map/ppermute | solution.py:278
  160.8 12.4 %collective-permute-start.12 = (f32[1,8,1024]{2,1,0:T(8,128)S(1)}, f32[1,8,1024]{2,1,0:T(8,128)S(1)}, u32[]{:S(2)}, u32[]{:S(2)}) collective-permute-start(f32[1,8,1024]{2,1,0:T(8,128)S(1)} %get-tuple-element.25), channel_id=1, source_target_pairs={{0,64},{32,96},{64,0},{96,32},{1,65},{33,97},{65,1},{97,33},{2,66}... | collective-permute-start | bytes 98312 | tf_op jit(solution)/shard_map/ppermute | solution.py:278
  161.4 11.8 %collective-permute-start.11 = (f32[1,8,1024]{2,1,0:T(8,128)S(1)}, f32[1,8,1024]{2,1,0:T(8,128)S(1)}, u32[]{:S(2)}, u32[]{:S(2)}) collective-permute-start(f32[1,8,1024]{2,1,0:T(8,128)S(1)} %get-tuple-element.26), channel_id=1, source_target_pairs={{0,32},{32,0},{64,96},{96,64},{1,33},{33,1},{65,97},{97,65},{2,34}... | collective-permute-start | bytes 98312 | tf_op jit(solution)/shard_map/ppermute | solution.py:278
  190.3 7.3 %collective-permute-start.14 = (f32[16,1024]{1,0:T(8,128)S(1)}, f32[16,1024]{1,0:T(8,128)S(1)}, u32[]{:S(2)}, u32[]{:S(2)}) collective-permute-start(f32[16,1024]{1,0:T(8,128)S(1)} %pad_maximum_fusion.1), channel_id=1, source_target_pairs={{0,128},{128,0},{1,129},{129,1},{2,130},{130,2},{3,131},{131,3},{4... | collective-permute-start | bytes 196616 | tf_op jit(solution)/shard_map/ppermute | solution.py:303
  197.6 6.2 %collective-permute-start.17 = (f32[16,1024]{1,0:T(8,128)S(1)}, f32[16,1024]{1,0:T(8,128)S(1)}, u32[]{:S(2)}, u32[]{:S(2)}) collective-permute-start(f32[16,1024]{1,0:T(8,128)S(1)} %fusion.3), channel_id=1, source_target_pairs={{0,3},{1,2},{2,1},{3,0},{4,7},{5,6},{6,5},{7,4},{8,11},{9,10},{10,... | collective-permute-start | bytes 196616 | tf_op jit(solution)/shard_map/ppermute | solution.py:278
  199.9 7.5 %collective-permute-start.16 = (f32[16,1024]{1,0:T(8,128)S(1)}, f32[16,1024]{1,0:T(8,128)S(1)}, u32[]{:S(2)}, u32[]{:S(2)}) collective-permute-start(f32[16,1024]{1,0:T(8,128)S(1)} %fusion.3), channel_id=1, source_target_pairs={{0,2},{1,3},{2,0},{3,1},{4,6},{5,7},{6,4},{7,5},{8,10},{9,11},{10,... | collective-permute-start | bytes 196616 | tf_op jit(solution)/shard_map/ppermute | solution.py:278
  203.8 3.8 %collective-permute-start.15 = (f32[16,1024]{1,0:T(8,128)S(1)}, f32[16,1024]{1,0:T(8,128)S(1)}, u32[]{:S(2)}, u32[]{:S(2)}) collective-permute-start(f32[16,1024]{1,0:T(8,128)S(1)} %fusion.3), channel_id=1, source_target_pairs={{0,1},{1,0},{2,3},{3,2},{4,5},{5,4},{6,7},{7,6},{8,9},{9,8},{10,11... | collective-permute-start | bytes 196616 | tf_op jit(solution)/shard_map/ppermute | solution.py:278
  219.8 7.3 %collective-permute-start.18 = (bf16[16,16,1024]{2,1,0:T(8,128)(2,1)S(1)}, bf16[16,16,1024]{2,1,0:T(8,128)(2,1)S(1)}, u32[]{:S(2)}, u32[]{:S(2)}) collective-permute-start(bf16[16,16,1024]{2,1,0:T(8,128)(2,1)S(1)} %all_to_all.26.coeffs_ref), channel_id=1, source_target_pairs={{0,16},{16,0},{1,17},{17,1},{2,18},{18,2},{3,19},{19,3},{4,20},{20... | collective-permute-start | bytes 1572872 | tf_op jit(solution)/shard_map/ppermute | solution.py:303
